TPU v7x, 128 devices: a whole 4x4x4 slice. The times are simulated.
128 devices in a mesh: grp: 8 (over z, core), pair: 2 (over x_lo), tp: 8 (over y, x_hi).
Axes of the slice: x: 4 (x_hi: 2, x_lo: 2; x = x_hi * 2 + x_lo), y: 4, z: 4, core: 2. Of those that a mesh axis runs over, the one named last changes fastest.
Arguments:
- rescaled_signals: bfloat16 [2, 4096, 8192], P(None, ('grp', 'pair')), parts along dimension 1, may hold values from -6 to 6
- linear_matrix: bfloat16 [8192, 10240], P('pair', 'tp'), may hold values from -0.0625 to 0.0625
- linear_offset: bfloat16 [10240], P('tp'), may hold values from -4 to 4
- retained_turned_probes: bfloat16 [5120, 128, 1024], P(('grp', 'pair', 'tp')), parts along dimension 0, may hold values from -250 to 250
- retained_payload: bfloat16 [5120, 128, 1024], P(('grp', 'pair', 'tp')), parts along dimension 0, may hold values from -6 to 6
- filled_extents: int32 [5120], P(('grp', 'pair', 'tp')), parts along dimension 0, may hold values from 1 to 128
- prior_owner_lines: int32 [4096], P('grp'), parts along dimension 0, may hold values from 0 to 639, as said below
Outputs:
- blended_result: bfloat16 [2, 4096, 8192], P(None, ('grp', 'pair'), 'tp'), parts along dimension 1
There are 8 independent parts, one for each index of `grp`. A program takes and returns all parts, laid end to end along the dimension named above; an argument that names none is the same for every part. Nothing has to cross between parts.
Inputs may be any that keep to these rules, and one draw needn't show every extreme that they name: `prior_owner_lines`: 512 distinct old rows.
All inputs are finite; a program needn't handle non-finite values.
Results may differ from a plain program's by a relative error of at most 0.0105.
The roundings to bfloat16 on the way count: a program that leaves them out, or rounds other values in their place, can miss the bound.
Values may be sent and summed in bfloat16 or wider, within the bound.
No kernel may reach another device: no remote copies, remote signals or barrier semaphores. Data moves between devices by JAX's collectives and lax.ppermute only.
A program may use at most 192 MiB of HBM per device.

v0:
```python
import jax
import jax.numpy as jnp
from jax import lax
from jax.sharding import PartitionSpec as P

ASKING_STREAMS = 64
RECALL_STREAMS = 8
FOCUS_BREADTHS = 128


ROPE_BASE = 1000000.0


def rope_angles(positions, head_dim):
    frequency = ROPE_BASE ** (-jnp.arange(0, head_dim, 2, dtype=jnp.float32) / head_dim)
    angles = positions.astype(jnp.float32)[..., None] * frequency
    cosine = jnp.cos(angles)
    sine_table = jnp.sin(angles)
    return (jnp.concatenate([cosine, cosine], -1), jnp.concatenate([sine_table, sine_table], -1))


def rotate(values, cosine, sine_table):
    front_half, back_half = jnp.split(values, 2, axis=-1)
    return values * cosine + jnp.concatenate([-back_half, front_half], -1) * sine_table


def attend(local_projection, retained_turned_probes, retained_payload, filled_extents):
    step_count = local_projection.shape[0]
    prior_owner = local_projection.shape[1]
    cache_capacity = retained_turned_probes.shape[1]
    group_list = ASKING_STREAMS // RECALL_STREAMS
    compacted_records = local_projection.reshape(
        step_count, prior_owner, RECALL_STREAMS, group_list + 2, FOCUS_BREADTHS
    )
    queries = compacted_records[:, :, :, :group_list, :]
    new_keys = compacted_records[:, :, :, group_list, :]
    new_values = compacted_records[:, :, :, group_list + 1, :]
    positions = filled_extents[None, :] + jnp.arange(step_count, dtype=jnp.int32)[:, None]
    cosine, sine_table = rope_angles(positions, FOCUS_BREADTHS)
    q_rot = rotate(
        queries.astype(jnp.float32), cosine[:, :, None, None, :], sine_table[:, :, None, None, :]
    ).astype(jnp.bfloat16)
    k_rot = rotate(
        new_keys.astype(jnp.float32), cosine[:, :, None, :], sine_table[:, :, None, :]
    ).astype(jnp.bfloat16)
    chance_starters = retained_turned_probes.reshape(
        prior_owner, cache_capacity, RECALL_STREAMS, FOCUS_BREADTHS
    )
    stashed_recall = retained_payload.reshape(
        prior_owner, cache_capacity, RECALL_STREAMS, FOCUS_BREADTHS
    )
    scale = FOCUS_BREADTHS ** (-0.5)
    cache_scores = (
        jnp.einsum("srkgd,rlkd->srkgl", q_rot, chance_starters, preferred_element_type=jnp.float32)
        * scale
    )
    valid = jnp.arange(cache_capacity, dtype=jnp.int32)[None, :] < filled_extents[:, None]
    cache_scores = jnp.where(valid[None, :, None, None, :], cache_scores, -1e30)
    new_scores = (
        jnp.einsum("srkgd,trkd->srkgt", q_rot, k_rot, preferred_element_type=jnp.float32) * scale
    )
    causal = jnp.arange(step_count)[:, None] >= jnp.arange(step_count)[None, :]
    new_scores = jnp.where(causal[:, None, None, None, :], new_scores, -1e30)
    joined = jnp.concatenate([cache_scores, new_scores], -1)
    top_score = jnp.max(joined, axis=-1, keepdims=True)
    expo = jnp.exp(joined - top_score)
    weights = (expo / jnp.sum(expo, axis=-1, keepdims=True)).astype(jnp.bfloat16)
    blended_result = jnp.einsum(
        "srkgl,rlkd->srkgd",
        weights[..., :cache_capacity],
        stashed_recall,
        preferred_element_type=jnp.float32,
    )
    blended_result = blended_result + jnp.einsum(
        "srkgt,trkd->srkgd",
        weights[..., cache_capacity:],
        new_values,
        preferred_element_type=jnp.float32,
    )
    return blended_result.astype(jnp.bfloat16)


def per_device(
    rescaled_signals,
    linear_matrix,
    linear_offset,
    retained_turned_probes,
    retained_payload,
    filled_extents,
    prior_owner_lines,
):
    couple_number = lax.axis_size("pair")
    n_tp = lax.axis_size("tp")
    groups_all = couple_number * n_tp
    counterpart_position = lax.axis_index("pair")
    tp_index = lax.axis_index("tp")
    my_device = counterpart_position * n_tp + tp_index
    step_count = rescaled_signals.shape[0]
    sequence_midpoint = rescaled_signals.shape[1]
    prior_owner = filled_extents.shape[0]
    columns = linear_matrix.shape[1]
    unrolled_array = rescaled_signals.reshape(
        step_count * sequence_midpoint, rescaled_signals.shape[2]
    )
    transformed_records = jnp.dot(
        unrolled_array,
        lax.all_gather(linear_matrix, "pair", axis=0, tiled=True),
        preferred_element_type=jnp.float32,
    )
    qkv_rows = (
        (transformed_records + linear_offset.astype(jnp.float32))
        .astype(jnp.bfloat16)
        .reshape(step_count, sequence_midpoint, columns)
    )
    sequences_belonging = lax.dynamic_slice_in_dim(
        prior_owner_lines, counterpart_position * sequence_midpoint, sequence_midpoint
    )
    target = sequences_belonging // prior_owner
    dest_hot = (target[:, None] == jnp.arange(groups_all, dtype=jnp.int32)[None, :]).astype(
        jnp.int32
    )
    before = jnp.cumsum(dest_hot, axis=0) - dest_hot
    my_rank = jnp.sum(before * dest_hot, axis=1)
    slot_index = target * prior_owner + my_rank
    packer = (
        jnp.arange(groups_all * prior_owner, dtype=jnp.int32)[:, None] == slot_index[None, :]
    ).astype(jnp.bfloat16)
    packer = packer.reshape(groups_all, prior_owner, sequence_midpoint)
    outgoing = jnp.einsum(
        "gcr,srn->gscn", packer, qkv_rows, preferred_element_type=jnp.float32
    ).astype(jnp.bfloat16)
    incoming = lax.all_to_all(outgoing, ("pair", "tp"), split_axis=0, concat_axis=0, tiled=True)
    incoming = incoming.reshape(couple_number, n_tp, step_count, prior_owner, columns)
    sequence_finder = prior_owner_lines.reshape(couple_number, sequence_midpoint)
    mine = (sequence_finder // prior_owner == my_device).astype(jnp.int32)
    owner_rank = jnp.cumsum(mine, axis=1) - mine
    local_row = sequence_finder % prior_owner
    local_hot = jnp.where(
        (local_row[..., None] == jnp.arange(prior_owner, dtype=jnp.int32)) & (mine[..., None] == 1),
        1.0,
        0.0,
    )
    rank_hot = jnp.where(
        owner_rank[..., None] == jnp.arange(prior_owner, dtype=jnp.int32), 1.0, 0.0
    )
    selector = jnp.einsum("prj,prc->jpc", local_hot, rank_hot).astype(jnp.bfloat16)
    local_projection = jnp.einsum(
        "jpc,ptscn->sjtn", selector, incoming, preferred_element_type=jnp.float32
    ).astype(jnp.bfloat16)
    attended = attend(local_projection, retained_turned_probes, retained_payload, filled_extents)
    head_cols = ASKING_STREAMS // n_tp * FOCUS_BREADTHS
    attended = attended.reshape(step_count, prior_owner, n_tp, head_cols)
    replies = jnp.einsum(
        "jpc,sjtn->ptscn", selector, attended, preferred_element_type=jnp.float32
    ).astype(jnp.bfloat16)
    returned = lax.all_to_all(
        replies.reshape(groups_all, step_count, prior_owner, head_cols),
        ("pair", "tp"),
        split_axis=0,
        concat_axis=0,
        tiled=True,
    )
    return jnp.einsum("gcr,gscn->srn", packer, returned, preferred_element_type=jnp.float32).astype(
        jnp.bfloat16
    )


def solution(mesh):
    in_specs = (
        P(None, ("grp", "pair"), None),
        P("pair", "tp"),
        P("tp"),
        P(("grp", "pair", "tp"), None, None),
        P(("grp", "pair", "tp"), None, None),
        P(("grp", "pair", "tp")),
        P("grp"),
    )
    out_specs = P(None, ("grp", "pair"), "tp")
    return jax.shard_map(
        per_device, mesh=mesh, in_specs=in_specs, out_specs=out_specs, check_vma=False
    )
```

profile of v0, /device:TPU:4, one launch (start us, length us, event | category | flops | bytes accessed | tf_op | source)
XLA Modules:
  0.0 421.6 jit_solution(1415152316937447867)
XLA Ops:
  6.5 0.7 all-gather.2.cloned.1.call-update
  7.4 0.6 reduce-window.16
  8.0 0.2 slice_reduce_fusion.1
  8.2 0.2 reduce-window.19
  8.5 0.6 reduce-window.14
  9.1 0.2 slice_reduce_fusion
  9.3 0.1 and_select_fusion.2
  9.4 0.1 fusion.44
  9.5 0.2 multiply_cosine_fusion
  9.7 0.1 pad_maximum_fusion
  9.8 0.1 multiply_add_fusion.1
  10.0 251.0 %all-gather.2.cloned.1.call-done = bf16[8192,1280]{1,0:T(8,128)(2,1)} async-done(((bf16[4096,1280]{1,0:T(8,128)(2,1)}), bf16[8192,1280]{1,0:T(8,128)(2,1)}) %all-gather.2.cloned.1.call-update) | async-done | bytes 20971536 | tf_op jit(solution)/shard_map/all_gather | solution.py:107
  261.0 16.6 %fusion.7 = bf16[512,1280]{1,0:T(8,128)(2,1)S(1)} fusion(bf16[512,8192]{1,0:T(8,128)(2,1)} %bitcast.144, bf16[8192,1280]{1,0:T(8,128)(2,1)} %all-gather.2.cloned.1.call-done, f32[1280]{0:T(1024)S(1)} %convert_element_type.85), kind=kOutput, calls=%fused_computation.14 | convolution fusion | flops 10738728960 | bytes 30675968 | tf_op jit(solution)/shard_map/dot_general | solution.py:105
  277.6 1.1 fusion.6
  278.6 1.9 copy.102
  280.5 7.3 %all-to-all-start = ((bf16[16,2,40,1280]{3,2,1,0:T(8,128)(2,1)}), bf16[16,2,40,1280]{3,2,1,0:T(8,128)(2,1)S(1)}, u32[]{:S(2)}, u32[]{:S(2)}) async-start(bf16[16,2,40,1280]{3,2,1,0:T(8,128)(2,1)} %copy.102), calls=%async_computation | async-start | bytes 6553600 | tf_op jit(solution)/shard_map/all_to_all | solution.py:132
  287.8 0.5 iota_compare_fusion.6
  288.4 10.7 %copy.144 = bf16[640,8,8,128]{3,2,1,0:T(8,128)(2,1)} copy(bf16[640,8,8,128]{3,1,2,0:T(8,128)(2,1)} %bitcast.137) | data formatting | bytes 20971520
  299.0 10.7 %copy.145 = bf16[640,8,8,128]{3,2,1,0:T(8,128)(2,1)} copy(bf16[640,8,8,128]{3,1,2,0:T(8,128)(2,1)} %bitcast.138) | data formatting | bytes 20971520
  309.8 0.1 convolution_convert_fusion.1
  309.9 9.0 %bitcast_bitcast_fusion.1 = bf16[40,128,8,128,1]{3,2,1,0,4:T(8,128)(2,1)} fusion(bf16[40,128,8,128]{3,2,1,0:T(8,128)(2,1)} %bitcast.131), kind=kLoop, calls=%fused_computation.1 | loop fusion | bytes 20971520 | tf_op jit(solution)/shard_map/reshape | solution.py:46
  319.0 9.2 %bitcast_bitcast_fusion = bf16[40,128,8,128,1]{3,2,1,0,4:T(8,128)(2,1)} fusion(bf16[40,128,8,128]{3,2,1,0:T(8,128)(2,1)} %bitcast.130), kind=kLoop, calls=%fused_computation | loop fusion | bytes 20971520 | tf_op jit(solution)/shard_map/reshape | solution.py:49
  328.1 6.7 %all-to-all-done = bf16[16,2,40,1280]{3,2,1,0:T(8,128)(2,1)S(1)} async-done(((bf16[16,2,40,1280]{3,2,1,0:T(8,128)(2,1)}), bf16[16,2,40,1280]{3,2,1,0:T(8,128)(2,1)S(1)}, u32[]{:S(2)}, u32[]{:S(2)}) %all-to-all-start) | async-done | bytes 3276832 | tf_op jit(solution)/shard_map/all_to_all | solution.py:132
  334.8 0.6 fusion.39
  335.5 0.1 copy.172
  335.6 0.3 copy.173
  335.9 0.3 slice_convert_fusion
  336.3 1.1 slice_negate_fusion
  337.4 0.2 slice_negate_fusion.1
  337.5 1.1 fusion.9
  338.6 0.2 fusion.27
  338.8 0.9 copy-done
  339.7 6.1 %fusion.18 = f32[40,8,2,2,8]{4,2,3,1,0:T(2,128)S(1)} fusion(bf16[2,40,8,8,128]{4,2,3,1,0:T(8,128)(2,1)S(1)} %fusion.9, bf16[2,40,8,128,1]{3,2,1,0,4:T(8,128)(2,1)S(1)} %fusion.27), kind=kOutput, calls=%fused_computation.31 | convolution fusion | flops 2621440 | bytes 1515520 | tf_op jit(solution)/shard_map/srkgd,trkd->srkgt/dot_general | solution.py:60
  345.7 0.5 copy.110
  346.3 0.3 copy.112
  346.6 2.3 copy.111
  349.0 8.8 %fusion.50 = (f32[2,40,8,8]{3,0,2,1:T(2,128)S(1)}, f32[2,40,8,8,128]{4,3,0,2,1:T(8,128)S(1)}) fusion(bf16[40,128,8,128,1]{3,2,1,0,4:T(8,128)(2,1)} %bitcast_bitcast_fusion.1, bf16[2,40,8,8,128]{4,2,3,1,0:T(8,128)(2,1)} %copy-done, pred[40,128]{1,0:T(8,128)(4,1)S(1)} %iota_compare_fusion.3), kind=kOutput, calls=%fused_computation.102 | convolution fusion | flops 169733120 | bytes 14443520 | tf_op jit(solution)/shard_map/srkgd,rlkd->srkgl/dot_general | solution.py:54
  357.9 0.2 reduce_max.22
  358.0 1.8 fusion.5
  359.9 1.8 divide_convert_fusion
  361.7 2.8 fusion
  364.5 0.6 fusion.10
  365.1 0.6 reshape.214
  365.7 2.1 convert_bitcast_fusion
  367.8 0.3 copy.117
  368.2 43.9 %all_to_all.10 = bf16[16,2,40,1024]{3,2,1,0:T(8,128)(2,1)S(1)} all-to-all(bf16[16,2,40,1024]{3,2,1,0:T(8,128)(2,1)S(1)} %bitcast.139), channel_id=1, replica_groups=mesh['grp'=8,'pair'=2,'tp'=8] {'pair','tp'}, dimensions={0} | all-to-all | bytes 5242880 | tf_op jit(solution)/shard_map/all_to_all | solution.py:156
  412.1 1.3 fusion.14
  413.4 1.3 copy.118
  (42 shorter events, 0.6 us)
Async XLA Ops:
  6.5 0.7 copy-start.1
  6.5 2.8 copy-start.4
  6.5 3.0 copy-start.6
  6.5 254.5 %all-gather.2.cloned.1.call-start = ((), (), s32[]{:S(2)}) async-start(), calls=%async_computation.2 | async-start | bytes 31457280 | tf_op jit(solution)/shard_map/all_gather | solution.py:107
  9.4 268.2 %copy-start.2 = (s32[16,40]{1,0:T(8,128)}, s32[16,40]{1,0:T(8,128)S(1)}, u32[]{:S(2)}) copy-start(s32[16,40]{1,0:T(8,128)S(1)} %multiply_add_fusion) | copy-start | bytes 7684
  280.5 54.3 %all-to-all-start = ((bf16[16,2,40,1280]{3,2,1,0:T(8,128)(2,1)}), bf16[16,2,40,1280]{3,2,1,0:T(8,128)(2,1)S(1)}, u32[]{:S(2)}, u32[]{:S(2)}) async-start(bf16[16,2,40,1280]{3,2,1,0:T(8,128)(2,1)} %copy.102), calls=%async_computation | async-start | bytes 6553600 | tf_op jit(solution)/shard_map/all_to_all | solution.py:132
  338.6 1.1 copy-start
  338.6 7.6 %copy-start.5 = (pred[2,2]{0,1:T(4,128)(4,1)S(1)}, pred[2,2]{0,1:T(4,128)(4,1)}, u32[]{:S(2)}) copy-start(pred[2,2]{0,1:T(4,128)(4,1)} %iota_compare_fusion.6) | copy-start | bytes 16
  349.0 12.7 %slice-start = ((s8[10485760]{0:T(1024)(128)(4,1)}), s8[4194304]{0:T(1024)(128)(4,1)S(1)}, s32[]{:S(2)}) async-start(s8[10485760]{0:T(1024)(128)(4,1)} %bitcast.128), calls=%async_computation.3 | async-start | bytes 8388608
  349.0 12.7 %slice-start.1 = ((s8[10485760]{0:T(1024)(128)(4,1)}), s8[2097152]{0:T(1024)(128)(4,1)S(1)}, s32[]{:S(2)}) async-start(s8[10485760]{0:T(1024)(128)(4,1)} %bitcast.128), calls=%async_computation.4 | async-start | bytes 4194304
  358.0 3.6 slice-start.2
  368.1 43.9 %copy-start.3 = (s32[16,40]{1,0:T(8,128)S(1)}, s32[16,40]{1,0:T(8,128)}, u32[]{:S(2)}) copy-start(s32[16,40]{1,0:T(8,128)} %copy-done.2) | copy-start | bytes 7684
Sparse Core Ops, SparseCore 0:
  9.0 251.9 all-gather.1
where the time goes:
time: 422 us
  waiting for transfers between devices  258 us (61%)
  local copies, waits for them, and re-layouts  48.6 us (12%)
  blocking collectives  43.9 us (10%)
  matrix products  40.1 us (10%)
  between operations  13.7 us (3%)
  other arithmetic  9.55 us (2%)
  starting transfers between devices  7.28 us (2%)
    all_gather x1, waiting for transfers between devices, per_device(): lax.all_gather(linear_matrix, 'pair', axis=0, tiled=True)  251 us
    all_to_all x1, blocking collectives, per_device(): lax.all_to_all(replies.reshape(groups_all, step_count, prior_owner, head_...  43.9 us
    unnamed x22, local copies, waits for them, and re-layouts  22.2 us
    dot_general x1, matrix products, per_device(): jnp.dot(unrolled_array, lax.all_gather(linear_matrix, 'pair', axis=0, til...  16.6 us
    reshape x1, local copies, waits for them, and re-layouts, attend(): retained_payload.reshape(prior_owner, cache_capacity, RECALL_STREAMS, FOC...  9.18 us
    reshape x1, local copies, waits for them, and re-layouts, attend(): retained_turned_probes.reshape(prior_owner, cache_capacity, RECALL_STREAM...  9.03 us
    dot_general x1, matrix products, attend(): jnp.einsum('srkgd,rlkd->srkgl', q_rot, chance_starters, preferred_element...  8.85 us
  transfers between devices with their start and end apart: 2, of which 2 were waited for; matrix products, arithmetic and copies ran while one was open for 10% of the time, Pallas kernels for 0%

commit v1 on v0

v1 whole, which is shorter than its diff:
```python
import functools

import jax
import jax.numpy as jnp
from jax import lax
from jax.experimental import pallas as pl
from jax.experimental.pallas import tpu as pltpu
from jax.sharding import PartitionSpec as P

HEAD = 128
SHARING = 8
ROPE_BASE = 1000000.0
SWAP = ((0, 1), (1, 0))
CHUNKS = ((4, 8), (0, 4))


def rope_tables(positions):
    frequency = ROPE_BASE ** (-jnp.arange(0, HEAD, 2, dtype=jnp.float32) / HEAD)
    angles = positions.astype(jnp.float32)[..., None] * frequency
    cosine = jnp.cos(angles)
    sine = jnp.sin(angles)
    return jnp.concatenate([cosine, cosine], -1), jnp.concatenate([-sine, sine], -1)


def attention_kernel(heads, rows, fill_ref, cos_ref, sin_ref, q_ref, k_new_ref, v_new_ref,
                     k_ref, v_ref, out_ref, q_rot, k_rot, v_new, blended):
    scale = HEAD ** (-0.5)
    width = 2 * heads

    def turned(values, step):
        values = values.astype(jnp.float32)
        turn = values * cos_ref[step] + pltpu.roll(values, HEAD // 2, 1) * sin_ref[step]
        return turn.astype(jnp.bfloat16).astype(jnp.float32)

    for step in range(2):
        for head in range(heads):
            block = q_ref[step, 0, :, head * HEAD:(head + 1) * HEAD]
            q_rot[pl.ds((step * heads + head) * rows, rows), :] = turned(block, step)
        k_rot[pl.ds(step * rows, rows), :] = turned(k_new_ref[step, 0], step)
        v_new[pl.ds(step * rows, rows), :] = v_new_ref[step, 0].astype(jnp.float32)

    place = lax.broadcasted_iota(jnp.int32, (width, HEAD), 1)
    second = lax.broadcasted_iota(jnp.int32, (width, 1), 0) >= heads

    def group(base, carry):
        for inner in range(8):
            row = base * 8 + inner
            q = q_rot[pl.ds(row, width, stride=rows), :]
            scores = lax.dot_general(
                q.astype(jnp.bfloat16), k_ref[row], (((1,), (1,)), ((), ())),
                preferred_element_type=jnp.float32,
            ) * scale
            scores = jnp.where(place < fill_ref[row], scores, -1e30)
            first_new = jnp.sum(q * k_rot[pl.ds(row, 1), :], -1, keepdims=True) * scale
            second_new = jnp.sum(q * k_rot[pl.ds(rows + row, 1), :], -1, keepdims=True) * scale
            second_new = jnp.where(second, second_new, -1e30)
            top = jnp.maximum(
                jnp.max(scores, -1, keepdims=True), jnp.maximum(first_new, second_new)
            )
            expo = jnp.exp(scores - top)
            expo_first = jnp.exp(first_new - top)
            expo_second = jnp.exp(second_new - top)
            total = jnp.sum(expo, -1, keepdims=True) + expo_first + expo_second
            share = 1.0 / total
            mixed = jnp.dot(
                (expo * share).astype(jnp.bfloat16), v_ref[row],
                preferred_element_type=jnp.float32,
            )
            w_first = (expo_first * share).astype(jnp.bfloat16).astype(jnp.float32)
            w_second = (expo_second * share).astype(jnp.bfloat16).astype(jnp.float32)
            mixed = mixed + w_first * v_new[pl.ds(row, 1), :]
            mixed = mixed + w_second * v_new[pl.ds(rows + row, 1), :]
            blended[pl.ds(row, width, stride=rows), :] = mixed
        return carry

    lax.fori_loop(0, rows // 8, group, 0)
    for step in range(2):
        for head in range(heads):
            done = blended[pl.ds((step * heads + head) * rows, rows), :].astype(jnp.bfloat16)
            for pair in range(2):
                out_ref[pair, 0, step, :, head * HEAD:(head + 1) * HEAD] = done


def attend(fill, cosine, sine, queries, q_at, new, k_at, keys, values, heads):
    _, n_tp, rows, _ = queries.shape
    places = keys.shape[1]
    width = 2 * heads * rows
    table = pl.BlockSpec((2, rows, HEAD), lambda t, f: (0, 0, 0))
    cache = pl.BlockSpec((rows, places, HEAD), lambda t, f: (0, 0, t))
    return pl.pallas_call(
        functools.partial(attention_kernel, heads, rows),
        out_shape=jax.ShapeDtypeStruct((2, n_tp, 2, rows, heads * HEAD), jnp.bfloat16),
        grid_spec=pltpu.PrefetchScalarGridSpec(
            num_scalar_prefetch=1,
            grid=(n_tp,),
            in_specs=[
                table,
                table,
                pl.BlockSpec((2, 1, rows, heads * HEAD), lambda t, f: (0, t, 0, q_at)),
                pl.BlockSpec((2, 1, rows, HEAD), lambda t, f: (0, t, 0, k_at)),
                pl.BlockSpec((2, 1, rows, HEAD), lambda t, f: (0, t, 0, k_at + 1)),
                cache,
                cache,
            ],
            out_specs=pl.BlockSpec((2, 1, 2, rows, heads * HEAD), lambda t, f: (0, t, 0, 0, 0)),
            scratch_shapes=[
                pltpu.VMEM((width, HEAD), jnp.float32),
                pltpu.VMEM((2 * rows, HEAD), jnp.float32),
                pltpu.VMEM((2 * rows, HEAD), jnp.float32),
                pltpu.VMEM((width, HEAD), jnp.float32),
            ],
        ),
        compiler_params=pltpu.CompilerParams(vmem_limit_bytes=32 << 20),
        cost_estimate=pl.CostEstimate(
            flops=4 * width * n_tp * places * HEAD,
            transcendentals=width * n_tp * places,
            bytes_accessed=4 * rows * places * n_tp * HEAD,
        ),
    )(
        fill, cosine, sine, queries, new, new,
        pltpu.with_memory_space_constraint(keys, pltpu.HBM),
        pltpu.with_memory_space_constraint(values, pltpu.HBM),
    )


def per_device(signals, matrix, offset, cached_keys, cached_values, fill, lines):
    n_pair, n_tp, n_grp = (lax.axis_size(a) for a in ("pair", "tp", "grp"))
    pair, tp, grp = (lax.axis_index(a) for a in ("pair", "tp", "grp"))
    share, features = signals.shape[1:]
    half = matrix.shape[0]
    rows = fill.shape[0]
    owners = n_pair * n_tp

    n_y = n_tp // 2
    y = tp // 2
    piece = share // n_y
    depth = half // n_grp
    mine = lax.dynamic_index_in_dim(signals, pair, 0, keepdims=False)
    theirs = lax.dynamic_index_in_dim(signals, 1 - pair, 0, keepdims=False)
    sent = lax.dynamic_slice_in_dim(theirs, y * piece, piece)
    sent_first, sent_second = sent[:piece // 2], sent[piece // 2:]
    slab = lax.dynamic_slice_in_dim(matrix, grp * depth, depth)
    spans = [
        (start * HEAD, (stop + 2 if stop == SHARING else stop) * HEAD) for start, stop in CHUNKS
    ]
    up = [(2 * a + h, 2 * ((a + 1) % n_y) + h) for a in range(n_y) for h in range(2)]
    down = [(d, s) for s, d in up]

    def after(value, *earlier):
        return lax.optimization_barrier((value, *earlier))[0]

    near_first = lax.ppermute(sent_first, "pair", SWAP)
    moved = lax.ppermute(slab[:, slice(*spans[0])], "pair", SWAP)
    far = [lax.all_gather(moved, "grp", axis=0, tiled=True)]
    near_second = lax.ppermute(after(sent_second, near_first, moved), "pair", SWAP)
    for span in spans[1:]:
        moved = lax.ppermute(after(slab[:, slice(*span)], near_second, moved), "pair", SWAP)
        far.append(lax.all_gather(after(moved, far[-1]), "grp", axis=0, tiled=True))
    below_first = lax.ppermute(near_first, "tp", up)
    above_first = lax.ppermute(near_first, "tp", down)
    below_second = lax.ppermute(near_second, "tp", up)
    above_second = lax.ppermute(near_second, "tp", down)
    far_first = lax.ppermute(below_first, "tp", up)
    far_second = lax.ppermute(above_second, "tp", down)
    theirs = jnp.concatenate(
        [near_first, near_second, below_first, below_second, above_first, above_second,
         far_first, far_second], 0
    )
    listed = [lax.dynamic_slice_in_dim(lines, pair * share, share)] + [
        lax.dynamic_slice_in_dim(
            lines, (1 - pair) * share + (y + turn) % n_y * piece, piece
        )
        for turn in (0, n_y - 1, 1, 2)
    ]
    listed = jnp.concatenate(listed)
    pack = (
        jnp.arange(owners * rows, dtype=jnp.int32)[:, None] == listed[None, :]
    ).astype(jnp.bfloat16)

    def split(block):
        return (
            lax.dynamic_slice_in_dim(block, pair * half, half, 1),
            lax.dynamic_slice_in_dim(block, (1 - pair) * half, half, 1),
        )

    mine_near, mine_far = split(mine)
    theirs_near, theirs_far = split(theirs)
    all_far = jnp.concatenate([mine_far, theirs_far], 0)
    f32 = functools.partial(jnp.dot, preferred_element_type=jnp.float32)
    mine_sum = f32(mine_near, matrix)
    theirs_sum = f32(theirs_near, matrix)
    partial = jnp.concatenate([mine_sum, theirs_sum], 0) + offset.astype(jnp.float32)

    positions = fill[None, :] + jnp.arange(2, dtype=jnp.int32)[:, None]
    cosine, sine = rope_tables(positions)
    own = lax.dynamic_slice_in_dim(lines, pair * share, share)
    pick = (
        own[:, None] == jnp.arange(owners * rows, dtype=jnp.int32)[None, :]
    ).astype(jnp.bfloat16).reshape(share, owners, rows)

    outs, new, k_at = {}, None, None
    for (start, stop), remote in zip(CHUNKS, far):
        end = stop + 2 if stop == SHARING else stop
        projected = partial[:, start * HEAD:end * HEAD] + f32(all_far, remote)
        packed = f32(pack, projected.astype(jnp.bfloat16)).astype(jnp.bfloat16)
        packed = packed.reshape(owners, rows, (end - start) * HEAD)
        arrived = lax.all_to_all(
            packed, ("pair", "tp"), split_axis=0, concat_axis=0, tiled=True
        ).reshape(n_pair, n_tp, rows, (end - start) * HEAD)
        if new is None:
            new, k_at = arrived, stop - start
        attended = attend(
            fill, cosine, sine, arrived, 0, new, k_at, cached_keys, cached_values, stop - start
        )
        back = lax.all_to_all(
            attended.reshape(owners, 2, rows, (stop - start) * HEAD),
            ("pair", "tp"), split_axis=0, concat_axis=0, tiled=True,
        )
        outs[start] = jnp.einsum(
            "rgj,gsjn->srn", pick, back, preferred_element_type=jnp.float32
        ).astype(jnp.bfloat16)
    return jnp.concatenate([outs[k] for k in sorted(outs)], -1)


def solution(mesh):
    in_specs = (
        P(None, ("grp", "pair"), None),
        P("pair", "tp"),
        P("tp"),
        P(("grp", "pair", "tp"), None, None),
        P(("grp", "pair", "tp"), None, None),
        P(("grp", "pair", "tp")),
        P("grp"),
    )
    out_specs = P(None, ("grp", "pair"), "tp")
    return jax.shard_map(
        per_device, mesh=mesh, in_specs=in_specs, out_specs=out_specs, check_vma=False
    )
```

time: 422 us -> 399 us (0.945)
  Pallas kernels: 0 us -> 221 us
  waiting for transfers between devices: 258 us -> 63.7 us
  blocking collectives: 43.9 us -> 0 us
  starting transfers between devices: 7.28 us -> 38.2 us
  local copies, waits for them, and re-layouts: 48.6 us -> 24.6 us
  other arithmetic: 9.55 us -> 0.58 us
    all_gather x1 -> x2, waiting for transfers between devices: 251 us -> 0.02 us  [the longest x1 0.02 us: per_device(): far.append(lax.all_gather(after(moved, far[-1]), 'grp', axis=0, tiled=True))]
    pallas_call x0 -> x2, Pallas kernels: none -> 221 us  [attend(): pl.pallas_call(functools.partial(attention_kernel, heads, rows), out_shap...]
    all_to_all x1 -> x0, blocking collectives: 43.9 us -> none  [per_device(): lax.all_to_all(replies.reshape(groups_all, step_count, prior_owner, head_...]
    ppermute x0 -> x10, waiting for transfers between devices: none -> 41.9 us  [the longest x1 18.1 us: per_device(): moved = lax.ppermute(slab[:, slice(*spans[0])], 'pair', SWAP)]
    reshape x3 -> x0, local copies, waits for them, and re-layouts: 18.8 us -> none  [the longest x1 9.18 us: attend(): retained_payload.reshape(prior_owner, cache_capacity, RECALL_STREAMS, FOC...]
    all_to_all x1 -> x4, starting transfers between devices: 7.27 us -> 24.5 us  [the longest x2 14.4 us: per_device(): lax.all_to_all(attended.reshape(owners, 2, rows, (stop - start) * HEAD),...]
    all_to_all x1 -> x4, waiting for transfers between devices: 6.7 us -> 21.7 us  [the longest x2 16.8 us: per_device(): lax.all_to_all(attended.reshape(owners, 2, rows, (stop - start) * HEAD),...]
    ppermute x0 -> x10, starting transfers between devices: none -> 13.7 us  [the longest x1 2.78 us: per_device(): far_second = lax.ppermute(above_second, 'tp', down)]
  transfers between devices with their start and end apart: 2 -> 16, of which waited for: 2 -> 7; matrix products, arithmetic and copies ran while one was open for 10% -> 14% of each run, Pallas kernels for 0% -> 56%
where the time goes in v1:
time: 399 us; the launch traced here: 398 us
  Pallas kernels  221 us (55%)
  waiting for transfers between devices  63.7 us (16%)
  starting transfers between devices  38.2 us (10%)
  matrix products  36.4 us (9%)
  local copies, waits for them, and re-layouts  24.6 us (6%)
  between operations  13.6 us (3%)
    pallas_call x2, Pallas kernels, attend(): pl.pallas_call(functools.partial(attention_kernel, heads, rows), out_shap...  221 us
    ppermute x1, waiting for transfers between devices, per_device(): moved = lax.ppermute(slab[:, slice(*spans[0])], 'pair', SWAP)  18.1 us
    dot_general x2, matrix products, per_device(): packed = f32(pack, projected.astype(jnp.bfloat16)).astype(jnp.bfloat16)  17.7 us
    all_to_all x2, waiting for transfers between devices, per_device(): lax.all_to_all(attended.reshape(owners, 2, rows, (stop - start) * HEAD),...  16.8 us
    all_to_all x2, starting transfers between devices, per_device(): lax.all_to_all(attended.reshape(owners, 2, rows, (stop - start) * HEAD),...  14.4 us
    all_to_all x2, starting transfers between devices, per_device(): lax.all_to_all(packed, ('pair', 'tp'), split_axis=0, concat_axis=0, tiled...  10 us
    unnamed x23, local copies, waits for them, and re-layouts  9.62 us
    ppermute x1, waiting for transfers between devices, per_device(): below_first = lax.ppermute(near_first, 'tp', up)  8.91 us
  transfers between devices with their start and end apart: 16, of which 7 were waited for; matrix products, arithmetic and copies ran while one was open for 14% of the time, Pallas kernels for 56%

profile of v1, /device:TPU:4, one launch (start us, length us, event | category | flops | bytes accessed | tf_op | source)
XLA Modules:
  0.0 398.1 jit_solution(16832634231857871837)
XLA Ops:
  6.5 1.2 dynamic-slice.8
  7.7 1.3 collective-permute-start.1
  9.0 18.1 %collective-permute-done.1 = bf16[512,768]{1,0:T(8,128)(2,1)S(1)} collective-permute-done((bf16[512,768]{1,0:T(8,128)(2,1)S(1)}, bf16[512,768]{1,0:T(8,128)(2,1)S(1)}, u32[]{:S(2)}, u32[]{:S(2)}) %collective-permute-start.1) | collective-permute-done | bytes 786464 | tf_op jit(solution)/shard_map/ppermute | solution.py:153
  27.1 0.9 copy-done.3
  28.1 1.6 dynamic-slice_bitcast_fusion.1
  29.6 1.3 collective-permute-start
  30.9 1.9 constant_dynamic-slice_fusion.1
  32.8 8.7 %fusion.2 = f32[256,1280]{1,0:T(8,128)} fusion(bf16[4096,1280]{1,0:T(8,128)(2,1)} %param.8, bf16[2,256,8192]{2,1,0:T(8,128)(2,1)} %param.7, s32[]{:T(128)S(6)} %select_n.81, s32[]{:T(128)S(6)} %select_n.83), kind=kOutput, calls=%fused_computation.4 | convolution fusion | flops 2684354560 | bytes 13893640 | tf_op jit(solution)/shard_map/dot_general | solution.py:190
  41.8 3.8 dynamic-slice_bitcast_fusion
  45.5 1.6 collective-permute-start.3
  47.1 1.7 collective-permute-start.5
  48.8 0.9 collective-permute-start.2
  49.7 0.8 constant_dynamic-update-slice_fusion.7
  50.5 8.9 %collective-permute-done.3 = bf16[32,8192]{1,0:T(8,128)(2,1)S(1)} collective-permute-done((bf16[32,8192]{1,0:T(8,128)(2,1)S(1)}, bf16[32,8192]{1,0:T(8,128)(2,1)S(1)}, u32[]{:S(2)}, u32[]{:S(2)}) %collective-permute-start.3) | collective-permute-done | bytes 524320 | tf_op jit(solution)/shard_map/ppermute | solution.py:159
  59.4 0.2 collective-permute-start.7
  59.7 1.2 collective-permute-done.2
  60.9 0.7 collective-permute-start.9
  61.7 0.5 collective-permute-start.4
  62.1 2.8 collective-permute-start.6
  64.9 0.8 constant_dynamic-update-slice_fusion.6
  65.7 0.8 constant_dynamic-update-slice_fusion.5
  66.5 7.5 %collective-permute-done.6 = bf16[32,8192]{1,0:T(8,128)(2,1)} collective-permute-done((bf16[32,8192]{1,0:T(8,128)(2,1)S(1)}, bf16[32,8192]{1,0:T(8,128)(2,1)}, u32[]{:S(2)}, u32[]{:S(2)}) %collective-permute-start.6) | collective-permute-done | bytes 524320 | tf_op jit(solution)/shard_map/ppermute | solution.py:162
  74.0 2.8 collective-permute-start.8
  76.8 0.8 copy-done.4
  77.6 6.3 %collective-permute-done.4 = bf16[32,8192]{1,0:T(8,128)(2,1)} collective-permute-done((bf16[32,8192]{1,0:T(8,128)(2,1)S(1)}, bf16[32,8192]{1,0:T(8,128)(2,1)}, u32[]{:S(2)}, u32[]{:S(2)}) %collective-permute-start.4) | collective-permute-done | bytes 524320 | tf_op jit(solution)/shard_map/ppermute | solution.py:161
  83.9 1.9 constant_dynamic-update-slice_fusion.4
  85.8 0.9 constant_dynamic-update-slice_fusion.3
  86.6 1.9 constant_dynamic-update-slice_fusion.2
  88.5 0.8 constant_dynamic-update-slice_fusion.1
  89.3 1.9 constant_dynamic-update-slice_fusion
  91.2 3.2 constant_dynamic-slice_fusion
  94.4 7.8 %fusion.4 = f32[256,1280]{1,0:T(8,128)S(1)} fusion(bf16[4096,1280]{1,0:T(8,128)(2,1)} %param.8, bf16[256,8192]{1,0:T(8,128)(2,1)} %constant_dynamic-update-slice_fusion, s32[]{:T(128)S(6)} %select_n.82), kind=kOutput, calls=%fused_computation.7 | convolution fusion | flops 2684354560 | bytes 13893636 | tf_op jit(solution)/shard_map/dot_general | solution.py:191
  102.2 0.2 maximum_add_fusion
  102.3 10.4 %convolution_convert_fusion = bf16[640,768]{1,0:T(8,128)(2,1)} fusion(f32[512,1280]{1,0:T(8,128)S(1)} %maximum_add_fusion, bf16[4096,768]{1,0:T(8,128)(2,1)} %all-gather.3.cloned.1.call-done, bf16[256,4096]{1,0:T(8,128)(2,1)} %constant_dynamic-slice_fusion, bf16[256,4096]{1,0:T(8,128)(2,1)} %dynamic-slice_bitcast_fusion, s32[512]{0:T(512)S(1)} %concatenate.23), kind=kOutput, calls=%fused_computation.12 | convolution fusion | flops 3734536192 | bytes 13043712 | tf_op jit(solution)/shard_map/dot_general | solution.py:205
  112.7 5.0 %all-to-all-start.1 = ((bf16[16,40,768]{2,1,0:T(8,128)(2,1)}), bf16[16,40,768]{2,1,0:T(8,128)(2,1)S(1)}, u32[]{:S(2)}, u32[]{:S(2)}) async-start(bf16[16,40,768]{2,1,0:T(8,128)(2,1)} %bitcast.50), calls=%async_computation.1 | async-start | bytes 1966080 | tf_op jit(solution)/shard_map/all_to_all | solution.py:207
  117.8 7.3 %convolution_convert_fusion.1 = bf16[640,512]{1,0:T(8,128)(2,1)} fusion(s32[512]{0:T(512)S(1)} %concatenate.23, f32[512,1280]{1,0:T(8,128)} %copy-done.1, bf16[4096,512]{1,0:T(8,128)(2,1)} %all-gather.5.cloned.1.call-done, bf16[256,4096]{1,0:T(8,128)(2,1)} %constant_dynamic-slice_fusion, bf16[256,4096]{1,0:T(8,128)(2,1)} %dynamic-slice_bitcast_fusion), kind=kOutput, calls=%fused_computation.15 | convolution fusion | flops 2492596224 | bytes 10094592 | tf_op jit(solution)/shard_map/dot_general | solution.py:205
  125.1 4.9 %all-to-all-done.1 = bf16[16,40,768]{2,1,0:T(8,128)(2,1)S(1)} async-done(((bf16[16,40,768]{2,1,0:T(8,128)(2,1)}), bf16[16,40,768]{2,1,0:T(8,128)(2,1)S(1)}, u32[]{:S(2)}, u32[]{:S(2)}) %all-to-all-start.1) | async-done | bytes 983072 | tf_op jit(solution)/shard_map/all_to_all | solution.py:207
  130.0 5.0 %all-to-all-start = ((bf16[16,40,512]{2,1,0:T(8,128)(2,1)}), bf16[16,40,512]{2,1,0:T(8,128)(2,1)S(1)}, u32[]{:S(2)}, u32[]{:S(2)}) async-start(bf16[16,40,512]{2,1,0:T(8,128)(2,1)} %bitcast.4), calls=%async_computation | async-start | bytes 1310720 | tf_op jit(solution)/shard_map/all_to_all | solution.py:207
  135.0 0.2 fusion.24
  135.2 0.1 pad_maximum_fusion.12
  135.3 110.5 %shard_map.74 = bf16[2,8,2,40,512]{4,3,2,1,0:T(8,128)(2,1)} custom-call(s32[40]{0:T(128)S(1)} %copy-done, f32[2,40,128]{2,1,0:T(8,128)S(1)} %get-tuple-element.20.cos_ref, f32[2,40,128]{2,1,0:T(8,128)S(1)} %get-tuple-element.21.sin_ref, bf16[2,8,40,768]{3,2,1,0:T(8,128)(2,1)S(1)} %bitcast.44, bf16[2,8,40,768]{3,2,1,0:T(8,128)(2,1)S(1)} %bitcast.45, ...), custom_call_target="tpu_custom_call" | custom-call | flops 167772160 | bytes 20971520 | tf_op jit(solution)/shard_map/pallas_call | solution.py:90
  245.8 7.2 %all-to-all-start.3 = ((bf16[16,2,40,512]{3,2,1,0:T(8,128)(2,1)}), bf16[16,2,40,512]{3,2,1,0:T(8,128)(2,1)S(1)}, u32[]{:S(2)}, u32[]{:S(2)}) async-start(bf16[16,2,40,512]{3,2,1,0:T(8,128)(2,1)} %bitcast.13), calls=%async_computation.3 | async-start | bytes 2621440 | tf_op jit(solution)/shard_map/all_to_all | solution.py:215
  253.1 110.5 %shard_map.73 = bf16[2,8,2,40,512]{4,3,2,1,0:T(8,128)(2,1)} custom-call(s32[40]{0:T(128)S(1)} %copy-done, f32[2,40,128]{2,1,0:T(8,128)S(1)} %get-tuple-element.20.cos_ref, f32[2,40,128]{2,1,0:T(8,128)S(1)} %get-tuple-element.21.sin_ref, bf16[2,8,40,512]{3,2,1,0:T(8,128)(2,1)S(1)} %bitcast.49, bf16[2,8,40,768]{3,2,1,0:T(8,128)(2,1)S(1)} %bitcast.47, ...), custom_call_target="tpu_custom_call" | custom-call | flops 167772160 | bytes 20971520 | tf_op jit(solution)/shard_map/pallas_call | solution.py:90
  363.6 7.2 %all-to-all-start.2 = ((bf16[16,2,40,512]{3,2,1,0:T(8,128)(2,1)}), bf16[16,2,40,512]{3,2,1,0:T(8,128)(2,1)S(1)}, u32[]{:S(2)}, u32[]{:S(2)}) async-start(bf16[16,2,40,512]{3,2,1,0:T(8,128)(2,1)} %bitcast.8), calls=%async_computation.2 | async-start | bytes 2621440 | tf_op jit(solution)/shard_map/all_to_all | solution.py:215
  370.8 1.5 fusion.10
  372.3 16.8 %all-to-all-done.2 = bf16[16,2,40,512]{3,2,1,0:T(8,128)(2,1)S(1)} async-done(((bf16[16,2,40,512]{3,2,1,0:T(8,128)(2,1)}), bf16[16,2,40,512]{3,2,1,0:T(8,128)(2,1)S(1)}, u32[]{:S(2)}, u32[]{:S(2)}) %all-to-all-start.2) | async-done | bytes 1310752 | tf_op jit(solution)/shard_map/all_to_all | solution.py:215
  389.2 0.7 fusion.11
  390.0 1.3 copy.13
  (35 shorter events, 0.5 us)
Async XLA Ops:
  6.5 70.2 %all-gather.3.cloned.1.call-start = ((), (), s32[]{:S(2)}) async-start(), calls=%async_computation.4 | async-start | bytes 7077888 | tf_op jit(solution)/shard_map/all_gather | solution.py:154
  7.7 19.4 %collective-permute-start.1 = (bf16[512,768]{1,0:T(8,128)(2,1)S(1)}, bf16[512,768]{1,0:T(8,128)(2,1)S(1)}, u32[]{:S(2)}, u32[]{:S(2)}) collective-permute-start(bf16[512,768]{1,0:T(8,128)(2,1)S(1)} %dynamic-slice.8), channel_id=1, source_target_pairs={{0,8},{8,0},{1,9},{9,1},{2,10},{10,2},{3,11},{11,3},{4,12},{12,4},... | collective-permute-start | bytes 2359304 | tf_op jit(solution)/shard_map/ppermute | solution.py:153
  27.1 0.9 copy-start.3
  28.0 89.8 %all-gather.5.cloned.1.call-start = ((), (), s32[]{:S(2)}) async-start(), calls=%async_computation.5 | async-start | bytes 4718592 | tf_op jit(solution)/shard_map/all_gather | solution.py:158
  29.6 15.9 %collective-permute-start = (bf16[32,8192]{1,0:T(8,128)(2,1)S(1)}, bf16[32,8192]{1,0:T(8,128)(2,1)S(1)}, u32[]{:S(2)}, u32[]{:S(2)}) collective-permute-start(bf16[32,8192]{1,0:T(8,128)(2,1)S(1)} %get-tuple-element.12), channel_id=1, source_target_pairs={{0,8},{8,0},{1,9},{9,1},{2,10},{10,2},{3,11},{11,3},{4,12},{12,4},... | collective-permute-start | bytes 1572872 | tf_op jit(solution)/shard_map/ppermute | solution.py:152
  32.8 8.7 %copy-start.6 = (s32[512]{0:T(512)S(1)}, s32[512]{0:T(512)}, u32[]{:S(2)}) copy-start(s32[512]{0:T(512)} %param.13) | copy-start | bytes 6148
  32.8 8.9 %copy-start.7 = (bf16[1280]{0:T(1024)(128)(2,1)S(1)}, bf16[1280]{0:T(1024)(128)(2,1)}, u32[]{:S(2)}) copy-start(bf16[1280]{0:T(1024)(128)(2,1)} %param.9) | copy-start | bytes 7684
  45.5 13.9 %collective-permute-start.3 = (bf16[32,8192]{1,0:T(8,128)(2,1)S(1)}, bf16[32,8192]{1,0:T(8,128)(2,1)S(1)}, u32[]{:S(2)}, u32[]{:S(2)}) collective-permute-start(bf16[32,8192]{1,0:T(8,128)(2,1)S(1)} %collective-permute-done), channel_id=1, source_target_pairs={{0,2},{1,3},{2,4},{3,5},{4,6},{5,7},{6,0},{7,1},{8,10},{9,11},{10,... | collective-permute-start | bytes 1572872 | tf_op jit(solution)/shard_map/ppermute | solution.py:159
  47.1 38.6 %collective-permute-start.5 = (bf16[32,8192]{1,0:T(8,128)(2,1)S(1)}, bf16[32,8192]{1,0:T(8,128)(2,1)S(1)}, u32[]{:S(2)}, u32[]{:S(2)}) collective-permute-start(bf16[32,8192]{1,0:T(8,128)(2,1)S(1)} %collective-permute-done), channel_id=1, source_target_pairs={{2,0},{3,1},{4,2},{5,3},{6,4},{7,5},{0,6},{1,7},{10,8},{11,9},{12,... | collective-permute-start | bytes 1572872 | tf_op jit(solution)/shard_map/ppermute | solution.py:160
  48.8 12.1 %collective-permute-start.2 = (bf16[32,8192]{1,0:T(8,128)(2,1)S(1)}, bf16[32,8192]{1,0:T(8,128)(2,1)S(1)}, u32[]{:S(2)}, u32[]{:S(2)}) collective-permute-start(bf16[32,8192]{1,0:T(8,128)(2,1)S(1)} %get-tuple-element.8), channel_id=1, source_target_pairs={{0,8},{8,0},{1,9},{9,1},{2,10},{10,2},{3,11},{11,3},{4,12},{12,4},... | collective-permute-start | bytes 1572872 | tf_op jit(solution)/shard_map/ppermute | solution.py:155
  59.4 29.1 %collective-permute-start.7 = (bf16[32,8192]{1,0:T(8,128)(2,1)S(1)}, bf16[32,8192]{1,0:T(8,128)(2,1)S(1)}, u32[]{:S(2)}, u32[]{:S(2)}) collective-permute-start(bf16[32,8192]{1,0:T(8,128)(2,1)S(1)} %collective-permute-done.3), channel_id=1, source_target_pairs={{0,2},{1,3},{2,4},{3,5},{4,6},{5,7},{6,0},{7,1},{8,10},{9,11},{10,... | collective-permute-start | bytes 1572872 | tf_op jit(solution)/shard_map/ppermute | solution.py:163
  60.9 15.9 %collective-permute-start.9 = (bf16[512,512]{1,0:T(8,128)(2,1)}, bf16[512,512]{1,0:T(8,128)(2,1)S(1)}, u32[]{:S(2)}, u32[]{:S(2)}) collective-permute-start(bf16[512,512]{1,0:T(8,128)(2,1)} %constant_dynamic-slice_fusion.1), channel_id=1, source_target_pairs={{0,8},{8,0},{1,9},{9,1},{2,10},{10,2},{3,11},{11,3},{4,12},{12,4},... | collective-permute-start | bytes 1572872 | tf_op jit(solution)/shard_map/ppermute | solution.py:157
  61.7 22.2 %collective-permute-start.4 = (bf16[32,8192]{1,0:T(8,128)(2,1)S(1)}, bf16[32,8192]{1,0:T(8,128)(2,1)}, u32[]{:S(2)}, u32[]{:S(2)}) collective-permute-start(bf16[32,8192]{1,0:T(8,128)(2,1)S(1)} %collective-permute-done.2), channel_id=1, source_target_pairs={{0,2},{1,3},{2,4},{3,5},{4,6},{5,7},{6,0},{7,1},{8,10},{9,11},{10,... | collective-permute-start | bytes 1572872 | tf_op jit(solution)/shard_map/ppermute | solution.py:161
  62.1 11.9 %collective-permute-start.6 = (bf16[32,8192]{1,0:T(8,128)(2,1)S(1)}, bf16[32,8192]{1,0:T(8,128)(2,1)}, u32[]{:S(2)}, u32[]{:S(2)}) collective-permute-start(bf16[32,8192]{1,0:T(8,128)(2,1)S(1)} %collective-permute-done.2), channel_id=1, source_target_pairs={{2,0},{3,1},{4,2},{5,3},{6,4},{7,5},{0,6},{1,7},{10,8},{11,9},{12,... | collective-permute-start | bytes 1572872 | tf_op jit(solution)/shard_map/ppermute | solution.py:162
  74.0 15.3 %collective-permute-start.8 = (bf16[32,8192]{1,0:T(8,128)(2,1)}, bf16[32,8192]{1,0:T(8,128)(2,1)}, u32[]{:S(2)}, u32[]{:S(2)}) collective-permute-start(bf16[32,8192]{1,0:T(8,128)(2,1)} %collective-permute-done.6), channel_id=1, source_target_pairs={{2,0},{3,1},{4,2},{5,3},{6,4},{7,5},{0,6},{1,7},{10,8},{11,9},{12,... | collective-permute-start | bytes 1572872 | tf_op jit(solution)/shard_map/ppermute | solution.py:164
  76.8 0.8 copy-start.4
  94.4 7.8 %copy-start.2 = (f32[256,1280]{1,0:T(8,128)S(1)}, f32[256,1280]{1,0:T(8,128)}, u32[]{:S(2)}) copy-start(f32[256,1280]{1,0:T(8,128)} %fusion.2) | copy-start | bytes 3932164
  102.3 10.4 %copy-start.1 = (f32[512,1280]{1,0:T(8,128)}, f32[512,1280]{1,0:T(8,128)S(1)}, u32[]{:S(2)}) copy-start(f32[512,1280]{1,0:T(8,128)S(1)} %maximum_add_fusion) | copy-start | bytes 7864324
  112.7 17.2 %all-to-all-start.1 = ((bf16[16,40,768]{2,1,0:T(8,128)(2,1)}), bf16[16,40,768]{2,1,0:T(8,128)(2,1)S(1)}, u32[]{:S(2)}, u32[]{:S(2)}) async-start(bf16[16,40,768]{2,1,0:T(8,128)(2,1)} %bitcast.50), calls=%async_computation.1 | async-start | bytes 1966080 | tf_op jit(solution)/shard_map/all_to_all | solution.py:207
  117.7 17.2 %copy-start = (s32[40]{0:T(128)S(1)}, s32[40]{0:T(128)}, u32[]{:S(2)}) copy-start(s32[40]{0:T(128)} %fill_ref.3) | copy-start | bytes 484
  130.0 115.9 %all-to-all-start = ((bf16[16,40,512]{2,1,0:T(8,128)(2,1)}), bf16[16,40,512]{2,1,0:T(8,128)(2,1)S(1)}, u32[]{:S(2)}, u32[]{:S(2)}) async-start(bf16[16,40,512]{2,1,0:T(8,128)(2,1)} %bitcast.4), calls=%async_computation | async-start | bytes 1310720 | tf_op jit(solution)/shard_map/all_to_all | solution.py:207
  245.8 117.7 %all-to-all-start.3 = ((bf16[16,2,40,512]{3,2,1,0:T(8,128)(2,1)}), bf16[16,2,40,512]{3,2,1,0:T(8,128)(2,1)S(1)}, u32[]{:S(2)}, u32[]{:S(2)}) async-start(bf16[16,2,40,512]{3,2,1,0:T(8,128)(2,1)} %bitcast.13), calls=%async_computation.3 | async-start | bytes 2621440 | tf_op jit(solution)/shard_map/all_to_all | solution.py:215
  363.6 25.6 %all-to-all-start.2 = ((bf16[16,2,40,512]{3,2,1,0:T(8,128)(2,1)}), bf16[16,2,40,512]{3,2,1,0:T(8,128)(2,1)S(1)}, u32[]{:S(2)}, u32[]{:S(2)}) async-start(bf16[16,2,40,512]{3,2,1,0:T(8,128)(2,1)} %bitcast.8), calls=%async_computation.2 | async-start | bytes 2621440 | tf_op jit(solution)/shard_map/all_to_all | solution.py:215
  372.3 17.5 %copy-start.5 = (bf16[2,256,512]{1,2,0:T(8,128)(2,1)S(1)}, bf16[2,256,512]{1,2,0:T(8,128)(2,1)}, u32[]{:S(2)}) copy-start(bf16[2,256,512]{1,2,0:T(8,128)(2,1)} %fusion.10) | copy-start | bytes 1572868
Sparse Core Ops, SparseCore 0:
  28.1 43.4 all-gather.2
  77.7 32.7 all-gather.4

commit v2 on v1

v2 whole, which is shorter than its diff:
```python
import functools

import jax
import jax.numpy as jnp
from jax import lax
from jax.experimental import pallas as pl
from jax.experimental.pallas import tpu as pltpu
from jax.sharding import PartitionSpec as P

HEAD = 128
SHARING = 8
ROPE_BASE = 1000000.0
SWAP = ((0, 1), (1, 0))
CHUNKS = ((0, 4), (4, 8))
ROW_BLOCK = 8
DEPTH_BLOCK = 1024
NT = (((1,), (1,)), ((), ()))


def in_hbm(value):
    return pltpu.with_memory_space_constraint(value, pltpu.HBM)


def rope_tables(positions):
    frequency = ROPE_BASE ** (-jnp.arange(0, HEAD, 2, dtype=jnp.float32) / HEAD)
    angles = positions.astype(jnp.float32)[..., None] * frequency
    cosine = jnp.cos(angles)
    sine = jnp.sin(angles)
    return jnp.concatenate([cosine, cosine], -1), jnp.concatenate([-sine, sine], -1)


def project_kernel(owners, rows, side_ref, x_ref, w_ref, partial_ref, pack_ref, out_ref, total):
    k = pl.program_id(0)
    product = jnp.dot(x_ref[...], w_ref[...], preferred_element_type=jnp.float32)

    @pl.when(k == 0)
    def _():
        total[...] = partial_ref[...] + product

    @pl.when(k > 0)
    def _():
        total[...] += product

    @pl.when(k == pl.num_programs(0) - 1)
    def _():
        share = pack_ref.shape[1]
        for step in range(2):
            rounded = total[pl.ds(step * share, share), :].astype(jnp.bfloat16)
            packed = jnp.dot(pack_ref[...], rounded, preferred_element_type=jnp.float32)
            for owner in range(owners):
                block = packed[owner * rows:(owner + 1) * rows]
                out_ref[owner, step] = block.astype(jnp.bfloat16)


def project(side, signals, matrix, partial, at, pack, owners):
    lines, _ = signals.shape
    depth, columns = matrix.shape
    slots, share = pack.shape
    rows = slots // owners
    steps = depth // DEPTH_BLOCK
    return pl.pallas_call(
        functools.partial(project_kernel, owners, rows),
        out_shape=pltpu.HBM((owners, 2, rows, columns), jnp.bfloat16),
        grid_spec=pltpu.PrefetchScalarGridSpec(
            num_scalar_prefetch=1,
            grid=(steps,),
            in_specs=[
                pl.BlockSpec((lines, DEPTH_BLOCK), lambda k, s: (0, s[0] * steps + k)),
                pl.BlockSpec((DEPTH_BLOCK, columns), lambda k, s: (k, 0)),
                pl.BlockSpec((lines, columns), lambda k, s: (0, at)),
                pl.BlockSpec((slots, share), lambda k, s: (0, 0)),
            ],
            out_specs=pl.BlockSpec((owners, 2, rows, columns), lambda k, s: (0, 0, 0, 0)),
            scratch_shapes=[pltpu.VMEM((lines, columns), jnp.float32)],
        ),
        compiler_params=pltpu.CompilerParams(vmem_limit_bytes=32 << 20),
        cost_estimate=pl.CostEstimate(
            flops=2 * lines * depth * columns,
            transcendentals=0,
            bytes_accessed=2 * (lines + columns) * depth,
        ),
    )(side, in_hbm(signals), in_hbm(matrix), partial, pack)


def attention_kernel(heads, fill_ref, cos_ref, sin_ref, q_ref, new_ref, k_ref, v_ref, out_ref,
                     q_rot, k_rot, v_new, cached_scores, new_scores, blended):
    n_tp = q_ref.shape[1]
    block = ROW_BLOCK
    scale = HEAD ** (-0.5)
    width = 2 * heads
    first = pl.program_id(0) * block
    size = block * width

    def both(ref, t, step, start):
        lanes = slice(start, start + HEAD)
        return ref[0, t, step, :, lanes].astype(jnp.float32) + ref[1, t, step, :, lanes].astype(jnp.float32)

    def turned(values, step):
        turn = values * cos_ref[step] + pltpu.roll(values, HEAD // 2, 1) * sin_ref[step]
        return turn.astype(jnp.bfloat16).astype(jnp.float32)

    place = lax.broadcasted_iota(jnp.int32, (width, HEAD), 1)
    line = lax.broadcasted_iota(jnp.int32, (size, 2 * block), 0)
    column = lax.broadcasted_iota(jnp.int32, (size, 2 * block), 1)
    seen = ((column % block) == (line // width)) & (
        (column < block) | (line % width >= heads)
    )
    filled = [place < fill_ref[first + i] for i in range(block)]

    for t in range(n_tp):
        for step in range(2):
            for head in range(heads):
                at = pl.ds(t * size + (step * heads + head) * block, block)
                q_rot[at, :] = turned(both(q_ref, t, step, head * HEAD), step)
            at = pl.ds(step * block, block)
            k_rot[t, at, :] = turned(both(new_ref, t, step, 0), step)
            v_new[t, at, :] = both(new_ref, t, step, HEAD)
    for t in range(n_tp):
        lanes = slice(t * HEAD, (t + 1) * HEAD)
        queries = [
            q_rot[pl.ds(t * size + i, width, stride=block), :].astype(jnp.bfloat16) for i in range(block)
        ]
        for i in range(block):
            scores = lax.dot_general(
                queries[i], k_ref[i, :, lanes], NT, preferred_element_type=jnp.float32
            ) * scale
            cached_scores[t, pl.ds(i * width, width), :] = jnp.where(filled[i], scores, -1e30)
        scores = lax.dot_general(
            jnp.concatenate(queries, 0), k_rot[t].astype(jnp.bfloat16), NT,
            preferred_element_type=jnp.float32,
        ) * scale
        new_scores[t] = jnp.where(seen, scores, -1e30)
    for t in range(n_tp):
        lanes = slice(t * HEAD, (t + 1) * HEAD)
        cached, new = cached_scores[t], new_scores[t]
        top = jnp.maximum(jnp.max(cached, -1, keepdims=True), jnp.max(new, -1, keepdims=True))
        cached, new = jnp.exp(cached - top), jnp.exp(new - top)
        share = 1.0 / (jnp.sum(cached, -1, keepdims=True) + jnp.sum(new, -1, keepdims=True))
        cached, new = (cached * share).astype(jnp.bfloat16), (new * share).astype(jnp.bfloat16)
        from_new = jnp.dot(new, v_new[t].astype(jnp.bfloat16), preferred_element_type=jnp.float32)
        for i in range(block):
            part = slice(i * width, (i + 1) * width)
            mixed = jnp.dot(cached[part], v_ref[i, :, lanes], preferred_element_type=jnp.float32)
            blended[pl.ds(t * size + i, width, stride=block), :] = mixed + from_new[part]
    for t in range(n_tp):
        for step in range(2):
            for head in range(heads):
                at = pl.ds(t * size + (step * heads + head) * block, block)
                done = blended[at, :].astype(jnp.bfloat16)
                for pair in range(2):
                    out_ref[pair, t, step, :, head * HEAD:(head + 1) * HEAD] = done


def attend(fill, cosine, sine, queries, new, keys, values, heads):
    _, n_tp, _, rows, _ = queries.shape
    places = keys.shape[1]
    block = ROW_BLOCK
    width = 2 * heads * block
    table = pl.BlockSpec((2, block, HEAD), lambda r, f: (0, r, 0))
    cache = pl.BlockSpec((block, places, n_tp * HEAD), lambda r, f: (r, 0, 0))

    def routed(columns):
        return pl.BlockSpec((2, n_tp, 2, block, columns), lambda r, f: (0, 0, 0, r, 0))

    return pl.pallas_call(
        functools.partial(attention_kernel, heads),
        out_shape=pltpu.HBM((2, n_tp, 2, rows, heads * HEAD), jnp.bfloat16),
        grid_spec=pltpu.PrefetchScalarGridSpec(
            num_scalar_prefetch=1,
            grid=(rows // block,),
            in_specs=[table, table, routed(heads * HEAD), routed(2 * HEAD), cache, cache],
            out_specs=routed(heads * HEAD),
            scratch_shapes=[
                pltpu.VMEM((n_tp * width, HEAD), jnp.float32),
                pltpu.VMEM((n_tp, 2 * block, HEAD), jnp.float32),
                pltpu.VMEM((n_tp, 2 * block, HEAD), jnp.float32),
                pltpu.VMEM((n_tp, width, HEAD), jnp.float32),
                pltpu.VMEM((n_tp, width, 2 * block), jnp.float32),
                pltpu.VMEM((n_tp * width, HEAD), jnp.float32),
            ],
        ),
        compiler_params=pltpu.CompilerParams(vmem_limit_bytes=32 << 20),
        cost_estimate=pl.CostEstimate(
            flops=8 * heads * rows * n_tp * places * HEAD,
            transcendentals=2 * heads * rows * n_tp * places,
            bytes_accessed=4 * rows * places * n_tp * HEAD,
        ),
    )(
        fill, cosine, sine, queries, new, in_hbm(keys), in_hbm(values)
    )


def unpack_kernel(owners, rows, pick_ref, back_ref, *refs):
    out_ref, gathered = refs[-2:]
    for owner in range(owners):
        gathered[pl.ds(owner * rows, rows), :] = back_ref[owner, 0].astype(jnp.float32)
    picked = jnp.dot(
        pick_ref[...], gathered[...].astype(jnp.bfloat16), preferred_element_type=jnp.float32
    )
    out_ref[0] = picked.astype(jnp.bfloat16)


def unpack(pick, back, at, columns, so_far):
    owners, _, rows, wide = back.shape
    share, slots = pick.shape
    before = [] if so_far is None else [so_far]
    return pl.pallas_call(
        functools.partial(unpack_kernel, owners, rows),
        out_shape=jax.ShapeDtypeStruct((2, share, columns), jnp.bfloat16),
        grid=(2,),
        in_specs=[
            pl.BlockSpec((share, slots), lambda s: (0, 0)),
            pl.BlockSpec((owners, 1, rows, wide), lambda s: (0, s, 0, 0)),
        ] + [pl.BlockSpec(memory_space=pl.ANY)] * len(before),
        out_specs=pl.BlockSpec((1, share, wide), lambda s: (s, 0, at)),
        scratch_shapes=[pltpu.VMEM((slots, wide), jnp.float32)],
        input_output_aliases={2: 0} if before else {},
        compiler_params=pltpu.CompilerParams(vmem_limit_bytes=32 << 20),
        cost_estimate=pl.CostEstimate(
            flops=4 * share * slots * wide, transcendentals=0, bytes_accessed=4 * slots * wide
        ),
    )(pick, back, *before)


def per_device(signals, matrix, offset, cached_keys, cached_values, fill, lines):
    n_pair, n_tp, n_grp = (int(lax.axis_size(a)) for a in ("pair", "tp", "grp"))
    pair, grp = (lax.axis_index(a) for a in ("pair", "grp"))
    share, features = signals.shape[1:]
    half, columns = matrix.shape
    rows = fill.shape[0]
    owners = n_pair * n_tp
    depth = half // n_grp

    def after(value, *earlier):
        return lax.optimization_barrier((value, *earlier))[0]

    spans = [(SHARING * HEAD, columns)] + [(a * HEAD, b * HEAD) for a, b in CHUNKS]
    moved = []
    for start, stop in spans:
        slab = lax.dynamic_slice(matrix, (grp * depth, start), (depth, stop - start))
        moved.append(lax.ppermute(after(slab, *moved[1:]), "pair", SWAP))

    flat = signals.reshape(2 * share, features)
    near = lax.dynamic_slice_in_dim(flat, pair * half, half, 1)
    partial = jnp.dot(near, matrix, preferred_element_type=jnp.float32)
    partial = partial + offset.astype(jnp.float32)
    side = jnp.reshape(1 - pair, (1,)).astype(jnp.int32)

    own = lax.dynamic_slice_in_dim(lines, pair * share, share)
    slots = jnp.arange(owners * rows, dtype=jnp.int32)
    pack = (slots[:, None] == own[None, :]).astype(jnp.bfloat16)
    pick = (own[:, None] == slots[None, :]).astype(jnp.bfloat16)
    positions = fill[None, :] + jnp.arange(2, dtype=jnp.int32)[:, None]
    cosine, sine = rope_tables(positions)

    def exchange(blocks):
        return lax.all_to_all(blocks, ("pair", "tp"), split_axis=0, concat_axis=0, tiled=True)

    arrived, remote, earlier = [], None, [partial, pack, pick, cosine, sine]
    for (start, stop), slab in zip(spans, moved):
        ready = slab if remote is None else after(slab, remote, *earlier)
        if remote is not None:
            earlier = [project(side, flat, *last)]
            arrived.append(exchange(earlier[0]))
        remote = lax.all_gather(ready, "grp", axis=0, tiled=True)
        last = (remote, partial, start // (stop - start), pack, owners)
    arrived.append(exchange(project(side, flat, *last)))
    arrived = [
        block.reshape(n_pair, n_tp, 2, rows, stop - start)
        for block, (start, stop) in zip(arrived, spans)
    ]
    out = None
    for (start, stop), queries in zip(spans[1:], arrived[1:]):
        heads = (stop - start) // HEAD
        attended = attend(
            fill, cosine, sine, queries, arrived[0], cached_keys, cached_values, heads
        )
        back = exchange(attended.reshape(owners, 2, rows, stop - start))
        out = unpack(pick, back, start // (stop - start), SHARING * HEAD, out)
    return out


def solution(mesh):
    in_specs = (
        P(None, ("grp", "pair"), None),
        P("pair", "tp"),
        P("tp"),
        P(("grp", "pair", "tp"), None, None),
        P(("grp", "pair", "tp"), None, None),
        P(("grp", "pair", "tp")),
        P("grp"),
    )
    out_specs = P(None, ("grp", "pair"), "tp")
    return jax.shard_map(
        per_device, mesh=mesh, in_specs=in_specs, out_specs=out_specs, check_vma=False
    )
```

time: 399 us -> 206 us (0.52)
  Pallas kernels: 221 us -> 52.1 us
  matrix products: 36.4 us -> 10.4 us
  waiting for transfers between devices: 63.7 us -> 86.2 us
  local copies, waits for them, and re-layouts: 24.6 us -> 7.61 us
  starting transfers between devices: 38.2 us -> 33.2 us
    pallas_call x2 -> x7, Pallas kernels: 221 us -> 52.1 us  [the longest x2 28.4 us: attend(): pl.pallas_call(functools.partial(attention_kernel, heads), out_shape=pltp...]
    all_gather x2 -> x3, waiting for transfers between devices: 0.02 us -> 40 us  [per_device(): remote = lax.all_gather(ready, 'grp', axis=0, tiled=True)]
    ppermute x10 -> x3, waiting for transfers between devices: 41.9 us -> 14.5 us  [per_device(): moved.append(lax.ppermute(after(slab, *moved[1:]), 'pair', SWAP))]
    dot_general x6 -> x1, matrix products: 36.4 us -> 10.4 us  [per_device(): partial = jnp.dot(near, matrix, preferred_element_type=jnp.float32)]
    ppermute x10 -> x3, starting transfers between devices: 13.7 us -> 3.73 us  [per_device(): moved.append(lax.ppermute(after(slab, *moved[1:]), 'pair', SWAP))]
    all_to_all x4 -> x5, waiting for transfers between devices: 21.7 us -> 31.6 us  [exchange(): lax.all_to_all(blocks, ('pair', 'tp'), split_axis=0, concat_axis=0, tiled...]
    unnamed x23 -> x14, local copies, waits for them, and re-layouts: 9.62 us -> 3.62 us
    all_to_all x4 -> x5, starting transfers between devices: 24.5 us -> 29.4 us  [exchange(): lax.all_to_all(blocks, ('pair', 'tp'), split_axis=0, concat_axis=0, tiled...]
  transfers between devices with their start and end apart: 16 -> 11, of which waited for: 7 -> 10; matrix products, arithmetic and copies ran while one was open for 14% -> 8% of each run, Pallas kernels for 56% -> 25%
where the time goes in v2:
time: 206 us; the launch traced here: 205 us
  waiting for transfers between devices  86.2 us (42%)
  Pallas kernels  52.1 us (25%)
  starting transfers between devices  33.2 us (16%)
  between operations  13.2 us (6%)
  matrix products  10.4 us (5%)
  local copies, waits for them, and re-layouts  7.61 us (4%)
  other arithmetic  2.64 us (1%)
    all_gather x3, waiting for transfers between devices, per_device(): remote = lax.all_gather(ready, 'grp', axis=0, tiled=True)  40 us
    all_to_all x5, waiting for transfers between devices, exchange(): lax.all_to_all(blocks, ('pair', 'tp'), split_axis=0, concat_axis=0, tiled...  31.6 us
    all_to_all x5, starting transfers between devices, exchange(): lax.all_to_all(blocks, ('pair', 'tp'), split_axis=0, concat_axis=0, tiled...  29.4 us
    pallas_call x2, Pallas kernels, attend(): pl.pallas_call(functools.partial(attention_kernel, heads), out_shape=pltp...  28.4 us
    pallas_call x3, Pallas kernels, project(): pl.pallas_call(functools.partial(project_kernel, owners, rows), out_shape...  20.6 us
    ppermute x3, waiting for transfers between devices, per_device(): moved.append(lax.ppermute(after(slab, *moved[1:]), 'pair', SWAP))  14.5 us
    dot_general x1, matrix products, per_device(): partial = jnp.dot(near, matrix, preferred_element_type=jnp.float32)  10.4 us
  transfers between devices with their start and end apart: 11, of which 10 were waited for; matrix products, arithmetic and copies ran while one was open for 8% of the time, Pallas kernels for 25%

profile of v2, /device:TPU:4, one launch (start us, length us, event | category | flops | bytes accessed | tf_op | source)
XLA Modules:
  0.0 205.3 jit_solution(5627862341222336464)
XLA Ops:
  6.5 0.0 all-gather.4.cloned.1.call-start
  6.5 1.0 constant_dynamic-slice_fusion
  7.5 1.3 collective-permute-start.2
  8.8 6.8 %collective-permute-done.2 = bf16[512,256]{1,0:T(8,128)(2,1)S(1)} collective-permute-done((bf16[512,256]{1,0:T(8,128)(2,1)S(1)}, bf16[512,256]{1,0:T(8,128)(2,1)S(1)}, u32[]{:S(2)}, u32[]{:S(2)}) %collective-permute-start.2) | collective-permute-done | bytes 262176 | tf_op jit(solution)/shard_map/ppermute | solution.py:241
  15.6 0.7 copy-done.6
  16.3 0.0 all-gather.4.cloned.1.call-update
  16.4 0.0 all-gather.6.cloned.1.call-start
  16.4 2.3 %constant_dynamic-slice_fusion.1 = (bf16[512,512]{1,0:T(8,128)(2,1)}, bf16[512,512]{1,0:T(8,128)(2,1)}) fusion(bf16[4096,1280]{1,0:T(8,128)(2,1)} %param.8, s32[]{:T(128)S(6)} %select_n.12), kind=kLoop, calls=%fused_computation.16 | loop fusion | bytes 2097156 | tf_op jit(solution)/shard_map/dynamic_slice | solution.py:240
  18.7 1.2 collective-permute-start
  19.9 0.7 convert_element_type.18
  20.6 0.8 dynamic_slice.15
  21.3 0.7 add_convert_fusion
  22.0 0.2 fusion.7
  22.2 10.4 %fusion.2.partial_ref = f32[512,1280]{1,0:T(8,128)S(1)} fusion(bf16[4096,1280]{1,0:T(8,128)(2,1)} %param.8, bf16[512,8192]{1,0:T(8,128)(2,1)} %bitcast.11, s32[]{:T(128)S(6)} %select_n.13, f32[1280]{0:T(1024)S(1)} %convert_element_type.18), kind=kOutput, calls=%fused_computation.2 | convolution fusion | flops 5369364480 | bytes 17306628 | tf_op jit(solution)/shard_map/dot_general | solution.py:245
  32.6 0.1 pad_maximum_fusion
  32.7 0.1 fusion.6.pack_ref
  32.9 0.0 copy-start
  32.9 0.9 fusion.5.pick_ref
  33.7 0.0 collective-permute-done
  33.7 10.5 %all-gather.4.cloned.1.call-done.w_ref = bf16[4096,256]{1,0:T(8,128)(2,1)} async-done(((bf16[512,256]{1,0:T(8,128)(2,1)}), bf16[4096,256]{1,0:T(8,128)(2,1)}) %all-gather.4.cloned.1.call-update) | async-done | bytes 2097168 | tf_op jit(solution)/shard_map/all_gather | solution.py:265
  44.2 0.0 all-gather.6.cloned.1.call-update
  44.3 0.0 all-gather.8.cloned.1.call-start
  44.3 1.3 collective-permute-start.1
  45.6 5.6 %shard_map.73 = bf16[16,2,40,256]{3,2,1,0:T(8,128)(2,1)} custom-call(s32[1]{0:T(128)} %bitcast.side_ref, bf16[512,8192]{1,0:T(8,128)(2,1)} %bitcast.12, bf16[4096,256]{1,0:T(8,128)(2,1)} %all-gather.4.cloned.1.call-done.w_ref, f32[512,1280]{1,0:T(8,128)S(1)} %fusion.2.partial_ref, bf16[640,256]{1,0:T(8,128)(2,1)S(1)} %fusion.6.pack_ref), custom_call_target="tpu_custom_call" | custom-call | flops 1073741824 | bytes 6291456 | tf_op jit(solution)/shard_map/pallas_call | solution.py:61
  51.1 0.0 copy-done
  51.1 7.7 %collective-permute-done.1 = bf16[512,512]{1,0:T(8,128)(2,1)} collective-permute-done((bf16[512,512]{1,0:T(8,128)(2,1)}, bf16[512,512]{1,0:T(8,128)(2,1)}, u32[]{:S(2)}, u32[]{:S(2)}) %collective-permute-start.1) | collective-permute-done | bytes 524320 | tf_op jit(solution)/shard_map/ppermute | solution.py:241
  58.8 19.9 %all-gather.6.cloned.1.call-done.w_ref = bf16[4096,512]{1,0:T(8,128)(2,1)} async-done(((bf16[512,512]{1,0:T(8,128)(2,1)}), bf16[4096,512]{1,0:T(8,128)(2,1)}) %all-gather.6.cloned.1.call-update) | async-done | bytes 4194320 | tf_op jit(solution)/shard_map/all_gather | solution.py:265
  78.7 0.0 all-gather.8.cloned.1.call-update
  78.7 7.3 %all-to-all-start.1 = ((bf16[16,2,40,256]{3,2,1,0:T(8,128)(2,1)}), bf16[16,2,40,256]{3,2,1,0:T(8,128)(2,1)S(1)}, u32[]{:S(2)}, u32[]{:S(2)}) async-start(bf16[16,2,40,256]{3,2,1,0:T(8,128)(2,1)} %shard_map.73), calls=%async_computation.1 | async-start | bytes 1310720 | tf_op jit(solution)/shard_map/all_to_all | solution.py:257
  86.0 1.0 copy-done.1
  87.0 7.7 %shard_map.76 = bf16[16,2,40,512]{3,2,1,0:T(8,128)(2,1)} custom-call(s32[1]{0:T(128)} %bitcast.side_ref, bf16[512,8192]{1,0:T(8,128)(2,1)} %bitcast.13, bf16[4096,512]{1,0:T(8,128)(2,1)} %all-gather.6.cloned.1.call-done.w_ref, f32[512,1280]{1,0:T(8,128)S(1)} %fusion.2.partial_ref, bf16[640,256]{1,0:T(8,128)(2,1)S(1)} %copy-done.1), custom_call_target="tpu_custom_call" | custom-call | flops 2147483648 | bytes 8388608 | tf_op jit(solution)/shard_map/pallas_call | solution.py:61
  94.7 2.4 %all-to-all-done.1 = bf16[16,2,40,256]{3,2,1,0:T(8,128)(2,1)S(1)} async-done(((bf16[16,2,40,256]{3,2,1,0:T(8,128)(2,1)}), bf16[16,2,40,256]{3,2,1,0:T(8,128)(2,1)S(1)}, u32[]{:S(2)}, u32[]{:S(2)}) %all-to-all-start.1) | async-done | bytes 655392 | tf_op jit(solution)/shard_map/all_to_all | solution.py:257
  97.1 5.9 %all-to-all-start.3 = ((bf16[16,2,40,512]{3,2,1,0:T(8,128)(2,1)}), bf16[16,2,40,512]{3,2,1,0:T(8,128)(2,1)}, u32[]{:S(2)}, u32[]{:S(2)}) async-start(bf16[16,2,40,512]{3,2,1,0:T(8,128)(2,1)} %shard_map.76), calls=%async_computation.3 | async-start | bytes 2621440 | tf_op jit(solution)/shard_map/all_to_all | solution.py:257
  102.9 9.6 %all-gather.8.cloned.1.call-done.w_ref = bf16[4096,512]{1,0:T(8,128)(2,1)} async-done(((bf16[512,512]{1,0:T(8,128)(2,1)}), bf16[4096,512]{1,0:T(8,128)(2,1)}) %all-gather.8.cloned.1.call-update) | async-done | bytes 4194320 | tf_op jit(solution)/shard_map/all_gather | solution.py:265
  112.6 1.0 copy-done.2
  113.5 7.3 %shard_map.74 = bf16[16,2,40,512]{3,2,1,0:T(8,128)(2,1)} custom-call(s32[1]{0:T(128)} %bitcast.side_ref, bf16[512,8192]{1,0:T(8,128)(2,1)} %bitcast.14, bf16[4096,512]{1,0:T(8,128)(2,1)} %all-gather.8.cloned.1.call-done.w_ref, f32[512,1280]{1,0:T(8,128)S(1)} %fusion.2.partial_ref, bf16[640,256]{1,0:T(8,128)(2,1)S(1)} %copy-done.2), custom_call_target="tpu_custom_call" | custom-call | flops 2147483648 | bytes 8388608 | tf_op jit(solution)/shard_map/pallas_call | solution.py:61
  120.9 0.7 all-to-all-done.3
  121.5 6.6 %all-to-all-start = ((bf16[16,2,40,512]{3,2,1,0:T(8,128)(2,1)}), bf16[16,2,40,512]{3,2,1,0:T(8,128)(2,1)S(1)}, u32[]{:S(2)}, u32[]{:S(2)}) async-start(bf16[16,2,40,512]{3,2,1,0:T(8,128)(2,1)} %shard_map.74), calls=%async_computation | async-start | bytes 2621440 | tf_op jit(solution)/shard_map/all_to_all | solution.py:257
  128.2 14.3 %shard_map.77 = bf16[2,8,2,40,512]{4,3,2,1,0:T(8,128)(2,1)} custom-call(s32[40]{0:T(128)S(1)} %copy-done.5, f32[2,40,128]{2,1,0:T(8,128)S(1)} %get-tuple-element.16.cos_ref, f32[2,40,128]{2,1,0:T(8,128)S(1)} %get-tuple-element.17.sin_ref, bf16[2,8,2,40,512]{4,3,2,1,0:T(8,128)(2,1)} %bitcast.5.q_ref, bf16[2,8,2,40,256]{4,3,2,1,0:T(8,128)(2,1)S(1)} %bitcast.8, ...), custom_call_target="tpu_custom_call" | custom-call | flops 167772160 | bytes 20971520 | tf_op jit(solution)/shard_map/pallas_call | solution.py:165
  142.4 6.2 %all-to-all-done = bf16[16,2,40,512]{3,2,1,0:T(8,128)(2,1)S(1)} async-done(((bf16[16,2,40,512]{3,2,1,0:T(8,128)(2,1)}), bf16[16,2,40,512]{3,2,1,0:T(8,128)(2,1)S(1)}, u32[]{:S(2)}, u32[]{:S(2)}) %all-to-all-start) | async-done | bytes 1310752 | tf_op jit(solution)/shard_map/all_to_all | solution.py:257
  148.6 4.8 %all-to-all-start.4 = ((bf16[16,2,40,512]{3,2,1,0:T(8,128)(2,1)}), bf16[16,2,40,512]{3,2,1,0:T(8,128)(2,1)S(1)}, u32[]{:S(2)}, u32[]{:S(2)}) async-start(bf16[16,2,40,512]{3,2,1,0:T(8,128)(2,1)} %bitcast.15), calls=%async_computation.4 | async-start | bytes 2621440 | tf_op jit(solution)/shard_map/all_to_all | solution.py:257
  153.4 14.1 %shard_map.75 = bf16[2,8,2,40,512]{4,3,2,1,0:T(8,128)(2,1)} custom-call(s32[40]{0:T(128)S(1)} %copy-done.5, f32[2,40,128]{2,1,0:T(8,128)S(1)} %get-tuple-element.16.cos_ref, f32[2,40,128]{2,1,0:T(8,128)S(1)} %get-tuple-element.17.sin_ref, bf16[2,8,2,40,512]{4,3,2,1,0:T(8,128)(2,1)S(1)} %bitcast.10, bf16[2,8,2,40,256]{4,3,2,1,0:T(8,128)(2,1)S(1)} %bitcast.9, ...), custom_call_target="tpu_custom_call" | custom-call | flops 167772160 | bytes 20971520 | tf_op jit(solution)/shard_map/pallas_call | solution.py:165
  167.5 5.4 %all-to-all-done.4.back_ref = bf16[16,2,40,512]{3,2,1,0:T(8,128)(2,1)S(1)} async-done(((bf16[16,2,40,512]{3,2,1,0:T(8,128)(2,1)}), bf16[16,2,40,512]{3,2,1,0:T(8,128)(2,1)S(1)}, u32[]{:S(2)}, u32[]{:S(2)}) %all-to-all-start.4) | async-done | bytes 1310752 | tf_op jit(solution)/shard_map/all_to_all | solution.py:257
  172.9 4.8 %all-to-all-start.2 = ((bf16[16,2,40,512]{3,2,1,0:T(8,128)(2,1)}), bf16[16,2,40,512]{3,2,1,0:T(8,128)(2,1)S(1)}, u32[]{:S(2)}, u32[]{:S(2)}) async-start(bf16[16,2,40,512]{3,2,1,0:T(8,128)(2,1)} %bitcast.16), calls=%async_computation.2 | async-start | bytes 2621440 | tf_op jit(solution)/shard_map/all_to_all | solution.py:257
  177.7 1.0 copy-done.3
  178.7 1.6 shard_map.78.refs_0_
  180.2 17.0 %all-to-all-done.2.back_ref = bf16[16,2,40,512]{3,2,1,0:T(8,128)(2,1)S(1)} async-done(((bf16[16,2,40,512]{3,2,1,0:T(8,128)(2,1)}), bf16[16,2,40,512]{3,2,1,0:T(8,128)(2,1)S(1)}, u32[]{:S(2)}, u32[]{:S(2)}) %all-to-all-start.2) | async-done | bytes 1310752 | tf_op jit(solution)/shard_map/all_to_all | solution.py:257
  197.2 1.6 shard_map.79
  (9 shorter events, 0.0 us)
Async XLA Ops:
  6.5 37.7 %all-gather.4.cloned.1.call-start = ((), (), s32[]{:S(2)}) async-start(), calls=%async_computation.5 | async-start | bytes 2359296 | tf_op jit(solution)/shard_map/all_gather | solution.py:265
  7.5 8.1 %collective-permute-start.2 = (bf16[512,256]{1,0:T(8,128)(2,1)S(1)}, bf16[512,256]{1,0:T(8,128)(2,1)S(1)}, u32[]{:S(2)}, u32[]{:S(2)}) collective-permute-start(bf16[512,256]{1,0:T(8,128)(2,1)S(1)} %constant_dynamic-slice_fusion), channel_id=1, source_target_pairs={{0,8},{8,0},{1,9},{9,1},{2,10},{10,2},{3,11},{11,3},{4,12},{12,4},... | collective-permute-start | bytes 786440 | tf_op jit(solution)/shard_map/ppermute | solution.py:241
  15.6 0.7 copy-start.6
  16.4 62.3 %all-gather.6.cloned.1.call-start = ((), (), s32[]{:S(2)}) async-start(), calls=%async_computation.6 | async-start | bytes 4718592 | tf_op jit(solution)/shard_map/all_gather | solution.py:265
  18.7 15.0 %collective-permute-start = (bf16[512,512]{1,0:T(8,128)(2,1)}, bf16[512,512]{1,0:T(8,128)(2,1)}, u32[]{:S(2)}, u32[]{:S(2)}) collective-permute-start(bf16[512,512]{1,0:T(8,128)(2,1)} %get-tuple-element.11), channel_id=1, source_target_pairs={{0,8},{8,0},{1,9},{9,1},{2,10},{10,2},{3,11},{11,3},{4,12},{12,4},... | collective-permute-start | bytes 1572872 | tf_op jit(solution)/shard_map/ppermute | solution.py:241
  32.9 18.3 %copy-start = (bf16[640,256]{1,0:T(8,128)(2,1)}, bf16[640,256]{1,0:T(8,128)(2,1)S(1)}, u32[]{:S(2)}) copy-start(bf16[640,256]{1,0:T(8,128)(2,1)S(1)} %fusion.6.pack_ref) | copy-start | bytes 983044
  44.3 68.3 %all-gather.8.cloned.1.call-start = ((), (), s32[]{:S(2)}) async-start(), calls=%async_computation.7 | async-start | bytes 4718592 | tf_op jit(solution)/shard_map/all_gather | solution.py:265
  44.3 14.5 %collective-permute-start.1 = (bf16[512,512]{1,0:T(8,128)(2,1)}, bf16[512,512]{1,0:T(8,128)(2,1)}, u32[]{:S(2)}, u32[]{:S(2)}) collective-permute-start(bf16[512,512]{1,0:T(8,128)(2,1)} %get-tuple-element.8), channel_id=1, source_target_pairs={{0,8},{8,0},{1,9},{9,1},{2,10},{10,2},{3,11},{11,3},{4,12},{12,4},... | collective-permute-start | bytes 1572872 | tf_op jit(solution)/shard_map/ppermute | solution.py:241
  78.7 18.4 %all-to-all-start.1 = ((bf16[16,2,40,256]{3,2,1,0:T(8,128)(2,1)}), bf16[16,2,40,256]{3,2,1,0:T(8,128)(2,1)S(1)}, u32[]{:S(2)}, u32[]{:S(2)}) async-start(bf16[16,2,40,256]{3,2,1,0:T(8,128)(2,1)} %shard_map.73), calls=%async_computation.1 | async-start | bytes 1310720 | tf_op jit(solution)/shard_map/all_to_all | solution.py:257
  86.0 1.0 copy-start.1
  97.1 24.5 %all-to-all-start.3 = ((bf16[16,2,40,512]{3,2,1,0:T(8,128)(2,1)}), bf16[16,2,40,512]{3,2,1,0:T(8,128)(2,1)}, u32[]{:S(2)}, u32[]{:S(2)}) async-start(bf16[16,2,40,512]{3,2,1,0:T(8,128)(2,1)} %shard_map.76), calls=%async_computation.3 | async-start | bytes 2621440 | tf_op jit(solution)/shard_map/all_to_all | solution.py:257
  112.6 1.0 copy-start.2
  113.5 14.6 %copy-start.5 = (s32[40]{0:T(128)S(1)}, s32[40]{0:T(128)}, u32[]{:S(2)}) copy-start(s32[40]{0:T(128)} %fill_ref.3) | copy-start | bytes 484
  121.5 27.1 %all-to-all-start = ((bf16[16,2,40,512]{3,2,1,0:T(8,128)(2,1)}), bf16[16,2,40,512]{3,2,1,0:T(8,128)(2,1)S(1)}, u32[]{:S(2)}, u32[]{:S(2)}) async-start(bf16[16,2,40,512]{3,2,1,0:T(8,128)(2,1)} %shard_map.74), calls=%async_computation | async-start | bytes 2621440 | tf_op jit(solution)/shard_map/all_to_all | solution.py:257
  148.6 24.3 %all-to-all-start.4 = ((bf16[16,2,40,512]{3,2,1,0:T(8,128)(2,1)}), bf16[16,2,40,512]{3,2,1,0:T(8,128)(2,1)S(1)}, u32[]{:S(2)}, u32[]{:S(2)}) async-start(bf16[16,2,40,512]{3,2,1,0:T(8,128)(2,1)} %bitcast.15), calls=%async_computation.4 | async-start | bytes 2621440 | tf_op jit(solution)/shard_map/all_to_all | solution.py:257
  167.5 29.7 %copy-start.4 = (bf16[256,640]{1,0:T(8,128)(2,1)S(1)}, bf16[256,640]{1,0:T(8,128)(2,1)}, u32[]{:S(2)}) copy-start(bf16[256,640]{1,0:T(8,128)(2,1)} %fusion.5.pick_ref) | copy-start | bytes 983044
  172.9 24.3 %all-to-all-start.2 = ((bf16[16,2,40,512]{3,2,1,0:T(8,128)(2,1)}), bf16[16,2,40,512]{3,2,1,0:T(8,128)(2,1)S(1)}, u32[]{:S(2)}, u32[]{:S(2)}) async-start(bf16[16,2,40,512]{3,2,1,0:T(8,128)(2,1)} %bitcast.16), calls=%async_computation.2 | async-start | bytes 2621440 | tf_op jit(solution)/shard_map/all_to_all | solution.py:257
  177.7 1.0 copy-start.3
Sparse Core Ops, SparseCore 0:
  16.5 27.7 all-gather.3
  45.9 32.6 all-gather.5
  80.4 32.1 all-gather.7

commit v3 on v2

--- a/solution.py
+++ b/solution.py
@@ -13,7 +13,6 @@
 SWAP = ((0, 1), (1, 0))
 CHUNKS = ((0, 4), (4, 8))
 ROW_BLOCK = 8
-DEPTH_BLOCK = 1024
 NT = (((1,), (1,)), ((), ()))
 
 
@@ -29,57 +28,60 @@
     return jnp.concatenate([cosine, cosine], -1), jnp.concatenate([-sine, sine], -1)
 
 
-def project_kernel(owners, rows, side_ref, x_ref, w_ref, partial_ref, pack_ref, out_ref, total):
-    k = pl.program_id(0)
-    product = jnp.dot(x_ref[...], w_ref[...], preferred_element_type=jnp.float32)
-
-    @pl.when(k == 0)
-    def _():
-        total[...] = partial_ref[...] + product
-
-    @pl.when(k > 0)
-    def _():
-        total[...] += product
-
-    @pl.when(k == pl.num_programs(0) - 1)
-    def _():
-        share = pack_ref.shape[1]
-        for step in range(2):
-            rounded = total[pl.ds(step * share, share), :].astype(jnp.bfloat16)
-            packed = jnp.dot(pack_ref[...], rounded, preferred_element_type=jnp.float32)
-            for owner in range(owners):
-                block = packed[owner * rows:(owner + 1) * rows]
-                out_ref[owner, step] = block.astype(jnp.bfloat16)
-
-
-def project(side, signals, matrix, partial, at, pack, owners):
+def project_kernel(columns, owners, rows, places_ref, x_ref, *refs):
+    slabs = refs[:-6]
+    partial_ref, pack_ref, out_ref, taken, total, arrived = refs[-6:]
+    depth = slabs[0].shape[0]
+    share = pack_ref.shape[1]
+    copies = []
+    for i in range(len(slabs)):
+        first = pl.multiple_of(places_ref[i] * depth, depth)
+        copies.append(
+            pltpu.make_async_copy(x_ref.at[:, pl.ds(first, depth)], taken.at[i], arrived.at[i])
+        )
+        copies[i].start()
+    for i, slab in enumerate(slabs):
+        copies[i].wait()
+        product = jnp.dot(taken[i], slab[...], preferred_element_type=jnp.float32)
+        if i == 0:
+            total[...] = partial_ref[:, slice(*columns)] + product
+        else:
+            total[...] += product
+    for step in range(2):
+        rounded = total[pl.ds(step * share, share), :].astype(jnp.bfloat16)
+        packed = jnp.dot(pack_ref[...], rounded, preferred_element_type=jnp.float32)
+        for owner in range(owners):
+            block = packed[owner * rows:(owner + 1) * rows]
+            out_ref[owner, step] = block.astype(jnp.bfloat16)
+
+
+def project(places, signals, slabs, partial, columns, pack, owners):
     lines, _ = signals.shape
-    depth, columns = matrix.shape
+    depth, wide = slabs[0].shape
     slots, share = pack.shape
     rows = slots // owners
-    steps = depth // DEPTH_BLOCK
+    local = pl.BlockSpec(memory_space=pltpu.VMEM)
     return pl.pallas_call(
-        functools.partial(project_kernel, owners, rows),
-        out_shape=pltpu.HBM((owners, 2, rows, columns), jnp.bfloat16),
+        functools.partial(project_kernel, columns, owners, rows),
+        out_shape=pltpu.HBM((owners, 2, rows, wide), jnp.bfloat16),
         grid_spec=pltpu.PrefetchScalarGridSpec(
             num_scalar_prefetch=1,
-            grid=(steps,),
-            in_specs=[
-                pl.BlockSpec((lines, DEPTH_BLOCK), lambda k, s: (0, s[0] * steps + k)),
-                pl.BlockSpec((DEPTH_BLOCK, columns), lambda k, s: (k, 0)),
-                pl.BlockSpec((lines, columns), lambda k, s: (0, at)),
-                pl.BlockSpec((slots, share), lambda k, s: (0, 0)),
+            grid=(1,),
+            in_specs=[pl.BlockSpec(memory_space=pl.ANY)] + [local] * (len(slabs) + 2),
+            out_specs=pl.BlockSpec((owners, 2, rows, wide), lambda k, s: (0, 0, 0, 0)),
+            scratch_shapes=[
+                pltpu.VMEM((len(slabs), lines, depth), jnp.bfloat16),
+                pltpu.VMEM((lines, wide), jnp.float32),
+                pltpu.SemaphoreType.DMA((len(slabs),)),
             ],
-            out_specs=pl.BlockSpec((owners, 2, rows, columns), lambda k, s: (0, 0, 0, 0)),
-            scratch_shapes=[pltpu.VMEM((lines, columns), jnp.float32)],
         ),
         compiler_params=pltpu.CompilerParams(vmem_limit_bytes=32 << 20),
         cost_estimate=pl.CostEstimate(
-            flops=2 * lines * depth * columns,
+            flops=2 * lines * depth * len(slabs) * wide,
             transcendentals=0,
-            bytes_accessed=2 * (lines + columns) * depth,
-        ),
-    )(side, in_hbm(signals), in_hbm(matrix), partial, pack)
+            bytes_accessed=2 * lines * depth * len(slabs),
+        ),
+    )(places, in_hbm(signals), *slabs, partial, pack)
 
 
 def attention_kernel(heads, fill_ref, cos_ref, sin_ref, q_ref, new_ref, k_ref, v_ref, out_ref,
@@ -234,18 +236,7 @@
     def after(value, *earlier):
         return lax.optimization_barrier((value, *earlier))[0]
 
-    spans = [(SHARING * HEAD, columns)] + [(a * HEAD, b * HEAD) for a, b in CHUNKS]
-    moved = []
-    for start, stop in spans:
-        slab = lax.dynamic_slice(matrix, (grp * depth, start), (depth, stop - start))
-        moved.append(lax.ppermute(after(slab, *moved[1:]), "pair", SWAP))
-
     flat = signals.reshape(2 * share, features)
-    near = lax.dynamic_slice_in_dim(flat, pair * half, half, 1)
-    partial = jnp.dot(near, matrix, preferred_element_type=jnp.float32)
-    partial = partial + offset.astype(jnp.float32)
-    side = jnp.reshape(1 - pair, (1,)).astype(jnp.int32)
-
     own = lax.dynamic_slice_in_dim(lines, pair * share, share)
     slots = jnp.arange(owners * rows, dtype=jnp.int32)
     pack = (slots[:, None] == own[None, :]).astype(jnp.bfloat16)
@@ -256,19 +247,43 @@
     def exchange(blocks):
         return lax.all_to_all(blocks, ("pair", "tp"), split_axis=0, concat_axis=0, tiled=True)
 
-    arrived, remote, earlier = [], None, [partial, pack, pick, cosine, sine]
-    for (start, stop), slab in zip(spans, moved):
-        ready = slab if remote is None else after(slab, remote, *earlier)
-        if remote is not None:
-            earlier = [project(side, flat, *last)]
-            arrived.append(exchange(earlier[0]))
-        remote = lax.all_gather(ready, "grp", axis=0, tiled=True)
-        last = (remote, partial, start // (stop - start), pack, owners)
-    arrived.append(exchange(project(side, flat, *last)))
-    arrived = [
-        block.reshape(n_pair, n_tp, 2, rows, stop - start)
-        for block, (start, stop) in zip(arrived, spans)
-    ]
+    spans = [(SHARING * HEAD, columns)] + [(a * HEAD, b * HEAD) for a, b in CHUNKS]
+    n_z = n_grp // 2
+    up = [(2 * a + c, 2 * ((a + 1) % n_z) + c) for a in range(n_z) for c in range(2)]
+    down = [(d, s) for s, d in up]
+    twin = [(2 * a + c, 2 * a + 1 - c) for a in range(n_z) for c in range(2)]
+    z, core = grp // 2, grp % 2
+    turns = (0, n_z - 1, 1, 2)
+    places = (1 - pair) * n_grp + jnp.stack(
+        [(z + turn) % n_z * 2 + core for turn in turns]
+        + [(z + turn) % n_z * 2 + 1 - core for turn in turns]
+    )
+    places = places.astype(jnp.int32)
+
+    first = []
+    for start, stop in spans:
+        slab = lax.dynamic_slice(matrix, (grp * depth, start), (depth, stop - start))
+        first.append(lax.ppermute(after(slab, *first[-1:]), "pair", SWAP))
+    near = lax.dynamic_slice_in_dim(flat, pair * half, half, 1)
+    partial = jnp.dot(near, matrix, preferred_element_type=jnp.float32)
+    partial = partial + offset.astype(jnp.float32)
+
+    arrived, ahead = [], []
+    for number, ((start, stop), slab) in enumerate(zip(spans, first)):
+        slab = after(slab, *ahead)
+        below = lax.ppermute(slab, "grp", up)
+        above = lax.ppermute(slab, "grp", down)
+        ahead = [below, above]
+        if number % 2:
+            opposite = lax.ppermute(above, "grp", down)
+        else:
+            opposite = lax.ppermute(below, "grp", up)
+        if number == 1:
+            opposite = after(opposite, arrived[0])
+        held = [slab, below, above, opposite]
+        held += [lax.ppermute(piece, "grp", twin) for piece in held]
+        packed = project(places, flat, held, partial, (start, stop), pack, owners)
+        arrived.append(exchange(packed).reshape(n_pair, n_tp, 2, rows, stop - start))
     out = None
     for (start, stop), queries in zip(spans[1:], arrived[1:]):
         heads = (stop - start) // HEAD

time: 206 us -> 191 us (0.927)
  waiting for transfers between devices: 86.2 us -> 69.9 us
  starting transfers between devices: 33.2 us -> 48.9 us
  between operations: 13.2 us -> 0.28 us
    all_gather x3 -> x0, waiting for transfers between devices: 40 us -> none  [per_device(): remote = lax.all_gather(ready, 'grp', axis=0, tiled=True)]
    ppermute x3 -> x24, waiting for transfers between devices: 14.5 us -> 39.3 us  [the longest x3 22.4 us: per_device(): below = lax.ppermute(slab, 'grp', up)]
    ppermute x3 -> x24, starting transfers between devices: 3.73 us -> 19.8 us  [the longest x3 8.59 us: per_device(): above = lax.ppermute(slab, 'grp', down)]
  transfers between devices with their start and end apart: 11 -> 29, of which waited for: 10 -> 14; matrix products, arithmetic and copies ran while one was open for 8% -> 7% of each run, Pallas kernels for 25% -> 27%
where the time goes in v3:
time: 191 us; the launch traced here: 190 us
  waiting for transfers between devices  69.9 us (37%)
  Pallas kernels  53.6 us (28%)
  starting transfers between devices  48.9 us (26%)
  matrix products  10.4 us (5%)
  local copies, waits for them, and re-layouts  6.01 us (3%)
    all_to_all x5, waiting for transfers between devices, exchange(): lax.all_to_all(blocks, ('pair', 'tp'), split_axis=0, concat_axis=0, tiled...  30.5 us
    all_to_all x5, starting transfers between devices, exchange(): lax.all_to_all(blocks, ('pair', 'tp'), split_axis=0, concat_axis=0, tiled...  29.1 us
    pallas_call x2, Pallas kernels, attend(): pl.pallas_call(functools.partial(attention_kernel, heads), out_shape=pltp...  28.4 us
    ppermute x3, waiting for transfers between devices, per_device(): below = lax.ppermute(slab, 'grp', up)  22.4 us
    pallas_call x3, Pallas kernels, project(): pl.pallas_call(functools.partial(project_kernel, columns, owners, rows),...  22 us
    ppermute x3, waiting for transfers between devices, per_device(): first.append(lax.ppermute(after(slab, *first[-1:]), 'pair', SWAP))  12.1 us
    dot_general x1, matrix products, per_device(): partial = jnp.dot(near, matrix, preferred_element_type=jnp.float32)  10.4 us
    ppermute x3, starting transfers between devices, per_device(): above = lax.ppermute(slab, 'grp', down)  8.59 us
  transfers between devices with their start and end apart: 29, of which 14 were waited for; matrix products, arithmetic and copies ran while one was open for 7% of the time, Pallas kernels for 27%

profile of v3, /device:TPU:4, one launch (start us, length us, event | category | flops | bytes accessed | tf_op | source)
XLA Modules:
  0.0 190.3 jit_solution(6140028049062353631)
XLA Ops:
  0.0 1.0 constant_dynamic-slice_fusion
  1.0 1.3 collective-permute-start
  2.2 6.8 %collective-permute-done.refs_0_ = bf16[512,256]{1,0:T(8,128)(2,1)S(1)} collective-permute-done((bf16[512,256]{1,0:T(8,128)(2,1)S(1)}, bf16[512,256]{1,0:T(8,128)(2,1)S(1)}, u32[]{:S(2)}, u32[]{:S(2)}) %collective-permute-start) | collective-permute-done | bytes 262176 | tf_op jit(solution)/shard_map/ppermute | solution.py:266
  9.1 1.9 %collective-permute-start.3 = (bf16[512,256]{1,0:T(8,128)(2,1)S(1)}, bf16[512,256]{1,0:T(8,128)(2,1)S(1)}, u32[]{:S(2)}, u32[]{:S(2)}) collective-permute-start(bf16[512,256]{1,0:T(8,128)(2,1)S(1)} %collective-permute-done.refs_0_), channel_id=1, source_target_pairs={{0,32},{16,48},{32,64},{48,80},{64,96},{80,112},{96,0},{112,16},{1... | collective-permute-start | bytes 786440 | tf_op jit(solution)/shard_map/ppermute | solution.py:274
  11.0 0.7 convert_element_type.18
  11.7 2.2 %constant_dynamic-slice_fusion.1 = (bf16[512,512]{1,0:T(8,128)(2,1)}, bf16[512,512]{1,0:T(8,128)(2,1)}) fusion(bf16[4096,1280]{1,0:T(8,128)(2,1)} %param.8, s32[]{:T(128)S(6)} %select_n.53), kind=kLoop, calls=%fused_computation.16 | loop fusion | bytes 2097156 | tf_op jit(solution)/shard_map/dynamic_slice | solution.py:265
  13.9 2.1 %collective-permute-start.4 = (bf16[512,256]{1,0:T(8,128)(2,1)S(1)}, bf16[512,256]{1,0:T(8,128)(2,1)S(1)}, u32[]{:S(2)}, u32[]{:S(2)}) collective-permute-start(bf16[512,256]{1,0:T(8,128)(2,1)S(1)} %collective-permute-done.refs_0_), channel_id=1, source_target_pairs={{32,0},{48,16},{64,32},{80,48},{96,64},{112,80},{0,96},{16,112},{3... | collective-permute-start | bytes 786440 | tf_op jit(solution)/shard_map/ppermute | solution.py:275
  16.1 1.2 collective-permute-start.1
  17.2 1.3 collective-permute-done.3.refs_1_
  18.6 10.4 %fusion.2.refs_8_ = f32[512,1280]{1,0:T(8,128)S(1)} fusion(bf16[4096,1280]{1,0:T(8,128)(2,1)} %param.8, bf16[512,8192]{1,0:T(8,128)(2,1)} %bitcast.18, s32[]{:T(128)S(6)} %select_n.54, f32[1280]{0:T(1024)S(1)} %convert_element_type.18), kind=kOutput, calls=%fused_computation.2 | convolution fusion | flops 5369364480 | bytes 17306628 | tf_op jit(solution)/shard_map/dot_general | solution.py:268
  29.2 0.5 collective-permute-start.16
  29.8 3.2 %collective-permute-start.6 = (bf16[512,512]{1,0:T(8,128)(2,1)}, bf16[512,512]{1,0:T(8,128)(2,1)}, u32[]{:S(2)}, u32[]{:S(2)}) collective-permute-start(bf16[512,512]{1,0:T(8,128)(2,1)} %collective-permute-done.1.refs_0_), channel_id=1, source_target_pairs={{32,0},{48,16},{64,32},{80,48},{96,64},{112,80},{0,96},{16,112},{3... | collective-permute-start | bytes 1572872 | tf_op jit(solution)/shard_map/ppermute | solution.py:275
  33.0 0.2 collective-permute-start.18
  33.4 1.5 collective-permute-done.18.refs_7_
  34.9 6.7 %shard_map.74 = bf16[16,2,40,256]{3,2,1,0:T(8,128)(2,1)} custom-call(s32[8]{0:T(128)S(1)} %broadcast_add_fusion.places_ref, bf16[512,8192]{1,0:T(8,128)(2,1)} %bitcast.19, bf16[512,256]{1,0:T(8,128)(2,1)S(1)} %collective-permute-done.refs_0_, bf16[512,256]{1,0:T(8,128)(2,1)S(1)} %collective-permute-done.3.refs_1_, ...), custom_call_target="tpu_custom_call" | custom-call | flops 1073741824 | bytes 4194304 | tf_op jit(solution)/shard_map/pallas_call | solution.py:64
  41.6 0.7 copy-done
  42.3 7.4 %all-to-all-start.1 = ((bf16[16,2,40,256]{3,2,1,0:T(8,128)(2,1)}), bf16[16,2,40,256]{3,2,1,0:T(8,128)(2,1)S(1)}, u32[]{:S(2)}, u32[]{:S(2)}) async-start(bf16[16,2,40,256]{3,2,1,0:T(8,128)(2,1)} %shard_map.74), calls=%async_computation.1 | async-start | bytes 1310720 | tf_op jit(solution)/shard_map/all_to_all | solution.py:248
  49.8 1.3 collective-permute-start.2
  51.0 3.1 %collective-permute-start.19 = (bf16[512,512]{1,0:T(8,128)(2,1)}, bf16[512,512]{1,0:T(8,128)(2,1)}, u32[]{:S(2)}, u32[]{:S(2)}) collective-permute-start(bf16[512,512]{1,0:T(8,128)(2,1)} %collective-permute-done.6.refs_2_), channel_id=1, source_target_pairs={{32,0},{48,16},{64,32},{80,48},{96,64},{112,80},{0,96},{16,112},{3... | collective-permute-start | bytes 1572872 | tf_op jit(solution)/shard_map/ppermute | solution.py:278
  54.2 10.5 %collective-permute-done.5.refs_1_ = bf16[512,512]{1,0:T(8,128)(2,1)} collective-permute-done((bf16[512,512]{1,0:T(8,128)(2,1)}, bf16[512,512]{1,0:T(8,128)(2,1)}, u32[]{:S(2)}, u32[]{:S(2)}) %collective-permute-start.5) | collective-permute-done | bytes 524320 | tf_op jit(solution)/shard_map/ppermute | solution.py:274
  64.7 5.2 %collective-permute-done.2.refs_0_ = bf16[512,512]{1,0:T(8,128)(2,1)} collective-permute-done((bf16[512,512]{1,0:T(8,128)(2,1)}, bf16[512,512]{1,0:T(8,128)(2,1)}, u32[]{:S(2)}, u32[]{:S(2)}) %collective-permute-start.2) | collective-permute-done | bytes 524320 | tf_op jit(solution)/shard_map/ppermute | solution.py:266
  70.0 0.5 collective-permute-start.21
  70.6 3.2 %collective-permute-start.8 = (bf16[512,512]{1,0:T(8,128)(2,1)}, bf16[512,512]{1,0:T(8,128)(2,1)}, u32[]{:S(2)}, u32[]{:S(2)}) collective-permute-start(bf16[512,512]{1,0:T(8,128)(2,1)} %collective-permute-done.2.refs_0_), channel_id=1, source_target_pairs={{32,0},{48,16},{64,32},{80,48},{96,64},{112,80},{0,96},{16,112},{3... | collective-permute-start | bytes 1572872 | tf_op jit(solution)/shard_map/ppermute | solution.py:275
  73.8 10.5 %collective-permute-done.7.refs_1_ = bf16[512,512]{1,0:T(8,128)(2,1)} collective-permute-done((bf16[512,512]{1,0:T(8,128)(2,1)}, bf16[512,512]{1,0:T(8,128)(2,1)}, u32[]{:S(2)}, u32[]{:S(2)}) %collective-permute-start.7) | collective-permute-done | bytes 524320 | tf_op jit(solution)/shard_map/ppermute | solution.py:274
  84.4 1.0 copy-done.1
  85.3 7.9 %shard_map.76 = bf16[16,2,40,512]{3,2,1,0:T(8,128)(2,1)} custom-call(s32[8]{0:T(128)S(1)} %broadcast_add_fusion.places_ref, bf16[512,8192]{1,0:T(8,128)(2,1)} %bitcast.20, bf16[512,512]{1,0:T(8,128)(2,1)} %collective-permute-done.1.refs_0_, bf16[512,512]{1,0:T(8,128)(2,1)} %collective-permute-done.5.refs_1_, ...), custom_call_target="tpu_custom_call" | custom-call | flops 2147483648 | bytes 4194304 | tf_op jit(solution)/shard_map/pallas_call | solution.py:64
  93.2 7.2 %all-to-all-start.3 = ((bf16[16,2,40,512]{3,2,1,0:T(8,128)(2,1)}), bf16[16,2,40,512]{3,2,1,0:T(8,128)(2,1)}, u32[]{:S(2)}, u32[]{:S(2)}) async-start(bf16[16,2,40,512]{3,2,1,0:T(8,128)(2,1)} %shard_map.76), calls=%async_computation.3 | async-start | bytes 2621440 | tf_op jit(solution)/shard_map/all_to_all | solution.py:248
  100.5 0.5 collective-permute-start.11
  101.1 0.4 collective-permute-start.13
  101.5 1.1 collective-permute-done.10.refs_4_
  102.6 0.7 collective-permute-done.11.refs_5_
  103.3 0.7 collective-permute-done.12.refs_6_
  104.1 0.7 collective-permute-done.13.refs_7_
  104.8 1.0 copy-done.2
  105.8 7.4 %shard_map.73 = bf16[16,2,40,512]{3,2,1,0:T(8,128)(2,1)} custom-call(s32[8]{0:T(128)S(1)} %broadcast_add_fusion.places_ref, bf16[512,8192]{1,0:T(8,128)(2,1)} %bitcast.21, bf16[512,512]{1,0:T(8,128)(2,1)} %collective-permute-done.2.refs_0_, bf16[512,512]{1,0:T(8,128)(2,1)} %collective-permute-done.7.refs_1_, ...), custom_call_target="tpu_custom_call" | custom-call | flops 2147483648 | bytes 4194304 | tf_op jit(solution)/shard_map/pallas_call | solution.py:64
  113.2 5.0 %all-to-all-done.3 = bf16[16,2,40,512]{3,2,1,0:T(8,128)(2,1)} async-done(((bf16[16,2,40,512]{3,2,1,0:T(8,128)(2,1)}), bf16[16,2,40,512]{3,2,1,0:T(8,128)(2,1)}, u32[]{:S(2)}, u32[]{:S(2)}) %all-to-all-start.3) | async-done | bytes 1310752 | tf_op jit(solution)/shard_map/all_to_all | solution.py:248
  118.2 4.8 %all-to-all-start = ((bf16[16,2,40,512]{3,2,1,0:T(8,128)(2,1)}), bf16[16,2,40,512]{3,2,1,0:T(8,128)(2,1)S(1)}, u32[]{:S(2)}, u32[]{:S(2)}) async-start(bf16[16,2,40,512]{3,2,1,0:T(8,128)(2,1)} %shard_map.73), calls=%async_computation | async-start | bytes 2621440 | tf_op jit(solution)/shard_map/all_to_all | solution.py:248
  123.0 0.2 fusion.7
  123.4 14.3 %shard_map.77 = bf16[2,8,2,40,512]{4,3,2,1,0:T(8,128)(2,1)} custom-call(s32[40]{0:T(128)S(1)} %copy-done.3, f32[2,40,128]{2,1,0:T(8,128)S(1)} %get-tuple-element.20.cos_ref, f32[2,40,128]{2,1,0:T(8,128)S(1)} %get-tuple-element.21.sin_ref, bf16[2,8,2,40,512]{4,3,2,1,0:T(8,128)(2,1)} %bitcast.12.q_ref, bf16[2,8,2,40,256]{4,3,2,1,0:T(8,128)(2,1)S(1)} %bitcast.15, ...), custom_call_target="tpu_custom_call" | custom-call | flops 167772160 | bytes 20971520 | tf_op jit(solution)/shard_map/pallas_call | solution.py:167
  137.7 4.2 %all-to-all-done = bf16[16,2,40,512]{3,2,1,0:T(8,128)(2,1)S(1)} async-done(((bf16[16,2,40,512]{3,2,1,0:T(8,128)(2,1)}), bf16[16,2,40,512]{3,2,1,0:T(8,128)(2,1)S(1)}, u32[]{:S(2)}, u32[]{:S(2)}) %all-to-all-start) | async-done | bytes 1310752 | tf_op jit(solution)/shard_map/all_to_all | solution.py:248
  141.9 4.8 %all-to-all-start.4 = ((bf16[16,2,40,512]{3,2,1,0:T(8,128)(2,1)}), bf16[16,2,40,512]{3,2,1,0:T(8,128)(2,1)S(1)}, u32[]{:S(2)}, u32[]{:S(2)}) async-start(bf16[16,2,40,512]{3,2,1,0:T(8,128)(2,1)} %bitcast.23), calls=%async_computation.4 | async-start | bytes 2621440 | tf_op jit(solution)/shard_map/all_to_all | solution.py:248
  146.7 14.1 %shard_map.75 = bf16[2,8,2,40,512]{4,3,2,1,0:T(8,128)(2,1)} custom-call(s32[40]{0:T(128)S(1)} %copy-done.3, f32[2,40,128]{2,1,0:T(8,128)S(1)} %get-tuple-element.20.cos_ref, f32[2,40,128]{2,1,0:T(8,128)S(1)} %get-tuple-element.21.sin_ref, bf16[2,8,2,40,512]{4,3,2,1,0:T(8,128)(2,1)S(1)} %bitcast.17, bf16[2,8,2,40,256]{4,3,2,1,0:T(8,128)(2,1)S(1)} %bitcast.16, ...), custom_call_target="tpu_custom_call" | custom-call | flops 167772160 | bytes 20971520 | tf_op jit(solution)/shard_map/pallas_call | solution.py:167
  160.8 4.5 %all-to-all-done.4.back_ref = bf16[16,2,40,512]{3,2,1,0:T(8,128)(2,1)S(1)} async-done(((bf16[16,2,40,512]{3,2,1,0:T(8,128)(2,1)}), bf16[16,2,40,512]{3,2,1,0:T(8,128)(2,1)S(1)}, u32[]{:S(2)}, u32[]{:S(2)}) %all-to-all-start.4) | async-done | bytes 1310752 | tf_op jit(solution)/shard_map/all_to_all | solution.py:248
  165.2 4.8 %all-to-all-start.2 = ((bf16[16,2,40,512]{3,2,1,0:T(8,128)(2,1)}), bf16[16,2,40,512]{3,2,1,0:T(8,128)(2,1)S(1)}, u32[]{:S(2)}, u32[]{:S(2)}) async-start(bf16[16,2,40,512]{3,2,1,0:T(8,128)(2,1)} %bitcast.22), calls=%async_computation.2 | async-start | bytes 2621440 | tf_op jit(solution)/shard_map/all_to_all | solution.py:248
  170.1 0.1 fusion.5.pick_ref
  170.2 1.6 shard_map.78.refs_0_
  171.8 16.9 %all-to-all-done.2.back_ref = bf16[16,2,40,512]{3,2,1,0:T(8,128)(2,1)S(1)} async-done(((bf16[16,2,40,512]{3,2,1,0:T(8,128)(2,1)}), bf16[16,2,40,512]{3,2,1,0:T(8,128)(2,1)S(1)}, u32[]{:S(2)}, u32[]{:S(2)}) %all-to-all-start.2) | async-done | bytes 1310752 | tf_op jit(solution)/shard_map/all_to_all | solution.py:248
  188.7 1.6 shard_map.79
  (40 shorter events, 0.7 us)
Async XLA Ops:
  1.0 8.1 %collective-permute-start = (bf16[512,256]{1,0:T(8,128)(2,1)S(1)}, bf16[512,256]{1,0:T(8,128)(2,1)S(1)}, u32[]{:S(2)}, u32[]{:S(2)}) collective-permute-start(bf16[512,256]{1,0:T(8,128)(2,1)S(1)} %constant_dynamic-slice_fusion), channel_id=1, source_target_pairs={{0,8},{8,0},{1,9},{9,1},{2,10},{10,2},{3,11},{11,3},{4,12},{12,4},... | collective-permute-start | bytes 786440 | tf_op jit(solution)/shard_map/ppermute | solution.py:266
  9.1 9.5 %collective-permute-start.3 = (bf16[512,256]{1,0:T(8,128)(2,1)S(1)}, bf16[512,256]{1,0:T(8,128)(2,1)S(1)}, u32[]{:S(2)}, u32[]{:S(2)}) collective-permute-start(bf16[512,256]{1,0:T(8,128)(2,1)S(1)} %collective-permute-done.refs_0_), channel_id=1, source_target_pairs={{0,32},{16,48},{32,64},{48,80},{64,96},{80,112},{96,0},{112,16},{1... | collective-permute-start | bytes 786440 | tf_op jit(solution)/shard_map/ppermute | solution.py:274
  13.9 15.8 %collective-permute-start.4 = (bf16[512,256]{1,0:T(8,128)(2,1)S(1)}, bf16[512,256]{1,0:T(8,128)(2,1)S(1)}, u32[]{:S(2)}, u32[]{:S(2)}) collective-permute-start(bf16[512,256]{1,0:T(8,128)(2,1)S(1)} %collective-permute-done.refs_0_), channel_id=1, source_target_pairs={{32,0},{48,16},{64,32},{80,48},{96,64},{112,80},{0,96},{16,112},{3... | collective-permute-start | bytes 786440 | tf_op jit(solution)/shard_map/ppermute | solution.py:275
  16.1 13.7 %collective-permute-start.1 = (bf16[512,512]{1,0:T(8,128)(2,1)}, bf16[512,512]{1,0:T(8,128)(2,1)}, u32[]{:S(2)}, u32[]{:S(2)}) collective-permute-start(bf16[512,512]{1,0:T(8,128)(2,1)} %get-tuple-element.10), channel_id=1, source_target_pairs={{0,8},{8,0},{1,9},{9,1},{2,10},{10,2},{3,11},{11,3},{4,12},{12,4},... | collective-permute-start | bytes 1572872 | tf_op jit(solution)/shard_map/ppermute | solution.py:266
  18.6 14.5 %collective-permute-start.14 = (bf16[512,256]{1,0:T(8,128)(2,1)S(1)}, bf16[512,256]{1,0:T(8,128)(2,1)}, u32[]{:S(2)}, u32[]{:S(2)}) collective-permute-start(bf16[512,256]{1,0:T(8,128)(2,1)S(1)} %collective-permute-done.3.refs_1_), channel_id=1, source_target_pairs={{0,32},{16,48},{32,64},{48,80},{64,96},{80,112},{96,0},{112,16},{1... | collective-permute-start | bytes 786440 | tf_op jit(solution)/shard_map/ppermute | solution.py:280
  18.6 14.6 %copy-start.4 = (s32[512]{0:T(512)S(1)}, s32[512]{0:T(512)}, u32[]{:S(2)}) copy-start(s32[512]{0:T(512)} %param.13) | copy-start | bytes 6148
  29.2 4.2 %collective-permute-start.15 = (bf16[512,256]{1,0:T(8,128)(2,1)S(1)}, bf16[512,256]{1,0:T(8,128)(2,1)}, u32[]{:S(2)}, u32[]{:S(2)}) collective-permute-start(bf16[512,256]{1,0:T(8,128)(2,1)S(1)} %collective-permute-done.refs_0_), channel_id=1, source_target_pairs={{0,16},{16,0},{32,48},{48,32},{64,80},{80,64},{96,112},{112,96},{1... | collective-permute-start | bytes 786440 | tf_op jit(solution)/shard_map/ppermute | solution.py:284
  29.2 4.2 %collective-permute-start.16 = (bf16[512,256]{1,0:T(8,128)(2,1)S(1)}, bf16[512,256]{1,0:T(8,128)(2,1)}, u32[]{:S(2)}, u32[]{:S(2)}) collective-permute-start(bf16[512,256]{1,0:T(8,128)(2,1)S(1)} %collective-permute-done.3.refs_1_), channel_id=1, source_target_pairs={{0,16},{16,0},{32,48},{48,32},{64,80},{80,64},{96,112},{112,96},{1... | collective-permute-start | bytes 786440 | tf_op jit(solution)/shard_map/ppermute | solution.py:284
  29.7 3.7 %collective-permute-start.17 = (bf16[512,256]{1,0:T(8,128)(2,1)S(1)}, bf16[512,256]{1,0:T(8,128)(2,1)}, u32[]{:S(2)}, u32[]{:S(2)}) collective-permute-start(bf16[512,256]{1,0:T(8,128)(2,1)S(1)} %collective-permute-done.4.refs_2_), channel_id=1, source_target_pairs={{0,16},{16,0},{32,48},{48,32},{64,80},{80,64},{96,112},{112,96},{1... | collective-permute-start | bytes 786440 | tf_op jit(solution)/shard_map/ppermute | solution.py:284
  29.8 21.2 %collective-permute-start.6 = (bf16[512,512]{1,0:T(8,128)(2,1)}, bf16[512,512]{1,0:T(8,128)(2,1)}, u32[]{:S(2)}, u32[]{:S(2)}) collective-permute-start(bf16[512,512]{1,0:T(8,128)(2,1)} %collective-permute-done.1.refs_0_), channel_id=1, source_target_pairs={{32,0},{48,16},{64,32},{80,48},{96,64},{112,80},{0,96},{16,112},{3... | collective-permute-start | bytes 1572872 | tf_op jit(solution)/shard_map/ppermute | solution.py:275
  33.0 1.9 collective-permute-start.18
  41.6 0.7 copy-start
  42.3 28.1 %all-to-all-start.1 = ((bf16[16,2,40,256]{3,2,1,0:T(8,128)(2,1)}), bf16[16,2,40,256]{3,2,1,0:T(8,128)(2,1)S(1)}, u32[]{:S(2)}, u32[]{:S(2)}) async-start(bf16[16,2,40,256]{3,2,1,0:T(8,128)(2,1)} %shard_map.74), calls=%async_computation.1 | async-start | bytes 1310720 | tf_op jit(solution)/shard_map/all_to_all | solution.py:248
  49.8 15.0 %collective-permute-start.5 = (bf16[512,512]{1,0:T(8,128)(2,1)}, bf16[512,512]{1,0:T(8,128)(2,1)}, u32[]{:S(2)}, u32[]{:S(2)}) collective-permute-start(bf16[512,512]{1,0:T(8,128)(2,1)} %collective-permute-done.1.refs_0_), channel_id=1, source_target_pairs={{0,32},{16,48},{32,64},{48,80},{64,96},{80,112},{96,0},{112,16},{1... | collective-permute-start | bytes 1572872 | tf_op jit(solution)/shard_map/ppermute | solution.py:274
  49.8 20.2 %collective-permute-start.2 = (bf16[512,512]{1,0:T(8,128)(2,1)}, bf16[512,512]{1,0:T(8,128)(2,1)}, u32[]{:S(2)}, u32[]{:S(2)}) collective-permute-start(bf16[512,512]{1,0:T(8,128)(2,1)} %get-tuple-element.11), channel_id=1, source_target_pairs={{0,8},{8,0},{1,9},{9,1},{2,10},{10,2},{3,11},{11,3},{4,12},{12,4},... | collective-permute-start | bytes 1572872 | tf_op jit(solution)/shard_map/ppermute | solution.py:266
  51.0 19.4 %collective-permute-start.19 = (bf16[512,512]{1,0:T(8,128)(2,1)}, bf16[512,512]{1,0:T(8,128)(2,1)}, u32[]{:S(2)}, u32[]{:S(2)}) collective-permute-start(bf16[512,512]{1,0:T(8,128)(2,1)} %collective-permute-done.6.refs_2_), channel_id=1, source_target_pairs={{32,0},{48,16},{64,32},{80,48},{96,64},{112,80},{0,96},{16,112},{3... | collective-permute-start | bytes 1572872 | tf_op jit(solution)/shard_map/ppermute | solution.py:278
  54.2 16.4 %collective-permute-start.20 = (bf16[512,512]{1,0:T(8,128)(2,1)}, bf16[512,512]{1,0:T(8,128)(2,1)}, u32[]{:S(2)}, u32[]{:S(2)}) collective-permute-start(bf16[512,512]{1,0:T(8,128)(2,1)} %collective-permute-done.1.refs_0_), channel_id=1, source_target_pairs={{0,16},{16,0},{32,48},{48,32},{64,80},{80,64},{96,112},{112,96},{1... | collective-permute-start | bytes 1572872 | tf_op jit(solution)/shard_map/ppermute | solution.py:284
  70.0 14.4 %collective-permute-start.7 = (bf16[512,512]{1,0:T(8,128)(2,1)}, bf16[512,512]{1,0:T(8,128)(2,1)}, u32[]{:S(2)}, u32[]{:S(2)}) collective-permute-start(bf16[512,512]{1,0:T(8,128)(2,1)} %collective-permute-done.2.refs_0_), channel_id=1, source_target_pairs={{0,32},{16,48},{32,64},{48,80},{64,96},{80,112},{96,0},{112,16},{1... | collective-permute-start | bytes 1572872 | tf_op jit(solution)/shard_map/ppermute | solution.py:274
  70.0 14.4 %collective-permute-start.22 = (bf16[512,512]{1,0:T(8,128)(2,1)}, bf16[512,512]{1,0:T(8,128)(2,1)}, u32[]{:S(2)}, u32[]{:S(2)}) collective-permute-start(bf16[512,512]{1,0:T(8,128)(2,1)} %collective-permute-done.6.refs_2_), channel_id=1, source_target_pairs={{0,16},{16,0},{32,48},{48,32},{64,80},{80,64},{96,112},{112,96},{1... | collective-permute-start | bytes 1572872 | tf_op jit(solution)/shard_map/ppermute | solution.py:284
  70.0 14.4 %collective-permute-start.21 = (bf16[512,512]{1,0:T(8,128)(2,1)}, bf16[512,512]{1,0:T(8,128)(2,1)}, u32[]{:S(2)}, u32[]{:S(2)}) collective-permute-start(bf16[512,512]{1,0:T(8,128)(2,1)} %collective-permute-done.5.refs_1_), channel_id=1, source_target_pairs={{0,16},{16,0},{32,48},{48,32},{64,80},{80,64},{96,112},{112,96},{1... | collective-permute-start | bytes 1572872 | tf_op jit(solution)/shard_map/ppermute | solution.py:284
  70.5 13.9 %collective-permute-start.23 = (bf16[512,512]{1,0:T(8,128)(2,1)}, bf16[512,512]{1,0:T(8,128)(2,1)S(1)}, u32[]{:S(2)}, u32[]{:S(2)}) collective-permute-start(bf16[512,512]{1,0:T(8,128)(2,1)} %collective-permute-done.19.refs_3_), channel_id=1, source_target_pairs={{0,16},{16,0},{32,48},{48,32},{64,80},{80,64},{96,112},{112,96},{1... | collective-permute-start | bytes 1572872 | tf_op jit(solution)/shard_map/ppermute | solution.py:284
  70.6 30.4 %collective-permute-start.8 = (bf16[512,512]{1,0:T(8,128)(2,1)}, bf16[512,512]{1,0:T(8,128)(2,1)}, u32[]{:S(2)}, u32[]{:S(2)}) collective-permute-start(bf16[512,512]{1,0:T(8,128)(2,1)} %collective-permute-done.2.refs_0_), channel_id=1, source_target_pairs={{32,0},{48,16},{64,32},{80,48},{96,64},{112,80},{0,96},{16,112},{3... | collective-permute-start | bytes 1572872 | tf_op jit(solution)/shard_map/ppermute | solution.py:275
  84.3 16.7 %collective-permute-start.9 = (bf16[512,512]{1,0:T(8,128)(2,1)}, bf16[512,512]{1,0:T(8,128)(2,1)}, u32[]{:S(2)}, u32[]{:S(2)}) collective-permute-start(bf16[512,512]{1,0:T(8,128)(2,1)} %collective-permute-done.7.refs_1_), channel_id=1, source_target_pairs={{0,32},{16,48},{32,64},{48,80},{64,96},{80,112},{96,0},{112,16},{1... | collective-permute-start | bytes 1572872 | tf_op jit(solution)/shard_map/ppermute | solution.py:280
  84.3 1.0 copy-start.1
  93.2 29.8 %copy-start.3 = (s32[40]{0:T(128)S(1)}, s32[40]{0:T(128)}, u32[]{:S(2)}) copy-start(s32[40]{0:T(128)} %fill_ref.3) | copy-start | bytes 484
  93.2 24.9 %all-to-all-start.3 = ((bf16[16,2,40,512]{3,2,1,0:T(8,128)(2,1)}), bf16[16,2,40,512]{3,2,1,0:T(8,128)(2,1)}, u32[]{:S(2)}, u32[]{:S(2)}) async-start(bf16[16,2,40,512]{3,2,1,0:T(8,128)(2,1)} %shard_map.76), calls=%async_computation.3 | async-start | bytes 2621440 | tf_op jit(solution)/shard_map/all_to_all | solution.py:248
  100.5 2.1 %collective-permute-start.10 = (bf16[512,512]{1,0:T(8,128)(2,1)}, bf16[512,512]{1,0:T(8,128)(2,1)S(1)}, u32[]{:S(2)}, u32[]{:S(2)}) collective-permute-start(bf16[512,512]{1,0:T(8,128)(2,1)} %collective-permute-done.2.refs_0_), channel_id=1, source_target_pairs={{0,16},{16,0},{32,48},{48,32},{64,80},{80,64},{96,112},{112,96},{1... | collective-permute-start | bytes 1572872 | tf_op jit(solution)/shard_map/ppermute | solution.py:284
  100.5 2.9 %collective-permute-start.11 = (bf16[512,512]{1,0:T(8,128)(2,1)}, bf16[512,512]{1,0:T(8,128)(2,1)S(1)}, u32[]{:S(2)}, u32[]{:S(2)}) collective-permute-start(bf16[512,512]{1,0:T(8,128)(2,1)} %collective-permute-done.7.refs_1_), channel_id=1, source_target_pairs={{0,16},{16,0},{32,48},{48,32},{64,80},{80,64},{96,112},{112,96},{1... | collective-permute-start | bytes 1572872 | tf_op jit(solution)/shard_map/ppermute | solution.py:284
  101.0 3.1 %collective-permute-start.12 = (bf16[512,512]{1,0:T(8,128)(2,1)}, bf16[512,512]{1,0:T(8,128)(2,1)S(1)}, u32[]{:S(2)}, u32[]{:S(2)}) collective-permute-start(bf16[512,512]{1,0:T(8,128)(2,1)} %collective-permute-done.8.refs_2_), channel_id=1, source_target_pairs={{0,16},{16,0},{32,48},{48,32},{64,80},{80,64},{96,112},{112,96},{1... | collective-permute-start | bytes 1572872 | tf_op jit(solution)/shard_map/ppermute | solution.py:284
  101.1 3.8 %collective-permute-start.13 = (bf16[512,512]{1,0:T(8,128)(2,1)}, bf16[512,512]{1,0:T(8,128)(2,1)S(1)}, u32[]{:S(2)}, u32[]{:S(2)}) collective-permute-start(bf16[512,512]{1,0:T(8,128)(2,1)} %collective-permute-done.9.refs_3_), channel_id=1, source_target_pairs={{0,16},{16,0},{32,48},{48,32},{64,80},{80,64},{96,112},{112,96},{1... | collective-permute-start | bytes 1572872 | tf_op jit(solution)/shard_map/ppermute | solution.py:284
  104.8 1.0 copy-start.2
  118.2 23.7 %all-to-all-start = ((bf16[16,2,40,512]{3,2,1,0:T(8,128)(2,1)}), bf16[16,2,40,512]{3,2,1,0:T(8,128)(2,1)S(1)}, u32[]{:S(2)}, u32[]{:S(2)}) async-start(bf16[16,2,40,512]{3,2,1,0:T(8,128)(2,1)} %shard_map.73), calls=%async_computation | async-start | bytes 2621440 | tf_op jit(solution)/shard_map/all_to_all | solution.py:248
  141.9 23.4 %all-to-all-start.4 = ((bf16[16,2,40,512]{3,2,1,0:T(8,128)(2,1)}), bf16[16,2,40,512]{3,2,1,0:T(8,128)(2,1)S(1)}, u32[]{:S(2)}, u32[]{:S(2)}) async-start(bf16[16,2,40,512]{3,2,1,0:T(8,128)(2,1)} %bitcast.23), calls=%async_computation.4 | async-start | bytes 2621440 | tf_op jit(solution)/shard_map/all_to_all | solution.py:248
  165.2 23.5 %all-to-all-start.2 = ((bf16[16,2,40,512]{3,2,1,0:T(8,128)(2,1)}), bf16[16,2,40,512]{3,2,1,0:T(8,128)(2,1)S(1)}, u32[]{:S(2)}, u32[]{:S(2)}) async-start(bf16[16,2,40,512]{3,2,1,0:T(8,128)(2,1)} %bitcast.22), calls=%async_computation.2 | async-start | bytes 2621440 | tf_op jit(solution)/shard_map/all_to_all | solution.py:248

commit v4 on v3

--- a/solution.py
+++ b/solution.py
@@ -11,7 +11,7 @@
 SHARING = 8
 ROPE_BASE = 1000000.0
 SWAP = ((0, 1), (1, 0))
-CHUNKS = ((0, 4), (4, 8))
+CHUNKS = ((4, 8), (0, 4))
 ROW_BLOCK = 8
 NT = (((1,), (1,)), ((), ()))
 
@@ -28,7 +28,7 @@
     return jnp.concatenate([cosine, cosine], -1), jnp.concatenate([-sine, sine], -1)
 
 
-def project_kernel(columns, owners, rows, places_ref, x_ref, *refs):
+def project_kernel(owners, rows, places_ref, x_ref, *refs):
     slabs = refs[:-6]
     partial_ref, pack_ref, out_ref, taken, total, arrived = refs[-6:]
     depth = slabs[0].shape[0]
@@ -44,7 +44,7 @@
         copies[i].wait()
         product = jnp.dot(taken[i], slab[...], preferred_element_type=jnp.float32)
         if i == 0:
-            total[...] = partial_ref[:, slice(*columns)] + product
+            total[...] = partial_ref[...] + product
         else:
             total[...] += product
     for step in range(2):
@@ -55,14 +55,14 @@
             out_ref[owner, step] = block.astype(jnp.bfloat16)
 
 
-def project(places, signals, slabs, partial, columns, pack, owners):
+def project(places, signals, slabs, partial, pack, owners):
     lines, _ = signals.shape
     depth, wide = slabs[0].shape
     slots, share = pack.shape
     rows = slots // owners
     local = pl.BlockSpec(memory_space=pltpu.VMEM)
     return pl.pallas_call(
-        functools.partial(project_kernel, columns, owners, rows),
+        functools.partial(project_kernel, owners, rows),
         out_shape=pltpu.HBM((owners, 2, rows, wide), jnp.bfloat16),
         grid_spec=pltpu.PrefetchScalarGridSpec(
             num_scalar_prefetch=1,
@@ -75,7 +75,7 @@
                 pltpu.SemaphoreType.DMA((len(slabs),)),
             ],
         ),
-        compiler_params=pltpu.CompilerParams(vmem_limit_bytes=32 << 20),
+        compiler_params=pltpu.CompilerParams(vmem_limit_bytes=26 << 20),
         cost_estimate=pl.CostEstimate(
             flops=2 * lines * depth * len(slabs) * wide,
             transcendentals=0,
@@ -84,7 +84,7 @@
     )(places, in_hbm(signals), *slabs, partial, pack)
 
 
-def attention_kernel(heads, fill_ref, cos_ref, sin_ref, q_ref, new_ref, k_ref, v_ref, out_ref,
+def attention_kernel(heads, fill_ref, cos_ref, sin_ref, q_ref, k_new_ref, v_new_ref, k_ref, v_ref, out_ref,
                      q_rot, k_rot, v_new, cached_scores, new_scores, blended):
     n_tp = q_ref.shape[1]
     block = ROW_BLOCK
@@ -115,8 +115,8 @@
                 at = pl.ds(t * size + (step * heads + head) * block, block)
                 q_rot[at, :] = turned(both(q_ref, t, step, head * HEAD), step)
             at = pl.ds(step * block, block)
-            k_rot[t, at, :] = turned(both(new_ref, t, step, 0), step)
-            v_new[t, at, :] = both(new_ref, t, step, HEAD)
+            k_rot[t, at, :] = turned(both(k_new_ref, t, step, 0), step)
+            v_new[t, at, :] = both(v_new_ref, t, step, 0)
     for t in range(n_tp):
         lanes = slice(t * HEAD, (t + 1) * HEAD)
         queries = [
@@ -153,7 +153,7 @@
                     out_ref[pair, t, step, :, head * HEAD:(head + 1) * HEAD] = done
 
 
-def attend(fill, cosine, sine, queries, new, keys, values, heads):
+def attend(fill, cosine, sine, queries, new, new_at, keys, values, heads):
     _, n_tp, _, rows, _ = queries.shape
     places = keys.shape[1]
     block = ROW_BLOCK
@@ -161,8 +161,8 @@
     table = pl.BlockSpec((2, block, HEAD), lambda r, f: (0, r, 0))
     cache = pl.BlockSpec((block, places, n_tp * HEAD), lambda r, f: (r, 0, 0))
 
-    def routed(columns):
-        return pl.BlockSpec((2, n_tp, 2, block, columns), lambda r, f: (0, 0, 0, r, 0))
+    def routed(columns, at=0):
+        return pl.BlockSpec((2, n_tp, 2, block, columns), lambda r, f: (0, 0, 0, r, at))
 
     return pl.pallas_call(
         functools.partial(attention_kernel, heads),
@@ -170,7 +170,10 @@
         grid_spec=pltpu.PrefetchScalarGridSpec(
             num_scalar_prefetch=1,
             grid=(rows // block,),
-            in_specs=[table, table, routed(heads * HEAD), routed(2 * HEAD), cache, cache],
+            in_specs=[
+                table, table, routed(heads * HEAD), routed(HEAD, new_at), routed(HEAD, new_at + 1),
+                cache, cache,
+            ],
             out_specs=routed(heads * HEAD),
             scratch_shapes=[
                 pltpu.VMEM((n_tp * width, HEAD), jnp.float32),
@@ -181,14 +184,14 @@
                 pltpu.VMEM((n_tp * width, HEAD), jnp.float32),
             ],
         ),
-        compiler_params=pltpu.CompilerParams(vmem_limit_bytes=32 << 20),
+        compiler_params=pltpu.CompilerParams(vmem_limit_bytes=18 << 20),
         cost_estimate=pl.CostEstimate(
             flops=8 * heads * rows * n_tp * places * HEAD,
             transcendentals=2 * heads * rows * n_tp * places,
             bytes_accessed=4 * rows * places * n_tp * HEAD,
         ),
     )(
-        fill, cosine, sine, queries, new, in_hbm(keys), in_hbm(values)
+        fill, cosine, sine, in_hbm(queries), in_hbm(new), in_hbm(new), in_hbm(keys), in_hbm(values)
     )
 
 
@@ -217,7 +220,7 @@
         out_specs=pl.BlockSpec((1, share, wide), lambda s: (s, 0, at)),
         scratch_shapes=[pltpu.VMEM((slots, wide), jnp.float32)],
         input_output_aliases={2: 0} if before else {},
-        compiler_params=pltpu.CompilerParams(vmem_limit_bytes=32 << 20),
+        compiler_params=pltpu.CompilerParams(vmem_limit_bytes=8 << 20),
         cost_estimate=pl.CostEstimate(
             flops=4 * share * slots * wide, transcendentals=0, bytes_accessed=4 * slots * wide
         ),
@@ -237,61 +240,70 @@
         return lax.optimization_barrier((value, *earlier))[0]
 
     flat = signals.reshape(2 * share, features)
-    own = lax.dynamic_slice_in_dim(lines, pair * share, share)
+    listed = lax.dynamic_slice_in_dim(lines, pair * share, share)
     slots = jnp.arange(owners * rows, dtype=jnp.int32)
-    pack = (slots[:, None] == own[None, :]).astype(jnp.bfloat16)
-    pick = (own[:, None] == slots[None, :]).astype(jnp.bfloat16)
+    pack = (slots[:, None] == listed[None, :]).astype(jnp.bfloat16)
+    pick = (listed[:, None] == slots[None, :]).astype(jnp.bfloat16)
     positions = fill[None, :] + jnp.arange(2, dtype=jnp.int32)[:, None]
     cosine, sine = rope_tables(positions)
 
     def exchange(blocks):
         return lax.all_to_all(blocks, ("pair", "tp"), split_axis=0, concat_axis=0, tiled=True)
 
-    spans = [(SHARING * HEAD, columns)] + [(a * HEAD, b * HEAD) for a, b in CHUNKS]
+    spans = [(a * HEAD, (b + 2 if b == SHARING else b) * HEAD) for a, b in CHUNKS]
     n_z = n_grp // 2
     up = [(2 * a + c, 2 * ((a + 1) % n_z) + c) for a in range(n_z) for c in range(2)]
     down = [(d, s) for s, d in up]
     twin = [(2 * a + c, 2 * a + 1 - c) for a in range(n_z) for c in range(2)]
     z, core = grp // 2, grp % 2
     turns = (0, n_z - 1, 1, 2)
+    slab_of = [(z + turn) % n_z * 2 + core for turn in turns]
     places = (1 - pair) * n_grp + jnp.stack(
-        [(z + turn) % n_z * 2 + core for turn in turns]
-        + [(z + turn) % n_z * 2 + 1 - core for turn in turns]
+        slab_of + [(z + turn) % n_z * 2 + 1 - core for turn in turns]
     )
     places = places.astype(jnp.int32)
 
-    first = []
-    for start, stop in spans:
-        slab = lax.dynamic_slice(matrix, (grp * depth, start), (depth, stop - start))
-        first.append(lax.ppermute(after(slab, *first[-1:]), "pair", SWAP))
+    def slab(at, span):
+        return lax.dynamic_slice(matrix, (at * depth, span[0]), (depth, span[1] - span[0]))
+
     near = lax.dynamic_slice_in_dim(flat, pair * half, half, 1)
-    partial = jnp.dot(near, matrix, preferred_element_type=jnp.float32)
-    partial = partial + offset.astype(jnp.float32)
-
-    arrived, ahead = [], []
-    for number, ((start, stop), slab) in enumerate(zip(spans, first)):
-        slab = after(slab, *ahead)
-        below = lax.ppermute(slab, "grp", up)
-        above = lax.ppermute(slab, "grp", down)
-        ahead = [below, above]
-        if number % 2:
-            opposite = lax.ppermute(above, "grp", down)
-        else:
-            opposite = lax.ppermute(below, "grp", up)
-        if number == 1:
-            opposite = after(opposite, arrived[0])
-        held = [slab, below, above, opposite]
-        held += [lax.ppermute(piece, "grp", twin) for piece in held]
-        packed = project(places, flat, held, partial, (start, stop), pack, owners)
-        arrived.append(exchange(packed).reshape(n_pair, n_tp, 2, rows, stop - start))
+    partials = [
+        jnp.dot(near, matrix[:, slice(*span)], preferred_element_type=jnp.float32)
+        + offset[slice(*span)].astype(jnp.float32)
+        for span in spans
+    ]
+
+    crossed = []
+    for distance in (0, 3):
+        for number, span in enumerate(spans):
+            with jax.named_scope("over_pair_%d" % number):
+                piece = after(slab(slab_of[distance], span), *crossed[-1:])
+                crossed.append(lax.ppermute(piece, "pair", SWAP))
+    crossed[0] = after(crossed[0], *partials)
+    held = []
+    for number in range(len(spans)):
+        own, far = crossed[number], crossed[len(spans) + number]
+        with jax.named_scope("from_neighbours_%d" % number):
+            below = lax.ppermute(own, "grp", up)
+            above = lax.ppermute(own, "grp", down)
+        with jax.named_scope("from_twin_%d" % number):
+            four = [own, below, above, far]
+            held.append(four + [lax.ppermute(piece, "grp", twin) for piece in four])
+    arrived = []
+    for number, (span, slabs) in enumerate(zip(spans, held)):
+        with jax.named_scope("project_%d" % number):
+            packed = project(places, flat, slabs, partials[number], pack, owners)
+        with jax.named_scope("route_%d" % number):
+            arrived.append(exchange(packed).reshape(n_pair, n_tp, 2, rows, span[1] - span[0]))
     out = None
-    for (start, stop), queries in zip(spans[1:], arrived[1:]):
-        heads = (stop - start) // HEAD
+    for (first, last), queries in zip(CHUNKS, arrived):
+        heads = last - first
         attended = attend(
-            fill, cosine, sine, queries, arrived[0], cached_keys, cached_values, heads
+            fill, cosine, sine, queries, arrived[0], SHARING - CHUNKS[0][0],
+            cached_keys, cached_values, heads,
         )
-        back = exchange(attended.reshape(owners, 2, rows, stop - start))
-        out = unpack(pick, back, start // (stop - start), SHARING * HEAD, out)
+        back = exchange(attended.reshape(owners, 2, rows, heads * HEAD))
+        out = unpack(pick, back, first // heads, SHARING * HEAD, out)
     return out
 
 

time: 191 us -> 199 us (1.042)
  waiting for transfers between devices: 69.9 us -> 93.4 us
  starting transfers between devices: 48.9 us -> 35.5 us
  Pallas kernels: 53.6 us -> 49.7 us
  matrix products: 10.4 us -> 12.8 us
    ppermute x24 -> x16, waiting for transfers between devices: 39.3 us -> 66.3 us  [the longest x4 32 us: per_device(): crossed.append(lax.ppermute(piece, 'pair', SWAP))]
    ppermute x24 -> x16, starting transfers between devices: 19.8 us -> 12.2 us  [the longest x2 7.15 us: per_device(): above = lax.ppermute(own, 'grp', down)]
    all_to_all x5 -> x4, starting transfers between devices: 29.1 us -> 23.3 us  [exchange(): lax.all_to_all(blocks, ('pair', 'tp'), split_axis=0, concat_axis=0, tiled...]
    pallas_call x3 -> x2, Pallas kernels: 22 us -> 17.6 us  [project(): pl.pallas_call(functools.partial(project_kernel, owners, rows), out_shape...]
    all_to_all x5 -> x4, waiting for transfers between devices: 30.5 us -> 27.2 us  [exchange(): lax.all_to_all(blocks, ('pair', 'tp'), split_axis=0, concat_axis=0, tiled...]
    unnamed x10 -> x8, local copies, waits for them, and re-layouts: 2.66 us -> 0.01 us
    dot_general x1 -> x2, matrix products: 10.4 us -> 12.8 us  [per_device(): jnp.dot(near, matrix[:, slice(*span)], preferred_element_type=jnp.float32)]
  transfers between devices with their start and end apart: 29 -> 20, of which waited for: 14 -> 14; matrix products, arithmetic and copies ran while one was open for 7% -> 9% of each run, Pallas kernels for 27% -> 18%
where the time goes in v4:
time: 199 us; the launch traced here: 198 us
  waiting for transfers between devices  93.4 us (47%)
  Pallas kernels  49.7 us (25%)
  starting transfers between devices  35.5 us (18%)
  matrix products  12.8 us (6%)
  local copies, waits for them, and re-layouts  4.77 us (2%)
    ppermute x4, waiting for transfers between devices, per_device(): crossed.append(lax.ppermute(piece, 'pair', SWAP))  32 us
    pallas_call x2, Pallas kernels, attend(): pl.pallas_call(functools.partial(attention_kernel, heads), out_shape=pltp...  28.9 us
    all_to_all x4, waiting for transfers between devices, exchange(): lax.all_to_all(blocks, ('pair', 'tp'), split_axis=0, concat_axis=0, tiled...  27.2 us
    all_to_all x4, starting transfers between devices, exchange(): lax.all_to_all(blocks, ('pair', 'tp'), split_axis=0, concat_axis=0, tiled...  23.3 us
    ppermute x2, waiting for transfers between devices, per_device(): above = lax.ppermute(own, 'grp', down)  22.6 us
    pallas_call x2, Pallas kernels, project(): pl.pallas_call(functools.partial(project_kernel, owners, rows), out_shape...  17.6 us
    dot_general x2, matrix products, per_device(): jnp.dot(near, matrix[:, slice(*span)], preferred_element_type=jnp.float32)  12.8 us
    ppermute x2, starting transfers between devices, per_device(): above = lax.ppermute(own, 'grp', down)  7.15 us
  transfers between devices with their start and end apart: 20, of which 14 were waited for; matrix products, arithmetic and copies ran while one was open for 9% of the time, Pallas kernels for 18%

profile of v4, /device:TPU:4, one launch (start us, length us, event | category | flops | bytes accessed | tf_op | source)
XLA Modules:
  0.0 198.3 jit_solution(3520670027351924373)
XLA Ops:
  0.0 2.4 %constant_dynamic-slice_fusion.2 = (bf16[512,768]{1,0:T(8,128)(2,1)}, bf16[512,768]{1,0:T(8,128)(2,1)S(1)}) fusion(bf16[4096,1280]{1,0:T(8,128)(2,1)} %param.8, s32[]{:T(128)S(6)} %select_n.57, s32[]{:T(128)S(6)} %select_n.56), kind=kLoop, calls=%fused_computation.25 | loop fusion | bytes 3145736 | tf_op jit(solution)/shard_map/over_pair_0/dynamic_slice | solution.py:267
  2.4 1.2 collective-permute-start
  3.5 0.7 slice_convert_fusion.1
  4.2 0.7 slice_convert_fusion
  4.9 2.3 %constant_dynamic-slice_fusion = (bf16[512,512]{1,0:T(8,128)(2,1)}, bf16[512,512]{1,0:T(8,128)(2,1)}) fusion(bf16[4096,1280]{1,0:T(8,128)(2,1)} %param.8, s32[]{:T(128)S(6)} %select_n.57, s32[]{:T(128)S(6)} %select_n.56), kind=kLoop, calls=%fused_computation.22 | loop fusion | bytes 2097160 | tf_op jit(solution)/shard_map/over_pair_1/dynamic_slice | solution.py:267
  7.2 7.0 %fusion.6.refs_8_ = f32[512,768]{1,0:T(8,128)S(1)} fusion(bf16[4096,1280]{1,0:T(8,128)(2,1)} %param.8, bf16[512,8192]{1,0:T(8,128)(2,1)} %bitcast.13, s32[]{:T(128)S(6)} %select_n.58, f32[768]{0:T(1024)S(1)} %slice_convert_fusion), kind=kOutput, calls=%fused_computation.6 | convolution fusion | flops 3221618688 | bytes 12061700 | tf_op jit(solution)/shard_map/dot_general | solution.py:271
  14.2 7.5 %collective-permute-done.refs_0_ = bf16[512,768]{1,0:T(8,128)(2,1)} collective-permute-done((bf16[512,768]{1,0:T(8,128)(2,1)S(1)}, bf16[512,768]{1,0:T(8,128)(2,1)}, u32[]{:S(2)}, u32[]{:S(2)}) %collective-permute-start) | collective-permute-done | bytes 786464 | tf_op jit(solution)/shard_map/over_pair_0/ppermute | solution.py:281
  21.7 1.2 collective-permute-start.1
  22.9 5.8 %fusion.11.refs_8_ = f32[512,512]{1,0:T(8,128)S(1)} fusion(bf16[4096,1280]{1,0:T(8,128)(2,1)} %param.8, bf16[512,8192]{1,0:T(8,128)(2,1)} %bitcast.14, s32[]{:T(128)S(6)} %select_n.58, f32[512]{0:T(512)S(1)} %slice_convert_fusion.1), kind=kOutput, calls=%fused_computation.7 | convolution fusion | flops 2147745792 | bytes 9439236 | tf_op jit(solution)/shard_map/dot_general | solution.py:271
  28.7 4.1 %collective-permute-start.11 = (bf16[512,768]{1,0:T(8,128)(2,1)}, bf16[512,768]{1,0:T(8,128)(2,1)}, u32[]{:S(2)}, u32[]{:S(2)}) collective-permute-start(bf16[512,768]{1,0:T(8,128)(2,1)} %collective-permute-done.refs_0_), channel_id=1, source_target_pairs={{32,0},{48,16},{64,32},{80,48},{96,64},{112,80},{0,96},{16,112},{3... | collective-permute-start | bytes 2359304 | tf_op jit(solution)/shard_map/from_neighbours_0/ppermute | solution.py:288
  32.8 0.0 collective-permute-start.10
  32.8 1.9 collective-permute-done.1.refs_0_
  34.7 1.2 collective-permute-start.4
  35.9 0.0 collective-permute-start.12
  35.9 12.9 %collective-permute-done.11.refs_2_ = bf16[512,768]{1,0:T(8,128)(2,1)} collective-permute-done((bf16[512,768]{1,0:T(8,128)(2,1)}, bf16[512,768]{1,0:T(8,128)(2,1)}, u32[]{:S(2)}, u32[]{:S(2)}) %collective-permute-start.11) | collective-permute-done | bytes 786464 | tf_op jit(solution)/shard_map/from_neighbours_0/ppermute | solution.py:288
  48.8 3.4 %collective-permute-done.10.refs_1_ = bf16[512,768]{1,0:T(8,128)(2,1)} collective-permute-done((bf16[512,768]{1,0:T(8,128)(2,1)}, bf16[512,768]{1,0:T(8,128)(2,1)}, u32[]{:S(2)}, u32[]{:S(2)}) %collective-permute-start.10) | collective-permute-done | bytes 786464 | tf_op jit(solution)/shard_map/from_neighbours_0/ppermute | solution.py:287
  52.2 0.0 collective-permute-start.13
  52.2 0.2 collective-permute-done.4.refs_3_
  52.4 0.3 collective-permute-start.15
  52.7 0.1 dynamic_slice.18
  52.8 0.1 stack.35
  52.9 0.1 fusion.17.refs_9_
  53.0 0.0 collective-permute-done.12.refs_4_
  53.0 1.8 collective-permute-done.13.refs_5_
  54.8 1.1 collective-permute-done.15.refs_7_
  56.0 11.7 %project_0.1 = bf16[16,2,40,768]{3,2,1,0:T(8,128)(2,1)} custom-call(s32[8]{0:T(128)S(1)} %broadcast_add_fusion.places_ref, bf16[512,8192]{1,0:T(8,128)(2,1)} %bitcast.15, bf16[512,768]{1,0:T(8,128)(2,1)} %collective-permute-done.refs_0_, bf16[512,768]{1,0:T(8,128)(2,1)} %collective-permute-done.10.refs_1_, bf16[512,768]{1,0:T(8,128)(2,1)} %collective-permute-done.11.refs_2_, ...), custom_call_target="tpu_custom_call" | custom-call | flops 3221225472 | bytes 4194304 | tf_op jit(solution)/shard_map/project_0/pallas_call | solution.py:64
  67.7 7.5 %all-to-all-start.1 = ((bf16[16,2,40,768]{3,2,1,0:T(8,128)(2,1)}), bf16[16,2,40,768]{3,2,1,0:T(8,128)(2,1)}, u32[]{:S(2)}, u32[]{:S(2)}) async-start(bf16[16,2,40,768]{3,2,1,0:T(8,128)(2,1)} %project_0.1), calls=%async_computation.1 | async-start | bytes 3932160 | tf_op jit(solution)/shard_map/route_0/all_to_all | solution.py:251
  75.2 3.0 %collective-permute-start.3 = (bf16[512,512]{1,0:T(8,128)(2,1)S(1)}, bf16[512,512]{1,0:T(8,128)(2,1)S(1)}, u32[]{:S(2)}, u32[]{:S(2)}) collective-permute-start(bf16[512,512]{1,0:T(8,128)(2,1)S(1)} %collective-permute-done.1.refs_0_), channel_id=1, source_target_pairs={{32,0},{48,16},{64,32},{80,48},{96,64},{112,80},{0,96},{16,112},{3... | collective-permute-start | bytes 1572872 | tf_op jit(solution)/shard_map/from_neighbours_1/ppermute | solution.py:288
  78.2 1.2 collective-permute-start.5
  79.4 9.7 %collective-permute-done.3.refs_2_ = bf16[512,512]{1,0:T(8,128)(2,1)S(1)} collective-permute-done((bf16[512,512]{1,0:T(8,128)(2,1)S(1)}, bf16[512,512]{1,0:T(8,128)(2,1)S(1)}, u32[]{:S(2)}, u32[]{:S(2)}) %collective-permute-start.3) | collective-permute-done | bytes 524320 | tf_op jit(solution)/shard_map/from_neighbours_1/ppermute | solution.py:288
  89.1 3.4 %collective-permute-done.2.refs_1_ = bf16[512,512]{1,0:T(8,128)(2,1)S(1)} collective-permute-done((bf16[512,512]{1,0:T(8,128)(2,1)S(1)}, bf16[512,512]{1,0:T(8,128)(2,1)S(1)}, u32[]{:S(2)}, u32[]{:S(2)}) %collective-permute-start.2) | collective-permute-done | bytes 524320 | tf_op jit(solution)/shard_map/from_neighbours_1/ppermute | solution.py:287
  92.6 0.0 collective-permute-start.7
  92.6 22.4 %collective-permute-done.5.refs_3_ = bf16[512,512]{1,0:T(8,128)(2,1)S(1)} collective-permute-done((bf16[512,512]{1,0:T(8,128)(2,1)}, bf16[512,512]{1,0:T(8,128)(2,1)S(1)}, u32[]{:S(2)}, u32[]{:S(2)}) %collective-permute-start.5) | collective-permute-done | bytes 524320 | tf_op jit(solution)/shard_map/over_pair_1/ppermute | solution.py:281
  114.9 1.9 collective-permute-done.9.refs_7_
  116.8 5.9 %project_1.1 = bf16[16,2,40,512]{3,2,1,0:T(8,128)(2,1)} custom-call(s32[8]{0:T(128)S(1)} %broadcast_add_fusion.places_ref, bf16[512,8192]{1,0:T(8,128)(2,1)} %bitcast.16, bf16[512,512]{1,0:T(8,128)(2,1)S(1)} %collective-permute-done.1.refs_0_, bf16[512,512]{1,0:T(8,128)(2,1)S(1)} %collective-permute-done.2.refs_1_, ...), custom_call_target="tpu_custom_call" | custom-call | flops 2147483648 | bytes 4194304 | tf_op jit(solution)/shard_map/project_1/pallas_call | solution.py:64
  122.7 6.2 %all-to-all-start = ((bf16[16,2,40,512]{3,2,1,0:T(8,128)(2,1)}), bf16[16,2,40,512]{3,2,1,0:T(8,128)(2,1)S(1)}, u32[]{:S(2)}, u32[]{:S(2)}) async-start(bf16[16,2,40,512]{3,2,1,0:T(8,128)(2,1)} %project_1.1), calls=%async_computation | async-start | bytes 2621440 | tf_op jit(solution)/shard_map/route_1/all_to_all | solution.py:251
  128.9 0.2 fusion.18
  129.2 0.1 pad_maximum_fusion
  129.3 14.5 %shard_map.74 = bf16[2,8,2,40,512]{4,3,2,1,0:T(8,128)(2,1)} custom-call(s32[40]{0:T(128)S(1)} %copy-done, f32[2,40,128]{2,1,0:T(8,128)S(1)} %get-tuple-element.20.cos_ref, f32[2,40,128]{2,1,0:T(8,128)S(1)} %get-tuple-element.21.sin_ref, bf16[2,8,2,40,768]{4,3,2,1,0:T(8,128)(2,1)} %bitcast.10.k_new_ref.v_new_ref.q_ref, ...), custom_call_target="tpu_custom_call" | custom-call | flops 167772160 | bytes 20971520 | tf_op jit(solution)/shard_map/pallas_call | solution.py:167
  143.7 5.6 %all-to-all-done = bf16[16,2,40,512]{3,2,1,0:T(8,128)(2,1)S(1)} async-done(((bf16[16,2,40,512]{3,2,1,0:T(8,128)(2,1)}), bf16[16,2,40,512]{3,2,1,0:T(8,128)(2,1)S(1)}, u32[]{:S(2)}, u32[]{:S(2)}) %all-to-all-start) | async-done | bytes 1310752 | tf_op jit(solution)/shard_map/route_1/all_to_all | solution.py:251
  149.4 4.8 %all-to-all-start.3 = ((bf16[16,2,40,512]{3,2,1,0:T(8,128)(2,1)}), bf16[16,2,40,512]{3,2,1,0:T(8,128)(2,1)S(1)}, u32[]{:S(2)}, u32[]{:S(2)}) async-start(bf16[16,2,40,512]{3,2,1,0:T(8,128)(2,1)} %bitcast.17), calls=%async_computation.3 | async-start | bytes 2621440 | tf_op jit(solution)/shard_map/all_to_all | solution.py:251
  154.2 14.5 %shard_map.73 = bf16[2,8,2,40,512]{4,3,2,1,0:T(8,128)(2,1)} custom-call(s32[40]{0:T(128)S(1)} %copy-done, f32[2,40,128]{2,1,0:T(8,128)S(1)} %get-tuple-element.20.cos_ref, f32[2,40,128]{2,1,0:T(8,128)S(1)} %get-tuple-element.21.sin_ref, bf16[2,8,2,40,512]{4,3,2,1,0:T(8,128)(2,1)} %bitcast.18, bf16[2,8,2,40,768]{4,3,2,1,0:T(8,128)(2,1)} %bitcast.10.k_new_ref.v_new_ref.q_ref, ...), custom_call_target="tpu_custom_call" | custom-call | flops 167772160 | bytes 20971520 | tf_op jit(solution)/shard_map/pallas_call | solution.py:167
  168.6 4.8 %all-to-all-done.3.back_ref = bf16[16,2,40,512]{3,2,1,0:T(8,128)(2,1)S(1)} async-done(((bf16[16,2,40,512]{3,2,1,0:T(8,128)(2,1)}), bf16[16,2,40,512]{3,2,1,0:T(8,128)(2,1)S(1)}, u32[]{:S(2)}, u32[]{:S(2)}) %all-to-all-start.3) | async-done | bytes 1310752 | tf_op jit(solution)/shard_map/all_to_all | solution.py:251
  173.4 4.8 %all-to-all-start.2 = ((bf16[16,2,40,512]{3,2,1,0:T(8,128)(2,1)}), bf16[16,2,40,512]{3,2,1,0:T(8,128)(2,1)S(1)}, u32[]{:S(2)}, u32[]{:S(2)}) async-start(bf16[16,2,40,512]{3,2,1,0:T(8,128)(2,1)} %bitcast.19), calls=%async_computation.2 | async-start | bytes 2621440 | tf_op jit(solution)/shard_map/all_to_all | solution.py:251
  178.2 0.1 fusion.16.pick_ref
  178.4 1.6 shard_map.75.refs_0_
  179.9 16.8 %all-to-all-done.2.back_ref = bf16[16,2,40,512]{3,2,1,0:T(8,128)(2,1)S(1)} async-done(((bf16[16,2,40,512]{3,2,1,0:T(8,128)(2,1)}), bf16[16,2,40,512]{3,2,1,0:T(8,128)(2,1)S(1)}, u32[]{:S(2)}, u32[]{:S(2)}) %all-to-all-start.2) | async-done | bytes 1310752 | tf_op jit(solution)/shard_map/all_to_all | solution.py:251
  196.7 1.6 shard_map.76
  (21 shorter events, 0.1 us)
Async XLA Ops:
  2.4 19.4 %collective-permute-start = (bf16[512,768]{1,0:T(8,128)(2,1)S(1)}, bf16[512,768]{1,0:T(8,128)(2,1)}, u32[]{:S(2)}, u32[]{:S(2)}) collective-permute-start(bf16[512,768]{1,0:T(8,128)(2,1)S(1)} %get-tuple-element.14), channel_id=1, source_target_pairs={{0,8},{8,0},{1,9},{9,1},{2,10},{10,2},{3,11},{11,3},{4,12},{12,4},... | collective-permute-start | bytes 2359304 | tf_op jit(solution)/shard_map/over_pair_0/ppermute | solution.py:281
  21.7 13.0 %copy-start.2 = (bf16[512,768]{1,0:T(8,128)(2,1)S(1)}, bf16[512,768]{1,0:T(8,128)(2,1)}, u32[]{:S(2)}) copy-start(bf16[512,768]{1,0:T(8,128)(2,1)} %get-tuple-element.10) | copy-start | bytes 2359300
  21.7 31.0 %copy-start.3 = (s32[512]{0:T(512)S(1)}, s32[512]{0:T(512)}, u32[]{:S(2)}) copy-start(s32[512]{0:T(512)} %param.13) | copy-start | bytes 6148
  21.7 13.0 %collective-permute-start.1 = (bf16[512,512]{1,0:T(8,128)(2,1)}, bf16[512,512]{1,0:T(8,128)(2,1)S(1)}, u32[]{:S(2)}, u32[]{:S(2)}) collective-permute-start(bf16[512,512]{1,0:T(8,128)(2,1)} %get-tuple-element.9), channel_id=1, source_target_pairs={{0,8},{8,0},{1,9},{9,1},{2,10},{10,2},{3,11},{11,3},{4,12},{12,4},... | collective-permute-start | bytes 1572872 | tf_op jit(solution)/shard_map/over_pair_1/ppermute | solution.py:281
  28.7 20.1 %collective-permute-start.11 = (bf16[512,768]{1,0:T(8,128)(2,1)}, bf16[512,768]{1,0:T(8,128)(2,1)}, u32[]{:S(2)}, u32[]{:S(2)}) collective-permute-start(bf16[512,768]{1,0:T(8,128)(2,1)} %collective-permute-done.refs_0_), channel_id=1, source_target_pairs={{32,0},{48,16},{64,32},{80,48},{96,64},{112,80},{0,96},{16,112},{3... | collective-permute-start | bytes 2359304 | tf_op jit(solution)/shard_map/from_neighbours_0/ppermute | solution.py:288
  32.8 19.4 %collective-permute-start.10 = (bf16[512,768]{1,0:T(8,128)(2,1)}, bf16[512,768]{1,0:T(8,128)(2,1)}, u32[]{:S(2)}, u32[]{:S(2)}) collective-permute-start(bf16[512,768]{1,0:T(8,128)(2,1)} %collective-permute-done.refs_0_), channel_id=1, source_target_pairs={{0,32},{16,48},{32,64},{48,80},{64,96},{80,112},{96,0},{112,16},{1... | collective-permute-start | bytes 2359304 | tf_op jit(solution)/shard_map/from_neighbours_0/ppermute | solution.py:287
  34.7 17.7 %collective-permute-start.4 = (bf16[512,768]{1,0:T(8,128)(2,1)S(1)}, bf16[512,768]{1,0:T(8,128)(2,1)}, u32[]{:S(2)}, u32[]{:S(2)}) collective-permute-start(bf16[512,768]{1,0:T(8,128)(2,1)S(1)} %copy-done.2), channel_id=1, source_target_pairs={{0,8},{8,0},{1,9},{9,1},{2,10},{10,2},{3,11},{11,3},{4,12},{12,4},... | collective-permute-start | bytes 2359304 | tf_op jit(solution)/shard_map/over_pair_0/ppermute | solution.py:281
  35.9 17.1 %collective-permute-start.12 = (bf16[512,768]{1,0:T(8,128)(2,1)}, bf16[512,768]{1,0:T(8,128)(2,1)}, u32[]{:S(2)}, u32[]{:S(2)}) collective-permute-start(bf16[512,768]{1,0:T(8,128)(2,1)} %collective-permute-done.refs_0_), channel_id=1, source_target_pairs={{0,16},{16,0},{32,48},{48,32},{64,80},{80,64},{96,112},{112,96},{1... | collective-permute-start | bytes 2359304 | tf_op jit(solution)/shard_map/from_twin_0/ppermute | solution.py:291
  48.8 4.2 %collective-permute-start.14 = (bf16[512,768]{1,0:T(8,128)(2,1)}, bf16[512,768]{1,0:T(8,128)(2,1)}, u32[]{:S(2)}, u32[]{:S(2)}) collective-permute-start(bf16[512,768]{1,0:T(8,128)(2,1)} %collective-permute-done.11.refs_2_), channel_id=1, source_target_pairs={{0,16},{16,0},{32,48},{48,32},{64,80},{80,64},{96,112},{112,96},{1... | collective-permute-start | bytes 2359304 | tf_op jit(solution)/shard_map/from_twin_0/ppermute | solution.py:291
  52.2 2.6 %collective-permute-start.13 = (bf16[512,768]{1,0:T(8,128)(2,1)}, bf16[512,768]{1,0:T(8,128)(2,1)}, u32[]{:S(2)}, u32[]{:S(2)}) collective-permute-start(bf16[512,768]{1,0:T(8,128)(2,1)} %collective-permute-done.10.refs_1_), channel_id=1, source_target_pairs={{0,16},{16,0},{32,48},{48,32},{64,80},{80,64},{96,112},{112,96},{1... | collective-permute-start | bytes 2359304 | tf_op jit(solution)/shard_map/from_twin_0/ppermute | solution.py:291
  52.4 3.5 %collective-permute-start.15 = (bf16[512,768]{1,0:T(8,128)(2,1)}, bf16[512,768]{1,0:T(8,128)(2,1)}, u32[]{:S(2)}, u32[]{:S(2)}) collective-permute-start(bf16[512,768]{1,0:T(8,128)(2,1)} %collective-permute-done.4.refs_3_), channel_id=1, source_target_pairs={{0,16},{16,0},{32,48},{48,32},{64,80},{80,64},{96,112},{112,96},{1... | collective-permute-start | bytes 2359304 | tf_op jit(solution)/shard_map/from_twin_0/ppermute | solution.py:291
  67.7 55.0 %all-to-all-start.1 = ((bf16[16,2,40,768]{3,2,1,0:T(8,128)(2,1)}), bf16[16,2,40,768]{3,2,1,0:T(8,128)(2,1)}, u32[]{:S(2)}, u32[]{:S(2)}) async-start(bf16[16,2,40,768]{3,2,1,0:T(8,128)(2,1)} %project_0.1), calls=%async_computation.1 | async-start | bytes 3932160 | tf_op jit(solution)/shard_map/route_0/all_to_all | solution.py:251
  75.2 14.0 %collective-permute-start.3 = (bf16[512,512]{1,0:T(8,128)(2,1)S(1)}, bf16[512,512]{1,0:T(8,128)(2,1)S(1)}, u32[]{:S(2)}, u32[]{:S(2)}) collective-permute-start(bf16[512,512]{1,0:T(8,128)(2,1)S(1)} %collective-permute-done.1.refs_0_), channel_id=1, source_target_pairs={{32,0},{48,16},{64,32},{80,48},{96,64},{112,80},{0,96},{16,112},{3... | collective-permute-start | bytes 1572872 | tf_op jit(solution)/shard_map/from_neighbours_1/ppermute | solution.py:288
  78.2 14.3 %collective-permute-start.2 = (bf16[512,512]{1,0:T(8,128)(2,1)S(1)}, bf16[512,512]{1,0:T(8,128)(2,1)S(1)}, u32[]{:S(2)}, u32[]{:S(2)}) collective-permute-start(bf16[512,512]{1,0:T(8,128)(2,1)S(1)} %collective-permute-done.1.refs_0_), channel_id=1, source_target_pairs={{0,32},{16,48},{32,64},{48,80},{64,96},{80,112},{96,0},{112,16},{1... | collective-permute-start | bytes 1572872 | tf_op jit(solution)/shard_map/from_neighbours_1/ppermute | solution.py:287
  78.2 50.7 %copy-start = (s32[40]{0:T(128)S(1)}, s32[40]{0:T(128)}, u32[]{:S(2)}) copy-start(s32[40]{0:T(128)} %fill_ref.3) | copy-start | bytes 484
  78.2 36.7 %collective-permute-start.5 = (bf16[512,512]{1,0:T(8,128)(2,1)}, bf16[512,512]{1,0:T(8,128)(2,1)S(1)}, u32[]{:S(2)}, u32[]{:S(2)}) collective-permute-start(bf16[512,512]{1,0:T(8,128)(2,1)} %get-tuple-element.11), channel_id=1, source_target_pairs={{0,8},{8,0},{1,9},{9,1},{2,10},{10,2},{3,11},{11,3},{4,12},{12,4},... | collective-permute-start | bytes 1572872 | tf_op jit(solution)/shard_map/over_pair_1/ppermute | solution.py:281
  79.4 35.5 %collective-permute-start.6 = (bf16[512,512]{1,0:T(8,128)(2,1)S(1)}, bf16[512,512]{1,0:T(8,128)(2,1)S(1)}, u32[]{:S(2)}, u32[]{:S(2)}) collective-permute-start(bf16[512,512]{1,0:T(8,128)(2,1)S(1)} %collective-permute-done.1.refs_0_), channel_id=1, source_target_pairs={{0,16},{16,0},{32,48},{48,32},{64,80},{80,64},{96,112},{112,96},{1... | collective-permute-start | bytes 1572872 | tf_op jit(solution)/shard_map/from_twin_1/ppermute | solution.py:291
  89.1 25.8 %collective-permute-start.8 = (bf16[512,512]{1,0:T(8,128)(2,1)S(1)}, bf16[512,512]{1,0:T(8,128)(2,1)S(1)}, u32[]{:S(2)}, u32[]{:S(2)}) collective-permute-start(bf16[512,512]{1,0:T(8,128)(2,1)S(1)} %collective-permute-done.3.refs_2_), channel_id=1, source_target_pairs={{0,16},{16,0},{32,48},{48,32},{64,80},{80,64},{96,112},{112,96},{1... | collective-permute-start | bytes 1572872 | tf_op jit(solution)/shard_map/from_twin_1/ppermute | solution.py:291
  92.6 22.4 %collective-permute-start.7 = (bf16[512,512]{1,0:T(8,128)(2,1)S(1)}, bf16[512,512]{1,0:T(8,128)(2,1)S(1)}, u32[]{:S(2)}, u32[]{:S(2)}) collective-permute-start(bf16[512,512]{1,0:T(8,128)(2,1)S(1)} %collective-permute-done.2.refs_1_), channel_id=1, source_target_pairs={{0,16},{16,0},{32,48},{48,32},{64,80},{80,64},{96,112},{112,96},{1... | collective-permute-start | bytes 1572872 | tf_op jit(solution)/shard_map/from_twin_1/ppermute | solution.py:291
  114.9 1.9 collective-permute-start.9
  122.7 26.6 %all-to-all-start = ((bf16[16,2,40,512]{3,2,1,0:T(8,128)(2,1)}), bf16[16,2,40,512]{3,2,1,0:T(8,128)(2,1)S(1)}, u32[]{:S(2)}, u32[]{:S(2)}) async-start(bf16[16,2,40,512]{3,2,1,0:T(8,128)(2,1)} %project_1.1), calls=%async_computation | async-start | bytes 2621440 | tf_op jit(solution)/shard_map/route_1/all_to_all | solution.py:251
  149.4 4.8 %copy-start.1 = (bf16[16,2,40,512]{3,2,1,0:T(8,128)(2,1)}, bf16[16,2,40,512]{3,2,1,0:T(8,128)(2,1)S(1)}, u32[]{:S(2)}) copy-start(bf16[16,2,40,512]{3,2,1,0:T(8,128)(2,1)S(1)} %all-to-all-done) | copy-start | bytes 3932164
  149.4 24.1 %all-to-all-start.3 = ((bf16[16,2,40,512]{3,2,1,0:T(8,128)(2,1)}), bf16[16,2,40,512]{3,2,1,0:T(8,128)(2,1)S(1)}, u32[]{:S(2)}, u32[]{:S(2)}) async-start(bf16[16,2,40,512]{3,2,1,0:T(8,128)(2,1)} %bitcast.17), calls=%async_computation.3 | async-start | bytes 2621440 | tf_op jit(solution)/shard_map/all_to_all | solution.py:251
  173.4 23.3 %all-to-all-start.2 = ((bf16[16,2,40,512]{3,2,1,0:T(8,128)(2,1)}), bf16[16,2,40,512]{3,2,1,0:T(8,128)(2,1)S(1)}, u32[]{:S(2)}, u32[]{:S(2)}) async-start(bf16[16,2,40,512]{3,2,1,0:T(8,128)(2,1)} %bitcast.19), calls=%async_computation.2 | async-start | bytes 2621440 | tf_op jit(solution)/shard_map/all_to_all | solution.py:251

commit v5 on v4

--- a/solution.py
+++ b/solution.py
@@ -11,7 +11,7 @@
 SHARING = 8
 ROPE_BASE = 1000000.0
 SWAP = ((0, 1), (1, 0))
-CHUNKS = ((4, 8), (0, 4))
+CHUNKS = ((0, 4), (4, 8))
 ROW_BLOCK = 8
 NT = (((1,), (1,)), ((), ()))
 
@@ -29,20 +29,23 @@
 
 
 def project_kernel(owners, rows, places_ref, x_ref, *refs):
-    slabs = refs[:-6]
-    partial_ref, pack_ref, out_ref, taken, total, arrived = refs[-6:]
+    slabs = refs[:-7]
+    partial_ref, pack_ref, out_ref, taken, met, total, arrived = refs[-7:]
     depth = slabs[0].shape[0]
     share = pack_ref.shape[1]
     copies = []
+    for i, slab in enumerate(slabs):
+        first = pl.multiple_of(places_ref[i] * depth, depth)
+        copies.append((
+            pltpu.make_async_copy(x_ref.at[:, pl.ds(first, depth)], taken.at[i], arrived.at[0, i]),
+            pltpu.make_async_copy(slab, met.at[i], arrived.at[1, i]),
+        ))
+        for copy in copies[i]:
+            copy.start()
     for i in range(len(slabs)):
-        first = pl.multiple_of(places_ref[i] * depth, depth)
-        copies.append(
-            pltpu.make_async_copy(x_ref.at[:, pl.ds(first, depth)], taken.at[i], arrived.at[i])
-        )
-        copies[i].start()
-    for i, slab in enumerate(slabs):
-        copies[i].wait()
-        product = jnp.dot(taken[i], slab[...], preferred_element_type=jnp.float32)
+        for copy in copies[i]:
+            copy.wait()
+        product = jnp.dot(taken[i], met[i], preferred_element_type=jnp.float32)
         if i == 0:
             total[...] = partial_ref[...] + product
         else:
@@ -60,28 +63,32 @@
     depth, wide = slabs[0].shape
     slots, share = pack.shape
     rows = slots // owners
-    local = pl.BlockSpec(memory_space=pltpu.VMEM)
+    count = len(slabs)
     return pl.pallas_call(
         functools.partial(project_kernel, owners, rows),
         out_shape=pltpu.HBM((owners, 2, rows, wide), jnp.bfloat16),
         grid_spec=pltpu.PrefetchScalarGridSpec(
             num_scalar_prefetch=1,
             grid=(1,),
-            in_specs=[pl.BlockSpec(memory_space=pl.ANY)] + [local] * (len(slabs) + 2),
+            in_specs=[pl.BlockSpec(memory_space=pl.ANY)] * (count + 1) + [
+                pl.BlockSpec((lines, wide), lambda k, s: (0, 0)),
+                pl.BlockSpec((slots, share), lambda k, s: (0, 0)),
+            ],
             out_specs=pl.BlockSpec((owners, 2, rows, wide), lambda k, s: (0, 0, 0, 0)),
             scratch_shapes=[
-                pltpu.VMEM((len(slabs), lines, depth), jnp.bfloat16),
+                pltpu.VMEM((count, lines, depth), jnp.bfloat16),
+                pltpu.VMEM((count, depth, wide), jnp.bfloat16),
                 pltpu.VMEM((lines, wide), jnp.float32),
-                pltpu.SemaphoreType.DMA((len(slabs),)),
+                pltpu.SemaphoreType.DMA((2, count)),
             ],
         ),
         compiler_params=pltpu.CompilerParams(vmem_limit_bytes=26 << 20),
         cost_estimate=pl.CostEstimate(
-            flops=2 * lines * depth * len(slabs) * wide,
+            flops=2 * lines * depth * count * wide,
             transcendentals=0,
-            bytes_accessed=2 * lines * depth * len(slabs),
-        ),
-    )(places, in_hbm(signals), *slabs, partial, pack)
+            bytes_accessed=2 * (lines + wide) * depth * count,
+        ),
+    )(places, in_hbm(signals), *(in_hbm(slab) for slab in slabs), in_hbm(partial), in_hbm(pack))
 
 
 def attention_kernel(heads, fill_ref, cos_ref, sin_ref, q_ref, k_new_ref, v_new_ref, k_ref, v_ref, out_ref,
@@ -153,7 +160,7 @@
                     out_ref[pair, t, step, :, head * HEAD:(head + 1) * HEAD] = done
 
 
-def attend(fill, cosine, sine, queries, new, new_at, keys, values, heads):
+def attend(fill, cosine, sine, queries, new, keys, values, heads):
     _, n_tp, _, rows, _ = queries.shape
     places = keys.shape[1]
     block = ROW_BLOCK
@@ -171,7 +178,7 @@
             num_scalar_prefetch=1,
             grid=(rows // block,),
             in_specs=[
-                table, table, routed(heads * HEAD), routed(HEAD, new_at), routed(HEAD, new_at + 1),
+                table, table, routed(heads * HEAD), routed(HEAD, 0), routed(HEAD, 1),
                 cache, cache,
             ],
             out_specs=routed(heads * HEAD),
@@ -250,21 +257,18 @@
     def exchange(blocks):
         return lax.all_to_all(blocks, ("pair", "tp"), split_axis=0, concat_axis=0, tiled=True)
 
-    spans = [(a * HEAD, (b + 2 if b == SHARING else b) * HEAD) for a, b in CHUNKS]
+    spans = [(SHARING * HEAD, columns)] + [(a * HEAD, b * HEAD) for a, b in CHUNKS]
     n_z = n_grp // 2
     up = [(2 * a + c, 2 * ((a + 1) % n_z) + c) for a in range(n_z) for c in range(2)]
     down = [(d, s) for s, d in up]
     twin = [(2 * a + c, 2 * a + 1 - c) for a in range(n_z) for c in range(2)]
     z, core = grp // 2, grp % 2
     turns = (0, n_z - 1, 1, 2)
-    slab_of = [(z + turn) % n_z * 2 + core for turn in turns]
     places = (1 - pair) * n_grp + jnp.stack(
-        slab_of + [(z + turn) % n_z * 2 + 1 - core for turn in turns]
+        [(z + turn) % n_z * 2 + core for turn in turns]
+        + [(z + turn) % n_z * 2 + 1 - core for turn in turns]
     )
     places = places.astype(jnp.int32)
-
-    def slab(at, span):
-        return lax.dynamic_slice(matrix, (at * depth, span[0]), (depth, span[1] - span[0]))
 
     near = lax.dynamic_slice_in_dim(flat, pair * half, half, 1)
     partials = [
@@ -274,33 +278,38 @@
     ]
 
     crossed = []
-    for distance in (0, 3):
-        for number, span in enumerate(spans):
-            with jax.named_scope("over_pair_%d" % number):
-                piece = after(slab(slab_of[distance], span), *crossed[-1:])
-                crossed.append(lax.ppermute(piece, "pair", SWAP))
-    crossed[0] = after(crossed[0], *partials)
-    held = []
-    for number in range(len(spans)):
-        own, far = crossed[number], crossed[len(spans) + number]
-        with jax.named_scope("from_neighbours_%d" % number):
-            below = lax.ppermute(own, "grp", up)
-            above = lax.ppermute(own, "grp", down)
+    for number, (start, stop) in enumerate(spans):
+        with jax.named_scope("over_pair_%d" % number):
+            slab = lax.dynamic_slice(matrix, (grp * depth, start), (depth, stop - start))
+            crossed.append(lax.ppermute(after(slab, *crossed[-1:]), "pair", SWAP))
+    ring, ahead = [], []
+    for number, slab in enumerate(crossed):
+        slab = after(slab, partials[number], *ahead)
+        with jax.named_scope("from_below_%d" % number):
+            below = lax.ppermute(slab, "grp", up)
+        with jax.named_scope("from_above_%d" % number):
+            above = lax.ppermute(slab, "grp", down)
+        with jax.named_scope("from_opposite_%d" % number):
+            if number % 2:
+                opposite = lax.ppermute(above, "grp", down)
+            else:
+                opposite = lax.ppermute(below, "grp", up)
+        ahead = [below, above] if number else [below, above, opposite]
+        ring.append([slab, below, above, opposite])
+    partials[0] = after(partials[0], crossed[2], ring[1][3], ring[2][1])
+    arrived = []
+    for number, (span, four) in enumerate(zip(spans, ring)):
         with jax.named_scope("from_twin_%d" % number):
-            four = [own, below, above, far]
-            held.append(four + [lax.ppermute(piece, "grp", twin) for piece in four])
-    arrived = []
-    for number, (span, slabs) in enumerate(zip(spans, held)):
+            slabs = four + [lax.ppermute(piece, "grp", twin) for piece in four]
         with jax.named_scope("project_%d" % number):
             packed = project(places, flat, slabs, partials[number], pack, owners)
         with jax.named_scope("route_%d" % number):
             arrived.append(exchange(packed).reshape(n_pair, n_tp, 2, rows, span[1] - span[0]))
     out = None
-    for (first, last), queries in zip(CHUNKS, arrived):
+    for (first, last), queries in zip(CHUNKS, arrived[1:]):
         heads = last - first
         attended = attend(
-            fill, cosine, sine, queries, arrived[0], SHARING - CHUNKS[0][0],
-            cached_keys, cached_values, heads,
+            fill, cosine, sine, queries, arrived[0], cached_keys, cached_values, heads
         )
         back = exchange(attended.reshape(owners, 2, rows, heads * HEAD))
         out = unpack(pick, back, first // heads, SHARING * HEAD, out)

time: 199 us -> 178 us (0.89)
  waiting for transfers between devices: 93.4 us -> 56.4 us
  starting transfers between devices: 35.5 us -> 43.9 us
  Pallas kernels: 49.7 us -> 53.6 us
  matrix products: 12.8 us -> 16.2 us
    ppermute x16 -> x24, waiting for transfers between devices: 66.3 us -> 23.4 us  [the longest x3 7.29 us: per_device(): below = lax.ppermute(slab, 'grp', up)]
    all_to_all x4 -> x5, waiting for transfers between devices: 27.2 us -> 33 us  [exchange(): lax.all_to_all(blocks, ('pair', 'tp'), split_axis=0, concat_axis=0, tiled...]
    all_to_all x4 -> x5, starting transfers between devices: 23.3 us -> 27.5 us  [exchange(): lax.all_to_all(blocks, ('pair', 'tp'), split_axis=0, concat_axis=0, tiled...]
    ppermute x16 -> x24, starting transfers between devices: 12.2 us -> 16.4 us  [the longest x3 4.77 us: per_device(): above = lax.ppermute(slab, 'grp', down)]
    pallas_call x2 -> x3, Pallas kernels: 17.6 us -> 21.6 us  [project(): pl.pallas_call(functools.partial(project_kernel, owners, rows), out_shape...]
    dot_general x2 -> x3, matrix products: 12.8 us -> 16.2 us  [per_device(): jnp.dot(near, matrix[:, slice(*span)], preferred_element_type=jnp.float32)]
    dynamic_slice x2, local copies, waits for them, and re-layouts: 4.6 us -> 2.24 us  [per_device(): lax.dynamic_slice(matrix, (grp * depth, start), (depth, stop - start))]
  transfers between devices with their start and end apart: 20 -> 29, of which waited for: 14 -> 18; matrix products, arithmetic and copies ran while one was open for 9% -> 11% of each run, Pallas kernels for 18% -> 30%
where the time goes in v5:
time: 178 us; the launch traced here: 176 us
  waiting for transfers between devices  56.4 us (32%)
  Pallas kernels  53.6 us (30%)
  starting transfers between devices  43.9 us (25%)
  matrix products  16.2 us (9%)
  local copies, waits for them, and re-layouts  4.05 us (2%)
  other arithmetic  1.97 us (1%)
    all_to_all x5, waiting for transfers between devices, exchange(): lax.all_to_all(blocks, ('pair', 'tp'), split_axis=0, concat_axis=0, tiled...  33 us
    pallas_call x2, Pallas kernels, attend(): pl.pallas_call(functools.partial(attention_kernel, heads), out_shape=pltp...  28.9 us
    all_to_all x5, starting transfers between devices, exchange(): lax.all_to_all(blocks, ('pair', 'tp'), split_axis=0, concat_axis=0, tiled...  27.5 us
    pallas_call x3, Pallas kernels, project(): pl.pallas_call(functools.partial(project_kernel, owners, rows), out_shape...  21.6 us
    dot_general x3, matrix products, per_device(): jnp.dot(near, matrix[:, slice(*span)], preferred_element_type=jnp.float32)  16.2 us
    ppermute x3, waiting for transfers between devices, per_device(): below = lax.ppermute(slab, 'grp', up)  7.29 us
    ppermute x1, waiting for transfers between devices, per_device(): opposite = lax.ppermute(above, 'grp', down)  4.86 us
    ppermute x3, starting transfers between devices, per_device(): above = lax.ppermute(slab, 'grp', down)  4.77 us
  transfers between devices with their start and end apart: 29, of which 18 were waited for; matrix products, arithmetic and copies ran while one was open for 11% of the time, Pallas kernels for 30%

profile of v5, /device:TPU:4, one launch (start us, length us, event | category | flops | bytes accessed | tf_op | source)
XLA Modules:
  0.0 176.4 jit_solution(17336730083779943279)
XLA Ops:
  0.0 1.0 constant_dynamic-slice_fusion
  1.0 1.3 collective-permute-start
  2.2 0.7 slice_convert_fusion.2
  2.9 5.1 %fusion.19.refs_8_ = f32[512,256]{1,0:T(8,128)} fusion(bf16[4096,1280]{1,0:T(8,128)(2,1)} %param.8, bf16[512,8192]{1,0:T(8,128)(2,1)} %bitcast.14, s32[]{:T(128)S(6)} %select_n.54, f32[256]{0:T(256)S(1)} %slice_convert_fusion.2), kind=kOutput, calls=%fused_computation.11 | convolution fusion | flops 1073872896 | bytes 6816772 | tf_op jit(solution)/shard_map/dot_general | solution.py:275
  8.0 1.1 collective-permute-done.refs_0_
  9.1 1.9 %collective-permute-start.3 = (bf16[512,256]{1,0:T(8,128)(2,1)S(1)}, bf16[512,256]{1,0:T(8,128)(2,1)S(1)}, u32[]{:S(2)}, u32[]{:S(2)}) collective-permute-start(bf16[512,256]{1,0:T(8,128)(2,1)S(1)} %collective-permute-done.refs_0_), channel_id=1, source_target_pairs={{0,32},{16,48},{32,64},{48,80},{64,96},{80,112},{96,0},{112,16},{1... | collective-permute-start | bytes 786440 | tf_op jit(solution)/shard_map/from_below_0/ppermute | solution.py:289
  11.0 1.3 constant_dynamic-slice_fusion.1
  12.3 2.3 %collective-permute-start.4 = (bf16[512,256]{1,0:T(8,128)(2,1)S(1)}, bf16[512,256]{1,0:T(8,128)(2,1)S(1)}, u32[]{:S(2)}, u32[]{:S(2)}) collective-permute-start(bf16[512,256]{1,0:T(8,128)(2,1)S(1)} %collective-permute-done.refs_0_), channel_id=1, source_target_pairs={{32,0},{48,16},{64,32},{80,48},{96,64},{112,80},{0,96},{16,112},{3... | collective-permute-start | bytes 786440 | tf_op jit(solution)/shard_map/from_above_0/ppermute | solution.py:291
  14.6 1.2 collective-permute-start.1
  15.8 2.8 %collective-permute-done.3.refs_1_ = bf16[512,256]{1,0:T(8,128)(2,1)S(1)} collective-permute-done((bf16[512,256]{1,0:T(8,128)(2,1)S(1)}, bf16[512,256]{1,0:T(8,128)(2,1)S(1)}, u32[]{:S(2)}, u32[]{:S(2)}) %collective-permute-start.3) | collective-permute-done | bytes 262176 | tf_op jit(solution)/shard_map/from_below_0/ppermute | solution.py:289
  18.6 5.6 %fusion.14.refs_8_ = f32[512,512]{1,0:T(8,128)} fusion(bf16[4096,1280]{1,0:T(8,128)(2,1)} %param.8, bf16[512,8192]{1,0:T(8,128)(2,1)S(1)} %bitcast.18, s32[]{:T(128)S(6)} %select_n.54, f32[512]{0:T(512)S(1)} %get-tuple-element.19), kind=kOutput, calls=%fused_computation.10 | convolution fusion | flops 2147745792 | bytes 9439236 | tf_op jit(solution)/shard_map/dot_general | solution.py:275
  24.2 2.1 %collective-permute-done.5.refs_3_ = bf16[512,256]{1,0:T(8,128)(2,1)S(1)} collective-permute-done((bf16[512,256]{1,0:T(8,128)(2,1)S(1)}, bf16[512,256]{1,0:T(8,128)(2,1)S(1)}, u32[]{:S(2)}, u32[]{:S(2)}) %collective-permute-start.5) | collective-permute-done | bytes 262176 | tf_op jit(solution)/shard_map/from_opposite_0/ppermute | solution.py:296
  26.3 0.8 collective-permute-done.1.refs_0_
  27.1 1.6 collective-permute-start.7
  29.1 1.2 collective-permute-start.2
  30.3 5.5 %fusion.9.refs_8_ = f32[512,512]{1,0:T(8,128)} fusion(bf16[4096,1280]{1,0:T(8,128)(2,1)} %param.8, bf16[512,8192]{1,0:T(8,128)(2,1)S(1)} %bitcast.19, s32[]{:T(128)S(6)} %select_n.54, f32[512]{0:T(512)S(1)} %get-tuple-element.20), kind=kOutput, calls=%fused_computation.9 | convolution fusion | flops 2147745792 | bytes 9439236 | tf_op jit(solution)/shard_map/dot_general | solution.py:275
  35.8 2.9 %collective-permute-done.7.refs_2_ = bf16[512,512]{1,0:T(8,128)(2,1)S(1)} collective-permute-done((bf16[512,512]{1,0:T(8,128)(2,1)S(1)}, bf16[512,512]{1,0:T(8,128)(2,1)S(1)}, u32[]{:S(2)}, u32[]{:S(2)}) %collective-permute-start.7) | collective-permute-done | bytes 524320 | tf_op jit(solution)/shard_map/from_above_1/ppermute | solution.py:291
  38.7 2.3 %collective-permute-done.6.refs_1_ = bf16[512,512]{1,0:T(8,128)(2,1)S(1)} collective-permute-done((bf16[512,512]{1,0:T(8,128)(2,1)S(1)}, bf16[512,512]{1,0:T(8,128)(2,1)S(1)}, u32[]{:S(2)}, u32[]{:S(2)}) %collective-permute-start.6) | collective-permute-done | bytes 524320 | tf_op jit(solution)/shard_map/from_below_1/ppermute | solution.py:289
  41.0 1.7 collective-permute-start.19
  43.1 0.5 collective-permute-start.16
  43.8 1.0 collective-permute-done.15.refs_4_
  44.9 0.8 fusion.25.refs_9_
  46.4 4.9 %collective-permute-done.19.refs_3_ = bf16[512,512]{1,0:T(8,128)(2,1)} collective-permute-done((bf16[512,512]{1,0:T(8,128)(2,1)S(1)}, bf16[512,512]{1,0:T(8,128)(2,1)}, u32[]{:S(2)}, u32[]{:S(2)}) %collective-permute-start.19) | collective-permute-done | bytes 524320 | tf_op jit(solution)/shard_map/from_opposite_1/ppermute | solution.py:294
  51.3 2.2 %collective-permute-done.8.refs_1_ = bf16[512,512]{1,0:T(8,128)(2,1)S(1)} collective-permute-done((bf16[512,512]{1,0:T(8,128)(2,1)S(1)}, bf16[512,512]{1,0:T(8,128)(2,1)S(1)}, u32[]{:S(2)}, u32[]{:S(2)}) %collective-permute-start.8) | collective-permute-done | bytes 524320 | tf_op jit(solution)/shard_map/from_below_2/ppermute | solution.py:289
  53.5 0.7 copy-done.18
  54.3 6.7 %project_0.1 = bf16[16,2,40,256]{3,2,1,0:T(8,128)(2,1)} custom-call(s32[8]{0:T(128)S(1)} %broadcast_add_fusion.places_ref, bf16[512,8192]{1,0:T(8,128)(2,1)} %bitcast.15, bf16[512,256]{1,0:T(8,128)(2,1)} %copy-done.14, bf16[512,256]{1,0:T(8,128)(2,1)} %copy-done.15, bf16[512,256]{1,0:T(8,128)(2,1)} %copy-done.16, bf16[512,256]{1,0:T(8,128)(2,1)} %copy-done.17, ...), custom_call_target="tpu_custom_call" | custom-call | flops 1073741824 | bytes 6291456 | tf_op jit(solution)/shard_map/project_0/pallas_call | solution.py:67
  61.0 7.6 %all-to-all-start.1 = ((bf16[16,2,40,256]{3,2,1,0:T(8,128)(2,1)}), bf16[16,2,40,256]{3,2,1,0:T(8,128)(2,1)S(1)}, u32[]{:S(2)}, u32[]{:S(2)}) async-start(bf16[16,2,40,256]{3,2,1,0:T(8,128)(2,1)} %project_0.1), calls=%async_computation.1 | async-start | bytes 1310720 | tf_op jit(solution)/shard_map/route_0/all_to_all | solution.py:258
  68.7 0.8 collective-permute-start.9
  69.5 1.2 collective-permute-start.10
  70.7 7.5 %project_1.1 = bf16[16,2,40,512]{3,2,1,0:T(8,128)(2,1)} custom-call(s32[8]{0:T(128)S(1)} %broadcast_add_fusion.places_ref, bf16[512,8192]{1,0:T(8,128)(2,1)} %bitcast.16, bf16[512,512]{1,0:T(8,128)(2,1)} %copy-done.7, bf16[512,512]{1,0:T(8,128)(2,1)} %copy-done.9, bf16[512,512]{1,0:T(8,128)(2,1)} %copy-done.8, ...), custom_call_target="tpu_custom_call" | custom-call | flops 2147483648 | bytes 8388608 | tf_op jit(solution)/shard_map/project_1/pallas_call | solution.py:67
  78.2 1.9 %all-to-all-done.1 = bf16[16,2,40,256]{3,2,1,0:T(8,128)(2,1)S(1)} async-done(((bf16[16,2,40,256]{3,2,1,0:T(8,128)(2,1)}), bf16[16,2,40,256]{3,2,1,0:T(8,128)(2,1)S(1)}, u32[]{:S(2)}, u32[]{:S(2)}) %all-to-all-start.1) | async-done | bytes 655392 | tf_op jit(solution)/shard_map/route_0/all_to_all | solution.py:258
  80.1 5.4 %all-to-all-start.3 = ((bf16[16,2,40,512]{3,2,1,0:T(8,128)(2,1)}), bf16[16,2,40,512]{3,2,1,0:T(8,128)(2,1)S(1)}, u32[]{:S(2)}, u32[]{:S(2)}) async-start(bf16[16,2,40,512]{3,2,1,0:T(8,128)(2,1)} %project_1.1), calls=%async_computation.3 | async-start | bytes 2621440 | tf_op jit(solution)/shard_map/route_1/all_to_all | solution.py:258
  86.6 0.9 collective-permute-done.11.refs_4_
  87.5 1.5 collective-permute-done.12.refs_5_
  89.2 0.7 collective-permute-done.14.refs_7_
  90.0 0.8 copy-done.13
  90.8 7.4 %project_2.1 = bf16[16,2,40,512]{3,2,1,0:T(8,128)(2,1)} custom-call(s32[8]{0:T(128)S(1)} %broadcast_add_fusion.places_ref, bf16[512,8192]{1,0:T(8,128)(2,1)} %bitcast.17, bf16[512,512]{1,0:T(8,128)(2,1)} %copy-done.5, bf16[512,512]{1,0:T(8,128)(2,1)} %copy-done.6, bf16[512,512]{1,0:T(8,128)(2,1)} %collective-permute-done.9.refs_2_, ...), custom_call_target="tpu_custom_call" | custom-call | flops 2147483648 | bytes 8388608 | tf_op jit(solution)/shard_map/project_2/pallas_call | solution.py:67
  98.2 6.4 %all-to-all-done.3 = bf16[16,2,40,512]{3,2,1,0:T(8,128)(2,1)S(1)} async-done(((bf16[16,2,40,512]{3,2,1,0:T(8,128)(2,1)}), bf16[16,2,40,512]{3,2,1,0:T(8,128)(2,1)S(1)}, u32[]{:S(2)}, u32[]{:S(2)}) %all-to-all-start.3) | async-done | bytes 1310752 | tf_op jit(solution)/shard_map/route_1/all_to_all | solution.py:258
  104.6 4.8 %all-to-all-start = ((bf16[16,2,40,512]{3,2,1,0:T(8,128)(2,1)}), bf16[16,2,40,512]{3,2,1,0:T(8,128)(2,1)S(1)}, u32[]{:S(2)}, u32[]{:S(2)}) async-start(bf16[16,2,40,512]{3,2,1,0:T(8,128)(2,1)} %project_2.1), calls=%async_computation | async-start | bytes 2621440 | tf_op jit(solution)/shard_map/route_2/all_to_all | solution.py:258
  109.8 14.4 %shard_map.74 = bf16[2,8,2,40,512]{4,3,2,1,0:T(8,128)(2,1)} custom-call(s32[40]{0:T(128)S(1)} %copy-done, f32[2,40,128]{2,1,0:T(8,128)S(1)} %get-tuple-element.24.cos_ref, f32[2,40,128]{2,1,0:T(8,128)S(1)} %get-tuple-element.25.sin_ref, bf16[2,8,2,40,512]{4,3,2,1,0:T(8,128)(2,1)} %bitcast.24, bf16[2,8,2,40,256]{4,3,2,1,0:T(8,128)(2,1)} %bitcast.20, ...), custom_call_target="tpu_custom_call" | custom-call | flops 167772160 | bytes 20971520 | tf_op jit(solution)/shard_map/pallas_call | solution.py:174
  124.2 3.7 %all-to-all-done = bf16[16,2,40,512]{3,2,1,0:T(8,128)(2,1)S(1)} async-done(((bf16[16,2,40,512]{3,2,1,0:T(8,128)(2,1)}), bf16[16,2,40,512]{3,2,1,0:T(8,128)(2,1)S(1)}, u32[]{:S(2)}, u32[]{:S(2)}) %all-to-all-start) | async-done | bytes 1310752 | tf_op jit(solution)/shard_map/route_2/all_to_all | solution.py:258
  127.9 4.8 %all-to-all-start.4 = ((bf16[16,2,40,512]{3,2,1,0:T(8,128)(2,1)}), bf16[16,2,40,512]{3,2,1,0:T(8,128)(2,1)S(1)}, u32[]{:S(2)}, u32[]{:S(2)}) async-start(bf16[16,2,40,512]{3,2,1,0:T(8,128)(2,1)} %bitcast.27), calls=%async_computation.4 | async-start | bytes 2621440 | tf_op jit(solution)/shard_map/all_to_all | solution.py:258
  132.7 14.5 %shard_map.73 = bf16[2,8,2,40,512]{4,3,2,1,0:T(8,128)(2,1)} custom-call(s32[40]{0:T(128)S(1)} %copy-done, f32[2,40,128]{2,1,0:T(8,128)S(1)} %get-tuple-element.24.cos_ref, f32[2,40,128]{2,1,0:T(8,128)S(1)} %get-tuple-element.25.sin_ref, bf16[2,8,2,40,512]{4,3,2,1,0:T(8,128)(2,1)} %bitcast.25, bf16[2,8,2,40,256]{4,3,2,1,0:T(8,128)(2,1)} %bitcast.22, ...), custom_call_target="tpu_custom_call" | custom-call | flops 167772160 | bytes 20971520 | tf_op jit(solution)/shard_map/pallas_call | solution.py:174
  147.2 4.2 %all-to-all-done.4.back_ref = bf16[16,2,40,512]{3,2,1,0:T(8,128)(2,1)S(1)} async-done(((bf16[16,2,40,512]{3,2,1,0:T(8,128)(2,1)}), bf16[16,2,40,512]{3,2,1,0:T(8,128)(2,1)S(1)}, u32[]{:S(2)}, u32[]{:S(2)}) %all-to-all-start.4) | async-done | bytes 1310752 | tf_op jit(solution)/shard_map/all_to_all | solution.py:258
  151.4 4.8 %all-to-all-start.2 = ((bf16[16,2,40,512]{3,2,1,0:T(8,128)(2,1)}), bf16[16,2,40,512]{3,2,1,0:T(8,128)(2,1)S(1)}, u32[]{:S(2)}, u32[]{:S(2)}) async-start(bf16[16,2,40,512]{3,2,1,0:T(8,128)(2,1)} %bitcast.26), calls=%async_computation.2 | async-start | bytes 2621440 | tf_op jit(solution)/shard_map/all_to_all | solution.py:258
  156.3 1.6 shard_map.75.refs_0_
  157.9 16.9 %all-to-all-done.2.back_ref = bf16[16,2,40,512]{3,2,1,0:T(8,128)(2,1)S(1)} async-done(((bf16[16,2,40,512]{3,2,1,0:T(8,128)(2,1)}), bf16[16,2,40,512]{3,2,1,0:T(8,128)(2,1)S(1)}, u32[]{:S(2)}, u32[]{:S(2)}) %all-to-all-start.2) | async-done | bytes 1310752 | tf_op jit(solution)/shard_map/all_to_all | solution.py:258
  174.8 1.6 shard_map.76
  (75 shorter events, 3.6 us)
Async XLA Ops:
  1.0 8.1 %collective-permute-start = (bf16[512,256]{1,0:T(8,128)(2,1)S(1)}, bf16[512,256]{1,0:T(8,128)(2,1)S(1)}, u32[]{:S(2)}, u32[]{:S(2)}) collective-permute-start(bf16[512,256]{1,0:T(8,128)(2,1)S(1)} %constant_dynamic-slice_fusion), channel_id=1, source_target_pairs={{0,8},{8,0},{1,9},{9,1},{2,10},{10,2},{3,11},{11,3},{4,12},{12,4},... | collective-permute-start | bytes 786440 | tf_op jit(solution)/shard_map/over_pair_0/ppermute | solution.py:284
  2.9 9.4 %copy-start.19 = (bf16[1280]{0:T(1024)(128)(2,1)S(1)}, bf16[1280]{0:T(1024)(128)(2,1)}, u32[]{:S(2)}) copy-start(bf16[1280]{0:T(1024)(128)(2,1)} %param.9) | copy-start | bytes 7684
  2.9 15.6 %copy-start.1 = (bf16[2,256,8192]{2,1,0:T(8,128)(2,1)S(1)}, bf16[2,256,8192]{2,1,0:T(8,128)(2,1)}, u32[]{:S(2)}) copy-start(bf16[2,256,8192]{2,1,0:T(8,128)(2,1)} %param.7) | copy-start | bytes 25165828
  9.1 34.0 %copy-start.14 = (bf16[512,256]{1,0:T(8,128)(2,1)}, bf16[512,256]{1,0:T(8,128)(2,1)S(1)}, u32[]{:S(2)}) copy-start(bf16[512,256]{1,0:T(8,128)(2,1)S(1)} %collective-permute-done.refs_0_) | copy-start | bytes 786436
  9.1 9.5 %collective-permute-start.3 = (bf16[512,256]{1,0:T(8,128)(2,1)S(1)}, bf16[512,256]{1,0:T(8,128)(2,1)S(1)}, u32[]{:S(2)}, u32[]{:S(2)}) collective-permute-start(bf16[512,256]{1,0:T(8,128)(2,1)S(1)} %collective-permute-done.refs_0_), channel_id=1, source_target_pairs={{0,32},{16,48},{32,64},{48,80},{64,96},{80,112},{96,0},{112,16},{1... | collective-permute-start | bytes 786440 | tf_op jit(solution)/shard_map/from_below_0/ppermute | solution.py:289
  12.3 11.9 %collective-permute-start.4 = (bf16[512,256]{1,0:T(8,128)(2,1)S(1)}, bf16[512,256]{1,0:T(8,128)(2,1)S(1)}, u32[]{:S(2)}, u32[]{:S(2)}) collective-permute-start(bf16[512,256]{1,0:T(8,128)(2,1)S(1)} %collective-permute-done.refs_0_), channel_id=1, source_target_pairs={{32,0},{48,16},{64,32},{80,48},{96,64},{112,80},{0,96},{16,112},{3... | collective-permute-start | bytes 786440 | tf_op jit(solution)/shard_map/from_above_0/ppermute | solution.py:291
  14.6 12.5 %collective-permute-start.1 = (bf16[512,512]{1,0:T(8,128)(2,1)S(1)}, bf16[512,512]{1,0:T(8,128)(2,1)S(1)}, u32[]{:S(2)}, u32[]{:S(2)}) collective-permute-start(bf16[512,512]{1,0:T(8,128)(2,1)S(1)} %get-tuple-element.11), channel_id=1, source_target_pairs={{0,8},{8,0},{1,9},{9,1},{2,10},{10,2},{3,11},{11,3},{4,12},{12,4},... | collective-permute-start | bytes 1572872 | tf_op jit(solution)/shard_map/over_pair_1/ppermute | solution.py:284
  18.6 24.5 %copy-start.15 = (bf16[512,256]{1,0:T(8,128)(2,1)}, bf16[512,256]{1,0:T(8,128)(2,1)S(1)}, u32[]{:S(2)}) copy-start(bf16[512,256]{1,0:T(8,128)(2,1)S(1)} %collective-permute-done.3.refs_1_) | copy-start | bytes 786436
  18.6 7.7 %collective-permute-start.5 = (bf16[512,256]{1,0:T(8,128)(2,1)S(1)}, bf16[512,256]{1,0:T(8,128)(2,1)S(1)}, u32[]{:S(2)}, u32[]{:S(2)}) collective-permute-start(bf16[512,256]{1,0:T(8,128)(2,1)S(1)} %collective-permute-done.3.refs_1_), channel_id=1, source_target_pairs={{0,32},{16,48},{32,64},{48,80},{64,96},{80,112},{96,0},{112,16},{1... | collective-permute-start | bytes 786440 | tf_op jit(solution)/shard_map/from_opposite_0/ppermute | solution.py:296
  24.2 19.4 %copy-start.16 = (bf16[512,256]{1,0:T(8,128)(2,1)}, bf16[512,256]{1,0:T(8,128)(2,1)S(1)}, u32[]{:S(2)}) copy-start(bf16[512,256]{1,0:T(8,128)(2,1)S(1)} %collective-permute-done.4.refs_2_) | copy-start | bytes 786436
  26.3 2.8 %copy-start.17 = (bf16[512,256]{1,0:T(8,128)(2,1)}, bf16[512,256]{1,0:T(8,128)(2,1)S(1)}, u32[]{:S(2)}) copy-start(bf16[512,256]{1,0:T(8,128)(2,1)S(1)} %collective-permute-done.5.refs_3_) | copy-start | bytes 786436
  27.1 18.7 %copy-start.7 = (bf16[512,512]{1,0:T(8,128)(2,1)}, bf16[512,512]{1,0:T(8,128)(2,1)S(1)}, u32[]{:S(2)}) copy-start(bf16[512,512]{1,0:T(8,128)(2,1)S(1)} %collective-permute-done.1.refs_0_) | copy-start | bytes 1572868
  27.1 11.6 %collective-permute-start.7 = (bf16[512,512]{1,0:T(8,128)(2,1)S(1)}, bf16[512,512]{1,0:T(8,128)(2,1)S(1)}, u32[]{:S(2)}, u32[]{:S(2)}) collective-permute-start(bf16[512,512]{1,0:T(8,128)(2,1)S(1)} %collective-permute-done.1.refs_0_), channel_id=1, source_target_pairs={{32,0},{48,16},{64,32},{80,48},{96,64},{112,80},{0,96},{16,112},{3... | collective-permute-start | bytes 1572872 | tf_op jit(solution)/shard_map/from_above_1/ppermute | solution.py:291
  28.8 12.2 %collective-permute-start.6 = (bf16[512,512]{1,0:T(8,128)(2,1)S(1)}, bf16[512,512]{1,0:T(8,128)(2,1)S(1)}, u32[]{:S(2)}, u32[]{:S(2)}) collective-permute-start(bf16[512,512]{1,0:T(8,128)(2,1)S(1)} %collective-permute-done.1.refs_0_), channel_id=1, source_target_pairs={{0,32},{16,48},{32,64},{48,80},{64,96},{80,112},{96,0},{112,16},{1... | collective-permute-start | bytes 1572872 | tf_op jit(solution)/shard_map/from_below_1/ppermute | solution.py:289
  29.1 11.9 %collective-permute-start.2 = (bf16[512,512]{1,0:T(8,128)(2,1)S(1)}, bf16[512,512]{1,0:T(8,128)(2,1)S(1)}, u32[]{:S(2)}, u32[]{:S(2)}) collective-permute-start(bf16[512,512]{1,0:T(8,128)(2,1)S(1)} %get-tuple-element.12), channel_id=1, source_target_pairs={{0,8},{8,0},{1,9},{9,1},{2,10},{10,2},{3,11},{11,3},{4,12},{12,4},... | collective-permute-start | bytes 1572872 | tf_op jit(solution)/shard_map/over_pair_2/ppermute | solution.py:284
  30.3 13.4 %copy-start.20 = (s32[512]{0:T(512)S(1)}, s32[512]{0:T(512)}, u32[]{:S(2)}) copy-start(s32[512]{0:T(512)} %param.13) | copy-start | bytes 6148
  38.7 22.3 %copy-start.8 = (bf16[512,512]{1,0:T(8,128)(2,1)}, bf16[512,512]{1,0:T(8,128)(2,1)S(1)}, u32[]{:S(2)}) copy-start(bf16[512,512]{1,0:T(8,128)(2,1)S(1)} %collective-permute-done.7.refs_2_) | copy-start | bytes 1572868
  41.0 20.0 %copy-start.9 = (bf16[512,512]{1,0:T(8,128)(2,1)}, bf16[512,512]{1,0:T(8,128)(2,1)S(1)}, u32[]{:S(2)}) copy-start(bf16[512,512]{1,0:T(8,128)(2,1)S(1)} %collective-permute-done.6.refs_1_) | copy-start | bytes 1572868
  41.0 44.4 %copy-start.5 = (bf16[512,512]{1,0:T(8,128)(2,1)}, bf16[512,512]{1,0:T(8,128)(2,1)S(1)}, u32[]{:S(2)}) copy-start(bf16[512,512]{1,0:T(8,128)(2,1)S(1)} %collective-permute-done.2.refs_0_) | copy-start | bytes 1572868
  41.0 10.3 %collective-permute-start.19 = (bf16[512,512]{1,0:T(8,128)(2,1)S(1)}, bf16[512,512]{1,0:T(8,128)(2,1)}, u32[]{:S(2)}, u32[]{:S(2)}) collective-permute-start(bf16[512,512]{1,0:T(8,128)(2,1)S(1)} %collective-permute-done.7.refs_2_), channel_id=1, source_target_pairs={{32,0},{48,16},{64,32},{80,48},{96,64},{112,80},{0,96},{16,112},{3... | collective-permute-start | bytes 1572872 | tf_op jit(solution)/shard_map/from_opposite_1/ppermute | solution.py:294
  42.8 10.8 %collective-permute-start.8 = (bf16[512,512]{1,0:T(8,128)(2,1)S(1)}, bf16[512,512]{1,0:T(8,128)(2,1)S(1)}, u32[]{:S(2)}, u32[]{:S(2)}) collective-permute-start(bf16[512,512]{1,0:T(8,128)(2,1)S(1)} %collective-permute-done.2.refs_0_), channel_id=1, source_target_pairs={{0,32},{16,48},{32,64},{48,80},{64,96},{80,112},{96,0},{112,16},{1... | collective-permute-start | bytes 1572872 | tf_op jit(solution)/shard_map/from_below_2/ppermute | solution.py:289
  43.1 1.7 collective-permute-start.15
  43.1 2.7 %collective-permute-start.16 = (bf16[512,256]{1,0:T(8,128)(2,1)S(1)}, bf16[512,256]{1,0:T(8,128)(2,1)}, u32[]{:S(2)}, u32[]{:S(2)}) collective-permute-start(bf16[512,256]{1,0:T(8,128)(2,1)S(1)} %collective-permute-done.3.refs_1_), channel_id=1, source_target_pairs={{0,16},{16,0},{32,48},{48,32},{64,80},{80,64},{96,112},{112,96},{1... | collective-permute-start | bytes 786440 | tf_op jit(solution)/shard_map/from_twin_0/ppermute | solution.py:303
  43.6 2.7 %collective-permute-start.17 = (bf16[512,256]{1,0:T(8,128)(2,1)S(1)}, bf16[512,256]{1,0:T(8,128)(2,1)}, u32[]{:S(2)}, u32[]{:S(2)}) collective-permute-start(bf16[512,256]{1,0:T(8,128)(2,1)S(1)} %collective-permute-done.4.refs_2_), channel_id=1, source_target_pairs={{0,16},{16,0},{32,48},{48,32},{64,80},{80,64},{96,112},{112,96},{1... | collective-permute-start | bytes 786440 | tf_op jit(solution)/shard_map/from_twin_0/ppermute | solution.py:303
  44.8 8.8 %collective-permute-start.18 = (bf16[512,256]{1,0:T(8,128)(2,1)}, bf16[512,256]{1,0:T(8,128)(2,1)S(1)}, u32[]{:S(2)}, u32[]{:S(2)}) collective-permute-start(bf16[512,256]{1,0:T(8,128)(2,1)} %copy-done.17), channel_id=1, source_target_pairs={{0,16},{16,0},{32,48},{48,32},{64,80},{80,64},{96,112},{112,96},{1... | collective-permute-start | bytes 786440 | tf_op jit(solution)/shard_map/from_twin_0/ppermute | solution.py:303
  45.8 23.7 %collective-permute-start.20 = (bf16[512,512]{1,0:T(8,128)(2,1)S(1)}, bf16[512,512]{1,0:T(8,128)(2,1)}, u32[]{:S(2)}, u32[]{:S(2)}) collective-permute-start(bf16[512,512]{1,0:T(8,128)(2,1)S(1)} %collective-permute-done.1.refs_0_), channel_id=1, source_target_pairs={{0,16},{16,0},{32,48},{48,32},{64,80},{80,64},{96,112},{112,96},{1... | collective-permute-start | bytes 1572872 | tf_op jit(solution)/shard_map/from_twin_1/ppermute | solution.py:303
  46.3 24.4 %collective-permute-start.22 = (bf16[512,512]{1,0:T(8,128)(2,1)S(1)}, bf16[512,512]{1,0:T(8,128)(2,1)}, u32[]{:S(2)}, u32[]{:S(2)}) collective-permute-start(bf16[512,512]{1,0:T(8,128)(2,1)S(1)} %collective-permute-done.7.refs_2_), channel_id=1, source_target_pairs={{0,16},{16,0},{32,48},{48,32},{64,80},{80,64},{96,112},{112,96},{1... | collective-permute-start | bytes 1572872 | tf_op jit(solution)/shard_map/from_twin_1/ppermute | solution.py:303
  51.3 19.4 %collective-permute-start.21 = (bf16[512,512]{1,0:T(8,128)(2,1)S(1)}, bf16[512,512]{1,0:T(8,128)(2,1)}, u32[]{:S(2)}, u32[]{:S(2)}) collective-permute-start(bf16[512,512]{1,0:T(8,128)(2,1)S(1)} %collective-permute-done.6.refs_1_), channel_id=1, source_target_pairs={{0,16},{16,0},{32,48},{48,32},{64,80},{80,64},{96,112},{112,96},{1... | collective-permute-start | bytes 1572872 | tf_op jit(solution)/shard_map/from_twin_1/ppermute | solution.py:303
  53.5 32.0 %copy-start.6 = (bf16[512,512]{1,0:T(8,128)(2,1)}, bf16[512,512]{1,0:T(8,128)(2,1)S(1)}, u32[]{:S(2)}) copy-start(bf16[512,512]{1,0:T(8,128)(2,1)S(1)} %collective-permute-done.8.refs_1_) | copy-start | bytes 1572868
  53.5 17.2 %collective-permute-start.23 = (bf16[512,512]{1,0:T(8,128)(2,1)}, bf16[512,512]{1,0:T(8,128)(2,1)}, u32[]{:S(2)}, u32[]{:S(2)}) collective-permute-start(bf16[512,512]{1,0:T(8,128)(2,1)} %collective-permute-done.19.refs_3_), channel_id=1, source_target_pairs={{0,16},{16,0},{32,48},{48,32},{64,80},{80,64},{96,112},{112,96},{1... | collective-permute-start | bytes 1572872 | tf_op jit(solution)/shard_map/from_twin_1/ppermute | solution.py:303
  61.0 19.0 %all-to-all-start.1 = ((bf16[16,2,40,256]{3,2,1,0:T(8,128)(2,1)}), bf16[16,2,40,256]{3,2,1,0:T(8,128)(2,1)S(1)}, u32[]{:S(2)}, u32[]{:S(2)}) async-start(bf16[16,2,40,256]{3,2,1,0:T(8,128)(2,1)} %project_0.1), calls=%async_computation.1 | async-start | bytes 1310720 | tf_op jit(solution)/shard_map/route_0/all_to_all | solution.py:258
  68.7 17.4 %collective-permute-start.9 = (bf16[512,512]{1,0:T(8,128)(2,1)S(1)}, bf16[512,512]{1,0:T(8,128)(2,1)}, u32[]{:S(2)}, u32[]{:S(2)}) collective-permute-start(bf16[512,512]{1,0:T(8,128)(2,1)S(1)} %collective-permute-done.2.refs_0_), channel_id=1, source_target_pairs={{32,0},{48,16},{64,32},{80,48},{96,64},{112,80},{0,96},{16,112},{3... | collective-permute-start | bytes 1572872 | tf_op jit(solution)/shard_map/from_above_2/ppermute | solution.py:291
  69.5 16.7 %collective-permute-start.10 = (bf16[512,512]{1,0:T(8,128)(2,1)S(1)}, bf16[512,512]{1,0:T(8,128)(2,1)}, u32[]{:S(2)}, u32[]{:S(2)}) collective-permute-start(bf16[512,512]{1,0:T(8,128)(2,1)S(1)} %collective-permute-done.8.refs_1_), channel_id=1, source_target_pairs={{0,32},{16,48},{32,64},{48,80},{64,96},{80,112},{96,0},{112,16},{1... | collective-permute-start | bytes 1572872 | tf_op jit(solution)/shard_map/from_opposite_2/ppermute | solution.py:296
  80.1 18.1 %copy-start.2 = (bf16[16,2,40,256]{3,2,1,0:T(8,128)(2,1)}, bf16[16,2,40,256]{3,2,1,0:T(8,128)(2,1)S(1)}, u32[]{:S(2)}) copy-start(bf16[16,2,40,256]{3,2,1,0:T(8,128)(2,1)S(1)} %all-to-all-done.1) | copy-start | bytes 1966084
  80.1 24.5 %all-to-all-start.3 = ((bf16[16,2,40,512]{3,2,1,0:T(8,128)(2,1)}), bf16[16,2,40,512]{3,2,1,0:T(8,128)(2,1)S(1)}, u32[]{:S(2)}, u32[]{:S(2)}) async-start(bf16[16,2,40,512]{3,2,1,0:T(8,128)(2,1)} %project_1.1), calls=%async_computation.3 | async-start | bytes 2621440 | tf_op jit(solution)/shard_map/route_1/all_to_all | solution.py:258
  85.5 24.0 %copy-start = (s32[40]{0:T(128)S(1)}, s32[40]{0:T(128)}, u32[]{:S(2)}) copy-start(s32[40]{0:T(128)} %fill_ref.3) | copy-start | bytes 484
  85.5 2.0 %collective-permute-start.11 = (bf16[512,512]{1,0:T(8,128)(2,1)S(1)}, bf16[512,512]{1,0:T(8,128)(2,1)S(1)}, u32[]{:S(2)}, u32[]{:S(2)}) collective-permute-start(bf16[512,512]{1,0:T(8,128)(2,1)S(1)} %collective-permute-done.2.refs_0_), channel_id=1, source_target_pairs={{0,16},{16,0},{32,48},{48,32},{64,80},{80,64},{96,112},{112,96},{1... | collective-permute-start | bytes 1572872 | tf_op jit(solution)/shard_map/from_twin_2/ppermute | solution.py:303
  85.6 3.4 %collective-permute-start.12 = (bf16[512,512]{1,0:T(8,128)(2,1)S(1)}, bf16[512,512]{1,0:T(8,128)(2,1)S(1)}, u32[]{:S(2)}, u32[]{:S(2)}) collective-permute-start(bf16[512,512]{1,0:T(8,128)(2,1)S(1)} %collective-permute-done.8.refs_1_), channel_id=1, source_target_pairs={{0,16},{16,0},{32,48},{48,32},{64,80},{80,64},{96,112},{112,96},{1... | collective-permute-start | bytes 1572872 | tf_op jit(solution)/shard_map/from_twin_2/ppermute | solution.py:303
  86.1 3.1 %collective-permute-start.13 = (bf16[512,512]{1,0:T(8,128)(2,1)}, bf16[512,512]{1,0:T(8,128)(2,1)S(1)}, u32[]{:S(2)}, u32[]{:S(2)}) collective-permute-start(bf16[512,512]{1,0:T(8,128)(2,1)} %collective-permute-done.9.refs_2_), channel_id=1, source_target_pairs={{0,16},{16,0},{32,48},{48,32},{64,80},{80,64},{96,112},{112,96},{1... | collective-permute-start | bytes 1572872 | tf_op jit(solution)/shard_map/from_twin_2/ppermute | solution.py:303
  86.2 3.7 %collective-permute-start.14 = (bf16[512,512]{1,0:T(8,128)(2,1)}, bf16[512,512]{1,0:T(8,128)(2,1)S(1)}, u32[]{:S(2)}, u32[]{:S(2)}) collective-permute-start(bf16[512,512]{1,0:T(8,128)(2,1)} %collective-permute-done.10.refs_3_), channel_id=1, source_target_pairs={{0,16},{16,0},{32,48},{48,32},{64,80},{80,64},{96,112},{112,96},{1... | collective-permute-start | bytes 1572872 | tf_op jit(solution)/shard_map/from_twin_2/ppermute | solution.py:303
  87.5 2.5 %copy-start.10 = (bf16[512,512]{1,0:T(8,128)(2,1)}, bf16[512,512]{1,0:T(8,128)(2,1)S(1)}, u32[]{:S(2)}) copy-start(bf16[512,512]{1,0:T(8,128)(2,1)S(1)} %collective-permute-done.11.refs_4_) | copy-start | bytes 1572868
  89.0 1.0 copy-start.11
  90.0 0.8 copy-start.13
  104.6 5.2 %copy-start.3 = (bf16[16,2,40,512]{3,2,1,0:T(8,128)(2,1)}, bf16[16,2,40,512]{3,2,1,0:T(8,128)(2,1)S(1)}, u32[]{:S(2)}) copy-start(bf16[16,2,40,512]{3,2,1,0:T(8,128)(2,1)S(1)} %all-to-all-done.3) | copy-start | bytes 3932164
  104.6 23.3 %all-to-all-start = ((bf16[16,2,40,512]{3,2,1,0:T(8,128)(2,1)}), bf16[16,2,40,512]{3,2,1,0:T(8,128)(2,1)S(1)}, u32[]{:S(2)}, u32[]{:S(2)}) async-start(bf16[16,2,40,512]{3,2,1,0:T(8,128)(2,1)} %project_2.1), calls=%async_computation | async-start | bytes 2621440 | tf_op jit(solution)/shard_map/route_2/all_to_all | solution.py:258
  127.9 4.8 %copy-start.4 = (bf16[16,2,40,512]{3,2,1,0:T(8,128)(2,1)}, bf16[16,2,40,512]{3,2,1,0:T(8,128)(2,1)S(1)}, u32[]{:S(2)}) copy-start(bf16[16,2,40,512]{3,2,1,0:T(8,128)(2,1)S(1)} %all-to-all-done) | copy-start | bytes 3932164
  127.9 23.5 %all-to-all-start.4 = ((bf16[16,2,40,512]{3,2,1,0:T(8,128)(2,1)}), bf16[16,2,40,512]{3,2,1,0:T(8,128)(2,1)S(1)}, u32[]{:S(2)}, u32[]{:S(2)}) async-start(bf16[16,2,40,512]{3,2,1,0:T(8,128)(2,1)} %bitcast.27), calls=%async_computation.4 | async-start | bytes 2621440 | tf_op jit(solution)/shard_map/all_to_all | solution.py:258
  151.4 23.4 %all-to-all-start.2 = ((bf16[16,2,40,512]{3,2,1,0:T(8,128)(2,1)}), bf16[16,2,40,512]{3,2,1,0:T(8,128)(2,1)S(1)}, u32[]{:S(2)}, u32[]{:S(2)}) async-start(bf16[16,2,40,512]{3,2,1,0:T(8,128)(2,1)} %bitcast.26), calls=%async_computation.2 | async-start | bytes 2621440 | tf_op jit(solution)/shard_map/all_to_all | solution.py:258
  (2 other events, 1.5 us)

commit v6 on v5

--- a/solution.py
+++ b/solution.py
@@ -28,26 +28,40 @@
     return jnp.concatenate([cosine, cosine], -1), jnp.concatenate([-sine, sine], -1)
 
 
-def project_kernel(owners, rows, places_ref, x_ref, *refs):
-    slabs = refs[:-7]
-    partial_ref, pack_ref, out_ref, taken, met, total, arrived = refs[-7:]
-    depth = slabs[0].shape[0]
+def project_kernel(parts, owners, rows, places_ref, x_ref, *refs):
+    slabs, refs = refs[:-(parts + 6)], refs[-(parts + 6):]
+    partials = refs[:parts]
+    pack_ref, out_ref, taken, met, total, arrived = refs[parts:]
+    count = taken.shape[0]
+    depth = met.shape[1]
     share = pack_ref.shape[1]
+    spans, at = [], 0
+    for part in partials:
+        spans.append((at, part.shape[1]))
+        at += part.shape[1]
     copies = []
-    for i, slab in enumerate(slabs):
+    for i in range(count):
         first = pl.multiple_of(places_ref[i] * depth, depth)
-        copies.append((
-            pltpu.make_async_copy(x_ref.at[:, pl.ds(first, depth)], taken.at[i], arrived.at[0, i]),
-            pltpu.make_async_copy(slab, met.at[i], arrived.at[1, i]),
-        ))
+        copies.append([
+            pltpu.make_async_copy(x_ref.at[:, pl.ds(first, depth)], taken.at[i], arrived.at[0, i])
+        ])
+        for part, (start, wide) in enumerate(spans):
+            copies[i].append(
+                pltpu.make_async_copy(
+                    slabs[part * count + i], met.at[i, :, pl.ds(start, wide)],
+                    arrived.at[part + 1, i],
+                )
+            )
         for copy in copies[i]:
             copy.start()
-    for i in range(len(slabs)):
+    for i in range(count):
         for copy in copies[i]:
             copy.wait()
         product = jnp.dot(taken[i], met[i], preferred_element_type=jnp.float32)
         if i == 0:
-            total[...] = partial_ref[...] + product
+            for part, (start, wide) in zip(partials, spans):
+                columns = slice(start, start + wide)
+                total[:, columns] = part[...] + product[:, columns]
         else:
             total[...] += product
     for step in range(2):
@@ -58,37 +72,40 @@
             out_ref[owner, step] = block.astype(jnp.bfloat16)
 
 
-def project(places, signals, slabs, partial, pack, owners):
+def project(places, signals, slabs, partials, pack, owners):
     lines, _ = signals.shape
-    depth, wide = slabs[0].shape
+    count, parts = len(slabs[0]), len(slabs)
+    depth = slabs[0][0].shape[0]
+    wide = sum(partial.shape[1] for partial in partials)
     slots, share = pack.shape
     rows = slots // owners
-    count = len(slabs)
     return pl.pallas_call(
-        functools.partial(project_kernel, owners, rows),
+        functools.partial(project_kernel, parts, owners, rows),
         out_shape=pltpu.HBM((owners, 2, rows, wide), jnp.bfloat16),
         grid_spec=pltpu.PrefetchScalarGridSpec(
             num_scalar_prefetch=1,
             grid=(1,),
-            in_specs=[pl.BlockSpec(memory_space=pl.ANY)] * (count + 1) + [
-                pl.BlockSpec((lines, wide), lambda k, s: (0, 0)),
-                pl.BlockSpec((slots, share), lambda k, s: (0, 0)),
-            ],
+            in_specs=[pl.BlockSpec(memory_space=pl.ANY)] * (1 + parts * count) + [
+                pl.BlockSpec(partial.shape, lambda k, s: (0, 0)) for partial in partials
+            ] + [pl.BlockSpec((slots, share), lambda k, s: (0, 0))],
             out_specs=pl.BlockSpec((owners, 2, rows, wide), lambda k, s: (0, 0, 0, 0)),
             scratch_shapes=[
                 pltpu.VMEM((count, lines, depth), jnp.bfloat16),
                 pltpu.VMEM((count, depth, wide), jnp.bfloat16),
                 pltpu.VMEM((lines, wide), jnp.float32),
-                pltpu.SemaphoreType.DMA((2, count)),
+                pltpu.SemaphoreType.DMA((parts + 1, count)),
             ],
         ),
-        compiler_params=pltpu.CompilerParams(vmem_limit_bytes=26 << 20),
+        compiler_params=pltpu.CompilerParams(vmem_limit_bytes=30 << 20),
         cost_estimate=pl.CostEstimate(
             flops=2 * lines * depth * count * wide,
             transcendentals=0,
             bytes_accessed=2 * (lines + wide) * depth * count,
         ),
-    )(places, in_hbm(signals), *(in_hbm(slab) for slab in slabs), in_hbm(partial), in_hbm(pack))
+    )(
+        places, in_hbm(signals), *(in_hbm(slab) for part in slabs for slab in part),
+        *(in_hbm(partial) for partial in partials), in_hbm(pack),
+    )
 
 
 def attention_kernel(heads, fill_ref, cos_ref, sin_ref, q_ref, k_new_ref, v_new_ref, k_ref, v_ref, out_ref,
@@ -160,7 +177,7 @@
                     out_ref[pair, t, step, :, head * HEAD:(head + 1) * HEAD] = done
 
 
-def attend(fill, cosine, sine, queries, new, keys, values, heads):
+def attend(fill, cosine, sine, queries, new, new_at, keys, values, heads):
     _, n_tp, _, rows, _ = queries.shape
     places = keys.shape[1]
     block = ROW_BLOCK
@@ -178,7 +195,7 @@
             num_scalar_prefetch=1,
             grid=(rows // block,),
             in_specs=[
-                table, table, routed(heads * HEAD), routed(HEAD, 0), routed(HEAD, 1),
+                table, table, routed(heads * HEAD), routed(HEAD, new_at), routed(HEAD, new_at + 1),
                 cache, cache,
             ],
             out_specs=routed(heads * HEAD),
@@ -202,14 +219,29 @@
     )
 
 
-def unpack_kernel(owners, rows, pick_ref, back_ref, *refs):
-    out_ref, gathered = refs[-2:]
+def unpack_kernel(owners, rows, at, pick_ref, back_ref, *refs):
+    out_ref, gathered, picked, written = refs[-4:]
+    step = pl.program_id(0)
     for owner in range(owners):
         gathered[pl.ds(owner * rows, rows), :] = back_ref[owner, 0].astype(jnp.float32)
-    picked = jnp.dot(
+    picked[step] = jnp.dot(
         pick_ref[...], gathered[...].astype(jnp.bfloat16), preferred_element_type=jnp.float32
-    )
-    out_ref[0] = picked.astype(jnp.bfloat16)
+    ).astype(jnp.bfloat16)
+    columns = pl.ds(at, picked.shape[2])
+    copies = [
+        pltpu.make_async_copy(picked.at[i], out_ref.at[i, :, columns], written.at[i])
+        for i in range(2)
+    ]
+
+    @pl.when(step == 0)
+    def _():
+        copies[0].start()
+
+    @pl.when(step == 1)
+    def _():
+        copies[1].start()
+        copies[0].wait()
+        copies[1].wait()
 
 
 def unpack(pick, back, at, columns, so_far):
@@ -217,17 +249,21 @@
     share, slots = pick.shape
     before = [] if so_far is None else [so_far]
     return pl.pallas_call(
-        functools.partial(unpack_kernel, owners, rows),
+        functools.partial(unpack_kernel, owners, rows, at),
         out_shape=jax.ShapeDtypeStruct((2, share, columns), jnp.bfloat16),
         grid=(2,),
         in_specs=[
             pl.BlockSpec((share, slots), lambda s: (0, 0)),
             pl.BlockSpec((owners, 1, rows, wide), lambda s: (0, s, 0, 0)),
         ] + [pl.BlockSpec(memory_space=pl.ANY)] * len(before),
-        out_specs=pl.BlockSpec((1, share, wide), lambda s: (s, 0, at)),
-        scratch_shapes=[pltpu.VMEM((slots, wide), jnp.float32)],
+        out_specs=pl.BlockSpec(memory_space=pl.ANY),
+        scratch_shapes=[
+            pltpu.VMEM((slots, wide), jnp.float32),
+            pltpu.VMEM((2, share, wide), jnp.bfloat16),
+            pltpu.SemaphoreType.DMA((2,)),
+        ],
         input_output_aliases={2: 0} if before else {},
-        compiler_params=pltpu.CompilerParams(vmem_limit_bytes=8 << 20),
+        compiler_params=pltpu.CompilerParams(vmem_limit_bytes=12 << 20),
         cost_estimate=pl.CostEstimate(
             flops=4 * share * slots * wide, transcendentals=0, bytes_accessed=4 * slots * wide
         ),
@@ -257,16 +293,16 @@
     def exchange(blocks):
         return lax.all_to_all(blocks, ("pair", "tp"), split_axis=0, concat_axis=0, tiled=True)
 
-    spans = [(SHARING * HEAD, columns)] + [(a * HEAD, b * HEAD) for a, b in CHUNKS]
+    spans = [(a * HEAD, b * HEAD) for a, b in CHUNKS]
+    spans.insert(0, (SHARING * HEAD, columns))
     n_z = n_grp // 2
     up = [(2 * a + c, 2 * ((a + 1) % n_z) + c) for a in range(n_z) for c in range(2)]
     down = [(d, s) for s, d in up]
     twin = [(2 * a + c, 2 * a + 1 - c) for a in range(n_z) for c in range(2)]
     z, core = grp // 2, grp % 2
-    turns = (0, n_z - 1, 1, 2)
+    held_of = [(z + turn) % n_z * 2 for turn in (0, n_z - 1, 1, 2)]
     places = (1 - pair) * n_grp + jnp.stack(
-        [(z + turn) % n_z * 2 + core for turn in turns]
-        + [(z + turn) % n_z * 2 + 1 - core for turn in turns]
+        [first + core for first in held_of] + [first + 1 - core for first in held_of]
     )
     places = places.astype(jnp.int32)
 
@@ -280,8 +316,8 @@
     crossed = []
     for number, (start, stop) in enumerate(spans):
         with jax.named_scope("over_pair_%d" % number):
-            slab = lax.dynamic_slice(matrix, (grp * depth, start), (depth, stop - start))
-            crossed.append(lax.ppermute(after(slab, *crossed[-1:]), "pair", SWAP))
+            slab = lax.dynamic_slice(matrix, ((held_of[0] + core) * depth, start), (depth, stop - start))
+            crossed.append(lax.ppermute(after(slab, *crossed[1:]), "pair", SWAP))
     ring, ahead = [], []
     for number, slab in enumerate(crossed):
         slab = after(slab, partials[number], *ahead)
@@ -296,23 +332,26 @@
                 opposite = lax.ppermute(below, "grp", up)
         ahead = [below, above] if number else [below, above, opposite]
         ring.append([slab, below, above, opposite])
-    partials[0] = after(partials[0], crossed[2], ring[1][3], ring[2][1])
+    partials[0] = after(partials[0], crossed[2], ring[2][1])
     arrived = []
-    for number, (span, four) in enumerate(zip(spans, ring)):
-        with jax.named_scope("from_twin_%d" % number):
-            slabs = four + [lax.ppermute(piece, "grp", twin) for piece in four]
-        with jax.named_scope("project_%d" % number):
-            packed = project(places, flat, slabs, partials[number], pack, owners)
-        with jax.named_scope("route_%d" % number):
-            arrived.append(exchange(packed).reshape(n_pair, n_tp, 2, rows, span[1] - span[0]))
+    for group in ((1, 0), (2,)):
+        slabs = []
+        for number in group:
+            with jax.named_scope("from_twin_%d" % number):
+                slabs.append(ring[number] + [lax.ppermute(piece, "grp", twin) for piece in ring[number]])
+        with jax.named_scope("project_%d" % group[0]):
+            packed = project(places, flat, slabs, [partials[number] for number in group], pack, owners)
+        with jax.named_scope("route_%d" % group[0]):
+            arrived.append(exchange(packed).reshape(n_pair, n_tp, 2, rows, packed.shape[-1]))
     out = None
-    for (first, last), queries in zip(CHUNKS, arrived[1:]):
+    for (first, last), queries in zip(CHUNKS, arrived):
         heads = last - first
         attended = attend(
-            fill, cosine, sine, queries, arrived[0], cached_keys, cached_values, heads
+            fill, cosine, sine, queries, arrived[0], CHUNKS[0][1] - CHUNKS[0][0],
+            cached_keys, cached_values, heads,
         )
         back = exchange(attended.reshape(owners, 2, rows, heads * HEAD))
-        out = unpack(pick, back, first // heads, SHARING * HEAD, out)
+        out = unpack(pick, back, first * HEAD, SHARING * HEAD, out)
     return out
 
 

time: 178 us -> 183 us (1.028)
  waiting for transfers between devices: 56.4 us -> 67.8 us
  Pallas kernels: 53.6 us -> 50.2 us
  starting transfers between devices: 43.9 us -> 41.7 us
    ppermute x3, waiting for transfers between devices: 2.87 us -> 19.7 us  [per_device(): above = lax.ppermute(slab, 'grp', down)]
    all_to_all x5 -> x4, waiting for transfers between devices: 33 us -> 27.9 us  [exchange(): lax.all_to_all(blocks, ('pair', 'tp'), split_axis=0, concat_axis=0, tiled...]
    ppermute x1, waiting for transfers between devices: 4.86 us -> 0.27 us  [per_device(): opposite = lax.ppermute(above, 'grp', down)]
    ppermute x3, waiting for transfers between devices: 7.29 us -> 11.3 us  [per_device(): below = lax.ppermute(slab, 'grp', up)]
    pallas_call x5 -> x4, Pallas kernels: 24.7 us -> 21.3 us  [the longest x2 18.2 us: project(): pl.pallas_call(functools.partial(project_kernel, parts, owners, rows), ou...]
    all_to_all x5 -> x4, starting transfers between devices: 27.5 us -> 25.6 us  [exchange(): lax.all_to_all(blocks, ('pair', 'tp'), split_axis=0, concat_axis=0, tiled...]
  transfers between devices with their start and end apart: 29 -> 28, of which waited for: 18 -> 19; matrix products, arithmetic and copies ran while one was open for 11% -> 11% of each run, Pallas kernels for 30% -> 21%
where the time goes in v6:
time: 183 us; the launch traced here: 182 us
  waiting for transfers between devices  67.8 us (37%)
  Pallas kernels  50.2 us (27%)
  starting transfers between devices  41.7 us (23%)
  matrix products  16.1 us (9%)
  local copies, waits for them, and re-layouts  4.1 us (2%)
  other arithmetic  1.97 us (1%)
    pallas_call x2, Pallas kernels, attend(): pl.pallas_call(functools.partial(attention_kernel, heads), out_shape=pltp...  28.9 us
    all_to_all x4, waiting for transfers between devices, exchange(): lax.all_to_all(blocks, ('pair', 'tp'), split_axis=0, concat_axis=0, tiled...  27.9 us
    all_to_all x4, starting transfers between devices, exchange(): lax.all_to_all(blocks, ('pair', 'tp'), split_axis=0, concat_axis=0, tiled...  25.6 us
    ppermute x3, waiting for transfers between devices, per_device(): above = lax.ppermute(slab, 'grp', down)  19.7 us
    pallas_call x2, Pallas kernels, project(): pl.pallas_call(functools.partial(project_kernel, parts, owners, rows), ou...  18.2 us
    dot_general x3, matrix products, per_device(): jnp.dot(near, matrix[:, slice(*span)], preferred_element_type=jnp.float32)  16.1 us
    ppermute x3, waiting for transfers between devices, per_device(): below = lax.ppermute(slab, 'grp', up)  11.3 us
    ppermute x12, waiting for transfers between devices, per_device(): lax.ppermute(piece, 'grp', twin)  4.08 us
  transfers between devices with their start and end apart: 28, of which 19 were waited for; matrix products, arithmetic and copies ran while one was open for 11% of the time, Pallas kernels for 21%

profile of v6, /device:TPU:4, one launch (start us, length us, event | category | flops | bytes accessed | tf_op | source)
XLA Modules:
  0.0 182.3 jit_solution(10145415632759181740)
XLA Ops:
  0.0 1.0 constant_dynamic-slice_fusion
  1.0 1.3 collective-permute-start.2
  2.2 0.7 slice_convert_fusion.2
  2.9 5.0 %fusion.19.refs_17_ = f32[512,256]{1,0:T(8,128)} fusion(bf16[4096,1280]{1,0:T(8,128)(2,1)} %param.8, bf16[512,8192]{1,0:T(8,128)(2,1)} %bitcast.18, s32[]{:T(128)S(6)} %select_n.46, f32[256]{0:T(256)S(1)} %slice_convert_fusion.2), kind=kOutput, calls=%fused_computation.11 | convolution fusion | flops 1073872896 | bytes 6816772 | tf_op jit(solution)/shard_map/dot_general | solution.py:311
  8.0 1.1 collective-permute-done.2.refs_8_
  9.1 1.9 %collective-permute-start.3 = (bf16[512,256]{1,0:T(8,128)(2,1)S(1)}, bf16[512,256]{1,0:T(8,128)(2,1)S(1)}, u32[]{:S(2)}, u32[]{:S(2)}) collective-permute-start(bf16[512,256]{1,0:T(8,128)(2,1)S(1)} %collective-permute-done.2.refs_8_), channel_id=1, source_target_pairs={{0,32},{16,48},{32,64},{48,80},{64,96},{80,112},{96,0},{112,16},{1... | collective-permute-start | bytes 786440 | tf_op jit(solution)/shard_map/from_below_0/ppermute | solution.py:325
  11.0 1.3 constant_dynamic-slice_fusion.1
  12.3 1.3 collective-permute-start
  13.6 2.2 %collective-permute-start.4 = (bf16[512,256]{1,0:T(8,128)(2,1)S(1)}, bf16[512,256]{1,0:T(8,128)(2,1)S(1)}, u32[]{:S(2)}, u32[]{:S(2)}) collective-permute-start(bf16[512,256]{1,0:T(8,128)(2,1)S(1)} %collective-permute-done.2.refs_8_), channel_id=1, source_target_pairs={{32,0},{48,16},{64,32},{80,48},{96,64},{112,80},{0,96},{16,112},{3... | collective-permute-start | bytes 786440 | tf_op jit(solution)/shard_map/from_above_0/ppermute | solution.py:327
  15.8 2.8 %collective-permute-done.3.refs_9_ = bf16[512,256]{1,0:T(8,128)(2,1)S(1)} collective-permute-done((bf16[512,256]{1,0:T(8,128)(2,1)S(1)}, bf16[512,256]{1,0:T(8,128)(2,1)S(1)}, u32[]{:S(2)}, u32[]{:S(2)}) %collective-permute-start.3) | collective-permute-done | bytes 262176 | tf_op jit(solution)/shard_map/from_below_0/ppermute | solution.py:325
  18.6 5.6 %fusion.14.refs_16_ = f32[512,512]{1,0:T(8,128)} fusion(bf16[4096,1280]{1,0:T(8,128)(2,1)} %param.8, bf16[512,8192]{1,0:T(8,128)(2,1)S(1)} %bitcast.21, s32[]{:T(128)S(6)} %select_n.46, f32[512]{0:T(512)S(1)} %get-tuple-element.17), kind=kOutput, calls=%fused_computation.10 | convolution fusion | flops 2147745792 | bytes 9439236 | tf_op jit(solution)/shard_map/dot_general | solution.py:311
  24.2 0.7 collective-permute-done.refs_0_
  24.9 1.4 collective-permute-done.5.refs_11_
  26.3 1.2 collective-permute-start.7
  27.5 1.2 collective-permute-start.1
  28.7 0.9 collective-permute-start.6
  29.5 8.9 %collective-permute-done.7.refs_2_ = bf16[512,512]{1,0:T(8,128)(2,1)S(1)} collective-permute-done((bf16[512,512]{1,0:T(8,128)(2,1)S(1)}, bf16[512,512]{1,0:T(8,128)(2,1)S(1)}, u32[]{:S(2)}, u32[]{:S(2)}) %collective-permute-start.7) | collective-permute-done | bytes 524320 | tf_op jit(solution)/shard_map/from_above_1/ppermute | solution.py:327
  38.4 2.2 %collective-permute-start.15 = (bf16[512,512]{1,0:T(8,128)(2,1)S(1)}, bf16[512,512]{1,0:T(8,128)(2,1)S(1)}, u32[]{:S(2)}, u32[]{:S(2)}) collective-permute-start(bf16[512,512]{1,0:T(8,128)(2,1)S(1)} %collective-permute-done.7.refs_2_), channel_id=1, source_target_pairs={{32,0},{48,16},{64,32},{80,48},{96,64},{112,80},{0,96},{16,112},{3... | collective-permute-start | bytes 1572872 | tf_op jit(solution)/shard_map/from_opposite_1/ppermute | solution.py:330
  40.6 5.5 %fusion.9.refs_8_ = f32[512,512]{1,0:T(8,128)} fusion(bf16[4096,1280]{1,0:T(8,128)(2,1)} %param.8, bf16[512,8192]{1,0:T(8,128)(2,1)S(1)} %bitcast.22, s32[]{:T(128)S(6)} %select_n.46, f32[512]{0:T(512)S(1)} %get-tuple-element.18), kind=kOutput, calls=%fused_computation.9 | convolution fusion | flops 2147745792 | bytes 9439236 | tf_op jit(solution)/shard_map/dot_general | solution.py:311
  46.3 0.5 collective-permute-start.21
  46.9 0.9 collective-permute-done.20.refs_12_
  47.9 0.2 collective-permute-done.21.refs_13_
  48.8 0.3 collective-permute-done.15.refs_3_
  49.5 8.6 %collective-permute-done.8.refs_1_ = bf16[512,512]{1,0:T(8,128)(2,1)S(1)} collective-permute-done((bf16[512,512]{1,0:T(8,128)(2,1)S(1)}, bf16[512,512]{1,0:T(8,128)(2,1)S(1)}, u32[]{:S(2)}, u32[]{:S(2)}) %collective-permute-start.8) | collective-permute-done | bytes 524320 | tf_op jit(solution)/shard_map/from_below_2/ppermute | solution.py:325
  58.1 0.8 fusion.25.refs_9_.refs_18_
  59.0 0.8 collective-permute-done.23.refs_15_
  59.8 0.6 copy-done.23
  60.5 10.8 %project_1.1 = bf16[16,2,40,768]{3,2,1,0:T(8,128)(2,1)} custom-call(s32[8]{0:T(128)S(1)} %broadcast_add_fusion.places_ref, bf16[512,8192]{1,0:T(8,128)(2,1)} %bitcast.19, bf16[512,512]{1,0:T(8,128)(2,1)} %copy-done.6, bf16[512,512]{1,0:T(8,128)(2,1)} %copy-done.8, bf16[512,512]{1,0:T(8,128)(2,1)} %copy-done.7, bf16[512,512]{1,0:T(8,128)(2,1)} %copy-done.9, ...), custom_call_target="tpu_custom_call" | custom-call | flops 3221225472 | bytes 10485760 | tf_op jit(solution)/shard_map/project_1/pallas_call | solution.py:82
  71.3 7.5 %all-to-all-start.1 = ((bf16[16,2,40,768]{3,2,1,0:T(8,128)(2,1)}), bf16[16,2,40,768]{3,2,1,0:T(8,128)(2,1)S(1)}, u32[]{:S(2)}, u32[]{:S(2)}) async-start(bf16[16,2,40,768]{3,2,1,0:T(8,128)(2,1)} %project_1.1), calls=%async_computation.1 | async-start | bytes 3932160 | tf_op jit(solution)/shard_map/route_1/all_to_all | solution.py:294
  78.8 2.0 %collective-permute-start.10 = (bf16[512,512]{1,0:T(8,128)(2,1)S(1)}, bf16[512,512]{1,0:T(8,128)(2,1)S(1)}, u32[]{:S(2)}, u32[]{:S(2)}) collective-permute-start(bf16[512,512]{1,0:T(8,128)(2,1)S(1)} %collective-permute-done.8.refs_1_), channel_id=1, source_target_pairs={{0,32},{16,48},{32,64},{48,80},{64,96},{80,112},{96,0},{112,16},{1... | collective-permute-start | bytes 1572872 | tf_op jit(solution)/shard_map/from_opposite_2/ppermute | solution.py:332
  80.8 0.5 collective-permute-start.12
  81.3 10.9 %collective-permute-done.9.refs_2_ = bf16[512,512]{1,0:T(8,128)(2,1)S(1)} collective-permute-done((bf16[512,512]{1,0:T(8,128)(2,1)S(1)}, bf16[512,512]{1,0:T(8,128)(2,1)S(1)}, u32[]{:S(2)}, u32[]{:S(2)}) %collective-permute-start.9) | collective-permute-done | bytes 524320 | tf_op jit(solution)/shard_map/from_above_2/ppermute | solution.py:327
  92.2 1.3 collective-permute-done.10.refs_3_
  93.5 0.6 collective-permute-done.13.refs_6_
  94.1 1.3 collective-permute-done.14.refs_7_
  95.4 0.8 copy-done.15
  96.2 7.4 %project_2.1 = bf16[16,2,40,512]{3,2,1,0:T(8,128)(2,1)} custom-call(s32[8]{0:T(128)S(1)} %broadcast_add_fusion.places_ref, bf16[512,8192]{1,0:T(8,128)(2,1)} %bitcast.20, bf16[512,512]{1,0:T(8,128)(2,1)} %copy-done.4, bf16[512,512]{1,0:T(8,128)(2,1)} %copy-done.5, bf16[512,512]{1,0:T(8,128)(2,1)} %copy-done.10, bf16[512,512]{1,0:T(8,128)(2,1)} %copy-done.11, ...), custom_call_target="tpu_custom_call" | custom-call | flops 2147483648 | bytes 8388608 | tf_op jit(solution)/shard_map/project_2/pallas_call | solution.py:82
  103.6 2.9 %all-to-all-done.1 = bf16[16,2,40,768]{3,2,1,0:T(8,128)(2,1)S(1)} async-done(((bf16[16,2,40,768]{3,2,1,0:T(8,128)(2,1)}), bf16[16,2,40,768]{3,2,1,0:T(8,128)(2,1)S(1)}, u32[]{:S(2)}, u32[]{:S(2)}) %all-to-all-start.1) | async-done | bytes 1966112 | tf_op jit(solution)/shard_map/route_1/all_to_all | solution.py:294
  106.5 8.5 %all-to-all-start = ((bf16[16,2,40,512]{3,2,1,0:T(8,128)(2,1)}), bf16[16,2,40,512]{3,2,1,0:T(8,128)(2,1)S(1)}, u32[]{:S(2)}, u32[]{:S(2)}) async-start(bf16[16,2,40,512]{3,2,1,0:T(8,128)(2,1)} %project_2.1), calls=%async_computation | async-start | bytes 2621440 | tf_op jit(solution)/shard_map/route_2/all_to_all | solution.py:294
  115.4 14.4 %shard_map.74 = bf16[2,8,2,40,512]{4,3,2,1,0:T(8,128)(2,1)} custom-call(s32[40]{0:T(128)S(1)} %copy-done, f32[2,40,128]{2,1,0:T(8,128)S(1)} %get-tuple-element.22.cos_ref, f32[2,40,128]{2,1,0:T(8,128)S(1)} %get-tuple-element.23.sin_ref, bf16[2,8,2,40,768]{4,3,2,1,0:T(8,128)(2,1)} %bitcast.13, bf16[2,8,2,40,768]{4,3,2,1,0:T(8,128)(2,1)} %bitcast.14, ...), custom_call_target="tpu_custom_call" | custom-call | flops 167772160 | bytes 20971520 | tf_op jit(solution)/shard_map/pallas_call | solution.py:191
  129.8 3.9 %all-to-all-done = bf16[16,2,40,512]{3,2,1,0:T(8,128)(2,1)S(1)} async-done(((bf16[16,2,40,512]{3,2,1,0:T(8,128)(2,1)}), bf16[16,2,40,512]{3,2,1,0:T(8,128)(2,1)S(1)}, u32[]{:S(2)}, u32[]{:S(2)}) %all-to-all-start) | async-done | bytes 1310752 | tf_op jit(solution)/shard_map/route_2/all_to_all | solution.py:294
  133.7 4.8 %all-to-all-start.3 = ((bf16[16,2,40,512]{3,2,1,0:T(8,128)(2,1)}), bf16[16,2,40,512]{3,2,1,0:T(8,128)(2,1)S(1)}, u32[]{:S(2)}, u32[]{:S(2)}) async-start(bf16[16,2,40,512]{3,2,1,0:T(8,128)(2,1)} %bitcast.23), calls=%async_computation.3 | async-start | bytes 2621440 | tf_op jit(solution)/shard_map/all_to_all | solution.py:294
  138.6 14.4 %shard_map.73 = bf16[2,8,2,40,512]{4,3,2,1,0:T(8,128)(2,1)} custom-call(s32[40]{0:T(128)S(1)} %copy-done, f32[2,40,128]{2,1,0:T(8,128)S(1)} %get-tuple-element.22.cos_ref, f32[2,40,128]{2,1,0:T(8,128)S(1)} %get-tuple-element.23.sin_ref, bf16[2,8,2,40,512]{4,3,2,1,0:T(8,128)(2,1)} %bitcast.24, bf16[2,8,2,40,768]{4,3,2,1,0:T(8,128)(2,1)} %bitcast.16, ...), custom_call_target="tpu_custom_call" | custom-call | flops 167772160 | bytes 20971520 | tf_op jit(solution)/shard_map/pallas_call | solution.py:191
  153.0 4.1 %all-to-all-done.3.back_ref = bf16[16,2,40,512]{3,2,1,0:T(8,128)(2,1)S(1)} async-done(((bf16[16,2,40,512]{3,2,1,0:T(8,128)(2,1)}), bf16[16,2,40,512]{3,2,1,0:T(8,128)(2,1)S(1)}, u32[]{:S(2)}, u32[]{:S(2)}) %all-to-all-start.3) | async-done | bytes 1310752 | tf_op jit(solution)/shard_map/all_to_all | solution.py:294
  157.2 4.8 %all-to-all-start.2 = ((bf16[16,2,40,512]{3,2,1,0:T(8,128)(2,1)}), bf16[16,2,40,512]{3,2,1,0:T(8,128)(2,1)S(1)}, u32[]{:S(2)}, u32[]{:S(2)}) async-start(bf16[16,2,40,512]{3,2,1,0:T(8,128)(2,1)} %bitcast.25), calls=%async_computation.2 | async-start | bytes 2621440 | tf_op jit(solution)/shard_map/all_to_all | solution.py:294
  162.1 1.6 shard_map.75.refs_0_
  163.7 16.9 %all-to-all-done.2.back_ref = bf16[16,2,40,512]{3,2,1,0:T(8,128)(2,1)S(1)} async-done(((bf16[16,2,40,512]{3,2,1,0:T(8,128)(2,1)}), bf16[16,2,40,512]{3,2,1,0:T(8,128)(2,1)S(1)}, u32[]{:S(2)}, u32[]{:S(2)}) %all-to-all-start.2) | async-done | bytes 1310752 | tf_op jit(solution)/shard_map/all_to_all | solution.py:294
  180.6 1.6 shard_map.76
  (82 shorter events, 2.2 us)
Async XLA Ops:
  1.0 8.1 %collective-permute-start.2 = (bf16[512,256]{1,0:T(8,128)(2,1)S(1)}, bf16[512,256]{1,0:T(8,128)(2,1)S(1)}, u32[]{:S(2)}, u32[]{:S(2)}) collective-permute-start(bf16[512,256]{1,0:T(8,128)(2,1)S(1)} %constant_dynamic-slice_fusion), channel_id=1, source_target_pairs={{0,8},{8,0},{1,9},{9,1},{2,10},{10,2},{3,11},{11,3},{4,12},{12,4},... | collective-permute-start | bytes 786440 | tf_op jit(solution)/shard_map/over_pair_0/ppermute | solution.py:320
  2.9 10.6 %copy-start.24 = (bf16[1280]{0:T(1024)(128)(2,1)S(1)}, bf16[1280]{0:T(1024)(128)(2,1)}, u32[]{:S(2)}) copy-start(bf16[1280]{0:T(1024)(128)(2,1)} %param.9) | copy-start | bytes 7684
  2.9 15.6 %copy-start.2 = (bf16[2,256,8192]{2,1,0:T(8,128)(2,1)S(1)}, bf16[2,256,8192]{2,1,0:T(8,128)(2,1)}, u32[]{:S(2)}) copy-start(bf16[2,256,8192]{2,1,0:T(8,128)(2,1)} %param.7) | copy-start | bytes 25165828
  9.1 37.1 %copy-start.16 = (bf16[512,256]{1,0:T(8,128)(2,1)}, bf16[512,256]{1,0:T(8,128)(2,1)S(1)}, u32[]{:S(2)}) copy-start(bf16[512,256]{1,0:T(8,128)(2,1)S(1)} %collective-permute-done.2.refs_8_) | copy-start | bytes 786436
  9.1 9.5 %collective-permute-start.3 = (bf16[512,256]{1,0:T(8,128)(2,1)S(1)}, bf16[512,256]{1,0:T(8,128)(2,1)S(1)}, u32[]{:S(2)}, u32[]{:S(2)}) collective-permute-start(bf16[512,256]{1,0:T(8,128)(2,1)S(1)} %collective-permute-done.2.refs_8_), channel_id=1, source_target_pairs={{0,32},{16,48},{32,64},{48,80},{64,96},{80,112},{96,0},{112,16},{1... | collective-permute-start | bytes 786440 | tf_op jit(solution)/shard_map/from_below_0/ppermute | solution.py:325
  12.3 12.6 %collective-permute-start = (bf16[512,512]{1,0:T(8,128)(2,1)S(1)}, bf16[512,512]{1,0:T(8,128)(2,1)S(1)}, u32[]{:S(2)}, u32[]{:S(2)}) collective-permute-start(bf16[512,512]{1,0:T(8,128)(2,1)S(1)} %get-tuple-element.15), channel_id=1, source_target_pairs={{0,8},{8,0},{1,9},{9,1},{2,10},{10,2},{3,11},{11,3},{4,12},{12,4},... | collective-permute-start | bytes 1572872 | tf_op jit(solution)/shard_map/over_pair_1/ppermute | solution.py:320
  13.6 11.3 %collective-permute-start.4 = (bf16[512,256]{1,0:T(8,128)(2,1)S(1)}, bf16[512,256]{1,0:T(8,128)(2,1)S(1)}, u32[]{:S(2)}, u32[]{:S(2)}) collective-permute-start(bf16[512,256]{1,0:T(8,128)(2,1)S(1)} %collective-permute-done.2.refs_8_), channel_id=1, source_target_pairs={{32,0},{48,16},{64,32},{80,48},{96,64},{112,80},{0,96},{16,112},{3... | collective-permute-start | bytes 786440 | tf_op jit(solution)/shard_map/from_above_0/ppermute | solution.py:327
  18.6 27.7 %copy-start.17 = (bf16[512,256]{1,0:T(8,128)(2,1)}, bf16[512,256]{1,0:T(8,128)(2,1)S(1)}, u32[]{:S(2)}) copy-start(bf16[512,256]{1,0:T(8,128)(2,1)S(1)} %collective-permute-done.3.refs_9_) | copy-start | bytes 786436
  18.6 7.7 %collective-permute-start.5 = (bf16[512,256]{1,0:T(8,128)(2,1)S(1)}, bf16[512,256]{1,0:T(8,128)(2,1)S(1)}, u32[]{:S(2)}, u32[]{:S(2)}) collective-permute-start(bf16[512,256]{1,0:T(8,128)(2,1)S(1)} %collective-permute-done.3.refs_9_), channel_id=1, source_target_pairs={{0,32},{16,48},{32,64},{48,80},{64,96},{80,112},{96,0},{112,16},{1... | collective-permute-start | bytes 786440 | tf_op jit(solution)/shard_map/from_opposite_0/ppermute | solution.py:332
  24.9 22.9 %copy-start.6 = (bf16[512,512]{1,0:T(8,128)(2,1)}, bf16[512,512]{1,0:T(8,128)(2,1)S(1)}, u32[]{:S(2)}) copy-start(bf16[512,512]{1,0:T(8,128)(2,1)S(1)} %collective-permute-done.refs_0_) | copy-start | bytes 1572868
  24.9 21.9 %copy-start.18 = (bf16[512,256]{1,0:T(8,128)(2,1)}, bf16[512,256]{1,0:T(8,128)(2,1)S(1)}, u32[]{:S(2)}) copy-start(bf16[512,256]{1,0:T(8,128)(2,1)S(1)} %collective-permute-done.4.refs_10_) | copy-start | bytes 786436
  26.3 12.1 %collective-permute-start.7 = (bf16[512,512]{1,0:T(8,128)(2,1)S(1)}, bf16[512,512]{1,0:T(8,128)(2,1)S(1)}, u32[]{:S(2)}, u32[]{:S(2)}) collective-permute-start(bf16[512,512]{1,0:T(8,128)(2,1)S(1)} %collective-permute-done.refs_0_), channel_id=1, source_target_pairs={{32,0},{48,16},{64,32},{80,48},{96,64},{112,80},{0,96},{16,112},{3... | collective-permute-start | bytes 1572872 | tf_op jit(solution)/shard_map/from_above_1/ppermute | solution.py:327
  27.5 18.6 %collective-permute-start.1 = (bf16[512,512]{1,0:T(8,128)(2,1)S(1)}, bf16[512,512]{1,0:T(8,128)(2,1)S(1)}, u32[]{:S(2)}, u32[]{:S(2)}) collective-permute-start(bf16[512,512]{1,0:T(8,128)(2,1)S(1)} %get-tuple-element.10), channel_id=1, source_target_pairs={{0,8},{8,0},{1,9},{9,1},{2,10},{10,2},{3,11},{11,3},{4,12},{12,4},... | collective-permute-start | bytes 1572872 | tf_op jit(solution)/shard_map/over_pair_2/ppermute | solution.py:320
  28.7 17.4 %collective-permute-start.6 = (bf16[512,512]{1,0:T(8,128)(2,1)S(1)}, bf16[512,512]{1,0:T(8,128)(2,1)S(1)}, u32[]{:S(2)}, u32[]{:S(2)}) collective-permute-start(bf16[512,512]{1,0:T(8,128)(2,1)S(1)} %collective-permute-done.refs_0_), channel_id=1, source_target_pairs={{0,32},{16,48},{32,64},{48,80},{64,96},{80,112},{96,0},{112,16},{1... | collective-permute-start | bytes 1572872 | tf_op jit(solution)/shard_map/from_below_1/ppermute | solution.py:325
  38.4 10.1 %copy-start.7 = (bf16[512,512]{1,0:T(8,128)(2,1)}, bf16[512,512]{1,0:T(8,128)(2,1)S(1)}, u32[]{:S(2)}) copy-start(bf16[512,512]{1,0:T(8,128)(2,1)S(1)} %collective-permute-done.7.refs_2_) | copy-start | bytes 1572868
  38.4 10.6 %collective-permute-start.15 = (bf16[512,512]{1,0:T(8,128)(2,1)S(1)}, bf16[512,512]{1,0:T(8,128)(2,1)S(1)}, u32[]{:S(2)}, u32[]{:S(2)}) collective-permute-start(bf16[512,512]{1,0:T(8,128)(2,1)S(1)} %collective-permute-done.7.refs_2_), channel_id=1, source_target_pairs={{32,0},{48,16},{64,32},{80,48},{96,64},{112,80},{0,96},{16,112},{3... | collective-permute-start | bytes 1572872 | tf_op jit(solution)/shard_map/from_opposite_1/ppermute | solution.py:330
  40.6 17.5 %copy-start.25 = (s32[512]{0:T(512)S(1)}, s32[512]{0:T(512)}, u32[]{:S(2)}) copy-start(s32[512]{0:T(512)} %param.13) | copy-start | bytes 6148
  46.1 34.8 %copy-start.4 = (bf16[512,512]{1,0:T(8,128)(2,1)}, bf16[512,512]{1,0:T(8,128)(2,1)S(1)}, u32[]{:S(2)}) copy-start(bf16[512,512]{1,0:T(8,128)(2,1)S(1)} %collective-permute-done.1.refs_0_) | copy-start | bytes 1572868
  46.1 13.7 %copy-start.8 = (bf16[512,512]{1,0:T(8,128)(2,1)}, bf16[512,512]{1,0:T(8,128)(2,1)S(1)}, u32[]{:S(2)}) copy-start(bf16[512,512]{1,0:T(8,128)(2,1)S(1)} %collective-permute-done.6.refs_1_) | copy-start | bytes 1572868
  46.1 11.9 %collective-permute-start.8 = (bf16[512,512]{1,0:T(8,128)(2,1)S(1)}, bf16[512,512]{1,0:T(8,128)(2,1)S(1)}, u32[]{:S(2)}, u32[]{:S(2)}) collective-permute-start(bf16[512,512]{1,0:T(8,128)(2,1)S(1)} %collective-permute-done.1.refs_0_), channel_id=1, source_target_pairs={{0,32},{16,48},{32,64},{48,80},{64,96},{80,112},{96,0},{112,16},{1... | collective-permute-start | bytes 1572872 | tf_op jit(solution)/shard_map/from_below_2/ppermute | solution.py:325
  46.2 1.6 collective-permute-start.20
  46.3 1.9 %collective-permute-start.21 = (bf16[512,256]{1,0:T(8,128)(2,1)S(1)}, bf16[512,256]{1,0:T(8,128)(2,1)S(1)}, u32[]{:S(2)}, u32[]{:S(2)}) collective-permute-start(bf16[512,256]{1,0:T(8,128)(2,1)S(1)} %collective-permute-done.3.refs_9_), channel_id=1, source_target_pairs={{0,16},{16,0},{32,48},{48,32},{64,80},{80,64},{96,112},{112,96},{1... | collective-permute-start | bytes 786440 | tf_op jit(solution)/shard_map/from_twin_0/ppermute | solution.py:341
  46.8 1.8 collective-permute-start.22
  47.8 12.0 %collective-permute-start.16 = (bf16[512,512]{1,0:T(8,128)(2,1)S(1)}, bf16[512,512]{1,0:T(8,128)(2,1)}, u32[]{:S(2)}, u32[]{:S(2)}) collective-permute-start(bf16[512,512]{1,0:T(8,128)(2,1)S(1)} %collective-permute-done.refs_0_), channel_id=1, source_target_pairs={{0,16},{16,0},{32,48},{48,32},{64,80},{80,64},{96,112},{112,96},{1... | collective-permute-start | bytes 1572872 | tf_op jit(solution)/shard_map/from_twin_1/ppermute | solution.py:341
  48.2 11.6 %collective-permute-start.17 = (bf16[512,512]{1,0:T(8,128)(2,1)S(1)}, bf16[512,512]{1,0:T(8,128)(2,1)}, u32[]{:S(2)}, u32[]{:S(2)}) collective-permute-start(bf16[512,512]{1,0:T(8,128)(2,1)S(1)} %collective-permute-done.6.refs_1_), channel_id=1, source_target_pairs={{0,16},{16,0},{32,48},{48,32},{64,80},{80,64},{96,112},{112,96},{1... | collective-permute-start | bytes 1572872 | tf_op jit(solution)/shard_map/from_twin_1/ppermute | solution.py:341
  48.5 11.2 %collective-permute-start.18 = (bf16[512,512]{1,0:T(8,128)(2,1)S(1)}, bf16[512,512]{1,0:T(8,128)(2,1)}, u32[]{:S(2)}, u32[]{:S(2)}) collective-permute-start(bf16[512,512]{1,0:T(8,128)(2,1)S(1)} %collective-permute-done.7.refs_2_), channel_id=1, source_target_pairs={{0,16},{16,0},{32,48},{48,32},{64,80},{80,64},{96,112},{112,96},{1... | collective-permute-start | bytes 1572872 | tf_op jit(solution)/shard_map/from_twin_1/ppermute | solution.py:341
  49.2 10.6 %copy-start.9 = (bf16[512,512]{1,0:T(8,128)(2,1)}, bf16[512,512]{1,0:T(8,128)(2,1)S(1)}, u32[]{:S(2)}) copy-start(bf16[512,512]{1,0:T(8,128)(2,1)S(1)} %collective-permute-done.15.refs_3_) | copy-start | bytes 1572868
  49.2 10.6 %collective-permute-start.19 = (bf16[512,512]{1,0:T(8,128)(2,1)S(1)}, bf16[512,512]{1,0:T(8,128)(2,1)}, u32[]{:S(2)}, u32[]{:S(2)}) collective-permute-start(bf16[512,512]{1,0:T(8,128)(2,1)S(1)} %collective-permute-done.15.refs_3_), channel_id=1, source_target_pairs={{0,16},{16,0},{32,48},{48,32},{64,80},{80,64},{96,112},{112,96},{1... | collective-permute-start | bytes 1572872 | tf_op jit(solution)/shard_map/from_twin_1/ppermute | solution.py:341
  58.0 22.8 %copy-start.5 = (bf16[512,512]{1,0:T(8,128)(2,1)}, bf16[512,512]{1,0:T(8,128)(2,1)S(1)}, u32[]{:S(2)}) copy-start(bf16[512,512]{1,0:T(8,128)(2,1)S(1)} %collective-permute-done.8.refs_1_) | copy-start | bytes 1572868
  58.0 1.7 collective-permute-start.23
  71.3 35.3 %all-to-all-start.1 = ((bf16[16,2,40,768]{3,2,1,0:T(8,128)(2,1)}), bf16[16,2,40,768]{3,2,1,0:T(8,128)(2,1)S(1)}, u32[]{:S(2)}, u32[]{:S(2)}) async-start(bf16[16,2,40,768]{3,2,1,0:T(8,128)(2,1)} %project_1.1), calls=%async_computation.1 | async-start | bytes 3932160 | tf_op jit(solution)/shard_map/route_1/all_to_all | solution.py:294
  78.7 36.3 %copy-start = (s32[40]{0:T(128)S(1)}, s32[40]{0:T(128)}, u32[]{:S(2)}) copy-start(s32[40]{0:T(128)} %fill_ref.3) | copy-start | bytes 484
  78.7 13.5 %collective-permute-start.9 = (bf16[512,512]{1,0:T(8,128)(2,1)S(1)}, bf16[512,512]{1,0:T(8,128)(2,1)S(1)}, u32[]{:S(2)}, u32[]{:S(2)}) collective-permute-start(bf16[512,512]{1,0:T(8,128)(2,1)S(1)} %collective-permute-done.1.refs_0_), channel_id=1, source_target_pairs={{32,0},{48,16},{64,32},{80,48},{96,64},{112,80},{0,96},{16,112},{3... | collective-permute-start | bytes 1572872 | tf_op jit(solution)/shard_map/from_above_2/ppermute | solution.py:327
  78.8 14.7 %collective-permute-start.10 = (bf16[512,512]{1,0:T(8,128)(2,1)S(1)}, bf16[512,512]{1,0:T(8,128)(2,1)S(1)}, u32[]{:S(2)}, u32[]{:S(2)}) collective-permute-start(bf16[512,512]{1,0:T(8,128)(2,1)S(1)} %collective-permute-done.8.refs_1_), channel_id=1, source_target_pairs={{0,32},{16,48},{32,64},{48,80},{64,96},{80,112},{96,0},{112,16},{1... | collective-permute-start | bytes 1572872 | tf_op jit(solution)/shard_map/from_opposite_2/ppermute | solution.py:332
  80.8 12.7 %collective-permute-start.11 = (bf16[512,512]{1,0:T(8,128)(2,1)S(1)}, bf16[512,512]{1,0:T(8,128)(2,1)S(1)}, u32[]{:S(2)}, u32[]{:S(2)}) collective-permute-start(bf16[512,512]{1,0:T(8,128)(2,1)S(1)} %collective-permute-done.1.refs_0_), channel_id=1, source_target_pairs={{0,16},{16,0},{32,48},{48,32},{64,80},{80,64},{96,112},{112,96},{1... | collective-permute-start | bytes 1572872 | tf_op jit(solution)/shard_map/from_twin_2/ppermute | solution.py:341
  80.8 12.7 %collective-permute-start.12 = (bf16[512,512]{1,0:T(8,128)(2,1)S(1)}, bf16[512,512]{1,0:T(8,128)(2,1)S(1)}, u32[]{:S(2)}, u32[]{:S(2)}) collective-permute-start(bf16[512,512]{1,0:T(8,128)(2,1)S(1)} %collective-permute-done.8.refs_1_), channel_id=1, source_target_pairs={{0,16},{16,0},{32,48},{48,32},{64,80},{80,64},{96,112},{112,96},{1... | collective-permute-start | bytes 1572872 | tf_op jit(solution)/shard_map/from_twin_2/ppermute | solution.py:341
  92.2 3.2 %copy-start.10 = (bf16[512,512]{1,0:T(8,128)(2,1)}, bf16[512,512]{1,0:T(8,128)(2,1)S(1)}, u32[]{:S(2)}) copy-start(bf16[512,512]{1,0:T(8,128)(2,1)S(1)} %collective-permute-done.9.refs_2_) | copy-start | bytes 1572868
  92.2 1.9 %collective-permute-start.13 = (bf16[512,512]{1,0:T(8,128)(2,1)S(1)}, bf16[512,512]{1,0:T(8,128)(2,1)S(1)}, u32[]{:S(2)}, u32[]{:S(2)}) collective-permute-start(bf16[512,512]{1,0:T(8,128)(2,1)S(1)} %collective-permute-done.9.refs_2_), channel_id=1, source_target_pairs={{0,16},{16,0},{32,48},{48,32},{64,80},{80,64},{96,112},{112,96},{1... | collective-permute-start | bytes 1572872 | tf_op jit(solution)/shard_map/from_twin_2/ppermute | solution.py:341
  93.5 1.9 %copy-start.11 = (bf16[512,512]{1,0:T(8,128)(2,1)}, bf16[512,512]{1,0:T(8,128)(2,1)S(1)}, u32[]{:S(2)}) copy-start(bf16[512,512]{1,0:T(8,128)(2,1)S(1)} %collective-permute-done.10.refs_3_) | copy-start | bytes 1572868
  93.5 1.9 %collective-permute-start.14 = (bf16[512,512]{1,0:T(8,128)(2,1)S(1)}, bf16[512,512]{1,0:T(8,128)(2,1)S(1)}, u32[]{:S(2)}, u32[]{:S(2)}) collective-permute-start(bf16[512,512]{1,0:T(8,128)(2,1)S(1)} %collective-permute-done.10.refs_3_), channel_id=1, source_target_pairs={{0,16},{16,0},{32,48},{48,32},{64,80},{80,64},{96,112},{112,96},{1... | collective-permute-start | bytes 1572872 | tf_op jit(solution)/shard_map/from_twin_2/ppermute | solution.py:341
  93.5 1.9 %copy-start.12 = (bf16[512,512]{1,0:T(8,128)(2,1)}, bf16[512,512]{1,0:T(8,128)(2,1)S(1)}, u32[]{:S(2)}) copy-start(bf16[512,512]{1,0:T(8,128)(2,1)S(1)} %collective-permute-done.11.refs_4_) | copy-start | bytes 1572868
  93.5 1.9 %copy-start.13 = (bf16[512,512]{1,0:T(8,128)(2,1)}, bf16[512,512]{1,0:T(8,128)(2,1)S(1)}, u32[]{:S(2)}) copy-start(bf16[512,512]{1,0:T(8,128)(2,1)S(1)} %collective-permute-done.12.refs_5_) | copy-start | bytes 1572868
  94.1 1.3 copy-start.14
  106.5 8.9 %copy-start.1 = (bf16[16,2,40,768]{3,2,1,0:T(8,128)(2,1)}, bf16[16,2,40,768]{3,2,1,0:T(8,128)(2,1)S(1)}, u32[]{:S(2)}) copy-start(bf16[16,2,40,768]{3,2,1,0:T(8,128)(2,1)S(1)} %all-to-all-done.1) | copy-start | bytes 5898244
  106.5 27.2 %all-to-all-start = ((bf16[16,2,40,512]{3,2,1,0:T(8,128)(2,1)}), bf16[16,2,40,512]{3,2,1,0:T(8,128)(2,1)S(1)}, u32[]{:S(2)}, u32[]{:S(2)}) async-start(bf16[16,2,40,512]{3,2,1,0:T(8,128)(2,1)} %project_2.1), calls=%async_computation | async-start | bytes 2621440 | tf_op jit(solution)/shard_map/route_2/all_to_all | solution.py:294
  133.7 4.8 %copy-start.3 = (bf16[16,2,40,512]{3,2,1,0:T(8,128)(2,1)}, bf16[16,2,40,512]{3,2,1,0:T(8,128)(2,1)S(1)}, u32[]{:S(2)}) copy-start(bf16[16,2,40,512]{3,2,1,0:T(8,128)(2,1)S(1)} %all-to-all-done) | copy-start | bytes 3932164
  133.7 23.4 %all-to-all-start.3 = ((bf16[16,2,40,512]{3,2,1,0:T(8,128)(2,1)}), bf16[16,2,40,512]{3,2,1,0:T(8,128)(2,1)S(1)}, u32[]{:S(2)}, u32[]{:S(2)}) async-start(bf16[16,2,40,512]{3,2,1,0:T(8,128)(2,1)} %bitcast.23), calls=%async_computation.3 | async-start | bytes 2621440 | tf_op jit(solution)/shard_map/all_to_all | solution.py:294
  157.2 23.4 %all-to-all-start.2 = ((bf16[16,2,40,512]{3,2,1,0:T(8,128)(2,1)}), bf16[16,2,40,512]{3,2,1,0:T(8,128)(2,1)S(1)}, u32[]{:S(2)}, u32[]{:S(2)}) async-start(bf16[16,2,40,512]{3,2,1,0:T(8,128)(2,1)} %bitcast.25), calls=%async_computation.2 | async-start | bytes 2621440 | tf_op jit(solution)/shard_map/all_to_all | solution.py:294
  (6 other events, 5.4 us)

commit v7 on v5

--- a/solution.py
+++ b/solution.py
@@ -282,29 +282,40 @@
         with jax.named_scope("over_pair_%d" % number):
             slab = lax.dynamic_slice(matrix, (grp * depth, start), (depth, stop - start))
             crossed.append(lax.ppermute(after(slab, *crossed[-1:]), "pair", SWAP))
-    ring, ahead = [], []
-    for number, slab in enumerate(crossed):
-        slab = after(slab, partials[number], *ahead)
+    def neighbours(number, slab):
         with jax.named_scope("from_below_%d" % number):
             below = lax.ppermute(slab, "grp", up)
         with jax.named_scope("from_above_%d" % number):
-            above = lax.ppermute(slab, "grp", down)
+            return below, lax.ppermute(slab, "grp", down)
+
+    def further(number, piece, way):
         with jax.named_scope("from_opposite_%d" % number):
-            if number % 2:
-                opposite = lax.ppermute(above, "grp", down)
-            else:
-                opposite = lax.ppermute(below, "grp", up)
-        ahead = [below, above] if number else [below, above, opposite]
-        ring.append([slab, below, above, opposite])
-    partials[0] = after(partials[0], crossed[2], ring[1][3], ring[2][1])
+            return lax.ppermute(piece, "grp", way)
+
     arrived = []
-    for number, (span, four) in enumerate(zip(spans, ring)):
+
+    def finish(number, four):
         with jax.named_scope("from_twin_%d" % number):
             slabs = four + [lax.ppermute(piece, "grp", twin) for piece in four]
         with jax.named_scope("project_%d" % number):
             packed = project(places, flat, slabs, partials[number], pack, owners)
         with jax.named_scope("route_%d" % number):
-            arrived.append(exchange(packed).reshape(n_pair, n_tp, 2, rows, span[1] - span[0]))
+            start, stop = spans[number]
+            arrived.append(exchange(packed).reshape(n_pair, n_tp, 2, rows, stop - start))
+        return packed
+
+    slab0 = after(crossed[0], partials[0])
+    below0, above0 = neighbours(0, slab0)
+    opposite0 = further(0, below0, up)
+    slab1 = after(crossed[1], partials[1], below0, above0, opposite0)
+    below1, above1 = neighbours(1, slab1)
+    slab2 = after(crossed[2], below1, above1)
+    below2, above2 = neighbours(2, slab2)
+    packed = finish(0, [slab0, below0, above0, opposite0])
+    opposite1 = further(1, after(above1, packed), down)
+    opposite2 = further(2, below2, up)
+    finish(1, [slab1, below1, above1, after(opposite1, partials[2], arrived[0], below2)])
+    finish(2, [slab2, below2, above2, opposite2])
     out = None
     for (first, last), queries in zip(CHUNKS, arrived[1:]):
         heads = last - first

time: 178 us -> 178 us (level)
  waiting for transfers between devices: 56.4 us -> 52.1 us
  starting transfers between devices: 43.9 us -> 46.6 us
    ppermute x21, waiting for transfers between devices: 21.5 us -> 15.7 us  [the longest x3 6.48 us: neighbours(): below = lax.ppermute(slab, 'grp', up)]
  transfers between devices with their start and end apart: 29 -> 29, of which waited for: 18 -> 16; matrix products, arithmetic and copies ran while one was open for 11% -> 12% of each run, Pallas kernels for 30% -> 29%
where the time goes in v7:
time: 178 us; the launch traced here: 177 us
  Pallas kernels  53.7 us (30%)
  waiting for transfers between devices  52.1 us (29%)
  starting transfers between devices  46.6 us (26%)
  matrix products  17.6 us (10%)
  local copies, waits for them, and re-layouts  4.85 us (3%)
  other arithmetic  1.97 us (1%)
    all_to_all x5, waiting for transfers between devices, exchange(): lax.all_to_all(blocks, ('pair', 'tp'), split_axis=0, concat_axis=0, tiled...  33 us
    all_to_all x5, starting transfers between devices, exchange(): lax.all_to_all(blocks, ('pair', 'tp'), split_axis=0, concat_axis=0, tiled...  29.2 us
    pallas_call x2, Pallas kernels, attend(): pl.pallas_call(functools.partial(attention_kernel, heads), out_shape=pltp...  28.9 us
    pallas_call x3, Pallas kernels, project(): pl.pallas_call(functools.partial(project_kernel, owners, rows), out_shape...  21.6 us
    dot_general x3, matrix products, per_device(): jnp.dot(near, matrix[:, slice(*span)], preferred_element_type=jnp.float32)  17.6 us
    ppermute x3, waiting for transfers between devices, neighbours(): below = lax.ppermute(slab, 'grp', up)  6.48 us
    ppermute x3, starting transfers between devices, further(): return lax.ppermute(piece, 'grp', way)  5.04 us
    ppermute x3, waiting for transfers between devices, further(): return lax.ppermute(piece, 'grp', way)  4.93 us
  transfers between devices with their start and end apart: 29, of which 16 were waited for; matrix products, arithmetic and copies ran while one was open for 12% of the time, Pallas kernels for 29%

profile of v7, /device:TPU:4, one launch (start us, length us, event | category | flops | bytes accessed | tf_op | source)
XLA Modules:
  0.0 177.1 jit_solution(17457007084305351456)
XLA Ops:
  0.0 1.0 constant_dynamic-slice_fusion
  1.0 1.3 collective-permute-start
  2.2 0.7 slice_convert_fusion.2
  2.9 5.0 %fusion.19.refs_8_ = f32[512,256]{1,0:T(8,128)} fusion(bf16[4096,1280]{1,0:T(8,128)(2,1)} %param.8, bf16[512,8192]{1,0:T(8,128)(2,1)} %bitcast.14, s32[]{:T(128)S(6)} %select_n.54, f32[256]{0:T(256)S(1)} %slice_convert_fusion.2), kind=kOutput, calls=%fused_computation.11 | convolution fusion | flops 1073872896 | bytes 6816772 | tf_op jit(solution)/shard_map/dot_general | solution.py:275
  8.0 1.1 collective-permute-done.refs_0_
  9.1 1.9 %collective-permute-start.3 = (bf16[512,256]{1,0:T(8,128)(2,1)S(1)}, bf16[512,256]{1,0:T(8,128)(2,1)}, u32[]{:S(2)}, u32[]{:S(2)}) collective-permute-start(bf16[512,256]{1,0:T(8,128)(2,1)S(1)} %collective-permute-done.refs_0_), channel_id=1, source_target_pairs={{0,32},{16,48},{32,64},{48,80},{64,96},{80,112},{96,0},{112,16},{1... | collective-permute-start | bytes 786440 | tf_op jit(solution)/shard_map/from_below_0/ppermute | solution.py:287
  11.0 1.3 constant_dynamic-slice_fusion.1
  12.3 2.3 %collective-permute-start.4 = (bf16[512,256]{1,0:T(8,128)(2,1)S(1)}, bf16[512,256]{1,0:T(8,128)(2,1)}, u32[]{:S(2)}, u32[]{:S(2)}) collective-permute-start(bf16[512,256]{1,0:T(8,128)(2,1)S(1)} %collective-permute-done.refs_0_), channel_id=1, source_target_pairs={{32,0},{48,16},{64,32},{80,48},{96,64},{112,80},{0,96},{16,112},{3... | collective-permute-start | bytes 786440 | tf_op jit(solution)/shard_map/from_above_0/ppermute | solution.py:289
  14.6 1.2 collective-permute-start.1
  15.8 2.9 %collective-permute-done.3.refs_1_ = bf16[512,256]{1,0:T(8,128)(2,1)} collective-permute-done((bf16[512,256]{1,0:T(8,128)(2,1)S(1)}, bf16[512,256]{1,0:T(8,128)(2,1)}, u32[]{:S(2)}, u32[]{:S(2)}) %collective-permute-start.3) | collective-permute-done | bytes 262176 | tf_op jit(solution)/shard_map/from_below_0/ppermute | solution.py:287
  18.7 5.5 %fusion.9.refs_8_ = f32[512,512]{1,0:T(8,128)} fusion(bf16[4096,1280]{1,0:T(8,128)(2,1)} %param.8, bf16[512,8192]{1,0:T(8,128)(2,1)S(1)} %bitcast.19, s32[]{:T(128)S(6)} %select_n.54, f32[512]{0:T(512)S(1)} %get-tuple-element.22), kind=kOutput, calls=%fused_computation.9 | convolution fusion | flops 2147745792 | bytes 9439236 | tf_op jit(solution)/shard_map/dot_general | solution.py:275
  24.3 0.6 collective-permute-start.17
  24.9 1.8 collective-permute-done.5.refs_3_
  26.6 2.3 %collective-permute-done.1.refs_0_ = bf16[512,512]{1,0:T(8,128)(2,1)S(1)} collective-permute-done((bf16[512,512]{1,0:T(8,128)(2,1)S(1)}, bf16[512,512]{1,0:T(8,128)(2,1)S(1)}, u32[]{:S(2)}, u32[]{:S(2)}) %collective-permute-start.1) | collective-permute-done | bytes 524320 | tf_op jit(solution)/shard_map/over_pair_1/ppermute | solution.py:284
  28.9 1.9 %collective-permute-start.7 = (bf16[512,512]{1,0:T(8,128)(2,1)S(1)}, bf16[512,512]{1,0:T(8,128)(2,1)S(1)}, u32[]{:S(2)}, u32[]{:S(2)}) collective-permute-start(bf16[512,512]{1,0:T(8,128)(2,1)S(1)} %collective-permute-done.1.refs_0_), channel_id=1, source_target_pairs={{32,0},{48,16},{64,32},{80,48},{96,64},{112,80},{0,96},{16,112},{3... | collective-permute-start | bytes 1572872 | tf_op jit(solution)/shard_map/from_above_1/ppermute | solution.py:289
  31.0 1.2 collective-permute-start.2
  32.3 0.8 fusion.25.refs_9_
  33.1 0.8 collective-permute-done.18.refs_7_
  33.9 0.7 copy-done.17
  34.6 6.7 %project_0.1 = bf16[16,2,40,256]{3,2,1,0:T(8,128)(2,1)} custom-call(s32[8]{0:T(128)S(1)} %broadcast_add_fusion.places_ref, bf16[512,8192]{1,0:T(8,128)(2,1)} %bitcast.15, bf16[512,256]{1,0:T(8,128)(2,1)} %copy-done.15, bf16[512,256]{1,0:T(8,128)(2,1)} %collective-permute-done.3.refs_1_, bf16[512,256]{1,0:T(8,128)(2,1)} %collective-permute-done.4.refs_2_, ...), custom_call_target="tpu_custom_call" | custom-call | flops 1073741824 | bytes 6291456 | tf_op jit(solution)/shard_map/project_0/pallas_call | solution.py:67
  41.4 7.5 %all-to-all-start.1 = ((bf16[16,2,40,256]{3,2,1,0:T(8,128)(2,1)}), bf16[16,2,40,256]{3,2,1,0:T(8,128)(2,1)S(1)}, u32[]{:S(2)}, u32[]{:S(2)}) async-start(bf16[16,2,40,256]{3,2,1,0:T(8,128)(2,1)} %project_0.1), calls=%async_computation.1 | async-start | bytes 1310720 | tf_op jit(solution)/shard_map/route_0/all_to_all | solution.py:258
  48.8 3.2 %collective-permute-start.19 = (bf16[512,512]{1,0:T(8,128)(2,1)S(1)}, bf16[512,512]{1,0:T(8,128)(2,1)}, u32[]{:S(2)}, u32[]{:S(2)}) collective-permute-start(bf16[512,512]{1,0:T(8,128)(2,1)S(1)} %collective-permute-done.7.refs_2_), channel_id=1, source_target_pairs={{32,0},{48,16},{64,32},{80,48},{96,64},{112,80},{0,96},{16,112},{3... | collective-permute-start | bytes 1572872 | tf_op jit(solution)/shard_map/from_opposite_1/ppermute | solution.py:293
  52.1 7.0 %fusion.14.refs_8_ = f32[512,512]{1,0:T(8,128)} fusion(bf16[4096,1280]{1,0:T(8,128)(2,1)} %param.8, bf16[512,8192]{1,0:T(8,128)(2,1)} %bitcast.16, s32[]{:T(128)S(6)} %select_n.54, f32[512]{0:T(512)S(1)} %get-tuple-element.21), kind=kOutput, calls=%fused_computation.10 | convolution fusion | flops 2147745792 | bytes 9439236 | tf_op jit(solution)/shard_map/dot_general | solution.py:275
  59.2 0.5 collective-permute-start.22
  59.8 3.2 %collective-permute-done.19.refs_3_ = bf16[512,512]{1,0:T(8,128)(2,1)} collective-permute-done((bf16[512,512]{1,0:T(8,128)(2,1)S(1)}, bf16[512,512]{1,0:T(8,128)(2,1)}, u32[]{:S(2)}, u32[]{:S(2)}) %collective-permute-start.19) | collective-permute-done | bytes 524320 | tf_op jit(solution)/shard_map/from_opposite_1/ppermute | solution.py:293
  63.0 3.6 %collective-permute-done.8.refs_1_ = bf16[512,512]{1,0:T(8,128)(2,1)} collective-permute-done((bf16[512,512]{1,0:T(8,128)(2,1)S(1)}, bf16[512,512]{1,0:T(8,128)(2,1)}, u32[]{:S(2)}, u32[]{:S(2)}) %collective-permute-start.8) | collective-permute-done | bytes 524320 | tf_op jit(solution)/shard_map/from_below_2/ppermute | solution.py:287
  66.8 1.8 %collective-permute-start.10 = (bf16[512,512]{1,0:T(8,128)(2,1)}, bf16[512,512]{1,0:T(8,128)(2,1)}, u32[]{:S(2)}, u32[]{:S(2)}) collective-permute-start(bf16[512,512]{1,0:T(8,128)(2,1)} %collective-permute-done.8.refs_1_), channel_id=1, source_target_pairs={{0,32},{16,48},{32,64},{48,80},{64,96},{80,112},{96,0},{112,16},{1... | collective-permute-start | bytes 1572872 | tf_op jit(solution)/shard_map/from_opposite_2/ppermute | solution.py:293
  68.7 0.8 copy-done.12
  69.5 7.5 %project_1.1 = bf16[16,2,40,512]{3,2,1,0:T(8,128)(2,1)} custom-call(s32[8]{0:T(128)S(1)} %broadcast_add_fusion.places_ref, bf16[512,8192]{1,0:T(8,128)(2,1)} %bitcast.17, bf16[512,512]{1,0:T(8,128)(2,1)} %copy-done.5, bf16[512,512]{1,0:T(8,128)(2,1)} %copy-done.8, bf16[512,512]{1,0:T(8,128)(2,1)} %copy-done.7, ...), custom_call_target="tpu_custom_call" | custom-call | flops 2147483648 | bytes 8388608 | tf_op jit(solution)/shard_map/project_1/pallas_call | solution.py:67
  77.0 7.2 %all-to-all-start.3 = ((bf16[16,2,40,512]{3,2,1,0:T(8,128)(2,1)}), bf16[16,2,40,512]{3,2,1,0:T(8,128)(2,1)S(1)}, u32[]{:S(2)}, u32[]{:S(2)}) async-start(bf16[16,2,40,512]{3,2,1,0:T(8,128)(2,1)} %project_1.1), calls=%async_computation.3 | async-start | bytes 2621440 | tf_op jit(solution)/shard_map/route_1/all_to_all | solution.py:258
  84.3 0.5 collective-permute-start.12
  85.3 0.9 collective-permute-done.11.refs_4_
  86.2 1.0 collective-permute-done.12.refs_5_
  87.2 0.7 collective-permute-done.13.refs_6_
  87.9 0.7 collective-permute-done.14.refs_7_
  88.7 0.8 copy-done.14
  89.6 7.4 %project_2.1 = bf16[16,2,40,512]{3,2,1,0:T(8,128)(2,1)} custom-call(s32[8]{0:T(128)S(1)} %broadcast_add_fusion.places_ref, bf16[512,8192]{1,0:T(8,128)(2,1)} %bitcast.18, bf16[512,512]{1,0:T(8,128)(2,1)} %copy-done.6, bf16[512,512]{1,0:T(8,128)(2,1)} %collective-permute-done.8.refs_1_, bf16[512,512]{1,0:T(8,128)(2,1)} %collective-permute-done.9.refs_2_, ...), custom_call_target="tpu_custom_call" | custom-call | flops 2147483648 | bytes 8388608 | tf_op jit(solution)/shard_map/project_2/pallas_call | solution.py:67
  97.0 7.7 %all-to-all-done.3 = bf16[16,2,40,512]{3,2,1,0:T(8,128)(2,1)S(1)} async-done(((bf16[16,2,40,512]{3,2,1,0:T(8,128)(2,1)}), bf16[16,2,40,512]{3,2,1,0:T(8,128)(2,1)S(1)}, u32[]{:S(2)}, u32[]{:S(2)}) %all-to-all-start.3) | async-done | bytes 1310752 | tf_op jit(solution)/shard_map/route_1/all_to_all | solution.py:258
  104.7 4.8 %all-to-all-start = ((bf16[16,2,40,512]{3,2,1,0:T(8,128)(2,1)}), bf16[16,2,40,512]{3,2,1,0:T(8,128)(2,1)S(1)}, u32[]{:S(2)}, u32[]{:S(2)}) async-start(bf16[16,2,40,512]{3,2,1,0:T(8,128)(2,1)} %project_2.1), calls=%async_computation | async-start | bytes 2621440 | tf_op jit(solution)/shard_map/route_2/all_to_all | solution.py:258
  109.8 14.5 %shard_map.74 = bf16[2,8,2,40,512]{4,3,2,1,0:T(8,128)(2,1)} custom-call(s32[40]{0:T(128)S(1)} %copy-done, f32[2,40,128]{2,1,0:T(8,128)S(1)} %get-tuple-element.26.cos_ref, f32[2,40,128]{2,1,0:T(8,128)S(1)} %get-tuple-element.27.sin_ref, bf16[2,8,2,40,512]{4,3,2,1,0:T(8,128)(2,1)} %bitcast.24, bf16[2,8,2,40,256]{4,3,2,1,0:T(8,128)(2,1)} %bitcast.20, ...), custom_call_target="tpu_custom_call" | custom-call | flops 167772160 | bytes 20971520 | tf_op jit(solution)/shard_map/pallas_call | solution.py:174
  124.3 4.4 %all-to-all-done = bf16[16,2,40,512]{3,2,1,0:T(8,128)(2,1)S(1)} async-done(((bf16[16,2,40,512]{3,2,1,0:T(8,128)(2,1)}), bf16[16,2,40,512]{3,2,1,0:T(8,128)(2,1)S(1)}, u32[]{:S(2)}, u32[]{:S(2)}) %all-to-all-start) | async-done | bytes 1310752 | tf_op jit(solution)/shard_map/route_2/all_to_all | solution.py:258
  128.7 4.8 %all-to-all-start.4 = ((bf16[16,2,40,512]{3,2,1,0:T(8,128)(2,1)}), bf16[16,2,40,512]{3,2,1,0:T(8,128)(2,1)S(1)}, u32[]{:S(2)}, u32[]{:S(2)}) async-start(bf16[16,2,40,512]{3,2,1,0:T(8,128)(2,1)} %bitcast.27), calls=%async_computation.4 | async-start | bytes 2621440 | tf_op jit(solution)/shard_map/all_to_all | solution.py:258
  133.6 14.5 %shard_map.73 = bf16[2,8,2,40,512]{4,3,2,1,0:T(8,128)(2,1)} custom-call(s32[40]{0:T(128)S(1)} %copy-done, f32[2,40,128]{2,1,0:T(8,128)S(1)} %get-tuple-element.26.cos_ref, f32[2,40,128]{2,1,0:T(8,128)S(1)} %get-tuple-element.27.sin_ref, bf16[2,8,2,40,512]{4,3,2,1,0:T(8,128)(2,1)} %bitcast.25, bf16[2,8,2,40,256]{4,3,2,1,0:T(8,128)(2,1)} %bitcast.22, ...), custom_call_target="tpu_custom_call" | custom-call | flops 167772160 | bytes 20971520 | tf_op jit(solution)/shard_map/pallas_call | solution.py:174
  148.0 4.0 %all-to-all-done.4.back_ref = bf16[16,2,40,512]{3,2,1,0:T(8,128)(2,1)S(1)} async-done(((bf16[16,2,40,512]{3,2,1,0:T(8,128)(2,1)}), bf16[16,2,40,512]{3,2,1,0:T(8,128)(2,1)S(1)}, u32[]{:S(2)}, u32[]{:S(2)}) %all-to-all-start.4) | async-done | bytes 1310752 | tf_op jit(solution)/shard_map/all_to_all | solution.py:258
  152.0 4.8 %all-to-all-start.2 = ((bf16[16,2,40,512]{3,2,1,0:T(8,128)(2,1)}), bf16[16,2,40,512]{3,2,1,0:T(8,128)(2,1)S(1)}, u32[]{:S(2)}, u32[]{:S(2)}) async-start(bf16[16,2,40,512]{3,2,1,0:T(8,128)(2,1)} %bitcast.26), calls=%async_computation.2 | async-start | bytes 2621440 | tf_op jit(solution)/shard_map/all_to_all | solution.py:258
  157.0 1.6 shard_map.75.refs_0_
  158.5 17.0 %all-to-all-done.2.back_ref = bf16[16,2,40,512]{3,2,1,0:T(8,128)(2,1)S(1)} async-done(((bf16[16,2,40,512]{3,2,1,0:T(8,128)(2,1)}), bf16[16,2,40,512]{3,2,1,0:T(8,128)(2,1)S(1)}, u32[]{:S(2)}, u32[]{:S(2)}) %all-to-all-start.2) | async-done | bytes 1310752 | tf_op jit(solution)/shard_map/all_to_all | solution.py:258
  175.5 1.6 shard_map.76
  (73 shorter events, 1.9 us)
Async XLA Ops:
  1.0 8.1 %collective-permute-start = (bf16[512,256]{1,0:T(8,128)(2,1)S(1)}, bf16[512,256]{1,0:T(8,128)(2,1)S(1)}, u32[]{:S(2)}, u32[]{:S(2)}) collective-permute-start(bf16[512,256]{1,0:T(8,128)(2,1)S(1)} %constant_dynamic-slice_fusion), channel_id=1, source_target_pairs={{0,8},{8,0},{1,9},{9,1},{2,10},{10,2},{3,11},{11,3},{4,12},{12,4},... | collective-permute-start | bytes 786440 | tf_op jit(solution)/shard_map/over_pair_0/ppermute | solution.py:284
  2.9 9.4 %copy-start.18 = (bf16[1280]{0:T(1024)(128)(2,1)S(1)}, bf16[1280]{0:T(1024)(128)(2,1)}, u32[]{:S(2)}) copy-start(bf16[1280]{0:T(1024)(128)(2,1)} %param.9) | copy-start | bytes 7684
  2.9 15.7 %copy-start.1 = (bf16[2,256,8192]{2,1,0:T(8,128)(2,1)S(1)}, bf16[2,256,8192]{2,1,0:T(8,128)(2,1)}, u32[]{:S(2)}) copy-start(bf16[2,256,8192]{2,1,0:T(8,128)(2,1)} %param.7) | copy-start | bytes 25165828
  9.1 15.1 %copy-start.15 = (bf16[512,256]{1,0:T(8,128)(2,1)}, bf16[512,256]{1,0:T(8,128)(2,1)S(1)}, u32[]{:S(2)}) copy-start(bf16[512,256]{1,0:T(8,128)(2,1)S(1)} %collective-permute-done.refs_0_) | copy-start | bytes 786436
  9.1 9.6 %collective-permute-start.3 = (bf16[512,256]{1,0:T(8,128)(2,1)S(1)}, bf16[512,256]{1,0:T(8,128)(2,1)}, u32[]{:S(2)}, u32[]{:S(2)}) collective-permute-start(bf16[512,256]{1,0:T(8,128)(2,1)S(1)} %collective-permute-done.refs_0_), channel_id=1, source_target_pairs={{0,32},{16,48},{32,64},{48,80},{64,96},{80,112},{96,0},{112,16},{1... | collective-permute-start | bytes 786440 | tf_op jit(solution)/shard_map/from_below_0/ppermute | solution.py:287
  12.3 12.0 %collective-permute-start.4 = (bf16[512,256]{1,0:T(8,128)(2,1)S(1)}, bf16[512,256]{1,0:T(8,128)(2,1)}, u32[]{:S(2)}, u32[]{:S(2)}) collective-permute-start(bf16[512,256]{1,0:T(8,128)(2,1)S(1)} %collective-permute-done.refs_0_), channel_id=1, source_target_pairs={{32,0},{48,16},{64,32},{80,48},{96,64},{112,80},{0,96},{16,112},{3... | collective-permute-start | bytes 786440 | tf_op jit(solution)/shard_map/from_above_0/ppermute | solution.py:289
  14.6 16.4 %collective-permute-start.15 = (bf16[512,256]{1,0:T(8,128)(2,1)S(1)}, bf16[512,256]{1,0:T(8,128)(2,1)}, u32[]{:S(2)}, u32[]{:S(2)}) collective-permute-start(bf16[512,256]{1,0:T(8,128)(2,1)S(1)} %collective-permute-done.refs_0_), channel_id=1, source_target_pairs={{0,16},{16,0},{32,48},{48,32},{64,80},{80,64},{96,112},{112,96},{1... | collective-permute-start | bytes 786440 | tf_op jit(solution)/shard_map/from_twin_0/ppermute | solution.py:299
  14.6 14.3 %collective-permute-start.1 = (bf16[512,512]{1,0:T(8,128)(2,1)S(1)}, bf16[512,512]{1,0:T(8,128)(2,1)S(1)}, u32[]{:S(2)}, u32[]{:S(2)}) collective-permute-start(bf16[512,512]{1,0:T(8,128)(2,1)S(1)} %get-tuple-element.12), channel_id=1, source_target_pairs={{0,8},{8,0},{1,9},{9,1},{2,10},{10,2},{3,11},{11,3},{4,12},{12,4},... | collective-permute-start | bytes 1572872 | tf_op jit(solution)/shard_map/over_pair_1/ppermute | solution.py:284
  18.7 8.0 %collective-permute-start.5 = (bf16[512,256]{1,0:T(8,128)(2,1)}, bf16[512,256]{1,0:T(8,128)(2,1)S(1)}, u32[]{:S(2)}, u32[]{:S(2)}) collective-permute-start(bf16[512,256]{1,0:T(8,128)(2,1)} %collective-permute-done.3.refs_1_), channel_id=1, source_target_pairs={{0,32},{16,48},{32,64},{48,80},{64,96},{80,112},{96,0},{112,16},{1... | collective-permute-start | bytes 786440 | tf_op jit(solution)/shard_map/from_opposite_0/ppermute | solution.py:293
  18.7 13.5 %collective-permute-start.16 = (bf16[512,256]{1,0:T(8,128)(2,1)}, bf16[512,256]{1,0:T(8,128)(2,1)}, u32[]{:S(2)}, u32[]{:S(2)}) collective-permute-start(bf16[512,256]{1,0:T(8,128)(2,1)} %collective-permute-done.3.refs_1_), channel_id=1, source_target_pairs={{0,16},{16,0},{32,48},{48,32},{64,80},{80,64},{96,112},{112,96},{1... | collective-permute-start | bytes 786440 | tf_op jit(solution)/shard_map/from_twin_0/ppermute | solution.py:299
  18.7 13.5 %copy-start.19 = (s32[512]{0:T(512)S(1)}, s32[512]{0:T(512)}, u32[]{:S(2)}) copy-start(s32[512]{0:T(512)} %param.13) | copy-start | bytes 6148
  24.3 8.8 %collective-permute-start.17 = (bf16[512,256]{1,0:T(8,128)(2,1)}, bf16[512,256]{1,0:T(8,128)(2,1)}, u32[]{:S(2)}, u32[]{:S(2)}) collective-permute-start(bf16[512,256]{1,0:T(8,128)(2,1)} %collective-permute-done.4.refs_2_), channel_id=1, source_target_pairs={{0,16},{16,0},{32,48},{48,32},{64,80},{80,64},{96,112},{112,96},{1... | collective-permute-start | bytes 786440 | tf_op jit(solution)/shard_map/from_twin_0/ppermute | solution.py:299
  26.6 4.3 %copy-start.16 = (bf16[512,256]{1,0:T(8,128)(2,1)}, bf16[512,256]{1,0:T(8,128)(2,1)S(1)}, u32[]{:S(2)}) copy-start(bf16[512,256]{1,0:T(8,128)(2,1)S(1)} %collective-permute-done.5.refs_3_) | copy-start | bytes 786436
  28.9 30.2 %copy-start.5 = (bf16[512,512]{1,0:T(8,128)(2,1)}, bf16[512,512]{1,0:T(8,128)(2,1)S(1)}, u32[]{:S(2)}) copy-start(bf16[512,512]{1,0:T(8,128)(2,1)S(1)} %collective-permute-done.1.refs_0_) | copy-start | bytes 1572868
  28.9 19.9 %collective-permute-start.7 = (bf16[512,512]{1,0:T(8,128)(2,1)S(1)}, bf16[512,512]{1,0:T(8,128)(2,1)S(1)}, u32[]{:S(2)}, u32[]{:S(2)}) collective-permute-start(bf16[512,512]{1,0:T(8,128)(2,1)S(1)} %collective-permute-done.1.refs_0_), channel_id=1, source_target_pairs={{32,0},{48,16},{64,32},{80,48},{96,64},{112,80},{0,96},{16,112},{3... | collective-permute-start | bytes 1572872 | tf_op jit(solution)/shard_map/from_above_1/ppermute | solution.py:289
  30.9 21.2 %collective-permute-start.6 = (bf16[512,512]{1,0:T(8,128)(2,1)S(1)}, bf16[512,512]{1,0:T(8,128)(2,1)S(1)}, u32[]{:S(2)}, u32[]{:S(2)}) collective-permute-start(bf16[512,512]{1,0:T(8,128)(2,1)S(1)} %collective-permute-done.1.refs_0_), channel_id=1, source_target_pairs={{0,32},{16,48},{32,64},{48,80},{64,96},{80,112},{96,0},{112,16},{1... | collective-permute-start | bytes 1572872 | tf_op jit(solution)/shard_map/from_below_1/ppermute | solution.py:287
  31.0 21.1 %collective-permute-start.2 = (bf16[512,512]{1,0:T(8,128)(2,1)S(1)}, bf16[512,512]{1,0:T(8,128)(2,1)S(1)}, u32[]{:S(2)}, u32[]{:S(2)}) collective-permute-start(bf16[512,512]{1,0:T(8,128)(2,1)S(1)} %get-tuple-element.13), channel_id=1, source_target_pairs={{0,8},{8,0},{1,9},{9,1},{2,10},{10,2},{3,11},{11,3},{4,12},{12,4},... | collective-permute-start | bytes 1572872 | tf_op jit(solution)/shard_map/over_pair_2/ppermute | solution.py:284
  32.2 1.7 collective-permute-start.18
  41.4 18.4 %all-to-all-start.1 = ((bf16[16,2,40,256]{3,2,1,0:T(8,128)(2,1)}), bf16[16,2,40,256]{3,2,1,0:T(8,128)(2,1)S(1)}, u32[]{:S(2)}, u32[]{:S(2)}) async-start(bf16[16,2,40,256]{3,2,1,0:T(8,128)(2,1)} %project_0.1), calls=%async_computation.1 | async-start | bytes 1310720 | tf_op jit(solution)/shard_map/route_0/all_to_all | solution.py:258
  48.8 10.4 %copy-start.7 = (bf16[512,512]{1,0:T(8,128)(2,1)}, bf16[512,512]{1,0:T(8,128)(2,1)S(1)}, u32[]{:S(2)}) copy-start(bf16[512,512]{1,0:T(8,128)(2,1)S(1)} %collective-permute-done.7.refs_2_) | copy-start | bytes 1572868
  48.8 14.1 %collective-permute-start.19 = (bf16[512,512]{1,0:T(8,128)(2,1)S(1)}, bf16[512,512]{1,0:T(8,128)(2,1)}, u32[]{:S(2)}, u32[]{:S(2)}) collective-permute-start(bf16[512,512]{1,0:T(8,128)(2,1)S(1)} %collective-permute-done.7.refs_2_), channel_id=1, source_target_pairs={{32,0},{48,16},{64,32},{80,48},{96,64},{112,80},{0,96},{16,112},{3... | collective-permute-start | bytes 1572872 | tf_op jit(solution)/shard_map/from_opposite_1/ppermute | solution.py:293
  52.0 7.7 %copy-start.8 = (bf16[512,512]{1,0:T(8,128)(2,1)}, bf16[512,512]{1,0:T(8,128)(2,1)S(1)}, u32[]{:S(2)}) copy-start(bf16[512,512]{1,0:T(8,128)(2,1)S(1)} %collective-permute-done.6.refs_1_) | copy-start | bytes 1572868
  52.1 32.2 %copy-start.6 = (bf16[512,512]{1,0:T(8,128)(2,1)}, bf16[512,512]{1,0:T(8,128)(2,1)S(1)}, u32[]{:S(2)}) copy-start(bf16[512,512]{1,0:T(8,128)(2,1)S(1)} %collective-permute-done.2.refs_0_) | copy-start | bytes 1572868
  52.1 14.5 %collective-permute-start.8 = (bf16[512,512]{1,0:T(8,128)(2,1)S(1)}, bf16[512,512]{1,0:T(8,128)(2,1)}, u32[]{:S(2)}, u32[]{:S(2)}) collective-permute-start(bf16[512,512]{1,0:T(8,128)(2,1)S(1)} %collective-permute-done.2.refs_0_), channel_id=1, source_target_pairs={{0,32},{16,48},{32,64},{48,80},{64,96},{80,112},{96,0},{112,16},{1... | collective-permute-start | bytes 1572872 | tf_op jit(solution)/shard_map/from_below_2/ppermute | solution.py:287
  59.2 7.6 %collective-permute-start.20 = (bf16[512,512]{1,0:T(8,128)(2,1)S(1)}, bf16[512,512]{1,0:T(8,128)(2,1)S(1)}, u32[]{:S(2)}, u32[]{:S(2)}) collective-permute-start(bf16[512,512]{1,0:T(8,128)(2,1)S(1)} %collective-permute-done.1.refs_0_), channel_id=1, source_target_pairs={{0,16},{16,0},{32,48},{48,32},{64,80},{80,64},{96,112},{112,96},{1... | collective-permute-start | bytes 1572872 | tf_op jit(solution)/shard_map/from_twin_1/ppermute | solution.py:299
  59.2 9.4 %collective-permute-start.22 = (bf16[512,512]{1,0:T(8,128)(2,1)S(1)}, bf16[512,512]{1,0:T(8,128)(2,1)}, u32[]{:S(2)}, u32[]{:S(2)}) collective-permute-start(bf16[512,512]{1,0:T(8,128)(2,1)S(1)} %collective-permute-done.7.refs_2_), channel_id=1, source_target_pairs={{0,16},{16,0},{32,48},{48,32},{64,80},{80,64},{96,112},{112,96},{1... | collective-permute-start | bytes 1572872 | tf_op jit(solution)/shard_map/from_twin_1/ppermute | solution.py:299
  59.7 8.9 %collective-permute-start.21 = (bf16[512,512]{1,0:T(8,128)(2,1)S(1)}, bf16[512,512]{1,0:T(8,128)(2,1)}, u32[]{:S(2)}, u32[]{:S(2)}) collective-permute-start(bf16[512,512]{1,0:T(8,128)(2,1)S(1)} %collective-permute-done.6.refs_1_), channel_id=1, source_target_pairs={{0,16},{16,0},{32,48},{48,32},{64,80},{80,64},{96,112},{112,96},{1... | collective-permute-start | bytes 1572872 | tf_op jit(solution)/shard_map/from_twin_1/ppermute | solution.py:299
  59.8 17.2 %copy-start.2 = (bf16[16,2,40,256]{3,2,1,0:T(8,128)(2,1)}, bf16[16,2,40,256]{3,2,1,0:T(8,128)(2,1)S(1)}, u32[]{:S(2)}) copy-start(bf16[16,2,40,256]{3,2,1,0:T(8,128)(2,1)S(1)} %all-to-all-done.1) | copy-start | bytes 1966084
  66.6 2.1 %collective-permute-start.23 = (bf16[512,512]{1,0:T(8,128)(2,1)}, bf16[512,512]{1,0:T(8,128)(2,1)S(1)}, u32[]{:S(2)}, u32[]{:S(2)}) collective-permute-start(bf16[512,512]{1,0:T(8,128)(2,1)} %collective-permute-done.19.refs_3_), channel_id=1, source_target_pairs={{0,16},{16,0},{32,48},{48,32},{64,80},{80,64},{96,112},{112,96},{1... | collective-permute-start | bytes 1572872 | tf_op jit(solution)/shard_map/from_twin_1/ppermute | solution.py:299
  66.6 18.3 %collective-permute-start.9 = (bf16[512,512]{1,0:T(8,128)(2,1)S(1)}, bf16[512,512]{1,0:T(8,128)(2,1)}, u32[]{:S(2)}, u32[]{:S(2)}) collective-permute-start(bf16[512,512]{1,0:T(8,128)(2,1)S(1)} %collective-permute-done.2.refs_0_), channel_id=1, source_target_pairs={{32,0},{48,16},{64,32},{80,48},{96,64},{112,80},{0,96},{16,112},{3... | collective-permute-start | bytes 1572872 | tf_op jit(solution)/shard_map/from_above_2/ppermute | solution.py:289
  66.8 1.9 %copy-start.9 = (bf16[512,512]{1,0:T(8,128)(2,1)}, bf16[512,512]{1,0:T(8,128)(2,1)S(1)}, u32[]{:S(2)}) copy-start(bf16[512,512]{1,0:T(8,128)(2,1)S(1)} %collective-permute-done.20.refs_4_) | copy-start | bytes 1572868
  66.8 18.1 %collective-permute-start.10 = (bf16[512,512]{1,0:T(8,128)(2,1)}, bf16[512,512]{1,0:T(8,128)(2,1)}, u32[]{:S(2)}, u32[]{:S(2)}) collective-permute-start(bf16[512,512]{1,0:T(8,128)(2,1)} %collective-permute-done.8.refs_1_), channel_id=1, source_target_pairs={{0,32},{16,48},{32,64},{48,80},{64,96},{80,112},{96,0},{112,16},{1... | collective-permute-start | bytes 1572872 | tf_op jit(solution)/shard_map/from_opposite_2/ppermute | solution.py:293
  68.7 0.8 copy-start.12
  77.0 27.7 %all-to-all-start.3 = ((bf16[16,2,40,512]{3,2,1,0:T(8,128)(2,1)}), bf16[16,2,40,512]{3,2,1,0:T(8,128)(2,1)S(1)}, u32[]{:S(2)}, u32[]{:S(2)}) async-start(bf16[16,2,40,512]{3,2,1,0:T(8,128)(2,1)} %project_1.1), calls=%async_computation.3 | async-start | bytes 2621440 | tf_op jit(solution)/shard_map/route_1/all_to_all | solution.py:258
  84.2 25.3 %copy-start = (s32[40]{0:T(128)S(1)}, s32[40]{0:T(128)}, u32[]{:S(2)}) copy-start(s32[40]{0:T(128)} %fill_ref.3) | copy-start | bytes 484
  84.2 2.0 %collective-permute-start.11 = (bf16[512,512]{1,0:T(8,128)(2,1)S(1)}, bf16[512,512]{1,0:T(8,128)(2,1)S(1)}, u32[]{:S(2)}, u32[]{:S(2)}) collective-permute-start(bf16[512,512]{1,0:T(8,128)(2,1)S(1)} %collective-permute-done.2.refs_0_), channel_id=1, source_target_pairs={{0,16},{16,0},{32,48},{48,32},{64,80},{80,64},{96,112},{112,96},{1... | collective-permute-start | bytes 1572872 | tf_op jit(solution)/shard_map/from_twin_2/ppermute | solution.py:299
  84.3 2.9 %collective-permute-start.12 = (bf16[512,512]{1,0:T(8,128)(2,1)}, bf16[512,512]{1,0:T(8,128)(2,1)S(1)}, u32[]{:S(2)}, u32[]{:S(2)}) collective-permute-start(bf16[512,512]{1,0:T(8,128)(2,1)} %collective-permute-done.8.refs_1_), channel_id=1, source_target_pairs={{0,16},{16,0},{32,48},{48,32},{64,80},{80,64},{96,112},{112,96},{1... | collective-permute-start | bytes 1572872 | tf_op jit(solution)/shard_map/from_twin_2/ppermute | solution.py:299
  84.8 3.1 %collective-permute-start.13 = (bf16[512,512]{1,0:T(8,128)(2,1)}, bf16[512,512]{1,0:T(8,128)(2,1)S(1)}, u32[]{:S(2)}, u32[]{:S(2)}) collective-permute-start(bf16[512,512]{1,0:T(8,128)(2,1)} %collective-permute-done.9.refs_2_), channel_id=1, source_target_pairs={{0,16},{16,0},{32,48},{48,32},{64,80},{80,64},{96,112},{112,96},{1... | collective-permute-start | bytes 1572872 | tf_op jit(solution)/shard_map/from_twin_2/ppermute | solution.py:299
  84.9 3.8 %collective-permute-start.14 = (bf16[512,512]{1,0:T(8,128)(2,1)}, bf16[512,512]{1,0:T(8,128)(2,1)S(1)}, u32[]{:S(2)}, u32[]{:S(2)}) collective-permute-start(bf16[512,512]{1,0:T(8,128)(2,1)} %collective-permute-done.10.refs_3_), channel_id=1, source_target_pairs={{0,16},{16,0},{32,48},{48,32},{64,80},{80,64},{96,112},{112,96},{1... | collective-permute-start | bytes 1572872 | tf_op jit(solution)/shard_map/from_twin_2/ppermute | solution.py:299
  86.2 2.5 %copy-start.10 = (bf16[512,512]{1,0:T(8,128)(2,1)}, bf16[512,512]{1,0:T(8,128)(2,1)S(1)}, u32[]{:S(2)}) copy-start(bf16[512,512]{1,0:T(8,128)(2,1)S(1)} %collective-permute-done.11.refs_4_) | copy-start | bytes 1572868
  87.2 1.5 copy-start.11
  87.9 0.8 copy-start.13
  88.7 0.8 copy-start.14
  104.7 5.2 %copy-start.3 = (bf16[16,2,40,512]{3,2,1,0:T(8,128)(2,1)}, bf16[16,2,40,512]{3,2,1,0:T(8,128)(2,1)S(1)}, u32[]{:S(2)}) copy-start(bf16[16,2,40,512]{3,2,1,0:T(8,128)(2,1)S(1)} %all-to-all-done.3) | copy-start | bytes 3932164
  104.7 24.1 %all-to-all-start = ((bf16[16,2,40,512]{3,2,1,0:T(8,128)(2,1)}), bf16[16,2,40,512]{3,2,1,0:T(8,128)(2,1)S(1)}, u32[]{:S(2)}, u32[]{:S(2)}) async-start(bf16[16,2,40,512]{3,2,1,0:T(8,128)(2,1)} %project_2.1), calls=%async_computation | async-start | bytes 2621440 | tf_op jit(solution)/shard_map/route_2/all_to_all | solution.py:258
  128.7 4.8 %copy-start.4 = (bf16[16,2,40,512]{3,2,1,0:T(8,128)(2,1)}, bf16[16,2,40,512]{3,2,1,0:T(8,128)(2,1)S(1)}, u32[]{:S(2)}) copy-start(bf16[16,2,40,512]{3,2,1,0:T(8,128)(2,1)S(1)} %all-to-all-done) | copy-start | bytes 3932164
  128.7 23.3 %all-to-all-start.4 = ((bf16[16,2,40,512]{3,2,1,0:T(8,128)(2,1)}), bf16[16,2,40,512]{3,2,1,0:T(8,128)(2,1)S(1)}, u32[]{:S(2)}, u32[]{:S(2)}) async-start(bf16[16,2,40,512]{3,2,1,0:T(8,128)(2,1)} %bitcast.27), calls=%async_computation.4 | async-start | bytes 2621440 | tf_op jit(solution)/shard_map/all_to_all | solution.py:258
  152.0 23.5 %all-to-all-start.2 = ((bf16[16,2,40,512]{3,2,1,0:T(8,128)(2,1)}), bf16[16,2,40,512]{3,2,1,0:T(8,128)(2,1)S(1)}, u32[]{:S(2)}, u32[]{:S(2)}) async-start(bf16[16,2,40,512]{3,2,1,0:T(8,128)(2,1)} %bitcast.26), calls=%async_computation.2 | async-start | bytes 2621440 | tf_op jit(solution)/shard_map/all_to_all | solution.py:258
  (1 other events, 0.7 us)

commit v8 on v7

--- a/solution.py
+++ b/solution.py
@@ -294,14 +294,16 @@
 
     arrived = []
 
-    def finish(number, four):
+    def finish(number, four, *earlier):
         with jax.named_scope("from_twin_%d" % number):
             slabs = four + [lax.ppermute(piece, "grp", twin) for piece in four]
         with jax.named_scope("project_%d" % number):
             packed = project(places, flat, slabs, partials[number], pack, owners)
         with jax.named_scope("route_%d" % number):
             start, stop = spans[number]
-            arrived.append(exchange(packed).reshape(n_pair, n_tp, 2, rows, stop - start))
+            arrived.append(
+                exchange(after(packed, *earlier)).reshape(n_pair, n_tp, 2, rows, stop - start)
+            )
         return packed
 
     slab0 = after(crossed[0], partials[0])
@@ -311,7 +313,7 @@
     below1, above1 = neighbours(1, slab1)
     slab2 = after(crossed[2], below1, above1)
     below2, above2 = neighbours(2, slab2)
-    packed = finish(0, [slab0, below0, above0, opposite0])
+    packed = finish(0, [slab0, below0, above0, opposite0], below1, above1, slab2)
     opposite1 = further(1, after(above1, packed), down)
     opposite2 = further(2, below2, up)
     finish(1, [slab1, below1, above1, after(opposite1, partials[2], arrived[0], below2)])

time: 178 us -> 173 us (0.972)
  waiting for transfers between devices: 52.1 us -> 48.2 us
    ppermute x3, waiting for transfers between devices: 6.48 us -> 2.77 us  [neighbours(): below = lax.ppermute(slab, 'grp', up)]
    ppermute x3, waiting for transfers between devices: 4.93 us -> 2.09 us  [further(): return lax.ppermute(piece, 'grp', way)]
    ppermute x3, starting transfers between devices: 4.41 us -> 7.15 us  [neighbours(): return (below, lax.ppermute(slab, 'grp', down))]
    all_to_all x5, waiting for transfers between devices: 33 us -> 35.1 us  [exchange(): lax.all_to_all(blocks, ('pair', 'tp'), split_axis=0, concat_axis=0, tiled...]
    ppermute x3, starting transfers between devices: 5.04 us -> 3.14 us  [further(): return lax.ppermute(piece, 'grp', way)]
  transfers between devices with their start and end apart: 29 -> 29, of which waited for: 16 -> 16; matrix products, arithmetic and copies ran while one was open for 12% -> 12% of each run, Pallas kernels for 29% -> 30%
where the time goes in v8:
time: 173 us
  Pallas kernels  53.6 us (31%)
  waiting for transfers between devices  48.2 us (28%)
  starting transfers between devices  45.5 us (26%)
  matrix products  17.4 us (10%)
  local copies, waits for them, and re-layouts  5.57 us (3%)
  other arithmetic  1.97 us (1%)
    all_to_all x5, waiting for transfers between devices, exchange(): lax.all_to_all(blocks, ('pair', 'tp'), split_axis=0, concat_axis=0, tiled...  35.1 us
    pallas_call x2, Pallas kernels, attend(): pl.pallas_call(functools.partial(attention_kernel, heads), out_shape=pltp...  28.9 us
    all_to_all x5, starting transfers between devices, exchange(): lax.all_to_all(blocks, ('pair', 'tp'), split_axis=0, concat_axis=0, tiled...  27.7 us
    pallas_call x3, Pallas kernels, project(): pl.pallas_call(functools.partial(project_kernel, owners, rows), out_shape...  21.6 us
    dot_general x3, matrix products, per_device(): jnp.dot(near, matrix[:, slice(*span)], preferred_element_type=jnp.float32)  17.4 us
    ppermute x3, starting transfers between devices, neighbours(): return (below, lax.ppermute(slab, 'grp', down))  7.15 us
    ppermute x12, waiting for transfers between devices, finish(): slabs = four + [lax.ppermute(piece, 'grp', twin) for piece in four]  4.01 us
    ppermute x3, starting transfers between devices, per_device(): crossed.append(lax.ppermute(after(slab, *crossed[-1:]), 'pair', SWAP))  3.67 us
  transfers between devices with their start and end apart: 29, of which 16 were waited for; matrix products, arithmetic and copies ran while one was open for 12% of the time, Pallas kernels for 30%

profile of v8, /device:TPU:4, one launch (start us, length us, event | category | flops | bytes accessed | tf_op | source)
XLA Modules:
  0.0 172.5 jit_solution(15246342198722889655)
XLA Ops:
  0.0 1.0 constant_dynamic-slice_fusion
  1.0 1.3 collective-permute-start
  2.2 0.7 slice_convert_fusion.2
  2.9 5.0 %fusion.19.refs_8_ = f32[512,256]{1,0:T(8,128)} fusion(bf16[4096,1280]{1,0:T(8,128)(2,1)} %param.8, bf16[512,8192]{1,0:T(8,128)(2,1)} %bitcast.14, s32[]{:T(128)S(6)} %select_n.54, f32[256]{0:T(256)S(1)} %slice_convert_fusion.2), kind=kOutput, calls=%fused_computation.11 | convolution fusion | flops 1073872896 | bytes 6816772 | tf_op jit(solution)/shard_map/dot_general | solution.py:275
  8.0 1.1 collective-permute-done.refs_0_
  9.1 1.9 %collective-permute-start.3 = (bf16[512,256]{1,0:T(8,128)(2,1)S(1)}, bf16[512,256]{1,0:T(8,128)(2,1)S(1)}, u32[]{:S(2)}, u32[]{:S(2)}) collective-permute-start(bf16[512,256]{1,0:T(8,128)(2,1)S(1)} %collective-permute-done.refs_0_), channel_id=1, source_target_pairs={{0,32},{16,48},{32,64},{48,80},{64,96},{80,112},{96,0},{112,16},{1... | collective-permute-start | bytes 786440 | tf_op jit(solution)/shard_map/from_below_0/ppermute | solution.py:287
  11.0 1.3 constant_dynamic-slice_fusion.1
  12.3 2.3 %collective-permute-start.4 = (bf16[512,256]{1,0:T(8,128)(2,1)S(1)}, bf16[512,256]{1,0:T(8,128)(2,1)}, u32[]{:S(2)}, u32[]{:S(2)}) collective-permute-start(bf16[512,256]{1,0:T(8,128)(2,1)S(1)} %collective-permute-done.refs_0_), channel_id=1, source_target_pairs={{32,0},{48,16},{64,32},{80,48},{96,64},{112,80},{0,96},{16,112},{3... | collective-permute-start | bytes 786440 | tf_op jit(solution)/shard_map/from_above_0/ppermute | solution.py:289
  14.6 1.2 collective-permute-start.1
  15.8 2.8 %collective-permute-done.3.refs_1_ = bf16[512,256]{1,0:T(8,128)(2,1)S(1)} collective-permute-done((bf16[512,256]{1,0:T(8,128)(2,1)S(1)}, bf16[512,256]{1,0:T(8,128)(2,1)S(1)}, u32[]{:S(2)}, u32[]{:S(2)}) %collective-permute-start.3) | collective-permute-done | bytes 262176 | tf_op jit(solution)/shard_map/from_below_0/ppermute | solution.py:287
  18.6 5.6 %fusion.9.refs_8_ = f32[512,512]{1,0:T(8,128)} fusion(bf16[4096,1280]{1,0:T(8,128)(2,1)} %param.8, bf16[512,8192]{1,0:T(8,128)(2,1)S(1)} %bitcast.19, s32[]{:T(128)S(6)} %select_n.54, f32[512]{0:T(512)S(1)} %get-tuple-element.24), kind=kOutput, calls=%fused_computation.9 | convolution fusion | flops 2147745792 | bytes 9439236 | tf_op jit(solution)/shard_map/dot_general | solution.py:275
  24.8 1.5 collective-permute-done.5.refs_3_
  26.3 0.7 copy-done.17
  27.0 1.9 %collective-permute-done.1.refs_0_ = bf16[512,512]{1,0:T(8,128)(2,1)S(1)} collective-permute-done((bf16[512,512]{1,0:T(8,128)(2,1)S(1)}, bf16[512,512]{1,0:T(8,128)(2,1)S(1)}, u32[]{:S(2)}, u32[]{:S(2)}) %collective-permute-start.1) | collective-permute-done | bytes 524320 | tf_op jit(solution)/shard_map/over_pair_1/ppermute | solution.py:284
  28.9 1.9 %collective-permute-start.7 = (bf16[512,512]{1,0:T(8,128)(2,1)S(1)}, bf16[512,512]{1,0:T(8,128)(2,1)S(1)}, u32[]{:S(2)}, u32[]{:S(2)}) collective-permute-start(bf16[512,512]{1,0:T(8,128)(2,1)S(1)} %collective-permute-done.1.refs_0_), channel_id=1, source_target_pairs={{32,0},{48,16},{64,32},{80,48},{96,64},{112,80},{0,96},{16,112},{3... | collective-permute-start | bytes 1572872 | tf_op jit(solution)/shard_map/from_above_1/ppermute | solution.py:289
  31.0 1.2 collective-permute-start.2
  32.3 0.8 fusion.25.refs_9_
  33.1 0.8 collective-permute-done.18.refs_7_
  33.9 0.7 copy-done.18
  34.6 6.7 %project_0.1 = bf16[16,2,40,256]{3,2,1,0:T(8,128)(2,1)} custom-call(s32[8]{0:T(128)S(1)} %broadcast_add_fusion.places_ref, bf16[512,8192]{1,0:T(8,128)(2,1)} %bitcast.15, bf16[512,256]{1,0:T(8,128)(2,1)} %copy-done.15, bf16[512,256]{1,0:T(8,128)(2,1)} %copy-done.16, bf16[512,256]{1,0:T(8,128)(2,1)} %collective-permute-done.4.refs_2_, ...), custom_call_target="tpu_custom_call" | custom-call | flops 1073741824 | bytes 6291456 | tf_op jit(solution)/shard_map/project_0/pallas_call | solution.py:67
  41.4 1.1 collective-permute-done.7.refs_2_
  42.5 3.1 %collective-permute-start.19 = (bf16[512,512]{1,0:T(8,128)(2,1)S(1)}, bf16[512,512]{1,0:T(8,128)(2,1)}, u32[]{:S(2)}, u32[]{:S(2)}) collective-permute-start(bf16[512,512]{1,0:T(8,128)(2,1)S(1)} %collective-permute-done.7.refs_2_), channel_id=1, source_target_pairs={{32,0},{48,16},{64,32},{80,48},{96,64},{112,80},{0,96},{16,112},{3... | collective-permute-start | bytes 1572872 | tf_op jit(solution)/shard_map/from_opposite_1/ppermute | solution.py:293
  45.7 7.5 %all-to-all-start.1 = ((bf16[16,2,40,256]{3,2,1,0:T(8,128)(2,1)}), bf16[16,2,40,256]{3,2,1,0:T(8,128)(2,1)S(1)}, u32[]{:S(2)}, u32[]{:S(2)}) async-start(bf16[16,2,40,256]{3,2,1,0:T(8,128)(2,1)} %project_0.1), calls=%async_computation.1 | async-start | bytes 1310720 | tf_op jit(solution)/shard_map/route_0/all_to_all | solution.py:258
  53.2 6.8 %fusion.14.refs_8_ = f32[512,512]{1,0:T(8,128)} fusion(bf16[4096,1280]{1,0:T(8,128)(2,1)} %param.8, bf16[512,8192]{1,0:T(8,128)(2,1)} %bitcast.16, s32[]{:T(128)S(6)} %select_n.54, f32[512]{0:T(512)S(1)} %get-tuple-element.23), kind=kOutput, calls=%fused_computation.10 | convolution fusion | flops 2147745792 | bytes 9439236 | tf_op jit(solution)/shard_map/dot_general | solution.py:275
  60.0 0.5 collective-permute-start.22
  60.6 2.2 %all-to-all-done.1 = bf16[16,2,40,256]{3,2,1,0:T(8,128)(2,1)S(1)} async-done(((bf16[16,2,40,256]{3,2,1,0:T(8,128)(2,1)}), bf16[16,2,40,256]{3,2,1,0:T(8,128)(2,1)S(1)}, u32[]{:S(2)}, u32[]{:S(2)}) %all-to-all-start.1) | async-done | bytes 655392 | tf_op jit(solution)/shard_map/route_0/all_to_all | solution.py:258
  62.8 2.9 %collective-permute-start.9 = (bf16[512,512]{1,0:T(8,128)(2,1)S(1)}, bf16[512,512]{1,0:T(8,128)(2,1)}, u32[]{:S(2)}, u32[]{:S(2)}) collective-permute-start(bf16[512,512]{1,0:T(8,128)(2,1)S(1)} %collective-permute-done.2.refs_0_), channel_id=1, source_target_pairs={{32,0},{48,16},{64,32},{80,48},{96,64},{112,80},{0,96},{16,112},{3... | collective-permute-start | bytes 1572872 | tf_op jit(solution)/shard_map/from_above_2/ppermute | solution.py:289
  65.8 0.8 copy-done.12
  66.6 7.4 %project_1.1 = bf16[16,2,40,512]{3,2,1,0:T(8,128)(2,1)} custom-call(s32[8]{0:T(128)S(1)} %broadcast_add_fusion.places_ref, bf16[512,8192]{1,0:T(8,128)(2,1)} %bitcast.17, bf16[512,512]{1,0:T(8,128)(2,1)} %copy-done.5, bf16[512,512]{1,0:T(8,128)(2,1)} %copy-done.8, bf16[512,512]{1,0:T(8,128)(2,1)} %copy-done.7, ...), custom_call_target="tpu_custom_call" | custom-call | flops 2147483648 | bytes 8388608 | tf_op jit(solution)/shard_map/project_1/pallas_call | solution.py:67
  74.1 5.8 %all-to-all-start.3 = ((bf16[16,2,40,512]{3,2,1,0:T(8,128)(2,1)}), bf16[16,2,40,512]{3,2,1,0:T(8,128)(2,1)S(1)}, u32[]{:S(2)}, u32[]{:S(2)}) async-start(bf16[16,2,40,512]{3,2,1,0:T(8,128)(2,1)} %project_1.1), calls=%async_computation.3 | async-start | bytes 2621440 | tf_op jit(solution)/shard_map/route_1/all_to_all | solution.py:258
  80.0 0.5 collective-permute-start.12
  80.6 0.6 collective-permute-done.10.refs_3_
  81.1 0.7 collective-permute-done.11.refs_4_
  81.9 1.5 collective-permute-done.12.refs_5_
  83.6 0.7 collective-permute-done.14.refs_7_
  84.4 0.8 copy-done.14
  85.2 7.4 %project_2.1 = bf16[16,2,40,512]{3,2,1,0:T(8,128)(2,1)} custom-call(s32[8]{0:T(128)S(1)} %broadcast_add_fusion.places_ref, bf16[512,8192]{1,0:T(8,128)(2,1)} %bitcast.18, bf16[512,512]{1,0:T(8,128)(2,1)} %copy-done.6, bf16[512,512]{1,0:T(8,128)(2,1)} %copy-done.9, bf16[512,512]{1,0:T(8,128)(2,1)} %collective-permute-done.9.refs_2_, ...), custom_call_target="tpu_custom_call" | custom-call | flops 2147483648 | bytes 8388608 | tf_op jit(solution)/shard_map/project_2/pallas_call | solution.py:67
  92.7 7.6 %all-to-all-done.3 = bf16[16,2,40,512]{3,2,1,0:T(8,128)(2,1)S(1)} async-done(((bf16[16,2,40,512]{3,2,1,0:T(8,128)(2,1)}), bf16[16,2,40,512]{3,2,1,0:T(8,128)(2,1)S(1)}, u32[]{:S(2)}, u32[]{:S(2)}) %all-to-all-start.3) | async-done | bytes 1310752 | tf_op jit(solution)/shard_map/route_1/all_to_all | solution.py:258
  100.2 4.8 %all-to-all-start = ((bf16[16,2,40,512]{3,2,1,0:T(8,128)(2,1)}), bf16[16,2,40,512]{3,2,1,0:T(8,128)(2,1)S(1)}, u32[]{:S(2)}, u32[]{:S(2)}) async-start(bf16[16,2,40,512]{3,2,1,0:T(8,128)(2,1)} %project_2.1), calls=%async_computation | async-start | bytes 2621440 | tf_op jit(solution)/shard_map/route_2/all_to_all | solution.py:258
  105.4 14.4 %shard_map.74 = bf16[2,8,2,40,512]{4,3,2,1,0:T(8,128)(2,1)} custom-call(s32[40]{0:T(128)S(1)} %copy-done, f32[2,40,128]{2,1,0:T(8,128)S(1)} %get-tuple-element.28.cos_ref, f32[2,40,128]{2,1,0:T(8,128)S(1)} %get-tuple-element.29.sin_ref, bf16[2,8,2,40,512]{4,3,2,1,0:T(8,128)(2,1)} %bitcast.24, bf16[2,8,2,40,256]{4,3,2,1,0:T(8,128)(2,1)} %bitcast.20, ...), custom_call_target="tpu_custom_call" | custom-call | flops 167772160 | bytes 20971520 | tf_op jit(solution)/shard_map/pallas_call | solution.py:174
  119.9 4.4 %all-to-all-done = bf16[16,2,40,512]{3,2,1,0:T(8,128)(2,1)S(1)} async-done(((bf16[16,2,40,512]{3,2,1,0:T(8,128)(2,1)}), bf16[16,2,40,512]{3,2,1,0:T(8,128)(2,1)S(1)}, u32[]{:S(2)}, u32[]{:S(2)}) %all-to-all-start) | async-done | bytes 1310752 | tf_op jit(solution)/shard_map/route_2/all_to_all | solution.py:258
  124.2 4.8 %all-to-all-start.4 = ((bf16[16,2,40,512]{3,2,1,0:T(8,128)(2,1)}), bf16[16,2,40,512]{3,2,1,0:T(8,128)(2,1)S(1)}, u32[]{:S(2)}, u32[]{:S(2)}) async-start(bf16[16,2,40,512]{3,2,1,0:T(8,128)(2,1)} %bitcast.27), calls=%async_computation.4 | async-start | bytes 2621440 | tf_op jit(solution)/shard_map/all_to_all | solution.py:258
  129.0 14.5 %shard_map.73 = bf16[2,8,2,40,512]{4,3,2,1,0:T(8,128)(2,1)} custom-call(s32[40]{0:T(128)S(1)} %copy-done, f32[2,40,128]{2,1,0:T(8,128)S(1)} %get-tuple-element.28.cos_ref, f32[2,40,128]{2,1,0:T(8,128)S(1)} %get-tuple-element.29.sin_ref, bf16[2,8,2,40,512]{4,3,2,1,0:T(8,128)(2,1)} %bitcast.25, bf16[2,8,2,40,256]{4,3,2,1,0:T(8,128)(2,1)} %bitcast.22, ...), custom_call_target="tpu_custom_call" | custom-call | flops 167772160 | bytes 20971520 | tf_op jit(solution)/shard_map/pallas_call | solution.py:174
  143.5 4.0 %all-to-all-done.4.back_ref = bf16[16,2,40,512]{3,2,1,0:T(8,128)(2,1)S(1)} async-done(((bf16[16,2,40,512]{3,2,1,0:T(8,128)(2,1)}), bf16[16,2,40,512]{3,2,1,0:T(8,128)(2,1)S(1)}, u32[]{:S(2)}, u32[]{:S(2)}) %all-to-all-start.4) | async-done | bytes 1310752 | tf_op jit(solution)/shard_map/all_to_all | solution.py:258
  147.5 4.8 %all-to-all-start.2 = ((bf16[16,2,40,512]{3,2,1,0:T(8,128)(2,1)}), bf16[16,2,40,512]{3,2,1,0:T(8,128)(2,1)S(1)}, u32[]{:S(2)}, u32[]{:S(2)}) async-start(bf16[16,2,40,512]{3,2,1,0:T(8,128)(2,1)} %bitcast.26), calls=%async_computation.2 | async-start | bytes 2621440 | tf_op jit(solution)/shard_map/all_to_all | solution.py:258
  152.5 1.6 shard_map.75.refs_0_
  154.0 16.9 %all-to-all-done.2.back_ref = bf16[16,2,40,512]{3,2,1,0:T(8,128)(2,1)S(1)} async-done(((bf16[16,2,40,512]{3,2,1,0:T(8,128)(2,1)}), bf16[16,2,40,512]{3,2,1,0:T(8,128)(2,1)S(1)}, u32[]{:S(2)}, u32[]{:S(2)}) %all-to-all-start.2) | async-done | bytes 1310752 | tf_op jit(solution)/shard_map/all_to_all | solution.py:258
  171.0 1.6 shard_map.76
  (75 shorter events, 1.9 us)
Async XLA Ops:
  1.0 8.1 %collective-permute-start = (bf16[512,256]{1,0:T(8,128)(2,1)S(1)}, bf16[512,256]{1,0:T(8,128)(2,1)S(1)}, u32[]{:S(2)}, u32[]{:S(2)}) collective-permute-start(bf16[512,256]{1,0:T(8,128)(2,1)S(1)} %constant_dynamic-slice_fusion), channel_id=1, source_target_pairs={{0,8},{8,0},{1,9},{9,1},{2,10},{10,2},{3,11},{11,3},{4,12},{12,4},... | collective-permute-start | bytes 786440 | tf_op jit(solution)/shard_map/over_pair_0/ppermute | solution.py:284
  2.9 9.4 %copy-start.19 = (bf16[1280]{0:T(1024)(128)(2,1)S(1)}, bf16[1280]{0:T(1024)(128)(2,1)}, u32[]{:S(2)}) copy-start(bf16[1280]{0:T(1024)(128)(2,1)} %param.9) | copy-start | bytes 7684
  2.9 15.6 %copy-start.1 = (bf16[2,256,8192]{2,1,0:T(8,128)(2,1)S(1)}, bf16[2,256,8192]{2,1,0:T(8,128)(2,1)}, u32[]{:S(2)}) copy-start(bf16[2,256,8192]{2,1,0:T(8,128)(2,1)} %param.7) | copy-start | bytes 25165828
  9.1 15.1 %copy-start.15 = (bf16[512,256]{1,0:T(8,128)(2,1)}, bf16[512,256]{1,0:T(8,128)(2,1)S(1)}, u32[]{:S(2)}) copy-start(bf16[512,256]{1,0:T(8,128)(2,1)S(1)} %collective-permute-done.refs_0_) | copy-start | bytes 786436
  9.1 9.5 %collective-permute-start.3 = (bf16[512,256]{1,0:T(8,128)(2,1)S(1)}, bf16[512,256]{1,0:T(8,128)(2,1)S(1)}, u32[]{:S(2)}, u32[]{:S(2)}) collective-permute-start(bf16[512,256]{1,0:T(8,128)(2,1)S(1)} %collective-permute-done.refs_0_), channel_id=1, source_target_pairs={{0,32},{16,48},{32,64},{48,80},{64,96},{80,112},{96,0},{112,16},{1... | collective-permute-start | bytes 786440 | tf_op jit(solution)/shard_map/from_below_0/ppermute | solution.py:287
  12.3 12.0 %collective-permute-start.4 = (bf16[512,256]{1,0:T(8,128)(2,1)S(1)}, bf16[512,256]{1,0:T(8,128)(2,1)}, u32[]{:S(2)}, u32[]{:S(2)}) collective-permute-start(bf16[512,256]{1,0:T(8,128)(2,1)S(1)} %collective-permute-done.refs_0_), channel_id=1, source_target_pairs={{32,0},{48,16},{64,32},{80,48},{96,64},{112,80},{0,96},{16,112},{3... | collective-permute-start | bytes 786440 | tf_op jit(solution)/shard_map/from_above_0/ppermute | solution.py:289
  14.6 16.4 %collective-permute-start.15 = (bf16[512,256]{1,0:T(8,128)(2,1)S(1)}, bf16[512,256]{1,0:T(8,128)(2,1)}, u32[]{:S(2)}, u32[]{:S(2)}) collective-permute-start(bf16[512,256]{1,0:T(8,128)(2,1)S(1)} %collective-permute-done.refs_0_), channel_id=1, source_target_pairs={{0,16},{16,0},{32,48},{48,32},{64,80},{80,64},{96,112},{112,96},{1... | collective-permute-start | bytes 786440 | tf_op jit(solution)/shard_map/from_twin_0/ppermute | solution.py:299
  14.6 14.3 %collective-permute-start.1 = (bf16[512,512]{1,0:T(8,128)(2,1)S(1)}, bf16[512,512]{1,0:T(8,128)(2,1)S(1)}, u32[]{:S(2)}, u32[]{:S(2)}) collective-permute-start(bf16[512,512]{1,0:T(8,128)(2,1)S(1)} %get-tuple-element.13), channel_id=1, source_target_pairs={{0,8},{8,0},{1,9},{9,1},{2,10},{10,2},{3,11},{11,3},{4,12},{12,4},... | collective-permute-start | bytes 1572872 | tf_op jit(solution)/shard_map/over_pair_1/ppermute | solution.py:284
  18.6 5.6 %copy-start.16 = (bf16[512,256]{1,0:T(8,128)(2,1)}, bf16[512,256]{1,0:T(8,128)(2,1)S(1)}, u32[]{:S(2)}) copy-start(bf16[512,256]{1,0:T(8,128)(2,1)S(1)} %collective-permute-done.3.refs_1_) | copy-start | bytes 786436
  18.6 7.7 %collective-permute-start.5 = (bf16[512,256]{1,0:T(8,128)(2,1)S(1)}, bf16[512,256]{1,0:T(8,128)(2,1)S(1)}, u32[]{:S(2)}, u32[]{:S(2)}) collective-permute-start(bf16[512,256]{1,0:T(8,128)(2,1)S(1)} %collective-permute-done.3.refs_1_), channel_id=1, source_target_pairs={{0,32},{16,48},{32,64},{48,80},{64,96},{80,112},{96,0},{112,16},{1... | collective-permute-start | bytes 786440 | tf_op jit(solution)/shard_map/from_opposite_0/ppermute | solution.py:293
  18.6 13.6 %collective-permute-start.16 = (bf16[512,256]{1,0:T(8,128)(2,1)S(1)}, bf16[512,256]{1,0:T(8,128)(2,1)}, u32[]{:S(2)}, u32[]{:S(2)}) collective-permute-start(bf16[512,256]{1,0:T(8,128)(2,1)S(1)} %collective-permute-done.3.refs_1_), channel_id=1, source_target_pairs={{0,16},{16,0},{32,48},{48,32},{64,80},{80,64},{96,112},{112,96},{1... | collective-permute-start | bytes 786440 | tf_op jit(solution)/shard_map/from_twin_0/ppermute | solution.py:299
  18.6 13.6 %copy-start.20 = (s32[512]{0:T(512)S(1)}, s32[512]{0:T(512)}, u32[]{:S(2)}) copy-start(s32[512]{0:T(512)} %param.13) | copy-start | bytes 6148
  24.3 8.8 %collective-permute-start.17 = (bf16[512,256]{1,0:T(8,128)(2,1)}, bf16[512,256]{1,0:T(8,128)(2,1)}, u32[]{:S(2)}, u32[]{:S(2)}) collective-permute-start(bf16[512,256]{1,0:T(8,128)(2,1)} %collective-permute-done.4.refs_2_), channel_id=1, source_target_pairs={{0,16},{16,0},{32,48},{48,32},{64,80},{80,64},{96,112},{112,96},{1... | collective-permute-start | bytes 786440 | tf_op jit(solution)/shard_map/from_twin_0/ppermute | solution.py:299
  28.9 31.0 %copy-start.5 = (bf16[512,512]{1,0:T(8,128)(2,1)}, bf16[512,512]{1,0:T(8,128)(2,1)S(1)}, u32[]{:S(2)}) copy-start(bf16[512,512]{1,0:T(8,128)(2,1)S(1)} %collective-permute-done.1.refs_0_) | copy-start | bytes 1572868
  28.9 13.6 %collective-permute-start.7 = (bf16[512,512]{1,0:T(8,128)(2,1)S(1)}, bf16[512,512]{1,0:T(8,128)(2,1)S(1)}, u32[]{:S(2)}, u32[]{:S(2)}) collective-permute-start(bf16[512,512]{1,0:T(8,128)(2,1)S(1)} %collective-permute-done.1.refs_0_), channel_id=1, source_target_pairs={{32,0},{48,16},{64,32},{80,48},{96,64},{112,80},{0,96},{16,112},{3... | collective-permute-start | bytes 1572872 | tf_op jit(solution)/shard_map/from_above_1/ppermute | solution.py:289
  30.9 14.8 %collective-permute-start.6 = (bf16[512,512]{1,0:T(8,128)(2,1)S(1)}, bf16[512,512]{1,0:T(8,128)(2,1)S(1)}, u32[]{:S(2)}, u32[]{:S(2)}) collective-permute-start(bf16[512,512]{1,0:T(8,128)(2,1)S(1)} %collective-permute-done.1.refs_0_), channel_id=1, source_target_pairs={{0,32},{16,48},{32,64},{48,80},{64,96},{80,112},{96,0},{112,16},{1... | collective-permute-start | bytes 1572872 | tf_op jit(solution)/shard_map/from_below_1/ppermute | solution.py:287
  31.0 14.7 %collective-permute-start.2 = (bf16[512,512]{1,0:T(8,128)(2,1)S(1)}, bf16[512,512]{1,0:T(8,128)(2,1)S(1)}, u32[]{:S(2)}, u32[]{:S(2)}) collective-permute-start(bf16[512,512]{1,0:T(8,128)(2,1)S(1)} %get-tuple-element.14), channel_id=1, source_target_pairs={{0,8},{8,0},{1,9},{9,1},{2,10},{10,2},{3,11},{11,3},{4,12},{12,4},... | collective-permute-start | bytes 1572872 | tf_op jit(solution)/shard_map/over_pair_2/ppermute | solution.py:284
  32.2 1.7 %collective-permute-start.18 = (bf16[512,256]{1,0:T(8,128)(2,1)}, bf16[512,256]{1,0:T(8,128)(2,1)S(1)}, u32[]{:S(2)}, u32[]{:S(2)}) collective-permute-start(bf16[512,256]{1,0:T(8,128)(2,1)} %copy-done.17), channel_id=1, source_target_pairs={{0,16},{16,0},{32,48},{48,32},{64,80},{80,64},{96,112},{112,96},{1... | collective-permute-start | bytes 786440 | tf_op jit(solution)/shard_map/from_twin_0/ppermute | solution.py:299
  42.5 17.5 %copy-start.7 = (bf16[512,512]{1,0:T(8,128)(2,1)}, bf16[512,512]{1,0:T(8,128)(2,1)S(1)}, u32[]{:S(2)}) copy-start(bf16[512,512]{1,0:T(8,128)(2,1)S(1)} %collective-permute-done.7.refs_2_) | copy-start | bytes 1572868
  42.5 18.1 %collective-permute-start.19 = (bf16[512,512]{1,0:T(8,128)(2,1)S(1)}, bf16[512,512]{1,0:T(8,128)(2,1)}, u32[]{:S(2)}, u32[]{:S(2)}) collective-permute-start(bf16[512,512]{1,0:T(8,128)(2,1)S(1)} %collective-permute-done.7.refs_2_), channel_id=1, source_target_pairs={{32,0},{48,16},{64,32},{80,48},{96,64},{112,80},{0,96},{16,112},{3... | collective-permute-start | bytes 1572872 | tf_op jit(solution)/shard_map/from_opposite_1/ppermute | solution.py:293
  45.6 14.8 %copy-start.8 = (bf16[512,512]{1,0:T(8,128)(2,1)}, bf16[512,512]{1,0:T(8,128)(2,1)S(1)}, u32[]{:S(2)}) copy-start(bf16[512,512]{1,0:T(8,128)(2,1)S(1)} %collective-permute-done.6.refs_1_) | copy-start | bytes 1572868
  45.7 34.2 %copy-start.6 = (bf16[512,512]{1,0:T(8,128)(2,1)}, bf16[512,512]{1,0:T(8,128)(2,1)S(1)}, u32[]{:S(2)}) copy-start(bf16[512,512]{1,0:T(8,128)(2,1)S(1)} %collective-permute-done.2.refs_0_) | copy-start | bytes 1572868
  45.7 14.9 %collective-permute-start.8 = (bf16[512,512]{1,0:T(8,128)(2,1)S(1)}, bf16[512,512]{1,0:T(8,128)(2,1)S(1)}, u32[]{:S(2)}, u32[]{:S(2)}) collective-permute-start(bf16[512,512]{1,0:T(8,128)(2,1)S(1)} %collective-permute-done.2.refs_0_), channel_id=1, source_target_pairs={{0,32},{16,48},{32,64},{48,80},{64,96},{80,112},{96,0},{112,16},{1... | collective-permute-start | bytes 1572872 | tf_op jit(solution)/shard_map/from_below_2/ppermute | solution.py:287
  45.7 17.1 %all-to-all-start.1 = ((bf16[16,2,40,256]{3,2,1,0:T(8,128)(2,1)}), bf16[16,2,40,256]{3,2,1,0:T(8,128)(2,1)S(1)}, u32[]{:S(2)}, u32[]{:S(2)}) async-start(bf16[16,2,40,256]{3,2,1,0:T(8,128)(2,1)} %project_0.1), calls=%async_computation.1 | async-start | bytes 1310720 | tf_op jit(solution)/shard_map/route_0/all_to_all | solution.py:258
  60.0 5.8 %collective-permute-start.20 = (bf16[512,512]{1,0:T(8,128)(2,1)S(1)}, bf16[512,512]{1,0:T(8,128)(2,1)}, u32[]{:S(2)}, u32[]{:S(2)}) collective-permute-start(bf16[512,512]{1,0:T(8,128)(2,1)S(1)} %collective-permute-done.1.refs_0_), channel_id=1, source_target_pairs={{0,16},{16,0},{32,48},{48,32},{64,80},{80,64},{96,112},{112,96},{1... | collective-permute-start | bytes 1572872 | tf_op jit(solution)/shard_map/from_twin_1/ppermute | solution.py:299
  60.0 5.8 %collective-permute-start.22 = (bf16[512,512]{1,0:T(8,128)(2,1)S(1)}, bf16[512,512]{1,0:T(8,128)(2,1)}, u32[]{:S(2)}, u32[]{:S(2)}) collective-permute-start(bf16[512,512]{1,0:T(8,128)(2,1)S(1)} %collective-permute-done.7.refs_2_), channel_id=1, source_target_pairs={{0,16},{16,0},{32,48},{48,32},{64,80},{80,64},{96,112},{112,96},{1... | collective-permute-start | bytes 1572872 | tf_op jit(solution)/shard_map/from_twin_1/ppermute | solution.py:299
  60.5 5.3 %collective-permute-start.21 = (bf16[512,512]{1,0:T(8,128)(2,1)S(1)}, bf16[512,512]{1,0:T(8,128)(2,1)}, u32[]{:S(2)}, u32[]{:S(2)}) collective-permute-start(bf16[512,512]{1,0:T(8,128)(2,1)S(1)} %collective-permute-done.6.refs_1_), channel_id=1, source_target_pairs={{0,16},{16,0},{32,48},{48,32},{64,80},{80,64},{96,112},{112,96},{1... | collective-permute-start | bytes 1572872 | tf_op jit(solution)/shard_map/from_twin_1/ppermute | solution.py:299
  60.6 19.4 %copy-start.9 = (bf16[512,512]{1,0:T(8,128)(2,1)}, bf16[512,512]{1,0:T(8,128)(2,1)S(1)}, u32[]{:S(2)}) copy-start(bf16[512,512]{1,0:T(8,128)(2,1)S(1)} %collective-permute-done.8.refs_1_) | copy-start | bytes 1572868
  62.8 11.2 %copy-start.2 = (bf16[16,2,40,256]{3,2,1,0:T(8,128)(2,1)}, bf16[16,2,40,256]{3,2,1,0:T(8,128)(2,1)S(1)}, u32[]{:S(2)}) copy-start(bf16[16,2,40,256]{3,2,1,0:T(8,128)(2,1)S(1)} %all-to-all-done.1) | copy-start | bytes 1966084
  62.8 3.0 %collective-permute-start.23 = (bf16[512,512]{1,0:T(8,128)(2,1)}, bf16[512,512]{1,0:T(8,128)(2,1)S(1)}, u32[]{:S(2)}, u32[]{:S(2)}) collective-permute-start(bf16[512,512]{1,0:T(8,128)(2,1)} %collective-permute-done.19.refs_3_), channel_id=1, source_target_pairs={{0,16},{16,0},{32,48},{48,32},{64,80},{80,64},{96,112},{112,96},{1... | collective-permute-start | bytes 1572872 | tf_op jit(solution)/shard_map/from_twin_1/ppermute | solution.py:299
  62.8 17.6 %collective-permute-start.9 = (bf16[512,512]{1,0:T(8,128)(2,1)S(1)}, bf16[512,512]{1,0:T(8,128)(2,1)}, u32[]{:S(2)}, u32[]{:S(2)}) collective-permute-start(bf16[512,512]{1,0:T(8,128)(2,1)S(1)} %collective-permute-done.2.refs_0_), channel_id=1, source_target_pairs={{32,0},{48,16},{64,32},{80,48},{96,64},{112,80},{0,96},{16,112},{3... | collective-permute-start | bytes 1572872 | tf_op jit(solution)/shard_map/from_above_2/ppermute | solution.py:289
  65.8 15.4 %collective-permute-start.10 = (bf16[512,512]{1,0:T(8,128)(2,1)S(1)}, bf16[512,512]{1,0:T(8,128)(2,1)}, u32[]{:S(2)}, u32[]{:S(2)}) collective-permute-start(bf16[512,512]{1,0:T(8,128)(2,1)S(1)} %collective-permute-done.8.refs_1_), channel_id=1, source_target_pairs={{0,32},{16,48},{32,64},{48,80},{64,96},{80,112},{96,0},{112,16},{1... | collective-permute-start | bytes 1572872 | tf_op jit(solution)/shard_map/from_opposite_2/ppermute | solution.py:293
  65.8 0.8 copy-start.12
  74.1 26.2 %all-to-all-start.3 = ((bf16[16,2,40,512]{3,2,1,0:T(8,128)(2,1)}), bf16[16,2,40,512]{3,2,1,0:T(8,128)(2,1)S(1)}, u32[]{:S(2)}, u32[]{:S(2)}) async-start(bf16[16,2,40,512]{3,2,1,0:T(8,128)(2,1)} %project_1.1), calls=%async_computation.3 | async-start | bytes 2621440 | tf_op jit(solution)/shard_map/route_1/all_to_all | solution.py:258
  79.9 25.2 %copy-start = (s32[40]{0:T(128)S(1)}, s32[40]{0:T(128)}, u32[]{:S(2)}) copy-start(s32[40]{0:T(128)} %fill_ref.3) | copy-start | bytes 484
  79.9 2.0 %collective-permute-start.11 = (bf16[512,512]{1,0:T(8,128)(2,1)S(1)}, bf16[512,512]{1,0:T(8,128)(2,1)S(1)}, u32[]{:S(2)}, u32[]{:S(2)}) collective-permute-start(bf16[512,512]{1,0:T(8,128)(2,1)S(1)} %collective-permute-done.2.refs_0_), channel_id=1, source_target_pairs={{0,16},{16,0},{32,48},{48,32},{64,80},{80,64},{96,112},{112,96},{1... | collective-permute-start | bytes 1572872 | tf_op jit(solution)/shard_map/from_twin_2/ppermute | solution.py:299
  80.0 3.4 %collective-permute-start.12 = (bf16[512,512]{1,0:T(8,128)(2,1)S(1)}, bf16[512,512]{1,0:T(8,128)(2,1)S(1)}, u32[]{:S(2)}, u32[]{:S(2)}) collective-permute-start(bf16[512,512]{1,0:T(8,128)(2,1)S(1)} %collective-permute-done.8.refs_1_), channel_id=1, source_target_pairs={{0,16},{16,0},{32,48},{48,32},{64,80},{80,64},{96,112},{112,96},{1... | collective-permute-start | bytes 1572872 | tf_op jit(solution)/shard_map/from_twin_2/ppermute | solution.py:299
  80.5 3.1 %collective-permute-start.13 = (bf16[512,512]{1,0:T(8,128)(2,1)}, bf16[512,512]{1,0:T(8,128)(2,1)S(1)}, u32[]{:S(2)}, u32[]{:S(2)}) collective-permute-start(bf16[512,512]{1,0:T(8,128)(2,1)} %collective-permute-done.9.refs_2_), channel_id=1, source_target_pairs={{0,16},{16,0},{32,48},{48,32},{64,80},{80,64},{96,112},{112,96},{1... | collective-permute-start | bytes 1572872 | tf_op jit(solution)/shard_map/from_twin_2/ppermute | solution.py:299
  81.1 3.2 %collective-permute-start.14 = (bf16[512,512]{1,0:T(8,128)(2,1)}, bf16[512,512]{1,0:T(8,128)(2,1)S(1)}, u32[]{:S(2)}, u32[]{:S(2)}) collective-permute-start(bf16[512,512]{1,0:T(8,128)(2,1)} %collective-permute-done.10.refs_3_), channel_id=1, source_target_pairs={{0,16},{16,0},{32,48},{48,32},{64,80},{80,64},{96,112},{112,96},{1... | collective-permute-start | bytes 1572872 | tf_op jit(solution)/shard_map/from_twin_2/ppermute | solution.py:299
  81.9 2.5 %copy-start.10 = (bf16[512,512]{1,0:T(8,128)(2,1)}, bf16[512,512]{1,0:T(8,128)(2,1)S(1)}, u32[]{:S(2)}) copy-start(bf16[512,512]{1,0:T(8,128)(2,1)S(1)} %collective-permute-done.11.refs_4_) | copy-start | bytes 1572868
  83.4 1.0 copy-start.11
  83.6 0.8 copy-start.13
  84.4 0.8 copy-start.14
  100.2 5.2 %copy-start.3 = (bf16[16,2,40,512]{3,2,1,0:T(8,128)(2,1)}, bf16[16,2,40,512]{3,2,1,0:T(8,128)(2,1)S(1)}, u32[]{:S(2)}) copy-start(bf16[16,2,40,512]{3,2,1,0:T(8,128)(2,1)S(1)} %all-to-all-done.3) | copy-start | bytes 3932164
  100.2 24.0 %all-to-all-start = ((bf16[16,2,40,512]{3,2,1,0:T(8,128)(2,1)}), bf16[16,2,40,512]{3,2,1,0:T(8,128)(2,1)S(1)}, u32[]{:S(2)}, u32[]{:S(2)}) async-start(bf16[16,2,40,512]{3,2,1,0:T(8,128)(2,1)} %project_2.1), calls=%async_computation | async-start | bytes 2621440 | tf_op jit(solution)/shard_map/route_2/all_to_all | solution.py:258
  124.2 4.8 %copy-start.4 = (bf16[16,2,40,512]{3,2,1,0:T(8,128)(2,1)}, bf16[16,2,40,512]{3,2,1,0:T(8,128)(2,1)S(1)}, u32[]{:S(2)}) copy-start(bf16[16,2,40,512]{3,2,1,0:T(8,128)(2,1)S(1)} %all-to-all-done) | copy-start | bytes 3932164
  124.2 23.3 %all-to-all-start.4 = ((bf16[16,2,40,512]{3,2,1,0:T(8,128)(2,1)}), bf16[16,2,40,512]{3,2,1,0:T(8,128)(2,1)S(1)}, u32[]{:S(2)}, u32[]{:S(2)}) async-start(bf16[16,2,40,512]{3,2,1,0:T(8,128)(2,1)} %bitcast.27), calls=%async_computation.4 | async-start | bytes 2621440 | tf_op jit(solution)/shard_map/all_to_all | solution.py:258
  147.5 23.5 %all-to-all-start.2 = ((bf16[16,2,40,512]{3,2,1,0:T(8,128)(2,1)}), bf16[16,2,40,512]{3,2,1,0:T(8,128)(2,1)S(1)}, u32[]{:S(2)}, u32[]{:S(2)}) async-start(bf16[16,2,40,512]{3,2,1,0:T(8,128)(2,1)} %bitcast.26), calls=%async_computation.2 | async-start | bytes 2621440 | tf_op jit(solution)/shard_map/all_to_all | solution.py:258
  (2 other events, 1.4 us)

commit v9 on v8

--- a/solution.py
+++ b/solution.py
@@ -11,7 +11,7 @@
 SHARING = 8
 ROPE_BASE = 1000000.0
 SWAP = ((0, 1), (1, 0))
-CHUNKS = ((0, 4), (4, 8))
+CHUNKS = ((0, 3), (3, 8))
 ROW_BLOCK = 8
 NT = (((1,), (1,)), ((), ()))
 
@@ -202,14 +202,29 @@
     )
 
 
-def unpack_kernel(owners, rows, pick_ref, back_ref, *refs):
-    out_ref, gathered = refs[-2:]
+def unpack_kernel(owners, rows, at, pick_ref, back_ref, *refs):
+    out_ref, gathered, picked, written = refs[-4:]
+    step = pl.program_id(0)
     for owner in range(owners):
         gathered[pl.ds(owner * rows, rows), :] = back_ref[owner, 0].astype(jnp.float32)
-    picked = jnp.dot(
+    picked[step] = jnp.dot(
         pick_ref[...], gathered[...].astype(jnp.bfloat16), preferred_element_type=jnp.float32
-    )
-    out_ref[0] = picked.astype(jnp.bfloat16)
+    ).astype(jnp.bfloat16)
+    columns = pl.ds(at, picked.shape[2])
+    copies = [
+        pltpu.make_async_copy(picked.at[i], out_ref.at[i, :, columns], written.at[i])
+        for i in range(2)
+    ]
+
+    @pl.when(step == 0)
+    def _():
+        copies[0].start()
+
+    @pl.when(step == 1)
+    def _():
+        copies[1].start()
+        copies[0].wait()
+        copies[1].wait()
 
 
 def unpack(pick, back, at, columns, so_far):
@@ -217,17 +232,21 @@
     share, slots = pick.shape
     before = [] if so_far is None else [so_far]
     return pl.pallas_call(
-        functools.partial(unpack_kernel, owners, rows),
+        functools.partial(unpack_kernel, owners, rows, at),
         out_shape=jax.ShapeDtypeStruct((2, share, columns), jnp.bfloat16),
         grid=(2,),
         in_specs=[
             pl.BlockSpec((share, slots), lambda s: (0, 0)),
             pl.BlockSpec((owners, 1, rows, wide), lambda s: (0, s, 0, 0)),
         ] + [pl.BlockSpec(memory_space=pl.ANY)] * len(before),
-        out_specs=pl.BlockSpec((1, share, wide), lambda s: (s, 0, at)),
-        scratch_shapes=[pltpu.VMEM((slots, wide), jnp.float32)],
+        out_specs=pl.BlockSpec(memory_space=pl.ANY),
+        scratch_shapes=[
+            pltpu.VMEM((slots, wide), jnp.float32),
+            pltpu.VMEM((2, share, wide), jnp.bfloat16),
+            pltpu.SemaphoreType.DMA((2,)),
+        ],
         input_output_aliases={2: 0} if before else {},
-        compiler_params=pltpu.CompilerParams(vmem_limit_bytes=8 << 20),
+        compiler_params=pltpu.CompilerParams(vmem_limit_bytes=12 << 20),
         cost_estimate=pl.CostEstimate(
             flops=4 * share * slots * wide, transcendentals=0, bytes_accessed=4 * slots * wide
         ),
@@ -271,11 +290,10 @@
     places = places.astype(jnp.int32)
 
     near = lax.dynamic_slice_in_dim(flat, pair * half, half, 1)
-    partials = [
-        jnp.dot(near, matrix[:, slice(*span)], preferred_element_type=jnp.float32)
-        + offset[slice(*span)].astype(jnp.float32)
-        for span in spans
-    ]
+    def against_own(span, bias):
+        columns = slice(*span)
+        product = jnp.dot(near, matrix[:, columns], preferred_element_type=jnp.float32)
+        return product + bias[columns].astype(jnp.float32)
 
     crossed = []
     for number, (start, stop) in enumerate(spans):
@@ -306,17 +324,21 @@
             )
         return packed
 
-    slab0 = after(crossed[0], partials[0])
+    longest = against_own(spans[2], offset)
+    slab0 = after(crossed[0], longest)
     below0, above0 = neighbours(0, slab0)
+    later = after(offset, below0)
+    partials = [against_own(spans[0], later), against_own(spans[1], later)]
+    partials.append(longest)
     opposite0 = further(0, below0, up)
-    slab1 = after(crossed[1], partials[1], below0, above0, opposite0)
+    slab1 = after(crossed[1], partials[0], partials[1], below0, above0, opposite0)
     below1, above1 = neighbours(1, slab1)
-    slab2 = after(crossed[2], below1, above1)
+    packed = finish(0, [slab0, below0, above0, opposite0], below1, above1)
+    slab2 = after(crossed[2], below1, above1, packed, partials[2])
     below2, above2 = neighbours(2, slab2)
-    packed = finish(0, [slab0, below0, above0, opposite0], below1, above1, slab2)
     opposite1 = further(1, after(above1, packed), down)
-    opposite2 = further(2, below2, up)
-    finish(1, [slab1, below1, above1, after(opposite1, partials[2], arrived[0], below2)])
+    opposite2 = further(2, after(below2, arrived[0]), up)
+    finish(1, [slab1, below1, above1, after(opposite1, below2)])
     finish(2, [slab2, below2, above2, opposite2])
     out = None
     for (first, last), queries in zip(CHUNKS, arrived[1:]):
@@ -325,7 +347,7 @@
             fill, cosine, sine, queries, arrived[0], cached_keys, cached_values, heads
         )
         back = exchange(attended.reshape(owners, 2, rows, heads * HEAD))
-        out = unpack(pick, back, first // heads, SHARING * HEAD, out)
+        out = unpack(pick, back, first * HEAD, SHARING * HEAD, out)
     return out
 
 

time: 173 us -> 190 us (1.098)
  starting transfers between devices: 45.5 us -> 51.3 us
  Pallas kernels: 53.6 us -> 56.9 us
  local copies, waits for them, and re-layouts: 5.57 us -> 8.32 us
  waiting for transfers between devices: 48.2 us -> 50.5 us
    all_to_all x5, starting transfers between devices: 27.7 us -> 35 us  [exchange(): lax.all_to_all(blocks, ('pair', 'tp'), split_axis=0, concat_axis=0, tiled...]
    ppermute x3, waiting for transfers between devices: 3.03 us -> 0.01 us  [per_device(): crossed.append(lax.ppermute(after(slab, *crossed[-1:]), 'pair', SWAP))]
    pallas_call x3, Pallas kernels: 21.6 us -> 24.3 us  [project(): pl.pallas_call(functools.partial(project_kernel, owners, rows), out_shape...]
    ppermute x12, waiting for transfers between devices: 4.01 us -> 6.52 us  [finish(): slabs = four + [lax.ppermute(piece, 'grp', twin) for piece in four]]
    ppermute x3, waiting for transfers between devices: 2.77 us -> 5.13 us  [neighbours(): below = lax.ppermute(slab, 'grp', up)]
    unnamed x42 -> x48, local copies, waits for them, and re-layouts: 3.17 us -> 5.01 us
  transfers between devices with their start and end apart: 29 -> 29, of which waited for: 16 -> 12; matrix products, arithmetic and copies ran while one was open for 12% -> 13% of each run, Pallas kernels for 30% -> 29%
where the time goes in v9:
time: 190 us; the launch traced here: 189 us
  Pallas kernels  56.9 us (30%)
  starting transfers between devices  51.3 us (27%)
  waiting for transfers between devices  50.5 us (27%)
  matrix products  18.5 us (10%)
  local copies, waits for them, and re-layouts  8.32 us (4%)
  other arithmetic  3.34 us (2%)
    all_to_all x5, waiting for transfers between devices, exchange(): lax.all_to_all(blocks, ('pair', 'tp'), split_axis=0, concat_axis=0, tiled...  36.1 us
    all_to_all x5, starting transfers between devices, exchange(): lax.all_to_all(blocks, ('pair', 'tp'), split_axis=0, concat_axis=0, tiled...  35 us
    pallas_call x2, Pallas kernels, attend(): pl.pallas_call(functools.partial(attention_kernel, heads), out_shape=pltp...  29.2 us
    pallas_call x3, Pallas kernels, project(): pl.pallas_call(functools.partial(project_kernel, owners, rows), out_shape...  24.3 us
    dot_general x3, matrix products, against_own(): jnp.dot(near, matrix[:, columns], preferred_element_type=jnp.float32)  18.5 us
    ppermute x12, waiting for transfers between devices, finish(): slabs = four + [lax.ppermute(piece, 'grp', twin) for piece in four]  6.52 us
    ppermute x3, starting transfers between devices, neighbours(): return (below, lax.ppermute(slab, 'grp', down))  5.53 us
    ppermute x3, waiting for transfers between devices, neighbours(): below = lax.ppermute(slab, 'grp', up)  5.13 us
  transfers between devices with their start and end apart: 29, of which 12 were waited for; matrix products, arithmetic and copies ran while one was open for 13% of the time, Pallas kernels for 29%

profile of v9, /device:TPU:4, one launch (start us, length us, event | category | flops | bytes accessed | tf_op | source)
XLA Modules:
  0.0 189.3 jit_solution(13564037265070966233)
XLA Ops:
  0.0 1.0 constant_dynamic-slice_fusion
  1.0 1.3 collective-permute-start
  2.2 0.7 slice_convert_fusion
  2.9 8.3 %fusion.9.refs_8_ = f32[512,640]{1,0:T(8,128)} fusion(bf16[4096,1280]{1,0:T(8,128)(2,1)} %param.8, bf16[512,8192]{1,0:T(8,128)(2,1)} %bitcast.14, s32[]{:T(128)S(6)} %select_n.54, f32[640]{0:T(1024)S(1)} %slice_convert_fusion), kind=kOutput, calls=%fused_computation.9 | convolution fusion | flops 2684682240 | bytes 10750468 | tf_op jit(solution)/shard_map/dot_general | solution.py:295
  11.2 1.9 %collective-permute-start.3 = (bf16[512,256]{1,0:T(8,128)(2,1)S(1)}, bf16[512,256]{1,0:T(8,128)(2,1)S(1)}, u32[]{:S(2)}, u32[]{:S(2)}) collective-permute-start(bf16[512,256]{1,0:T(8,128)(2,1)S(1)} %collective-permute-done.refs_0_), channel_id=1, source_target_pairs={{0,32},{16,48},{32,64},{48,80},{64,96},{80,112},{96,0},{112,16},{1... | collective-permute-start | bytes 786440 | tf_op jit(solution)/shard_map/from_below_0/ppermute | solution.py:305
  13.2 1.0 constant_dynamic-slice_fusion.2
  14.3 1.2 constant_dynamic-slice_fusion.1
  15.4 2.3 %collective-permute-start.4 = (bf16[512,256]{1,0:T(8,128)(2,1)S(1)}, bf16[512,256]{1,0:T(8,128)(2,1)S(1)}, u32[]{:S(2)}, u32[]{:S(2)}) collective-permute-start(bf16[512,256]{1,0:T(8,128)(2,1)S(1)} %collective-permute-done.refs_0_), channel_id=1, source_target_pairs={{32,0},{48,16},{64,32},{80,48},{96,64},{112,80},{0,96},{16,112},{3... | collective-permute-start | bytes 786440 | tf_op jit(solution)/shard_map/from_above_0/ppermute | solution.py:307
  17.7 0.8 collective-permute-start.1
  18.5 2.7 %collective-permute-done.3.refs_1_ = bf16[512,256]{1,0:T(8,128)(2,1)S(1)} collective-permute-done((bf16[512,256]{1,0:T(8,128)(2,1)S(1)}, bf16[512,256]{1,0:T(8,128)(2,1)S(1)}, u32[]{:S(2)}, u32[]{:S(2)}) %collective-permute-start.3) | collective-permute-done | bytes 262176 | tf_op jit(solution)/shard_map/from_below_0/ppermute | solution.py:305
  21.3 0.7 slice_convert_fusion.2
  22.0 0.7 slice_convert_fusion.1
  22.7 6.6 %fusion.14.refs_8_ = f32[512,384]{1,0:T(8,128)} fusion(bf16[4096,1280]{1,0:T(8,128)(2,1)} %param.8, bf16[512,8192]{1,0:T(8,128)(2,1)} %bitcast.15, s32[]{:T(128)S(6)} %select_n.54, f32[384]{0:T(512)S(1)} %slice_convert_fusion.1), kind=kOutput, calls=%fused_computation.10 | convolution fusion | flops 1610809344 | bytes 8128004 | tf_op jit(solution)/shard_map/dot_general | solution.py:295
  29.3 0.9 collective-permute-start.2
  30.2 3.7 %fusion.19.refs_8_ = f32[512,256]{1,0:T(8,128)} fusion(bf16[4096,1280]{1,0:T(8,128)(2,1)} %param.8, bf16[512,8192]{1,0:T(8,128)(2,1)S(1)} %bitcast.19, s32[]{:T(128)S(6)} %select_n.54, f32[256]{0:T(256)S(1)} %slice_convert_fusion.2), kind=kOutput, calls=%fused_computation.11 | convolution fusion | flops 1073872896 | bytes 6816772 | tf_op jit(solution)/shard_map/dot_general | solution.py:295
  33.8 0.7 collective-permute-start.10
  34.5 3.1 %collective-permute-start.7 = (bf16[512,384]{1,0:T(8,128)(2,1)S(1)}, bf16[512,384]{1,0:T(8,128)(2,1)}, u32[]{:S(2)}, u32[]{:S(2)}) collective-permute-start(bf16[512,384]{1,0:T(8,128)(2,1)S(1)} %collective-permute-done.1.refs_0_), channel_id=1, source_target_pairs={{32,0},{48,16},{64,32},{80,48},{96,64},{112,80},{0,96},{16,112},{3... | collective-permute-start | bytes 1179656 | tf_op jit(solution)/shard_map/from_above_1/ppermute | solution.py:307
  37.6 0.8 copy-done.21
  38.6 0.8 fusion.25.refs_9_
  39.5 0.7 collective-permute-done.11.refs_7_
  40.1 0.7 copy-done.22
  40.9 6.7 %project_0.1 = bf16[16,2,40,256]{3,2,1,0:T(8,128)(2,1)} custom-call(s32[8]{0:T(128)S(1)} %broadcast_add_fusion.places_ref, bf16[512,8192]{1,0:T(8,128)(2,1)} %bitcast.16, bf16[512,256]{1,0:T(8,128)(2,1)} %copy-done.17, bf16[512,256]{1,0:T(8,128)(2,1)} %copy-done.18, bf16[512,256]{1,0:T(8,128)(2,1)} %copy-done.19, ...), custom_call_target="tpu_custom_call" | custom-call | flops 1073741824 | bytes 6291456 | tf_op jit(solution)/shard_map/project_0/pallas_call | solution.py:67
  47.6 2.4 %collective-permute-done.6.refs_1_ = bf16[512,384]{1,0:T(8,128)(2,1)S(1)} collective-permute-done((bf16[512,384]{1,0:T(8,128)(2,1)S(1)}, bf16[512,384]{1,0:T(8,128)(2,1)S(1)}, u32[]{:S(2)}, u32[]{:S(2)}) %collective-permute-start.6) | collective-permute-done | bytes 393248 | tf_op jit(solution)/shard_map/from_below_1/ppermute | solution.py:305
  50.0 0.7 copy-done.13
  50.8 7.5 %all-to-all-start = ((bf16[16,2,40,256]{3,2,1,0:T(8,128)(2,1)}), bf16[16,2,40,256]{3,2,1,0:T(8,128)(2,1)S(1)}, u32[]{:S(2)}, u32[]{:S(2)}) async-start(bf16[16,2,40,256]{3,2,1,0:T(8,128)(2,1)} %project_0.1), calls=%async_computation | async-start | bytes 1310720 | tf_op jit(solution)/shard_map/route_0/all_to_all | solution.py:277
  58.2 3.2 %collective-permute-start.19 = (bf16[512,384]{1,0:T(8,128)(2,1)}, bf16[512,384]{1,0:T(8,128)(2,1)}, u32[]{:S(2)}, u32[]{:S(2)}) collective-permute-start(bf16[512,384]{1,0:T(8,128)(2,1)} %collective-permute-done.7.refs_2_), channel_id=1, source_target_pairs={{32,0},{48,16},{64,32},{80,48},{96,64},{112,80},{0,96},{16,112},{3... | collective-permute-start | bytes 1179656 | tf_op jit(solution)/shard_map/from_opposite_1/ppermute | solution.py:311
  61.6 6.7 %all-to-all-done = bf16[16,2,40,256]{3,2,1,0:T(8,128)(2,1)S(1)} async-done(((bf16[16,2,40,256]{3,2,1,0:T(8,128)(2,1)}), bf16[16,2,40,256]{3,2,1,0:T(8,128)(2,1)S(1)}, u32[]{:S(2)}, u32[]{:S(2)}) %all-to-all-start) | async-done | bytes 655392 | tf_op jit(solution)/shard_map/route_0/all_to_all | solution.py:277
  68.5 2.8 %collective-permute-done.19.refs_3_ = bf16[512,384]{1,0:T(8,128)(2,1)} collective-permute-done((bf16[512,384]{1,0:T(8,128)(2,1)}, bf16[512,384]{1,0:T(8,128)(2,1)}, u32[]{:S(2)}, u32[]{:S(2)}) %collective-permute-start.19) | collective-permute-done | bytes 393248 | tf_op jit(solution)/shard_map/from_opposite_1/ppermute | solution.py:311
  71.8 1.4 collective-permute-done.22.refs_6_
  73.3 0.6 collective-permute-done.23.refs_7_
  74.0 0.8 copy-done.16
  74.8 7.1 %project_1.1 = bf16[16,2,40,384]{3,2,1,0:T(8,128)(2,1)} custom-call(s32[8]{0:T(128)S(1)} %broadcast_add_fusion.places_ref, bf16[512,8192]{1,0:T(8,128)(2,1)} %bitcast.17, bf16[512,384]{1,0:T(8,128)(2,1)} %copy-done.12, bf16[512,384]{1,0:T(8,128)(2,1)} %copy-done.13, bf16[512,384]{1,0:T(8,128)(2,1)} %collective-permute-done.7.refs_2_, ...), custom_call_target="tpu_custom_call" | custom-call | flops 1610612736 | bytes 7340032 | tf_op jit(solution)/shard_map/project_1/pallas_call | solution.py:67
  82.0 7.2 %all-to-all-start.3 = ((bf16[16,2,40,384]{3,2,1,0:T(8,128)(2,1)}), bf16[16,2,40,384]{3,2,1,0:T(8,128)(2,1)S(1)}, u32[]{:S(2)}, u32[]{:S(2)}) async-start(bf16[16,2,40,384]{3,2,1,0:T(8,128)(2,1)} %project_1.1), calls=%async_computation.3 | async-start | bytes 1966080 | tf_op jit(solution)/shard_map/route_1/all_to_all | solution.py:277
  90.3 1.1 collective-permute-done.15.refs_4_
  91.4 1.9 collective-permute-done.16.refs_5_
  93.3 0.9 collective-permute-done.17.refs_6_
  94.2 0.8 copy-done.10
  95.1 0.8 copy-done.11
  95.9 10.5 %project_2.1 = bf16[16,2,40,640]{3,2,1,0:T(8,128)(2,1)} custom-call(s32[8]{0:T(128)S(1)} %broadcast_add_fusion.places_ref, bf16[512,8192]{1,0:T(8,128)(2,1)} %bitcast.18, bf16[512,640]{1,0:T(8,128)(2,1)} %copy-done.5, bf16[512,640]{1,0:T(8,128)(2,1)} %copy-done.6, bf16[512,640]{1,0:T(8,128)(2,1)} %copy-done.7, ...), custom_call_target="tpu_custom_call" | custom-call | flops 2684354560 | bytes 9437184 | tf_op jit(solution)/shard_map/project_2/pallas_call | solution.py:67
  106.5 7.2 %all-to-all-start.1 = ((bf16[16,2,40,640]{3,2,1,0:T(8,128)(2,1)}), bf16[16,2,40,640]{3,2,1,0:T(8,128)(2,1)S(1)}, u32[]{:S(2)}, u32[]{:S(2)}) async-start(bf16[16,2,40,640]{3,2,1,0:T(8,128)(2,1)} %project_2.1), calls=%async_computation.1 | async-start | bytes 3276800 | tf_op jit(solution)/shard_map/route_2/all_to_all | solution.py:277
  114.1 14.4 %shard_map.74 = bf16[2,8,2,40,384]{4,3,2,1,0:T(8,128)(2,1)} custom-call(s32[40]{0:T(128)S(1)} %copy-done, f32[2,40,128]{2,1,0:T(8,128)S(1)} %get-tuple-element.28.cos_ref, f32[2,40,128]{2,1,0:T(8,128)S(1)} %get-tuple-element.29.sin_ref, bf16[2,8,2,40,384]{4,3,2,1,0:T(8,128)(2,1)} %bitcast.26, bf16[2,8,2,40,256]{4,3,2,1,0:T(8,128)(2,1)} %bitcast.20, ...), custom_call_target="tpu_custom_call" | custom-call | flops 125829120 | bytes 20971520 | tf_op jit(solution)/shard_map/pallas_call | solution.py:174
  128.4 9.2 %all-to-all-done.1 = bf16[16,2,40,640]{3,2,1,0:T(8,128)(2,1)S(1)} async-done(((bf16[16,2,40,640]{3,2,1,0:T(8,128)(2,1)}), bf16[16,2,40,640]{3,2,1,0:T(8,128)(2,1)S(1)}, u32[]{:S(2)}, u32[]{:S(2)}) %all-to-all-start.1) | async-done | bytes 1638432 | tf_op jit(solution)/shard_map/route_2/all_to_all | solution.py:277
  137.7 5.8 %all-to-all-start.4 = ((bf16[16,2,40,384]{3,2,1,0:T(8,128)(2,1)}), bf16[16,2,40,384]{3,2,1,0:T(8,128)(2,1)S(1)}, u32[]{:S(2)}, u32[]{:S(2)}) async-start(bf16[16,2,40,384]{3,2,1,0:T(8,128)(2,1)} %bitcast.27), calls=%async_computation.4 | async-start | bytes 1966080 | tf_op jit(solution)/shard_map/all_to_all | solution.py:277
  143.5 14.8 %shard_map.73 = bf16[2,8,2,40,640]{4,3,2,1,0:T(8,128)(2,1)} custom-call(s32[40]{0:T(128)S(1)} %copy-done, f32[2,40,128]{2,1,0:T(8,128)S(1)} %get-tuple-element.28.cos_ref, f32[2,40,128]{2,1,0:T(8,128)S(1)} %get-tuple-element.29.sin_ref, bf16[2,8,2,40,640]{4,3,2,1,0:T(8,128)(2,1)} %bitcast.24, bf16[2,8,2,40,256]{4,3,2,1,0:T(8,128)(2,1)} %bitcast.22, ...), custom_call_target="tpu_custom_call" | custom-call | flops 209715200 | bytes 20971520 | tf_op jit(solution)/shard_map/pallas_call | solution.py:174
  158.3 7.2 %all-to-all-start.2 = ((bf16[16,2,40,640]{3,2,1,0:T(8,128)(2,1)}), bf16[16,2,40,640]{3,2,1,0:T(8,128)(2,1)S(1)}, u32[]{:S(2)}, u32[]{:S(2)}) async-start(bf16[16,2,40,640]{3,2,1,0:T(8,128)(2,1)} %bitcast.25), calls=%async_computation.2 | async-start | bytes 3276800 | tf_op jit(solution)/shard_map/all_to_all | solution.py:277
  165.7 1.5 shard_map.75.refs_0_
  167.2 20.1 %all-to-all-done.2.back_ref = bf16[16,2,40,640]{3,2,1,0:T(8,128)(2,1)S(1)} async-done(((bf16[16,2,40,640]{3,2,1,0:T(8,128)(2,1)}), bf16[16,2,40,640]{3,2,1,0:T(8,128)(2,1)S(1)}, u32[]{:S(2)}, u32[]{:S(2)}) %all-to-all-start.2) | async-done | bytes 1638432 | tf_op jit(solution)/shard_map/all_to_all | solution.py:277
  187.3 1.8 shard_map.76
  (83 shorter events, 3.1 us)
Async XLA Ops:
  1.0 10.2 %collective-permute-start = (bf16[512,256]{1,0:T(8,128)(2,1)S(1)}, bf16[512,256]{1,0:T(8,128)(2,1)S(1)}, u32[]{:S(2)}, u32[]{:S(2)}) collective-permute-start(bf16[512,256]{1,0:T(8,128)(2,1)S(1)} %constant_dynamic-slice_fusion), channel_id=1, source_target_pairs={{0,8},{8,0},{1,9},{9,1},{2,10},{10,2},{3,11},{11,3},{4,12},{12,4},... | collective-permute-start | bytes 786440 | tf_op jit(solution)/shard_map/over_pair_0/ppermute | solution.py:302
  11.2 18.0 %copy-start.17 = (bf16[512,256]{1,0:T(8,128)(2,1)}, bf16[512,256]{1,0:T(8,128)(2,1)S(1)}, u32[]{:S(2)}) copy-start(bf16[512,256]{1,0:T(8,128)(2,1)S(1)} %collective-permute-done.refs_0_) | copy-start | bytes 786436
  11.2 10.1 %collective-permute-start.3 = (bf16[512,256]{1,0:T(8,128)(2,1)S(1)}, bf16[512,256]{1,0:T(8,128)(2,1)S(1)}, u32[]{:S(2)}, u32[]{:S(2)}) collective-permute-start(bf16[512,256]{1,0:T(8,128)(2,1)S(1)} %collective-permute-done.refs_0_), channel_id=1, source_target_pairs={{0,32},{16,48},{32,64},{48,80},{64,96},{80,112},{96,0},{112,16},{1... | collective-permute-start | bytes 786440 | tf_op jit(solution)/shard_map/from_below_0/ppermute | solution.py:305
  15.4 18.4 %collective-permute-start.4 = (bf16[512,256]{1,0:T(8,128)(2,1)S(1)}, bf16[512,256]{1,0:T(8,128)(2,1)S(1)}, u32[]{:S(2)}, u32[]{:S(2)}) collective-permute-start(bf16[512,256]{1,0:T(8,128)(2,1)S(1)} %collective-permute-done.refs_0_), channel_id=1, source_target_pairs={{32,0},{48,16},{64,32},{80,48},{96,64},{112,80},{0,96},{16,112},{3... | collective-permute-start | bytes 786440 | tf_op jit(solution)/shard_map/from_above_0/ppermute | solution.py:307
  17.7 19.9 %collective-permute-start.8 = (bf16[512,256]{1,0:T(8,128)(2,1)S(1)}, bf16[512,256]{1,0:T(8,128)(2,1)S(1)}, u32[]{:S(2)}, u32[]{:S(2)}) collective-permute-start(bf16[512,256]{1,0:T(8,128)(2,1)S(1)} %collective-permute-done.refs_0_), channel_id=1, source_target_pairs={{0,16},{16,0},{32,48},{48,32},{64,80},{80,64},{96,112},{112,96},{1... | collective-permute-start | bytes 786440 | tf_op jit(solution)/shard_map/from_twin_0/ppermute | solution.py:317
  17.7 11.5 %collective-permute-start.1 = (bf16[512,384]{1,0:T(8,128)(2,1)S(1)}, bf16[512,384]{1,0:T(8,128)(2,1)S(1)}, u32[]{:S(2)}, u32[]{:S(2)}) collective-permute-start(bf16[512,384]{1,0:T(8,128)(2,1)S(1)} %constant_dynamic-slice_fusion.2), channel_id=1, source_target_pairs={{0,8},{8,0},{1,9},{9,1},{2,10},{10,2},{3,11},{11,3},{4,12},{12,4},... | collective-permute-start | bytes 1179656 | tf_op jit(solution)/shard_map/over_pair_1/ppermute | solution.py:302
  21.3 8.0 %copy-start.18 = (bf16[512,256]{1,0:T(8,128)(2,1)}, bf16[512,256]{1,0:T(8,128)(2,1)S(1)}, u32[]{:S(2)}) copy-start(bf16[512,256]{1,0:T(8,128)(2,1)S(1)} %collective-permute-done.3.refs_1_) | copy-start | bytes 786436
  22.6 7.5 %copy-start.1 = (bf16[2,256,8192]{2,1,0:T(8,128)(2,1)S(1)}, bf16[2,256,8192]{2,1,0:T(8,128)(2,1)}, u32[]{:S(2)}) copy-start(bf16[2,256,8192]{2,1,0:T(8,128)(2,1)} %param.7) | copy-start | bytes 25165828
  22.6 11.9 %collective-permute-start.5 = (bf16[512,256]{1,0:T(8,128)(2,1)S(1)}, bf16[512,256]{1,0:T(8,128)(2,1)}, u32[]{:S(2)}, u32[]{:S(2)}) collective-permute-start(bf16[512,256]{1,0:T(8,128)(2,1)S(1)} %collective-permute-done.3.refs_1_), channel_id=1, source_target_pairs={{0,32},{16,48},{32,64},{48,80},{64,96},{80,112},{96,0},{112,16},{1... | collective-permute-start | bytes 786440 | tf_op jit(solution)/shard_map/from_opposite_0/ppermute | solution.py:311
  22.6 15.0 %collective-permute-start.9 = (bf16[512,256]{1,0:T(8,128)(2,1)S(1)}, bf16[512,256]{1,0:T(8,128)(2,1)S(1)}, u32[]{:S(2)}, u32[]{:S(2)}) collective-permute-start(bf16[512,256]{1,0:T(8,128)(2,1)S(1)} %collective-permute-done.3.refs_1_), channel_id=1, source_target_pairs={{0,16},{16,0},{32,48},{48,32},{64,80},{80,64},{96,112},{112,96},{1... | collective-permute-start | bytes 786440 | tf_op jit(solution)/shard_map/from_twin_0/ppermute | solution.py:317
  29.2 9.3 %copy-start.23 = (s32[512]{0:T(512)S(1)}, s32[512]{0:T(512)}, u32[]{:S(2)}) copy-start(s32[512]{0:T(512)} %param.13) | copy-start | bytes 6148
  29.2 32.2 %copy-start.12 = (bf16[512,384]{1,0:T(8,128)(2,1)}, bf16[512,384]{1,0:T(8,128)(2,1)S(1)}, u32[]{:S(2)}) copy-start(bf16[512,384]{1,0:T(8,128)(2,1)S(1)} %collective-permute-done.1.refs_0_) | copy-start | bytes 1179652
  29.3 21.5 %collective-permute-start.2 = (bf16[512,640]{1,0:T(8,128)(2,1)S(1)}, bf16[512,640]{1,0:T(8,128)(2,1)S(1)}, u32[]{:S(2)}, u32[]{:S(2)}) collective-permute-start(bf16[512,640]{1,0:T(8,128)(2,1)S(1)} %constant_dynamic-slice_fusion.1), channel_id=1, source_target_pairs={{0,8},{8,0},{1,9},{9,1},{2,10},{10,2},{3,11},{11,3},{4,12},{12,4},... | collective-permute-start | bytes 1966088 | tf_op jit(solution)/shard_map/over_pair_2/ppermute | solution.py:302
  33.8 6.3 %copy-start.19 = (bf16[512,256]{1,0:T(8,128)(2,1)}, bf16[512,256]{1,0:T(8,128)(2,1)S(1)}, u32[]{:S(2)}) copy-start(bf16[512,256]{1,0:T(8,128)(2,1)S(1)} %collective-permute-done.4.refs_2_) | copy-start | bytes 786436
  33.8 5.6 %collective-permute-start.10 = (bf16[512,256]{1,0:T(8,128)(2,1)S(1)}, bf16[512,256]{1,0:T(8,128)(2,1)}, u32[]{:S(2)}, u32[]{:S(2)}) collective-permute-start(bf16[512,256]{1,0:T(8,128)(2,1)S(1)} %collective-permute-done.4.refs_2_), channel_id=1, source_target_pairs={{0,16},{16,0},{32,48},{48,32},{64,80},{80,64},{96,112},{112,96},{1... | collective-permute-start | bytes 786440 | tf_op jit(solution)/shard_map/from_twin_0/ppermute | solution.py:317
  34.5 13.1 %collective-permute-start.7 = (bf16[512,384]{1,0:T(8,128)(2,1)S(1)}, bf16[512,384]{1,0:T(8,128)(2,1)}, u32[]{:S(2)}, u32[]{:S(2)}) collective-permute-start(bf16[512,384]{1,0:T(8,128)(2,1)S(1)} %collective-permute-done.1.refs_0_), channel_id=1, source_target_pairs={{32,0},{48,16},{64,32},{80,48},{96,64},{112,80},{0,96},{16,112},{3... | collective-permute-start | bytes 1179656 | tf_op jit(solution)/shard_map/from_above_1/ppermute | solution.py:307
  37.6 2.5 %copy-start.20 = (bf16[512,256]{1,0:T(8,128)(2,1)}, bf16[512,256]{1,0:T(8,128)(2,1)S(1)}, u32[]{:S(2)}) copy-start(bf16[512,256]{1,0:T(8,128)(2,1)S(1)} %collective-permute-done.8.refs_4_) | copy-start | bytes 786436
  37.6 12.4 %collective-permute-start.6 = (bf16[512,384]{1,0:T(8,128)(2,1)S(1)}, bf16[512,384]{1,0:T(8,128)(2,1)S(1)}, u32[]{:S(2)}, u32[]{:S(2)}) collective-permute-start(bf16[512,384]{1,0:T(8,128)(2,1)S(1)} %collective-permute-done.1.refs_0_), channel_id=1, source_target_pairs={{0,32},{16,48},{32,64},{48,80},{64,96},{80,112},{96,0},{112,16},{1... | collective-permute-start | bytes 1179656 | tf_op jit(solution)/shard_map/from_below_1/ppermute | solution.py:305
  38.4 1.7 collective-permute-start.11
  50.7 38.5 %copy-start.5 = (bf16[512,640]{1,0:T(8,128)(2,1)}, bf16[512,640]{1,0:T(8,128)(2,1)S(1)}, u32[]{:S(2)}) copy-start(bf16[512,640]{1,0:T(8,128)(2,1)S(1)} %collective-permute-done.2.refs_0_) | copy-start | bytes 1966084
  50.7 17.6 %collective-permute-start.12 = (bf16[512,640]{1,0:T(8,128)(2,1)S(1)}, bf16[512,640]{1,0:T(8,128)(2,1)S(1)}, u32[]{:S(2)}, u32[]{:S(2)}) collective-permute-start(bf16[512,640]{1,0:T(8,128)(2,1)S(1)} %collective-permute-done.2.refs_0_), channel_id=1, source_target_pairs={{0,32},{16,48},{32,64},{48,80},{64,96},{80,112},{96,0},{112,16},{1... | collective-permute-start | bytes 1966088 | tf_op jit(solution)/shard_map/from_below_2/ppermute | solution.py:305
  50.8 17.6 %all-to-all-start = ((bf16[16,2,40,256]{3,2,1,0:T(8,128)(2,1)}), bf16[16,2,40,256]{3,2,1,0:T(8,128)(2,1)S(1)}, u32[]{:S(2)}, u32[]{:S(2)}) async-start(bf16[16,2,40,256]{3,2,1,0:T(8,128)(2,1)} %project_0.1), calls=%async_computation | async-start | bytes 1310720 | tf_op jit(solution)/shard_map/route_0/all_to_all | solution.py:277
  58.2 13.1 %collective-permute-start.19 = (bf16[512,384]{1,0:T(8,128)(2,1)}, bf16[512,384]{1,0:T(8,128)(2,1)}, u32[]{:S(2)}, u32[]{:S(2)}) collective-permute-start(bf16[512,384]{1,0:T(8,128)(2,1)} %collective-permute-done.7.refs_2_), channel_id=1, source_target_pairs={{32,0},{48,16},{64,32},{80,48},{96,64},{112,80},{0,96},{16,112},{3... | collective-permute-start | bytes 1179656 | tf_op jit(solution)/shard_map/from_opposite_1/ppermute | solution.py:311
  61.4 9.9 %collective-permute-start.20 = (bf16[512,384]{1,0:T(8,128)(2,1)S(1)}, bf16[512,384]{1,0:T(8,128)(2,1)}, u32[]{:S(2)}, u32[]{:S(2)}) collective-permute-start(bf16[512,384]{1,0:T(8,128)(2,1)S(1)} %collective-permute-done.1.refs_0_), channel_id=1, source_target_pairs={{0,16},{16,0},{32,48},{48,32},{64,80},{80,64},{96,112},{112,96},{1... | collective-permute-start | bytes 1179656 | tf_op jit(solution)/shard_map/from_twin_1/ppermute | solution.py:317
  61.4 28.4 %collective-permute-start.13 = (bf16[512,640]{1,0:T(8,128)(2,1)S(1)}, bf16[512,640]{1,0:T(8,128)(2,1)S(1)}, u32[]{:S(2)}, u32[]{:S(2)}) collective-permute-start(bf16[512,640]{1,0:T(8,128)(2,1)S(1)} %collective-permute-done.2.refs_0_), channel_id=1, source_target_pairs={{32,0},{48,16},{64,32},{80,48},{96,64},{112,80},{0,96},{16,112},{3... | collective-permute-start | bytes 1966088 | tf_op jit(solution)/shard_map/from_above_2/ppermute | solution.py:307
  68.3 13.6 %copy-start.2 = (bf16[16,2,40,256]{3,2,1,0:T(8,128)(2,1)}, bf16[16,2,40,256]{3,2,1,0:T(8,128)(2,1)S(1)}, u32[]{:S(2)}) copy-start(bf16[16,2,40,256]{3,2,1,0:T(8,128)(2,1)S(1)} %all-to-all-done) | copy-start | bytes 1966084
  68.4 21.0 %copy-start.6 = (bf16[512,640]{1,0:T(8,128)(2,1)}, bf16[512,640]{1,0:T(8,128)(2,1)S(1)}, u32[]{:S(2)}) copy-start(bf16[512,640]{1,0:T(8,128)(2,1)S(1)} %collective-permute-done.12.refs_1_) | copy-start | bytes 1966084
  68.4 21.6 %collective-permute-start.14 = (bf16[512,640]{1,0:T(8,128)(2,1)S(1)}, bf16[512,640]{1,0:T(8,128)(2,1)}, u32[]{:S(2)}, u32[]{:S(2)}) collective-permute-start(bf16[512,640]{1,0:T(8,128)(2,1)S(1)} %collective-permute-done.12.refs_1_), channel_id=1, source_target_pairs={{0,32},{16,48},{32,64},{48,80},{64,96},{80,112},{96,0},{112,16},{1... | collective-permute-start | bytes 1966088 | tf_op jit(solution)/shard_map/from_opposite_2/ppermute | solution.py:311
  68.5 3.4 %collective-permute-start.21 = (bf16[512,384]{1,0:T(8,128)(2,1)}, bf16[512,384]{1,0:T(8,128)(2,1)S(1)}, u32[]{:S(2)}, u32[]{:S(2)}) collective-permute-start(bf16[512,384]{1,0:T(8,128)(2,1)} %copy-done.13), channel_id=1, source_target_pairs={{0,16},{16,0},{32,48},{48,32},{64,80},{80,64},{96,112},{112,96},{1... | collective-permute-start | bytes 1179656 | tf_op jit(solution)/shard_map/from_twin_1/ppermute | solution.py:317
  71.3 1.9 %collective-permute-start.22 = (bf16[512,384]{1,0:T(8,128)(2,1)}, bf16[512,384]{1,0:T(8,128)(2,1)S(1)}, u32[]{:S(2)}, u32[]{:S(2)}) collective-permute-start(bf16[512,384]{1,0:T(8,128)(2,1)} %collective-permute-done.7.refs_2_), channel_id=1, source_target_pairs={{0,16},{16,0},{32,48},{48,32},{64,80},{80,64},{96,112},{112,96},{1... | collective-permute-start | bytes 1179656 | tf_op jit(solution)/shard_map/from_twin_1/ppermute | solution.py:317
  71.3 2.5 %collective-permute-start.23 = (bf16[512,384]{1,0:T(8,128)(2,1)}, bf16[512,384]{1,0:T(8,128)(2,1)S(1)}, u32[]{:S(2)}, u32[]{:S(2)}) collective-permute-start(bf16[512,384]{1,0:T(8,128)(2,1)} %collective-permute-done.19.refs_3_), channel_id=1, source_target_pairs={{0,16},{16,0},{32,48},{48,32},{64,80},{80,64},{96,112},{112,96},{1... | collective-permute-start | bytes 1179656 | tf_op jit(solution)/shard_map/from_twin_1/ppermute | solution.py:317
  71.8 2.0 %copy-start.14 = (bf16[512,384]{1,0:T(8,128)(2,1)}, bf16[512,384]{1,0:T(8,128)(2,1)S(1)}, u32[]{:S(2)}) copy-start(bf16[512,384]{1,0:T(8,128)(2,1)S(1)} %collective-permute-done.21.refs_5_) | copy-start | bytes 1179652
  82.0 24.5 %all-to-all-start.3 = ((bf16[16,2,40,384]{3,2,1,0:T(8,128)(2,1)}), bf16[16,2,40,384]{3,2,1,0:T(8,128)(2,1)S(1)}, u32[]{:S(2)}, u32[]{:S(2)}) async-start(bf16[16,2,40,384]{3,2,1,0:T(8,128)(2,1)} %project_1.1), calls=%async_computation.3 | async-start | bytes 1966080 | tf_op jit(solution)/shard_map/route_1/all_to_all | solution.py:277
  89.2 24.5 %copy-start = (s32[40]{0:T(128)S(1)}, s32[40]{0:T(128)}, u32[]{:S(2)}) copy-start(s32[40]{0:T(128)} %fill_ref.3) | copy-start | bytes 484
  89.2 2.2 %collective-permute-start.15 = (bf16[512,640]{1,0:T(8,128)(2,1)S(1)}, bf16[512,640]{1,0:T(8,128)(2,1)S(1)}, u32[]{:S(2)}, u32[]{:S(2)}) collective-permute-start(bf16[512,640]{1,0:T(8,128)(2,1)S(1)} %collective-permute-done.2.refs_0_), channel_id=1, source_target_pairs={{0,16},{16,0},{32,48},{48,32},{64,80},{80,64},{96,112},{112,96},{1... | collective-permute-start | bytes 1966088 | tf_op jit(solution)/shard_map/from_twin_2/ppermute | solution.py:317
  89.3 3.9 %collective-permute-start.16 = (bf16[512,640]{1,0:T(8,128)(2,1)S(1)}, bf16[512,640]{1,0:T(8,128)(2,1)S(1)}, u32[]{:S(2)}, u32[]{:S(2)}) collective-permute-start(bf16[512,640]{1,0:T(8,128)(2,1)S(1)} %collective-permute-done.12.refs_1_), channel_id=1, source_target_pairs={{0,16},{16,0},{32,48},{48,32},{64,80},{80,64},{96,112},{112,96},{1... | collective-permute-start | bytes 1966088 | tf_op jit(solution)/shard_map/from_twin_2/ppermute | solution.py:317
  89.8 4.4 %copy-start.7 = (bf16[512,640]{1,0:T(8,128)(2,1)}, bf16[512,640]{1,0:T(8,128)(2,1)S(1)}, u32[]{:S(2)}) copy-start(bf16[512,640]{1,0:T(8,128)(2,1)S(1)} %collective-permute-done.13.refs_2_) | copy-start | bytes 1966084
  89.8 4.4 %collective-permute-start.17 = (bf16[512,640]{1,0:T(8,128)(2,1)S(1)}, bf16[512,640]{1,0:T(8,128)(2,1)S(1)}, u32[]{:S(2)}, u32[]{:S(2)}) collective-permute-start(bf16[512,640]{1,0:T(8,128)(2,1)S(1)} %collective-permute-done.13.refs_2_), channel_id=1, source_target_pairs={{0,16},{16,0},{32,48},{48,32},{64,80},{80,64},{96,112},{112,96},{1... | collective-permute-start | bytes 1966088 | tf_op jit(solution)/shard_map/from_twin_2/ppermute | solution.py:317
  89.9 4.3 %collective-permute-start.18 = (bf16[512,640]{1,0:T(8,128)(2,1)}, bf16[512,640]{1,0:T(8,128)(2,1)S(1)}, u32[]{:S(2)}, u32[]{:S(2)}) collective-permute-start(bf16[512,640]{1,0:T(8,128)(2,1)} %collective-permute-done.14.refs_3_), channel_id=1, source_target_pairs={{0,16},{16,0},{32,48},{48,32},{64,80},{80,64},{96,112},{112,96},{1... | collective-permute-start | bytes 1966088 | tf_op jit(solution)/shard_map/from_twin_2/ppermute | solution.py:317
  91.4 2.8 %copy-start.8 = (bf16[512,640]{1,0:T(8,128)(2,1)}, bf16[512,640]{1,0:T(8,128)(2,1)S(1)}, u32[]{:S(2)}) copy-start(bf16[512,640]{1,0:T(8,128)(2,1)S(1)} %collective-permute-done.15.refs_4_) | copy-start | bytes 1966084
  93.3 1.0 copy-start.9
  94.2 0.9 copy-start.10
  95.1 0.9 copy-start.11
  106.5 7.6 %copy-start.4 = (bf16[16,2,40,384]{3,2,1,0:T(8,128)(2,1)}, bf16[16,2,40,384]{3,2,1,0:T(8,128)(2,1)S(1)}, u32[]{:S(2)}) copy-start(bf16[16,2,40,384]{3,2,1,0:T(8,128)(2,1)S(1)} %all-to-all-done.3) | copy-start | bytes 2949124
  106.5 31.2 %all-to-all-start.1 = ((bf16[16,2,40,640]{3,2,1,0:T(8,128)(2,1)}), bf16[16,2,40,640]{3,2,1,0:T(8,128)(2,1)S(1)}, u32[]{:S(2)}, u32[]{:S(2)}) async-start(bf16[16,2,40,640]{3,2,1,0:T(8,128)(2,1)} %project_2.1), calls=%async_computation.1 | async-start | bytes 3276800 | tf_op jit(solution)/shard_map/route_2/all_to_all | solution.py:277
  137.7 5.8 %copy-start.3 = (bf16[16,2,40,640]{3,2,1,0:T(8,128)(2,1)}, bf16[16,2,40,640]{3,2,1,0:T(8,128)(2,1)S(1)}, u32[]{:S(2)}) copy-start(bf16[16,2,40,640]{3,2,1,0:T(8,128)(2,1)S(1)} %all-to-all-done.1) | copy-start | bytes 4915204
  137.7 20.6 %all-to-all-start.4 = ((bf16[16,2,40,384]{3,2,1,0:T(8,128)(2,1)}), bf16[16,2,40,384]{3,2,1,0:T(8,128)(2,1)S(1)}, u32[]{:S(2)}, u32[]{:S(2)}) async-start(bf16[16,2,40,384]{3,2,1,0:T(8,128)(2,1)} %bitcast.27), calls=%async_computation.4 | async-start | bytes 1966080 | tf_op jit(solution)/shard_map/all_to_all | solution.py:277
  158.3 29.0 %all-to-all-start.2 = ((bf16[16,2,40,640]{3,2,1,0:T(8,128)(2,1)}), bf16[16,2,40,640]{3,2,1,0:T(8,128)(2,1)S(1)}, u32[]{:S(2)}, u32[]{:S(2)}) async-start(bf16[16,2,40,640]{3,2,1,0:T(8,128)(2,1)} %bitcast.25), calls=%async_computation.2 | async-start | bytes 3276800 | tf_op jit(solution)/shard_map/all_to_all | solution.py:277
  (5 other events, 3.8 us)

commit v10 on v8

--- a/solution.py
+++ b/solution.py
@@ -37,13 +37,13 @@
     for i, slab in enumerate(slabs):
         first = pl.multiple_of(places_ref[i] * depth, depth)
         copies.append((
-            pltpu.make_async_copy(x_ref.at[:, pl.ds(first, depth)], taken.at[i], arrived.at[0, i]),
-            pltpu.make_async_copy(slab, met.at[i], arrived.at[1, i]),
+            pltpu.make_async_copy(x_ref.at[:, pl.ds(first, depth)], taken.at[i // 2, :, pl.ds(i % 2 * depth, depth)], arrived.at[0, i]),
+            pltpu.make_async_copy(slab, met.at[i // 2, pl.ds(i % 2 * depth, depth)], arrived.at[1, i]),
         ))
         for copy in copies[i]:
             copy.start()
-    for i in range(len(slabs)):
-        for copy in copies[i]:
+    for i in range(len(slabs) // 2):
+        for copy in copies[2 * i] + copies[2 * i + 1]:
             copy.wait()
         product = jnp.dot(taken[i], met[i], preferred_element_type=jnp.float32)
         if i == 0:
@@ -76,8 +76,8 @@
             ],
             out_specs=pl.BlockSpec((owners, 2, rows, wide), lambda k, s: (0, 0, 0, 0)),
             scratch_shapes=[
-                pltpu.VMEM((count, lines, depth), jnp.bfloat16),
-                pltpu.VMEM((count, depth, wide), jnp.bfloat16),
+                pltpu.VMEM((count // 2, lines, 2 * depth), jnp.bfloat16),
+                pltpu.VMEM((count // 2, 2 * depth, wide), jnp.bfloat16),
                 pltpu.VMEM((lines, wide), jnp.float32),
                 pltpu.SemaphoreType.DMA((2, count)),
             ],

time: 173 us -> 173 us (level)
  no operation moved by 1% of the time
where the time goes in v10:
time: 173 us
  Pallas kernels  54 us (31%)
  waiting for transfers between devices  47.6 us (28%)
  starting transfers between devices  45.7 us (26%)
  matrix products  17.4 us (10%)
  local copies, waits for them, and re-layouts  5.57 us (3%)
  other arithmetic  1.97 us (1%)
    all_to_all x5, waiting for transfers between devices, exchange(): lax.all_to_all(blocks, ('pair', 'tp'), split_axis=0, concat_axis=0, tiled...  34.8 us
    pallas_call x2, Pallas kernels, attend(): pl.pallas_call(functools.partial(attention_kernel, heads), out_shape=pltp...  28.9 us
    all_to_all x5, starting transfers between devices, exchange(): lax.all_to_all(blocks, ('pair', 'tp'), split_axis=0, concat_axis=0, tiled...  27.8 us
    pallas_call x3, Pallas kernels, project(): pl.pallas_call(functools.partial(project_kernel, owners, rows), out_shape...  22 us
    dot_general x3, matrix products, per_device(): jnp.dot(near, matrix[:, slice(*span)], preferred_element_type=jnp.float32)  17.4 us
    ppermute x3, starting transfers between devices, neighbours(): return (below, lax.ppermute(slab, 'grp', down))  7.15 us
    ppermute x12, waiting for transfers between devices, finish(): slabs = four + [lax.ppermute(piece, 'grp', twin) for piece in four]  4.16 us
    ppermute x3, starting transfers between devices, per_device(): crossed.append(lax.ppermute(after(slab, *crossed[-1:]), 'pair', SWAP))  3.67 us
  transfers between devices with their start and end apart: 29, of which 16 were waited for; matrix products, arithmetic and copies ran while one was open for 12% of the time, Pallas kernels for 30%

profile of v10, /device:TPU:4, one launch (start us, length us, event | category | flops | bytes accessed | tf_op | source)
XLA Modules:
  0.0 172.6 jit_solution(12253466881307950828)
XLA Ops:
  0.0 1.0 constant_dynamic-slice_fusion
  1.0 1.3 collective-permute-start
  2.2 0.7 slice_convert_fusion.2
  2.9 5.0 %fusion.19.refs_8_ = f32[512,256]{1,0:T(8,128)} fusion(bf16[4096,1280]{1,0:T(8,128)(2,1)} %param.8, bf16[512,8192]{1,0:T(8,128)(2,1)} %bitcast.14, s32[]{:T(128)S(6)} %select_n.54, f32[256]{0:T(256)S(1)} %slice_convert_fusion.2), kind=kOutput, calls=%fused_computation.11 | convolution fusion | flops 1073872896 | bytes 6816772 | tf_op jit(solution)/shard_map/dot_general | solution.py:275
  8.0 1.1 collective-permute-done.refs_0_
  9.1 1.9 %collective-permute-start.3 = (bf16[512,256]{1,0:T(8,128)(2,1)S(1)}, bf16[512,256]{1,0:T(8,128)(2,1)S(1)}, u32[]{:S(2)}, u32[]{:S(2)}) collective-permute-start(bf16[512,256]{1,0:T(8,128)(2,1)S(1)} %collective-permute-done.refs_0_), channel_id=1, source_target_pairs={{0,32},{16,48},{32,64},{48,80},{64,96},{80,112},{96,0},{112,16},{1... | collective-permute-start | bytes 786440 | tf_op jit(solution)/shard_map/from_below_0/ppermute | solution.py:287
  11.0 1.3 constant_dynamic-slice_fusion.1
  12.3 2.3 %collective-permute-start.4 = (bf16[512,256]{1,0:T(8,128)(2,1)S(1)}, bf16[512,256]{1,0:T(8,128)(2,1)}, u32[]{:S(2)}, u32[]{:S(2)}) collective-permute-start(bf16[512,256]{1,0:T(8,128)(2,1)S(1)} %collective-permute-done.refs_0_), channel_id=1, source_target_pairs={{32,0},{48,16},{64,32},{80,48},{96,64},{112,80},{0,96},{16,112},{3... | collective-permute-start | bytes 786440 | tf_op jit(solution)/shard_map/from_above_0/ppermute | solution.py:289
  14.6 1.2 collective-permute-start.1
  15.8 2.8 %collective-permute-done.3.refs_1_ = bf16[512,256]{1,0:T(8,128)(2,1)S(1)} collective-permute-done((bf16[512,256]{1,0:T(8,128)(2,1)S(1)}, bf16[512,256]{1,0:T(8,128)(2,1)S(1)}, u32[]{:S(2)}, u32[]{:S(2)}) %collective-permute-start.3) | collective-permute-done | bytes 262176 | tf_op jit(solution)/shard_map/from_below_0/ppermute | solution.py:287
  18.6 5.6 %fusion.9.refs_8_ = f32[512,512]{1,0:T(8,128)} fusion(bf16[4096,1280]{1,0:T(8,128)(2,1)} %param.8, bf16[512,8192]{1,0:T(8,128)(2,1)S(1)} %bitcast.19, s32[]{:T(128)S(6)} %select_n.54, f32[512]{0:T(512)S(1)} %get-tuple-element.24), kind=kOutput, calls=%fused_computation.9 | convolution fusion | flops 2147745792 | bytes 9439236 | tf_op jit(solution)/shard_map/dot_general | solution.py:275
  24.3 0.5 collective-permute-start.17
  24.8 1.5 collective-permute-done.5.refs_3_
  26.3 0.7 copy-done.17
  27.0 1.9 %collective-permute-done.1.refs_0_ = bf16[512,512]{1,0:T(8,128)(2,1)S(1)} collective-permute-done((bf16[512,512]{1,0:T(8,128)(2,1)S(1)}, bf16[512,512]{1,0:T(8,128)(2,1)S(1)}, u32[]{:S(2)}, u32[]{:S(2)}) %collective-permute-start.1) | collective-permute-done | bytes 524320 | tf_op jit(solution)/shard_map/over_pair_1/ppermute | solution.py:284
  28.9 1.9 %collective-permute-start.7 = (bf16[512,512]{1,0:T(8,128)(2,1)S(1)}, bf16[512,512]{1,0:T(8,128)(2,1)S(1)}, u32[]{:S(2)}, u32[]{:S(2)}) collective-permute-start(bf16[512,512]{1,0:T(8,128)(2,1)S(1)} %collective-permute-done.1.refs_0_), channel_id=1, source_target_pairs={{32,0},{48,16},{64,32},{80,48},{96,64},{112,80},{0,96},{16,112},{3... | collective-permute-start | bytes 1572872 | tf_op jit(solution)/shard_map/from_above_1/ppermute | solution.py:289
  31.0 1.2 collective-permute-start.2
  32.3 0.8 fusion.25.refs_9_
  33.1 0.8 collective-permute-done.18.refs_7_
  33.9 0.7 copy-done.18
  34.6 6.8 %project_0.1 = bf16[16,2,40,256]{3,2,1,0:T(8,128)(2,1)} custom-call(s32[8]{0:T(128)S(1)} %broadcast_add_fusion.places_ref, bf16[512,8192]{1,0:T(8,128)(2,1)} %bitcast.15, bf16[512,256]{1,0:T(8,128)(2,1)} %copy-done.15, bf16[512,256]{1,0:T(8,128)(2,1)} %copy-done.16, bf16[512,256]{1,0:T(8,128)(2,1)} %collective-permute-done.4.refs_2_, ...), custom_call_target="tpu_custom_call" | custom-call | flops 1073741824 | bytes 6291456 | tf_op jit(solution)/shard_map/project_0/pallas_call | solution.py:67
  41.4 1.1 collective-permute-done.7.refs_2_
  42.5 3.1 %collective-permute-start.19 = (bf16[512,512]{1,0:T(8,128)(2,1)S(1)}, bf16[512,512]{1,0:T(8,128)(2,1)}, u32[]{:S(2)}, u32[]{:S(2)}) collective-permute-start(bf16[512,512]{1,0:T(8,128)(2,1)S(1)} %collective-permute-done.7.refs_2_), channel_id=1, source_target_pairs={{32,0},{48,16},{64,32},{80,48},{96,64},{112,80},{0,96},{16,112},{3... | collective-permute-start | bytes 1572872 | tf_op jit(solution)/shard_map/from_opposite_1/ppermute | solution.py:293
  45.7 7.5 %all-to-all-start.1 = ((bf16[16,2,40,256]{3,2,1,0:T(8,128)(2,1)}), bf16[16,2,40,256]{3,2,1,0:T(8,128)(2,1)S(1)}, u32[]{:S(2)}, u32[]{:S(2)}) async-start(bf16[16,2,40,256]{3,2,1,0:T(8,128)(2,1)} %project_0.1), calls=%async_computation.1 | async-start | bytes 1310720 | tf_op jit(solution)/shard_map/route_0/all_to_all | solution.py:258
  53.2 6.8 %fusion.14.refs_8_ = f32[512,512]{1,0:T(8,128)} fusion(bf16[4096,1280]{1,0:T(8,128)(2,1)} %param.8, bf16[512,8192]{1,0:T(8,128)(2,1)} %bitcast.16, s32[]{:T(128)S(6)} %select_n.54, f32[512]{0:T(512)S(1)} %get-tuple-element.23), kind=kOutput, calls=%fused_computation.10 | convolution fusion | flops 2147745792 | bytes 9439236 | tf_op jit(solution)/shard_map/dot_general | solution.py:275
  60.0 0.5 collective-permute-start.22
  60.6 2.3 %all-to-all-done.1 = bf16[16,2,40,256]{3,2,1,0:T(8,128)(2,1)S(1)} async-done(((bf16[16,2,40,256]{3,2,1,0:T(8,128)(2,1)}), bf16[16,2,40,256]{3,2,1,0:T(8,128)(2,1)S(1)}, u32[]{:S(2)}, u32[]{:S(2)}) %all-to-all-start.1) | async-done | bytes 655392 | tf_op jit(solution)/shard_map/route_0/all_to_all | solution.py:258
  62.9 2.9 %collective-permute-start.9 = (bf16[512,512]{1,0:T(8,128)(2,1)S(1)}, bf16[512,512]{1,0:T(8,128)(2,1)}, u32[]{:S(2)}, u32[]{:S(2)}) collective-permute-start(bf16[512,512]{1,0:T(8,128)(2,1)S(1)} %collective-permute-done.2.refs_0_), channel_id=1, source_target_pairs={{32,0},{48,16},{64,32},{80,48},{96,64},{112,80},{0,96},{16,112},{3... | collective-permute-start | bytes 1572872 | tf_op jit(solution)/shard_map/from_above_2/ppermute | solution.py:289
  65.9 0.8 copy-done.12
  66.7 7.6 %project_1.1 = bf16[16,2,40,512]{3,2,1,0:T(8,128)(2,1)} custom-call(s32[8]{0:T(128)S(1)} %broadcast_add_fusion.places_ref, bf16[512,8192]{1,0:T(8,128)(2,1)} %bitcast.17, bf16[512,512]{1,0:T(8,128)(2,1)} %copy-done.5, bf16[512,512]{1,0:T(8,128)(2,1)} %copy-done.8, bf16[512,512]{1,0:T(8,128)(2,1)} %copy-done.7, ...), custom_call_target="tpu_custom_call" | custom-call | flops 2147483648 | bytes 8388608 | tf_op jit(solution)/shard_map/project_1/pallas_call | solution.py:67
  74.3 5.9 %all-to-all-start.3 = ((bf16[16,2,40,512]{3,2,1,0:T(8,128)(2,1)}), bf16[16,2,40,512]{3,2,1,0:T(8,128)(2,1)S(1)}, u32[]{:S(2)}, u32[]{:S(2)}) async-start(bf16[16,2,40,512]{3,2,1,0:T(8,128)(2,1)} %project_1.1), calls=%async_computation.3 | async-start | bytes 2621440 | tf_op jit(solution)/shard_map/route_1/all_to_all | solution.py:258
  80.3 0.5 collective-permute-start.12
  81.3 0.9 collective-permute-done.11.refs_4_
  82.2 1.5 collective-permute-done.12.refs_5_
  83.9 0.7 collective-permute-done.14.refs_7_
  84.7 0.8 copy-done.14
  85.6 7.5 %project_2.1 = bf16[16,2,40,512]{3,2,1,0:T(8,128)(2,1)} custom-call(s32[8]{0:T(128)S(1)} %broadcast_add_fusion.places_ref, bf16[512,8192]{1,0:T(8,128)(2,1)} %bitcast.18, bf16[512,512]{1,0:T(8,128)(2,1)} %copy-done.6, bf16[512,512]{1,0:T(8,128)(2,1)} %copy-done.9, bf16[512,512]{1,0:T(8,128)(2,1)} %collective-permute-done.9.refs_2_, ...), custom_call_target="tpu_custom_call" | custom-call | flops 2147483648 | bytes 8388608 | tf_op jit(solution)/shard_map/project_2/pallas_call | solution.py:67
  93.1 7.4 %all-to-all-done.3 = bf16[16,2,40,512]{3,2,1,0:T(8,128)(2,1)S(1)} async-done(((bf16[16,2,40,512]{3,2,1,0:T(8,128)(2,1)}), bf16[16,2,40,512]{3,2,1,0:T(8,128)(2,1)S(1)}, u32[]{:S(2)}, u32[]{:S(2)}) %all-to-all-start.3) | async-done | bytes 1310752 | tf_op jit(solution)/shard_map/route_1/all_to_all | solution.py:258
  100.5 4.8 %all-to-all-start = ((bf16[16,2,40,512]{3,2,1,0:T(8,128)(2,1)}), bf16[16,2,40,512]{3,2,1,0:T(8,128)(2,1)S(1)}, u32[]{:S(2)}, u32[]{:S(2)}) async-start(bf16[16,2,40,512]{3,2,1,0:T(8,128)(2,1)} %project_2.1), calls=%async_computation | async-start | bytes 2621440 | tf_op jit(solution)/shard_map/route_2/all_to_all | solution.py:258
  105.7 14.4 %shard_map.74 = bf16[2,8,2,40,512]{4,3,2,1,0:T(8,128)(2,1)} custom-call(s32[40]{0:T(128)S(1)} %copy-done, f32[2,40,128]{2,1,0:T(8,128)S(1)} %get-tuple-element.28.cos_ref, f32[2,40,128]{2,1,0:T(8,128)S(1)} %get-tuple-element.29.sin_ref, bf16[2,8,2,40,512]{4,3,2,1,0:T(8,128)(2,1)} %bitcast.24, bf16[2,8,2,40,256]{4,3,2,1,0:T(8,128)(2,1)} %bitcast.20, ...), custom_call_target="tpu_custom_call" | custom-call | flops 167772160 | bytes 20971520 | tf_op jit(solution)/shard_map/pallas_call | solution.py:174
  120.2 4.0 %all-to-all-done = bf16[16,2,40,512]{3,2,1,0:T(8,128)(2,1)S(1)} async-done(((bf16[16,2,40,512]{3,2,1,0:T(8,128)(2,1)}), bf16[16,2,40,512]{3,2,1,0:T(8,128)(2,1)S(1)}, u32[]{:S(2)}, u32[]{:S(2)}) %all-to-all-start) | async-done | bytes 1310752 | tf_op jit(solution)/shard_map/route_2/all_to_all | solution.py:258
  124.2 4.8 %all-to-all-start.4 = ((bf16[16,2,40,512]{3,2,1,0:T(8,128)(2,1)}), bf16[16,2,40,512]{3,2,1,0:T(8,128)(2,1)S(1)}, u32[]{:S(2)}, u32[]{:S(2)}) async-start(bf16[16,2,40,512]{3,2,1,0:T(8,128)(2,1)} %bitcast.27), calls=%async_computation.4 | async-start | bytes 2621440 | tf_op jit(solution)/shard_map/all_to_all | solution.py:258
  129.0 14.5 %shard_map.73 = bf16[2,8,2,40,512]{4,3,2,1,0:T(8,128)(2,1)} custom-call(s32[40]{0:T(128)S(1)} %copy-done, f32[2,40,128]{2,1,0:T(8,128)S(1)} %get-tuple-element.28.cos_ref, f32[2,40,128]{2,1,0:T(8,128)S(1)} %get-tuple-element.29.sin_ref, bf16[2,8,2,40,512]{4,3,2,1,0:T(8,128)(2,1)} %bitcast.25, bf16[2,8,2,40,256]{4,3,2,1,0:T(8,128)(2,1)} %bitcast.22, ...), custom_call_target="tpu_custom_call" | custom-call | flops 167772160 | bytes 20971520 | tf_op jit(solution)/shard_map/pallas_call | solution.py:174
  143.5 4.1 %all-to-all-done.4.back_ref = bf16[16,2,40,512]{3,2,1,0:T(8,128)(2,1)S(1)} async-done(((bf16[16,2,40,512]{3,2,1,0:T(8,128)(2,1)}), bf16[16,2,40,512]{3,2,1,0:T(8,128)(2,1)S(1)}, u32[]{:S(2)}, u32[]{:S(2)}) %all-to-all-start.4) | async-done | bytes 1310752 | tf_op jit(solution)/shard_map/all_to_all | solution.py:258
  147.6 4.8 %all-to-all-start.2 = ((bf16[16,2,40,512]{3,2,1,0:T(8,128)(2,1)}), bf16[16,2,40,512]{3,2,1,0:T(8,128)(2,1)S(1)}, u32[]{:S(2)}, u32[]{:S(2)}) async-start(bf16[16,2,40,512]{3,2,1,0:T(8,128)(2,1)} %bitcast.26), calls=%async_computation.2 | async-start | bytes 2621440 | tf_op jit(solution)/shard_map/all_to_all | solution.py:258
  152.5 1.6 shard_map.75.refs_0_
  154.1 16.9 %all-to-all-done.2.back_ref = bf16[16,2,40,512]{3,2,1,0:T(8,128)(2,1)S(1)} async-done(((bf16[16,2,40,512]{3,2,1,0:T(8,128)(2,1)}), bf16[16,2,40,512]{3,2,1,0:T(8,128)(2,1)S(1)}, u32[]{:S(2)}, u32[]{:S(2)}) %all-to-all-start.2) | async-done | bytes 1310752 | tf_op jit(solution)/shard_map/all_to_all | solution.py:258
  171.0 1.6 shard_map.76
  (75 shorter events, 1.9 us)
Async XLA Ops:
  1.0 8.1 %collective-permute-start = (bf16[512,256]{1,0:T(8,128)(2,1)S(1)}, bf16[512,256]{1,0:T(8,128)(2,1)S(1)}, u32[]{:S(2)}, u32[]{:S(2)}) collective-permute-start(bf16[512,256]{1,0:T(8,128)(2,1)S(1)} %constant_dynamic-slice_fusion), channel_id=1, source_target_pairs={{0,8},{8,0},{1,9},{9,1},{2,10},{10,2},{3,11},{11,3},{4,12},{12,4},... | collective-permute-start | bytes 786440 | tf_op jit(solution)/shard_map/over_pair_0/ppermute | solution.py:284
  2.9 9.4 %copy-start.19 = (bf16[1280]{0:T(1024)(128)(2,1)S(1)}, bf16[1280]{0:T(1024)(128)(2,1)}, u32[]{:S(2)}) copy-start(bf16[1280]{0:T(1024)(128)(2,1)} %param.9) | copy-start | bytes 7684
  2.9 15.6 %copy-start.1 = (bf16[2,256,8192]{2,1,0:T(8,128)(2,1)S(1)}, bf16[2,256,8192]{2,1,0:T(8,128)(2,1)}, u32[]{:S(2)}) copy-start(bf16[2,256,8192]{2,1,0:T(8,128)(2,1)} %param.7) | copy-start | bytes 25165828
  9.1 15.1 %copy-start.15 = (bf16[512,256]{1,0:T(8,128)(2,1)}, bf16[512,256]{1,0:T(8,128)(2,1)S(1)}, u32[]{:S(2)}) copy-start(bf16[512,256]{1,0:T(8,128)(2,1)S(1)} %collective-permute-done.refs_0_) | copy-start | bytes 786436
  9.1 9.5 %collective-permute-start.3 = (bf16[512,256]{1,0:T(8,128)(2,1)S(1)}, bf16[512,256]{1,0:T(8,128)(2,1)S(1)}, u32[]{:S(2)}, u32[]{:S(2)}) collective-permute-start(bf16[512,256]{1,0:T(8,128)(2,1)S(1)} %collective-permute-done.refs_0_), channel_id=1, source_target_pairs={{0,32},{16,48},{32,64},{48,80},{64,96},{80,112},{96,0},{112,16},{1... | collective-permute-start | bytes 786440 | tf_op jit(solution)/shard_map/from_below_0/ppermute | solution.py:287
  12.3 12.0 %collective-permute-start.4 = (bf16[512,256]{1,0:T(8,128)(2,1)S(1)}, bf16[512,256]{1,0:T(8,128)(2,1)}, u32[]{:S(2)}, u32[]{:S(2)}) collective-permute-start(bf16[512,256]{1,0:T(8,128)(2,1)S(1)} %collective-permute-done.refs_0_), channel_id=1, source_target_pairs={{32,0},{48,16},{64,32},{80,48},{96,64},{112,80},{0,96},{16,112},{3... | collective-permute-start | bytes 786440 | tf_op jit(solution)/shard_map/from_above_0/ppermute | solution.py:289
  14.6 16.4 %collective-permute-start.15 = (bf16[512,256]{1,0:T(8,128)(2,1)S(1)}, bf16[512,256]{1,0:T(8,128)(2,1)}, u32[]{:S(2)}, u32[]{:S(2)}) collective-permute-start(bf16[512,256]{1,0:T(8,128)(2,1)S(1)} %collective-permute-done.refs_0_), channel_id=1, source_target_pairs={{0,16},{16,0},{32,48},{48,32},{64,80},{80,64},{96,112},{112,96},{1... | collective-permute-start | bytes 786440 | tf_op jit(solution)/shard_map/from_twin_0/ppermute | solution.py:299
  14.6 14.3 %collective-permute-start.1 = (bf16[512,512]{1,0:T(8,128)(2,1)S(1)}, bf16[512,512]{1,0:T(8,128)(2,1)S(1)}, u32[]{:S(2)}, u32[]{:S(2)}) collective-permute-start(bf16[512,512]{1,0:T(8,128)(2,1)S(1)} %get-tuple-element.13), channel_id=1, source_target_pairs={{0,8},{8,0},{1,9},{9,1},{2,10},{10,2},{3,11},{11,3},{4,12},{12,4},... | collective-permute-start | bytes 1572872 | tf_op jit(solution)/shard_map/over_pair_1/ppermute | solution.py:284
  18.6 5.6 %copy-start.16 = (bf16[512,256]{1,0:T(8,128)(2,1)}, bf16[512,256]{1,0:T(8,128)(2,1)S(1)}, u32[]{:S(2)}) copy-start(bf16[512,256]{1,0:T(8,128)(2,1)S(1)} %collective-permute-done.3.refs_1_) | copy-start | bytes 786436
  18.6 7.7 %collective-permute-start.5 = (bf16[512,256]{1,0:T(8,128)(2,1)S(1)}, bf16[512,256]{1,0:T(8,128)(2,1)S(1)}, u32[]{:S(2)}, u32[]{:S(2)}) collective-permute-start(bf16[512,256]{1,0:T(8,128)(2,1)S(1)} %collective-permute-done.3.refs_1_), channel_id=1, source_target_pairs={{0,32},{16,48},{32,64},{48,80},{64,96},{80,112},{96,0},{112,16},{1... | collective-permute-start | bytes 786440 | tf_op jit(solution)/shard_map/from_opposite_0/ppermute | solution.py:293
  18.6 13.6 %collective-permute-start.16 = (bf16[512,256]{1,0:T(8,128)(2,1)S(1)}, bf16[512,256]{1,0:T(8,128)(2,1)}, u32[]{:S(2)}, u32[]{:S(2)}) collective-permute-start(bf16[512,256]{1,0:T(8,128)(2,1)S(1)} %collective-permute-done.3.refs_1_), channel_id=1, source_target_pairs={{0,16},{16,0},{32,48},{48,32},{64,80},{80,64},{96,112},{112,96},{1... | collective-permute-start | bytes 786440 | tf_op jit(solution)/shard_map/from_twin_0/ppermute | solution.py:299
  18.6 13.6 %copy-start.20 = (s32[512]{0:T(512)S(1)}, s32[512]{0:T(512)}, u32[]{:S(2)}) copy-start(s32[512]{0:T(512)} %param.13) | copy-start | bytes 6148
  24.3 8.8 %collective-permute-start.17 = (bf16[512,256]{1,0:T(8,128)(2,1)}, bf16[512,256]{1,0:T(8,128)(2,1)}, u32[]{:S(2)}, u32[]{:S(2)}) collective-permute-start(bf16[512,256]{1,0:T(8,128)(2,1)} %collective-permute-done.4.refs_2_), channel_id=1, source_target_pairs={{0,16},{16,0},{32,48},{48,32},{64,80},{80,64},{96,112},{112,96},{1... | collective-permute-start | bytes 786440 | tf_op jit(solution)/shard_map/from_twin_0/ppermute | solution.py:299
  28.9 31.0 %copy-start.5 = (bf16[512,512]{1,0:T(8,128)(2,1)}, bf16[512,512]{1,0:T(8,128)(2,1)S(1)}, u32[]{:S(2)}) copy-start(bf16[512,512]{1,0:T(8,128)(2,1)S(1)} %collective-permute-done.1.refs_0_) | copy-start | bytes 1572868
  28.9 13.6 %collective-permute-start.7 = (bf16[512,512]{1,0:T(8,128)(2,1)S(1)}, bf16[512,512]{1,0:T(8,128)(2,1)S(1)}, u32[]{:S(2)}, u32[]{:S(2)}) collective-permute-start(bf16[512,512]{1,0:T(8,128)(2,1)S(1)} %collective-permute-done.1.refs_0_), channel_id=1, source_target_pairs={{32,0},{48,16},{64,32},{80,48},{96,64},{112,80},{0,96},{16,112},{3... | collective-permute-start | bytes 1572872 | tf_op jit(solution)/shard_map/from_above_1/ppermute | solution.py:289
  30.9 14.8 %collective-permute-start.6 = (bf16[512,512]{1,0:T(8,128)(2,1)S(1)}, bf16[512,512]{1,0:T(8,128)(2,1)S(1)}, u32[]{:S(2)}, u32[]{:S(2)}) collective-permute-start(bf16[512,512]{1,0:T(8,128)(2,1)S(1)} %collective-permute-done.1.refs_0_), channel_id=1, source_target_pairs={{0,32},{16,48},{32,64},{48,80},{64,96},{80,112},{96,0},{112,16},{1... | collective-permute-start | bytes 1572872 | tf_op jit(solution)/shard_map/from_below_1/ppermute | solution.py:287
  31.0 14.7 %collective-permute-start.2 = (bf16[512,512]{1,0:T(8,128)(2,1)S(1)}, bf16[512,512]{1,0:T(8,128)(2,1)S(1)}, u32[]{:S(2)}, u32[]{:S(2)}) collective-permute-start(bf16[512,512]{1,0:T(8,128)(2,1)S(1)} %get-tuple-element.14), channel_id=1, source_target_pairs={{0,8},{8,0},{1,9},{9,1},{2,10},{10,2},{3,11},{11,3},{4,12},{12,4},... | collective-permute-start | bytes 1572872 | tf_op jit(solution)/shard_map/over_pair_2/ppermute | solution.py:284
  32.2 1.7 %collective-permute-start.18 = (bf16[512,256]{1,0:T(8,128)(2,1)}, bf16[512,256]{1,0:T(8,128)(2,1)S(1)}, u32[]{:S(2)}, u32[]{:S(2)}) collective-permute-start(bf16[512,256]{1,0:T(8,128)(2,1)} %copy-done.17), channel_id=1, source_target_pairs={{0,16},{16,0},{32,48},{48,32},{64,80},{80,64},{96,112},{112,96},{1... | collective-permute-start | bytes 786440 | tf_op jit(solution)/shard_map/from_twin_0/ppermute | solution.py:299
  42.5 17.5 %copy-start.7 = (bf16[512,512]{1,0:T(8,128)(2,1)}, bf16[512,512]{1,0:T(8,128)(2,1)S(1)}, u32[]{:S(2)}) copy-start(bf16[512,512]{1,0:T(8,128)(2,1)S(1)} %collective-permute-done.7.refs_2_) | copy-start | bytes 1572868
  42.5 18.1 %collective-permute-start.19 = (bf16[512,512]{1,0:T(8,128)(2,1)S(1)}, bf16[512,512]{1,0:T(8,128)(2,1)}, u32[]{:S(2)}, u32[]{:S(2)}) collective-permute-start(bf16[512,512]{1,0:T(8,128)(2,1)S(1)} %collective-permute-done.7.refs_2_), channel_id=1, source_target_pairs={{32,0},{48,16},{64,32},{80,48},{96,64},{112,80},{0,96},{16,112},{3... | collective-permute-start | bytes 1572872 | tf_op jit(solution)/shard_map/from_opposite_1/ppermute | solution.py:293
  45.6 14.8 %copy-start.8 = (bf16[512,512]{1,0:T(8,128)(2,1)}, bf16[512,512]{1,0:T(8,128)(2,1)S(1)}, u32[]{:S(2)}) copy-start(bf16[512,512]{1,0:T(8,128)(2,1)S(1)} %collective-permute-done.6.refs_1_) | copy-start | bytes 1572868
  45.7 34.5 %copy-start.6 = (bf16[512,512]{1,0:T(8,128)(2,1)}, bf16[512,512]{1,0:T(8,128)(2,1)S(1)}, u32[]{:S(2)}) copy-start(bf16[512,512]{1,0:T(8,128)(2,1)S(1)} %collective-permute-done.2.refs_0_) | copy-start | bytes 1572868
  45.7 14.9 %collective-permute-start.8 = (bf16[512,512]{1,0:T(8,128)(2,1)S(1)}, bf16[512,512]{1,0:T(8,128)(2,1)S(1)}, u32[]{:S(2)}, u32[]{:S(2)}) collective-permute-start(bf16[512,512]{1,0:T(8,128)(2,1)S(1)} %collective-permute-done.2.refs_0_), channel_id=1, source_target_pairs={{0,32},{16,48},{32,64},{48,80},{64,96},{80,112},{96,0},{112,16},{1... | collective-permute-start | bytes 1572872 | tf_op jit(solution)/shard_map/from_below_2/ppermute | solution.py:287
  45.7 17.2 %all-to-all-start.1 = ((bf16[16,2,40,256]{3,2,1,0:T(8,128)(2,1)}), bf16[16,2,40,256]{3,2,1,0:T(8,128)(2,1)S(1)}, u32[]{:S(2)}, u32[]{:S(2)}) async-start(bf16[16,2,40,256]{3,2,1,0:T(8,128)(2,1)} %project_0.1), calls=%async_computation.1 | async-start | bytes 1310720 | tf_op jit(solution)/shard_map/route_0/all_to_all | solution.py:258
  60.0 5.9 %collective-permute-start.20 = (bf16[512,512]{1,0:T(8,128)(2,1)S(1)}, bf16[512,512]{1,0:T(8,128)(2,1)}, u32[]{:S(2)}, u32[]{:S(2)}) collective-permute-start(bf16[512,512]{1,0:T(8,128)(2,1)S(1)} %collective-permute-done.1.refs_0_), channel_id=1, source_target_pairs={{0,16},{16,0},{32,48},{48,32},{64,80},{80,64},{96,112},{112,96},{1... | collective-permute-start | bytes 1572872 | tf_op jit(solution)/shard_map/from_twin_1/ppermute | solution.py:299
  60.0 5.9 %collective-permute-start.22 = (bf16[512,512]{1,0:T(8,128)(2,1)S(1)}, bf16[512,512]{1,0:T(8,128)(2,1)}, u32[]{:S(2)}, u32[]{:S(2)}) collective-permute-start(bf16[512,512]{1,0:T(8,128)(2,1)S(1)} %collective-permute-done.7.refs_2_), channel_id=1, source_target_pairs={{0,16},{16,0},{32,48},{48,32},{64,80},{80,64},{96,112},{112,96},{1... | collective-permute-start | bytes 1572872 | tf_op jit(solution)/shard_map/from_twin_1/ppermute | solution.py:299
  60.5 5.4 %collective-permute-start.21 = (bf16[512,512]{1,0:T(8,128)(2,1)S(1)}, bf16[512,512]{1,0:T(8,128)(2,1)}, u32[]{:S(2)}, u32[]{:S(2)}) collective-permute-start(bf16[512,512]{1,0:T(8,128)(2,1)S(1)} %collective-permute-done.6.refs_1_), channel_id=1, source_target_pairs={{0,16},{16,0},{32,48},{48,32},{64,80},{80,64},{96,112},{112,96},{1... | collective-permute-start | bytes 1572872 | tf_op jit(solution)/shard_map/from_twin_1/ppermute | solution.py:299
  60.6 19.7 %copy-start.9 = (bf16[512,512]{1,0:T(8,128)(2,1)}, bf16[512,512]{1,0:T(8,128)(2,1)S(1)}, u32[]{:S(2)}) copy-start(bf16[512,512]{1,0:T(8,128)(2,1)S(1)} %collective-permute-done.8.refs_1_) | copy-start | bytes 1572868
  62.9 11.4 %copy-start.2 = (bf16[16,2,40,256]{3,2,1,0:T(8,128)(2,1)}, bf16[16,2,40,256]{3,2,1,0:T(8,128)(2,1)S(1)}, u32[]{:S(2)}) copy-start(bf16[16,2,40,256]{3,2,1,0:T(8,128)(2,1)S(1)} %all-to-all-done.1) | copy-start | bytes 1966084
  62.9 3.0 %collective-permute-start.23 = (bf16[512,512]{1,0:T(8,128)(2,1)}, bf16[512,512]{1,0:T(8,128)(2,1)S(1)}, u32[]{:S(2)}, u32[]{:S(2)}) collective-permute-start(bf16[512,512]{1,0:T(8,128)(2,1)} %collective-permute-done.19.refs_3_), channel_id=1, source_target_pairs={{0,16},{16,0},{32,48},{48,32},{64,80},{80,64},{96,112},{112,96},{1... | collective-permute-start | bytes 1572872 | tf_op jit(solution)/shard_map/from_twin_1/ppermute | solution.py:299
  62.9 17.9 %collective-permute-start.9 = (bf16[512,512]{1,0:T(8,128)(2,1)S(1)}, bf16[512,512]{1,0:T(8,128)(2,1)}, u32[]{:S(2)}, u32[]{:S(2)}) collective-permute-start(bf16[512,512]{1,0:T(8,128)(2,1)S(1)} %collective-permute-done.2.refs_0_), channel_id=1, source_target_pairs={{32,0},{48,16},{64,32},{80,48},{96,64},{112,80},{0,96},{16,112},{3... | collective-permute-start | bytes 1572872 | tf_op jit(solution)/shard_map/from_above_2/ppermute | solution.py:289
  65.8 15.4 %collective-permute-start.10 = (bf16[512,512]{1,0:T(8,128)(2,1)S(1)}, bf16[512,512]{1,0:T(8,128)(2,1)}, u32[]{:S(2)}, u32[]{:S(2)}) collective-permute-start(bf16[512,512]{1,0:T(8,128)(2,1)S(1)} %collective-permute-done.8.refs_1_), channel_id=1, source_target_pairs={{0,32},{16,48},{32,64},{48,80},{64,96},{80,112},{96,0},{112,16},{1... | collective-permute-start | bytes 1572872 | tf_op jit(solution)/shard_map/from_opposite_2/ppermute | solution.py:293
  65.9 0.8 copy-start.12
  74.3 26.2 %all-to-all-start.3 = ((bf16[16,2,40,512]{3,2,1,0:T(8,128)(2,1)}), bf16[16,2,40,512]{3,2,1,0:T(8,128)(2,1)S(1)}, u32[]{:S(2)}, u32[]{:S(2)}) async-start(bf16[16,2,40,512]{3,2,1,0:T(8,128)(2,1)} %project_1.1), calls=%async_computation.3 | async-start | bytes 2621440 | tf_op jit(solution)/shard_map/route_1/all_to_all | solution.py:258
  80.2 25.2 %copy-start = (s32[40]{0:T(128)S(1)}, s32[40]{0:T(128)}, u32[]{:S(2)}) copy-start(s32[40]{0:T(128)} %fill_ref.3) | copy-start | bytes 484
  80.2 2.0 %collective-permute-start.11 = (bf16[512,512]{1,0:T(8,128)(2,1)S(1)}, bf16[512,512]{1,0:T(8,128)(2,1)S(1)}, u32[]{:S(2)}, u32[]{:S(2)}) collective-permute-start(bf16[512,512]{1,0:T(8,128)(2,1)S(1)} %collective-permute-done.2.refs_0_), channel_id=1, source_target_pairs={{0,16},{16,0},{32,48},{48,32},{64,80},{80,64},{96,112},{112,96},{1... | collective-permute-start | bytes 1572872 | tf_op jit(solution)/shard_map/from_twin_2/ppermute | solution.py:299
  80.3 3.4 %collective-permute-start.12 = (bf16[512,512]{1,0:T(8,128)(2,1)S(1)}, bf16[512,512]{1,0:T(8,128)(2,1)S(1)}, u32[]{:S(2)}, u32[]{:S(2)}) collective-permute-start(bf16[512,512]{1,0:T(8,128)(2,1)S(1)} %collective-permute-done.8.refs_1_), channel_id=1, source_target_pairs={{0,16},{16,0},{32,48},{48,32},{64,80},{80,64},{96,112},{112,96},{1... | collective-permute-start | bytes 1572872 | tf_op jit(solution)/shard_map/from_twin_2/ppermute | solution.py:299
  80.8 3.1 %collective-permute-start.13 = (bf16[512,512]{1,0:T(8,128)(2,1)}, bf16[512,512]{1,0:T(8,128)(2,1)S(1)}, u32[]{:S(2)}, u32[]{:S(2)}) collective-permute-start(bf16[512,512]{1,0:T(8,128)(2,1)} %collective-permute-done.9.refs_2_), channel_id=1, source_target_pairs={{0,16},{16,0},{32,48},{48,32},{64,80},{80,64},{96,112},{112,96},{1... | collective-permute-start | bytes 1572872 | tf_op jit(solution)/shard_map/from_twin_2/ppermute | solution.py:299
  81.2 3.4 %collective-permute-start.14 = (bf16[512,512]{1,0:T(8,128)(2,1)}, bf16[512,512]{1,0:T(8,128)(2,1)S(1)}, u32[]{:S(2)}, u32[]{:S(2)}) collective-permute-start(bf16[512,512]{1,0:T(8,128)(2,1)} %collective-permute-done.10.refs_3_), channel_id=1, source_target_pairs={{0,16},{16,0},{32,48},{48,32},{64,80},{80,64},{96,112},{112,96},{1... | collective-permute-start | bytes 1572872 | tf_op jit(solution)/shard_map/from_twin_2/ppermute | solution.py:299
  82.2 2.5 %copy-start.10 = (bf16[512,512]{1,0:T(8,128)(2,1)}, bf16[512,512]{1,0:T(8,128)(2,1)S(1)}, u32[]{:S(2)}) copy-start(bf16[512,512]{1,0:T(8,128)(2,1)S(1)} %collective-permute-done.11.refs_4_) | copy-start | bytes 1572868
  83.7 1.0 copy-start.11
  83.9 0.8 copy-start.13
  84.7 0.8 copy-start.14
  100.5 5.2 %copy-start.3 = (bf16[16,2,40,512]{3,2,1,0:T(8,128)(2,1)}, bf16[16,2,40,512]{3,2,1,0:T(8,128)(2,1)S(1)}, u32[]{:S(2)}) copy-start(bf16[16,2,40,512]{3,2,1,0:T(8,128)(2,1)S(1)} %all-to-all-done.3) | copy-start | bytes 3932164
  100.5 23.6 %all-to-all-start = ((bf16[16,2,40,512]{3,2,1,0:T(8,128)(2,1)}), bf16[16,2,40,512]{3,2,1,0:T(8,128)(2,1)S(1)}, u32[]{:S(2)}, u32[]{:S(2)}) async-start(bf16[16,2,40,512]{3,2,1,0:T(8,128)(2,1)} %project_2.1), calls=%async_computation | async-start | bytes 2621440 | tf_op jit(solution)/shard_map/route_2/all_to_all | solution.py:258
  124.2 4.8 %copy-start.4 = (bf16[16,2,40,512]{3,2,1,0:T(8,128)(2,1)}, bf16[16,2,40,512]{3,2,1,0:T(8,128)(2,1)S(1)}, u32[]{:S(2)}) copy-start(bf16[16,2,40,512]{3,2,1,0:T(8,128)(2,1)S(1)} %all-to-all-done) | copy-start | bytes 3932164
  124.2 23.4 %all-to-all-start.4 = ((bf16[16,2,40,512]{3,2,1,0:T(8,128)(2,1)}), bf16[16,2,40,512]{3,2,1,0:T(8,128)(2,1)S(1)}, u32[]{:S(2)}, u32[]{:S(2)}) async-start(bf16[16,2,40,512]{3,2,1,0:T(8,128)(2,1)} %bitcast.27), calls=%async_computation.4 | async-start | bytes 2621440 | tf_op jit(solution)/shard_map/all_to_all | solution.py:258
  147.6 23.5 %all-to-all-start.2 = ((bf16[16,2,40,512]{3,2,1,0:T(8,128)(2,1)}), bf16[16,2,40,512]{3,2,1,0:T(8,128)(2,1)S(1)}, u32[]{:S(2)}, u32[]{:S(2)}) async-start(bf16[16,2,40,512]{3,2,1,0:T(8,128)(2,1)} %bitcast.26), calls=%async_computation.2 | async-start | bytes 2621440 | tf_op jit(solution)/shard_map/all_to_all | solution.py:258
  (2 other events, 1.4 us)

commit v11 on v10

--- a/solution.py
+++ b/solution.py
@@ -316,7 +316,7 @@
     packed = finish(0, [slab0, below0, above0, opposite0], below1, above1, slab2)
     opposite1 = further(1, after(above1, packed), down)
     opposite2 = further(2, below2, up)
-    finish(1, [slab1, below1, above1, after(opposite1, partials[2], arrived[0], below2)])
+    finish(1, [slab1, below1, above1, after(opposite1, partials[2], below2)])
     finish(2, [slab2, below2, above2, opposite2])
     out = None
     for (first, last), queries in zip(CHUNKS, arrived[1:]):

time: 173 us -> 176 us (1.017)
  waiting for transfers between devices: 47.6 us -> 52 us
    ppermute x3, waiting for transfers between devices: 2.77 us -> 6.48 us  [neighbours(): below = lax.ppermute(slab, 'grp', up)]
    ppermute x3, waiting for transfers between devices: 1.84 us -> 4.77 us  [further(): return lax.ppermute(piece, 'grp', way)]
    ppermute x3, starting transfers between devices: 7.15 us -> 4.41 us  [neighbours(): return (below, lax.ppermute(slab, 'grp', down))]
    all_to_all x5, waiting for transfers between devices: 34.8 us -> 32.8 us  [exchange(): lax.all_to_all(blocks, ('pair', 'tp'), split_axis=0, concat_axis=0, tiled...]
    ppermute x3, starting transfers between devices: 3.14 us -> 4.97 us  [further(): return lax.ppermute(piece, 'grp', way)]
  transfers between devices with their start and end apart: 29 -> 29, of which waited for: 16 -> 17; matrix products, arithmetic and copies ran while one was open for 12% -> 12% of each run, Pallas kernels for 30% -> 30%
where the time goes in v11:
time: 176 us; the launch traced here: 175 us
  Pallas kernels  54 us (31%)
  waiting for transfers between devices  52 us (30%)
  starting transfers between devices  44.8 us (25%)
  matrix products  17.6 us (10%)
  local copies, waits for them, and re-layouts  4.78 us (3%)
  other arithmetic  1.97 us (1%)
    all_to_all x5, waiting for transfers between devices, exchange(): lax.all_to_all(blocks, ('pair', 'tp'), split_axis=0, concat_axis=0, tiled...  32.8 us
    pallas_call x2, Pallas kernels, attend(): pl.pallas_call(functools.partial(attention_kernel, heads), out_shape=pltp...  28.9 us
    all_to_all x5, starting transfers between devices, exchange(): lax.all_to_all(blocks, ('pair', 'tp'), split_axis=0, concat_axis=0, tiled...  27.4 us
    pallas_call x3, Pallas kernels, project(): pl.pallas_call(functools.partial(project_kernel, owners, rows), out_shape...  22 us
    dot_general x3, matrix products, per_device(): jnp.dot(near, matrix[:, slice(*span)], preferred_element_type=jnp.float32)  17.6 us
    ppermute x3, waiting for transfers between devices, neighbours(): below = lax.ppermute(slab, 'grp', up)  6.48 us
    ppermute x3, starting transfers between devices, further(): return lax.ppermute(piece, 'grp', way)  4.97 us
    ppermute x3, waiting for transfers between devices, further(): return lax.ppermute(piece, 'grp', way)  4.77 us
  transfers between devices with their start and end apart: 29, of which 17 were waited for; matrix products, arithmetic and copies ran while one was open for 12% of the time, Pallas kernels for 30%

profile of v11, /device:TPU:4, one launch (start us, length us, event | category | flops | bytes accessed | tf_op | source)
XLA Modules:
  0.0 175.3 jit_solution(5619796225230961736)
XLA Ops:
  0.0 1.0 constant_dynamic-slice_fusion
  1.0 1.3 collective-permute-start
  2.2 0.7 slice_convert_fusion.2
  2.9 5.0 %fusion.19.refs_8_ = f32[512,256]{1,0:T(8,128)} fusion(bf16[4096,1280]{1,0:T(8,128)(2,1)} %param.8, bf16[512,8192]{1,0:T(8,128)(2,1)} %bitcast.14, s32[]{:T(128)S(6)} %select_n.54, f32[256]{0:T(256)S(1)} %slice_convert_fusion.2), kind=kOutput, calls=%fused_computation.11 | convolution fusion | flops 1073872896 | bytes 6816772 | tf_op jit(solution)/shard_map/dot_general | solution.py:275
  8.0 1.1 collective-permute-done.refs_0_
  9.1 1.9 %collective-permute-start.3 = (bf16[512,256]{1,0:T(8,128)(2,1)S(1)}, bf16[512,256]{1,0:T(8,128)(2,1)}, u32[]{:S(2)}, u32[]{:S(2)}) collective-permute-start(bf16[512,256]{1,0:T(8,128)(2,1)S(1)} %collective-permute-done.refs_0_), channel_id=1, source_target_pairs={{0,32},{16,48},{32,64},{48,80},{64,96},{80,112},{96,0},{112,16},{1... | collective-permute-start | bytes 786440 | tf_op jit(solution)/shard_map/from_below_0/ppermute | solution.py:287
  11.0 1.3 constant_dynamic-slice_fusion.1
  12.3 2.3 %collective-permute-start.4 = (bf16[512,256]{1,0:T(8,128)(2,1)S(1)}, bf16[512,256]{1,0:T(8,128)(2,1)}, u32[]{:S(2)}, u32[]{:S(2)}) collective-permute-start(bf16[512,256]{1,0:T(8,128)(2,1)S(1)} %collective-permute-done.refs_0_), channel_id=1, source_target_pairs={{32,0},{48,16},{64,32},{80,48},{96,64},{112,80},{0,96},{16,112},{3... | collective-permute-start | bytes 786440 | tf_op jit(solution)/shard_map/from_above_0/ppermute | solution.py:289
  14.6 1.2 collective-permute-start.1
  15.8 2.9 %collective-permute-done.3.refs_1_ = bf16[512,256]{1,0:T(8,128)(2,1)} collective-permute-done((bf16[512,256]{1,0:T(8,128)(2,1)S(1)}, bf16[512,256]{1,0:T(8,128)(2,1)}, u32[]{:S(2)}, u32[]{:S(2)}) %collective-permute-start.3) | collective-permute-done | bytes 262176 | tf_op jit(solution)/shard_map/from_below_0/ppermute | solution.py:287
  18.7 5.5 %fusion.9.refs_8_ = f32[512,512]{1,0:T(8,128)} fusion(bf16[4096,1280]{1,0:T(8,128)(2,1)} %param.8, bf16[512,8192]{1,0:T(8,128)(2,1)S(1)} %bitcast.19, s32[]{:T(128)S(6)} %select_n.54, f32[512]{0:T(512)S(1)} %get-tuple-element.24), kind=kOutput, calls=%fused_computation.9 | convolution fusion | flops 2147745792 | bytes 9439236 | tf_op jit(solution)/shard_map/dot_general | solution.py:275
  24.3 0.6 collective-permute-start.17
  24.9 1.8 %collective-permute-done.5.refs_3_ = bf16[512,256]{1,0:T(8,128)(2,1)S(1)} collective-permute-done((bf16[512,256]{1,0:T(8,128)(2,1)}, bf16[512,256]{1,0:T(8,128)(2,1)S(1)}, u32[]{:S(2)}, u32[]{:S(2)}) %collective-permute-start.5) | collective-permute-done | bytes 262176 | tf_op jit(solution)/shard_map/from_opposite_0/ppermute | solution.py:293
  26.6 2.3 %collective-permute-done.1.refs_0_ = bf16[512,512]{1,0:T(8,128)(2,1)S(1)} collective-permute-done((bf16[512,512]{1,0:T(8,128)(2,1)S(1)}, bf16[512,512]{1,0:T(8,128)(2,1)S(1)}, u32[]{:S(2)}, u32[]{:S(2)}) %collective-permute-start.1) | collective-permute-done | bytes 524320 | tf_op jit(solution)/shard_map/over_pair_1/ppermute | solution.py:284
  28.9 1.9 %collective-permute-start.7 = (bf16[512,512]{1,0:T(8,128)(2,1)S(1)}, bf16[512,512]{1,0:T(8,128)(2,1)S(1)}, u32[]{:S(2)}, u32[]{:S(2)}) collective-permute-start(bf16[512,512]{1,0:T(8,128)(2,1)S(1)} %collective-permute-done.1.refs_0_), channel_id=1, source_target_pairs={{32,0},{48,16},{64,32},{80,48},{96,64},{112,80},{0,96},{16,112},{3... | collective-permute-start | bytes 1572872 | tf_op jit(solution)/shard_map/from_above_1/ppermute | solution.py:289
  31.0 1.2 collective-permute-start.2
  32.2 0.8 dynamic_slice.15
  32.9 0.8 fusion.25.refs_9_
  33.9 0.7 copy-done.16
  34.6 6.8 %project_0.1 = bf16[16,2,40,256]{3,2,1,0:T(8,128)(2,1)} custom-call(s32[8]{0:T(128)S(1)} %broadcast_add_fusion.places_ref, bf16[512,8192]{1,0:T(8,128)(2,1)} %bitcast.15, bf16[512,256]{1,0:T(8,128)(2,1)} %copy-done.14, bf16[512,256]{1,0:T(8,128)(2,1)} %collective-permute-done.3.refs_1_, bf16[512,256]{1,0:T(8,128)(2,1)} %collective-permute-done.4.refs_2_, ...), custom_call_target="tpu_custom_call" | custom-call | flops 1073741824 | bytes 6291456 | tf_op jit(solution)/shard_map/project_0/pallas_call | solution.py:67
  41.5 1.0 collective-permute-done.7.refs_2_
  42.5 3.1 %collective-permute-start.19 = (bf16[512,512]{1,0:T(8,128)(2,1)S(1)}, bf16[512,512]{1,0:T(8,128)(2,1)}, u32[]{:S(2)}, u32[]{:S(2)}) collective-permute-start(bf16[512,512]{1,0:T(8,128)(2,1)S(1)} %collective-permute-done.7.refs_2_), channel_id=1, source_target_pairs={{32,0},{48,16},{64,32},{80,48},{96,64},{112,80},{0,96},{16,112},{3... | collective-permute-start | bytes 1572872 | tf_op jit(solution)/shard_map/from_opposite_1/ppermute | solution.py:293
  45.7 7.0 %fusion.14.refs_8_ = f32[512,512]{1,0:T(8,128)} fusion(bf16[4096,1280]{1,0:T(8,128)(2,1)} %param.8, bf16[512,8192]{1,0:T(8,128)(2,1)} %bitcast.16, s32[]{:T(128)S(6)} %select_n.54, f32[512]{0:T(512)S(1)} %get-tuple-element.23), kind=kOutput, calls=%fused_computation.10 | convolution fusion | flops 2147745792 | bytes 9439236 | tf_op jit(solution)/shard_map/dot_general | solution.py:275
  52.8 0.5 collective-permute-start.22
  53.4 3.0 %collective-permute-done.19.refs_3_ = bf16[512,512]{1,0:T(8,128)(2,1)} collective-permute-done((bf16[512,512]{1,0:T(8,128)(2,1)S(1)}, bf16[512,512]{1,0:T(8,128)(2,1)}, u32[]{:S(2)}, u32[]{:S(2)}) %collective-permute-start.19) | collective-permute-done | bytes 524320 | tf_op jit(solution)/shard_map/from_opposite_1/ppermute | solution.py:293
  56.4 3.6 %collective-permute-done.8.refs_1_ = bf16[512,512]{1,0:T(8,128)(2,1)} collective-permute-done((bf16[512,512]{1,0:T(8,128)(2,1)S(1)}, bf16[512,512]{1,0:T(8,128)(2,1)}, u32[]{:S(2)}, u32[]{:S(2)}) %collective-permute-start.8) | collective-permute-done | bytes 524320 | tf_op jit(solution)/shard_map/from_below_2/ppermute | solution.py:287
  60.0 7.4 %all-to-all-start.1 = ((bf16[16,2,40,256]{3,2,1,0:T(8,128)(2,1)}), bf16[16,2,40,256]{3,2,1,0:T(8,128)(2,1)S(1)}, u32[]{:S(2)}, u32[]{:S(2)}) async-start(bf16[16,2,40,256]{3,2,1,0:T(8,128)(2,1)} %project_0.1), calls=%async_computation.1 | async-start | bytes 1310720 | tf_op jit(solution)/shard_map/route_0/all_to_all | solution.py:258
  67.6 1.8 %collective-permute-start.10 = (bf16[512,512]{1,0:T(8,128)(2,1)}, bf16[512,512]{1,0:T(8,128)(2,1)}, u32[]{:S(2)}, u32[]{:S(2)}) collective-permute-start(bf16[512,512]{1,0:T(8,128)(2,1)} %collective-permute-done.8.refs_1_), channel_id=1, source_target_pairs={{0,32},{16,48},{32,64},{48,80},{64,96},{80,112},{96,0},{112,16},{1... | collective-permute-start | bytes 1572872 | tf_op jit(solution)/shard_map/from_opposite_2/ppermute | solution.py:293
  69.5 7.6 %project_1.1 = bf16[16,2,40,512]{3,2,1,0:T(8,128)(2,1)} custom-call(s32[8]{0:T(128)S(1)} %broadcast_add_fusion.places_ref, bf16[512,8192]{1,0:T(8,128)(2,1)} %bitcast.17, bf16[512,512]{1,0:T(8,128)(2,1)} %copy-done.5, bf16[512,512]{1,0:T(8,128)(2,1)} %copy-done.8, bf16[512,512]{1,0:T(8,128)(2,1)} %copy-done.7, ...), custom_call_target="tpu_custom_call" | custom-call | flops 2147483648 | bytes 8388608 | tf_op jit(solution)/shard_map/project_1/pallas_call | solution.py:67
  77.1 1.8 %all-to-all-done.1 = bf16[16,2,40,256]{3,2,1,0:T(8,128)(2,1)S(1)} async-done(((bf16[16,2,40,256]{3,2,1,0:T(8,128)(2,1)}), bf16[16,2,40,256]{3,2,1,0:T(8,128)(2,1)S(1)}, u32[]{:S(2)}, u32[]{:S(2)}) %all-to-all-start.1) | async-done | bytes 655392 | tf_op jit(solution)/shard_map/route_0/all_to_all | solution.py:258
  78.9 5.4 %all-to-all-start.3 = ((bf16[16,2,40,512]{3,2,1,0:T(8,128)(2,1)}), bf16[16,2,40,512]{3,2,1,0:T(8,128)(2,1)S(1)}, u32[]{:S(2)}, u32[]{:S(2)}) async-start(bf16[16,2,40,512]{3,2,1,0:T(8,128)(2,1)} %project_1.1), calls=%async_computation.3 | async-start | bytes 2621440 | tf_op jit(solution)/shard_map/route_1/all_to_all | solution.py:258
  85.5 0.9 collective-permute-done.11.refs_4_
  86.4 1.0 collective-permute-done.12.refs_5_
  87.4 0.7 collective-permute-done.13.refs_6_
  88.1 0.7 collective-permute-done.14.refs_7_
  88.9 0.8 copy-done.13
  89.8 7.5 %project_2.1 = bf16[16,2,40,512]{3,2,1,0:T(8,128)(2,1)} custom-call(s32[8]{0:T(128)S(1)} %broadcast_add_fusion.places_ref, bf16[512,8192]{1,0:T(8,128)(2,1)} %bitcast.18, bf16[512,512]{1,0:T(8,128)(2,1)} %copy-done.6, bf16[512,512]{1,0:T(8,128)(2,1)} %collective-permute-done.8.refs_1_, bf16[512,512]{1,0:T(8,128)(2,1)} %collective-permute-done.9.refs_2_, ...), custom_call_target="tpu_custom_call" | custom-call | flops 2147483648 | bytes 8388608 | tf_op jit(solution)/shard_map/project_2/pallas_call | solution.py:67
  97.3 6.2 %all-to-all-done.3 = bf16[16,2,40,512]{3,2,1,0:T(8,128)(2,1)S(1)} async-done(((bf16[16,2,40,512]{3,2,1,0:T(8,128)(2,1)}), bf16[16,2,40,512]{3,2,1,0:T(8,128)(2,1)S(1)}, u32[]{:S(2)}, u32[]{:S(2)}) %all-to-all-start.3) | async-done | bytes 1310752 | tf_op jit(solution)/shard_map/route_1/all_to_all | solution.py:258
  103.6 4.8 %all-to-all-start = ((bf16[16,2,40,512]{3,2,1,0:T(8,128)(2,1)}), bf16[16,2,40,512]{3,2,1,0:T(8,128)(2,1)S(1)}, u32[]{:S(2)}, u32[]{:S(2)}) async-start(bf16[16,2,40,512]{3,2,1,0:T(8,128)(2,1)} %project_2.1), calls=%async_computation | async-start | bytes 2621440 | tf_op jit(solution)/shard_map/route_2/all_to_all | solution.py:258
  108.8 14.4 %shard_map.74 = bf16[2,8,2,40,512]{4,3,2,1,0:T(8,128)(2,1)} custom-call(s32[40]{0:T(128)S(1)} %copy-done, f32[2,40,128]{2,1,0:T(8,128)S(1)} %get-tuple-element.28.cos_ref, f32[2,40,128]{2,1,0:T(8,128)S(1)} %get-tuple-element.29.sin_ref, bf16[2,8,2,40,512]{4,3,2,1,0:T(8,128)(2,1)} %bitcast.24, bf16[2,8,2,40,256]{4,3,2,1,0:T(8,128)(2,1)} %bitcast.20, ...), custom_call_target="tpu_custom_call" | custom-call | flops 167772160 | bytes 20971520 | tf_op jit(solution)/shard_map/pallas_call | solution.py:174
  123.2 3.7 %all-to-all-done = bf16[16,2,40,512]{3,2,1,0:T(8,128)(2,1)S(1)} async-done(((bf16[16,2,40,512]{3,2,1,0:T(8,128)(2,1)}), bf16[16,2,40,512]{3,2,1,0:T(8,128)(2,1)S(1)}, u32[]{:S(2)}, u32[]{:S(2)}) %all-to-all-start) | async-done | bytes 1310752 | tf_op jit(solution)/shard_map/route_2/all_to_all | solution.py:258
  126.9 4.8 %all-to-all-start.4 = ((bf16[16,2,40,512]{3,2,1,0:T(8,128)(2,1)}), bf16[16,2,40,512]{3,2,1,0:T(8,128)(2,1)S(1)}, u32[]{:S(2)}, u32[]{:S(2)}) async-start(bf16[16,2,40,512]{3,2,1,0:T(8,128)(2,1)} %bitcast.27), calls=%async_computation.4 | async-start | bytes 2621440 | tf_op jit(solution)/shard_map/all_to_all | solution.py:258
  131.7 14.5 %shard_map.73 = bf16[2,8,2,40,512]{4,3,2,1,0:T(8,128)(2,1)} custom-call(s32[40]{0:T(128)S(1)} %copy-done, f32[2,40,128]{2,1,0:T(8,128)S(1)} %get-tuple-element.28.cos_ref, f32[2,40,128]{2,1,0:T(8,128)S(1)} %get-tuple-element.29.sin_ref, bf16[2,8,2,40,512]{4,3,2,1,0:T(8,128)(2,1)} %bitcast.25, bf16[2,8,2,40,256]{4,3,2,1,0:T(8,128)(2,1)} %bitcast.22, ...), custom_call_target="tpu_custom_call" | custom-call | flops 167772160 | bytes 20971520 | tf_op jit(solution)/shard_map/pallas_call | solution.py:174
  146.2 4.2 %all-to-all-done.4.back_ref = bf16[16,2,40,512]{3,2,1,0:T(8,128)(2,1)S(1)} async-done(((bf16[16,2,40,512]{3,2,1,0:T(8,128)(2,1)}), bf16[16,2,40,512]{3,2,1,0:T(8,128)(2,1)S(1)}, u32[]{:S(2)}, u32[]{:S(2)}) %all-to-all-start.4) | async-done | bytes 1310752 | tf_op jit(solution)/shard_map/all_to_all | solution.py:258
  150.4 4.8 %all-to-all-start.2 = ((bf16[16,2,40,512]{3,2,1,0:T(8,128)(2,1)}), bf16[16,2,40,512]{3,2,1,0:T(8,128)(2,1)S(1)}, u32[]{:S(2)}, u32[]{:S(2)}) async-start(bf16[16,2,40,512]{3,2,1,0:T(8,128)(2,1)} %bitcast.26), calls=%async_computation.2 | async-start | bytes 2621440 | tf_op jit(solution)/shard_map/all_to_all | solution.py:258
  155.3 1.6 shard_map.75.refs_0_
  156.9 16.9 %all-to-all-done.2.back_ref = bf16[16,2,40,512]{3,2,1,0:T(8,128)(2,1)S(1)} async-done(((bf16[16,2,40,512]{3,2,1,0:T(8,128)(2,1)}), bf16[16,2,40,512]{3,2,1,0:T(8,128)(2,1)S(1)}, u32[]{:S(2)}, u32[]{:S(2)}) %all-to-all-start.2) | async-done | bytes 1310752 | tf_op jit(solution)/shard_map/all_to_all | solution.py:258
  173.8 1.6 shard_map.76
  (69 shorter events, 2.4 us)
Async XLA Ops:
  1.0 8.1 %collective-permute-start = (bf16[512,256]{1,0:T(8,128)(2,1)S(1)}, bf16[512,256]{1,0:T(8,128)(2,1)S(1)}, u32[]{:S(2)}, u32[]{:S(2)}) collective-permute-start(bf16[512,256]{1,0:T(8,128)(2,1)S(1)} %constant_dynamic-slice_fusion), channel_id=1, source_target_pairs={{0,8},{8,0},{1,9},{9,1},{2,10},{10,2},{3,11},{11,3},{4,12},{12,4},... | collective-permute-start | bytes 786440 | tf_op jit(solution)/shard_map/over_pair_0/ppermute | solution.py:284
  2.9 9.4 %copy-start.17 = (bf16[1280]{0:T(1024)(128)(2,1)S(1)}, bf16[1280]{0:T(1024)(128)(2,1)}, u32[]{:S(2)}) copy-start(bf16[1280]{0:T(1024)(128)(2,1)} %param.9) | copy-start | bytes 7684
  2.9 15.7 %copy-start.1 = (bf16[2,256,8192]{2,1,0:T(8,128)(2,1)S(1)}, bf16[2,256,8192]{2,1,0:T(8,128)(2,1)}, u32[]{:S(2)}) copy-start(bf16[2,256,8192]{2,1,0:T(8,128)(2,1)} %param.7) | copy-start | bytes 25165828
  9.1 15.1 %copy-start.14 = (bf16[512,256]{1,0:T(8,128)(2,1)}, bf16[512,256]{1,0:T(8,128)(2,1)S(1)}, u32[]{:S(2)}) copy-start(bf16[512,256]{1,0:T(8,128)(2,1)S(1)} %collective-permute-done.refs_0_) | copy-start | bytes 786436
  9.1 9.6 %collective-permute-start.3 = (bf16[512,256]{1,0:T(8,128)(2,1)S(1)}, bf16[512,256]{1,0:T(8,128)(2,1)}, u32[]{:S(2)}, u32[]{:S(2)}) collective-permute-start(bf16[512,256]{1,0:T(8,128)(2,1)S(1)} %collective-permute-done.refs_0_), channel_id=1, source_target_pairs={{0,32},{16,48},{32,64},{48,80},{64,96},{80,112},{96,0},{112,16},{1... | collective-permute-start | bytes 786440 | tf_op jit(solution)/shard_map/from_below_0/ppermute | solution.py:287
  12.3 12.0 %collective-permute-start.4 = (bf16[512,256]{1,0:T(8,128)(2,1)S(1)}, bf16[512,256]{1,0:T(8,128)(2,1)}, u32[]{:S(2)}, u32[]{:S(2)}) collective-permute-start(bf16[512,256]{1,0:T(8,128)(2,1)S(1)} %collective-permute-done.refs_0_), channel_id=1, source_target_pairs={{32,0},{48,16},{64,32},{80,48},{96,64},{112,80},{0,96},{16,112},{3... | collective-permute-start | bytes 786440 | tf_op jit(solution)/shard_map/from_above_0/ppermute | solution.py:289
  14.6 16.4 %collective-permute-start.15 = (bf16[512,256]{1,0:T(8,128)(2,1)S(1)}, bf16[512,256]{1,0:T(8,128)(2,1)}, u32[]{:S(2)}, u32[]{:S(2)}) collective-permute-start(bf16[512,256]{1,0:T(8,128)(2,1)S(1)} %collective-permute-done.refs_0_), channel_id=1, source_target_pairs={{0,16},{16,0},{32,48},{48,32},{64,80},{80,64},{96,112},{112,96},{1... | collective-permute-start | bytes 786440 | tf_op jit(solution)/shard_map/from_twin_0/ppermute | solution.py:299
  14.6 14.3 %collective-permute-start.1 = (bf16[512,512]{1,0:T(8,128)(2,1)S(1)}, bf16[512,512]{1,0:T(8,128)(2,1)S(1)}, u32[]{:S(2)}, u32[]{:S(2)}) collective-permute-start(bf16[512,512]{1,0:T(8,128)(2,1)S(1)} %get-tuple-element.13), channel_id=1, source_target_pairs={{0,8},{8,0},{1,9},{9,1},{2,10},{10,2},{3,11},{11,3},{4,12},{12,4},... | collective-permute-start | bytes 1572872 | tf_op jit(solution)/shard_map/over_pair_1/ppermute | solution.py:284
  18.7 8.0 %collective-permute-start.5 = (bf16[512,256]{1,0:T(8,128)(2,1)}, bf16[512,256]{1,0:T(8,128)(2,1)S(1)}, u32[]{:S(2)}, u32[]{:S(2)}) collective-permute-start(bf16[512,256]{1,0:T(8,128)(2,1)} %collective-permute-done.3.refs_1_), channel_id=1, source_target_pairs={{0,32},{16,48},{32,64},{48,80},{64,96},{80,112},{96,0},{112,16},{1... | collective-permute-start | bytes 786440 | tf_op jit(solution)/shard_map/from_opposite_0/ppermute | solution.py:293
  18.7 13.5 %collective-permute-start.16 = (bf16[512,256]{1,0:T(8,128)(2,1)}, bf16[512,256]{1,0:T(8,128)(2,1)}, u32[]{:S(2)}, u32[]{:S(2)}) collective-permute-start(bf16[512,256]{1,0:T(8,128)(2,1)} %collective-permute-done.3.refs_1_), channel_id=1, source_target_pairs={{0,16},{16,0},{32,48},{48,32},{64,80},{80,64},{96,112},{112,96},{1... | collective-permute-start | bytes 786440 | tf_op jit(solution)/shard_map/from_twin_0/ppermute | solution.py:299
  24.3 9.5 %collective-permute-start.17 = (bf16[512,256]{1,0:T(8,128)(2,1)}, bf16[512,256]{1,0:T(8,128)(2,1)}, u32[]{:S(2)}, u32[]{:S(2)}) collective-permute-start(bf16[512,256]{1,0:T(8,128)(2,1)} %collective-permute-done.4.refs_2_), channel_id=1, source_target_pairs={{0,16},{16,0},{32,48},{48,32},{64,80},{80,64},{96,112},{112,96},{1... | collective-permute-start | bytes 786440 | tf_op jit(solution)/shard_map/from_twin_0/ppermute | solution.py:299
  26.6 4.3 %copy-start.15 = (bf16[512,256]{1,0:T(8,128)(2,1)}, bf16[512,256]{1,0:T(8,128)(2,1)S(1)}, u32[]{:S(2)}) copy-start(bf16[512,256]{1,0:T(8,128)(2,1)S(1)} %collective-permute-done.5.refs_3_) | copy-start | bytes 786436
  28.9 23.8 %copy-start.5 = (bf16[512,512]{1,0:T(8,128)(2,1)}, bf16[512,512]{1,0:T(8,128)(2,1)S(1)}, u32[]{:S(2)}) copy-start(bf16[512,512]{1,0:T(8,128)(2,1)S(1)} %collective-permute-done.1.refs_0_) | copy-start | bytes 1572868
  28.9 13.6 %collective-permute-start.7 = (bf16[512,512]{1,0:T(8,128)(2,1)S(1)}, bf16[512,512]{1,0:T(8,128)(2,1)S(1)}, u32[]{:S(2)}, u32[]{:S(2)}) collective-permute-start(bf16[512,512]{1,0:T(8,128)(2,1)S(1)} %collective-permute-done.1.refs_0_), channel_id=1, source_target_pairs={{32,0},{48,16},{64,32},{80,48},{96,64},{112,80},{0,96},{16,112},{3... | collective-permute-start | bytes 1572872 | tf_op jit(solution)/shard_map/from_above_1/ppermute | solution.py:289
  30.9 14.8 %collective-permute-start.6 = (bf16[512,512]{1,0:T(8,128)(2,1)S(1)}, bf16[512,512]{1,0:T(8,128)(2,1)S(1)}, u32[]{:S(2)}, u32[]{:S(2)}) collective-permute-start(bf16[512,512]{1,0:T(8,128)(2,1)S(1)} %collective-permute-done.1.refs_0_), channel_id=1, source_target_pairs={{0,32},{16,48},{32,64},{48,80},{64,96},{80,112},{96,0},{112,16},{1... | collective-permute-start | bytes 1572872 | tf_op jit(solution)/shard_map/from_below_1/ppermute | solution.py:287
  31.0 14.7 %collective-permute-start.2 = (bf16[512,512]{1,0:T(8,128)(2,1)S(1)}, bf16[512,512]{1,0:T(8,128)(2,1)S(1)}, u32[]{:S(2)}, u32[]{:S(2)}) collective-permute-start(bf16[512,512]{1,0:T(8,128)(2,1)S(1)} %get-tuple-element.14), channel_id=1, source_target_pairs={{0,8},{8,0},{1,9},{9,1},{2,10},{10,2},{3,11},{11,3},{4,12},{12,4},... | collective-permute-start | bytes 1572872 | tf_op jit(solution)/shard_map/over_pair_2/ppermute | solution.py:284
  32.2 1.7 collective-permute-start.18
  33.9 0.7 copy-start.16
  42.5 10.3 %copy-start.7 = (bf16[512,512]{1,0:T(8,128)(2,1)}, bf16[512,512]{1,0:T(8,128)(2,1)S(1)}, u32[]{:S(2)}) copy-start(bf16[512,512]{1,0:T(8,128)(2,1)S(1)} %collective-permute-done.7.refs_2_) | copy-start | bytes 1572868
  42.5 13.9 %collective-permute-start.19 = (bf16[512,512]{1,0:T(8,128)(2,1)S(1)}, bf16[512,512]{1,0:T(8,128)(2,1)}, u32[]{:S(2)}, u32[]{:S(2)}) collective-permute-start(bf16[512,512]{1,0:T(8,128)(2,1)S(1)} %collective-permute-done.7.refs_2_), channel_id=1, source_target_pairs={{32,0},{48,16},{64,32},{80,48},{96,64},{112,80},{0,96},{16,112},{3... | collective-permute-start | bytes 1572872 | tf_op jit(solution)/shard_map/from_opposite_1/ppermute | solution.py:293
  45.6 7.7 %copy-start.8 = (bf16[512,512]{1,0:T(8,128)(2,1)}, bf16[512,512]{1,0:T(8,128)(2,1)S(1)}, u32[]{:S(2)}) copy-start(bf16[512,512]{1,0:T(8,128)(2,1)S(1)} %collective-permute-done.6.refs_1_) | copy-start | bytes 1572868
  45.7 38.7 %copy-start.6 = (bf16[512,512]{1,0:T(8,128)(2,1)}, bf16[512,512]{1,0:T(8,128)(2,1)S(1)}, u32[]{:S(2)}) copy-start(bf16[512,512]{1,0:T(8,128)(2,1)S(1)} %collective-permute-done.2.refs_0_) | copy-start | bytes 1572868
  45.7 14.3 %collective-permute-start.8 = (bf16[512,512]{1,0:T(8,128)(2,1)S(1)}, bf16[512,512]{1,0:T(8,128)(2,1)}, u32[]{:S(2)}, u32[]{:S(2)}) collective-permute-start(bf16[512,512]{1,0:T(8,128)(2,1)S(1)} %collective-permute-done.2.refs_0_), channel_id=1, source_target_pairs={{0,32},{16,48},{32,64},{48,80},{64,96},{80,112},{96,0},{112,16},{1... | collective-permute-start | bytes 1572872 | tf_op jit(solution)/shard_map/from_below_2/ppermute | solution.py:287
  52.8 14.9 %collective-permute-start.20 = (bf16[512,512]{1,0:T(8,128)(2,1)S(1)}, bf16[512,512]{1,0:T(8,128)(2,1)S(1)}, u32[]{:S(2)}, u32[]{:S(2)}) collective-permute-start(bf16[512,512]{1,0:T(8,128)(2,1)S(1)} %collective-permute-done.1.refs_0_), channel_id=1, source_target_pairs={{0,16},{16,0},{32,48},{48,32},{64,80},{80,64},{96,112},{112,96},{1... | collective-permute-start | bytes 1572872 | tf_op jit(solution)/shard_map/from_twin_1/ppermute | solution.py:299
  52.8 16.7 %collective-permute-start.22 = (bf16[512,512]{1,0:T(8,128)(2,1)S(1)}, bf16[512,512]{1,0:T(8,128)(2,1)}, u32[]{:S(2)}, u32[]{:S(2)}) collective-permute-start(bf16[512,512]{1,0:T(8,128)(2,1)S(1)} %collective-permute-done.7.refs_2_), channel_id=1, source_target_pairs={{0,16},{16,0},{32,48},{48,32},{64,80},{80,64},{96,112},{112,96},{1... | collective-permute-start | bytes 1572872 | tf_op jit(solution)/shard_map/from_twin_1/ppermute | solution.py:299
  53.3 16.2 %collective-permute-start.21 = (bf16[512,512]{1,0:T(8,128)(2,1)S(1)}, bf16[512,512]{1,0:T(8,128)(2,1)}, u32[]{:S(2)}, u32[]{:S(2)}) collective-permute-start(bf16[512,512]{1,0:T(8,128)(2,1)S(1)} %collective-permute-done.6.refs_1_), channel_id=1, source_target_pairs={{0,16},{16,0},{32,48},{48,32},{64,80},{80,64},{96,112},{112,96},{1... | collective-permute-start | bytes 1572872 | tf_op jit(solution)/shard_map/from_twin_1/ppermute | solution.py:299
  60.0 9.5 %collective-permute-start.23 = (bf16[512,512]{1,0:T(8,128)(2,1)}, bf16[512,512]{1,0:T(8,128)(2,1)}, u32[]{:S(2)}, u32[]{:S(2)}) collective-permute-start(bf16[512,512]{1,0:T(8,128)(2,1)} %collective-permute-done.19.refs_3_), channel_id=1, source_target_pairs={{0,16},{16,0},{32,48},{48,32},{64,80},{80,64},{96,112},{112,96},{1... | collective-permute-start | bytes 1572872 | tf_op jit(solution)/shard_map/from_twin_1/ppermute | solution.py:299
  60.0 18.9 %all-to-all-start.1 = ((bf16[16,2,40,256]{3,2,1,0:T(8,128)(2,1)}), bf16[16,2,40,256]{3,2,1,0:T(8,128)(2,1)S(1)}, u32[]{:S(2)}, u32[]{:S(2)}) async-start(bf16[16,2,40,256]{3,2,1,0:T(8,128)(2,1)} %project_0.1), calls=%async_computation.1 | async-start | bytes 1310720 | tf_op jit(solution)/shard_map/route_0/all_to_all | solution.py:258
  67.4 17.5 %collective-permute-start.9 = (bf16[512,512]{1,0:T(8,128)(2,1)S(1)}, bf16[512,512]{1,0:T(8,128)(2,1)}, u32[]{:S(2)}, u32[]{:S(2)}) collective-permute-start(bf16[512,512]{1,0:T(8,128)(2,1)S(1)} %collective-permute-done.2.refs_0_), channel_id=1, source_target_pairs={{32,0},{48,16},{64,32},{80,48},{96,64},{112,80},{0,96},{16,112},{3... | collective-permute-start | bytes 1572872 | tf_op jit(solution)/shard_map/from_above_2/ppermute | solution.py:289
  67.6 1.8 %copy-start.9 = (bf16[512,512]{1,0:T(8,128)(2,1)}, bf16[512,512]{1,0:T(8,128)(2,1)S(1)}, u32[]{:S(2)}) copy-start(bf16[512,512]{1,0:T(8,128)(2,1)S(1)} %collective-permute-done.20.refs_4_) | copy-start | bytes 1572868
  67.6 17.4 %collective-permute-start.10 = (bf16[512,512]{1,0:T(8,128)(2,1)}, bf16[512,512]{1,0:T(8,128)(2,1)}, u32[]{:S(2)}, u32[]{:S(2)}) collective-permute-start(bf16[512,512]{1,0:T(8,128)(2,1)} %collective-permute-done.8.refs_1_), channel_id=1, source_target_pairs={{0,32},{16,48},{32,64},{48,80},{64,96},{80,112},{96,0},{112,16},{1... | collective-permute-start | bytes 1572872 | tf_op jit(solution)/shard_map/from_opposite_2/ppermute | solution.py:293
  78.9 18.4 %copy-start.2 = (bf16[16,2,40,256]{3,2,1,0:T(8,128)(2,1)}, bf16[16,2,40,256]{3,2,1,0:T(8,128)(2,1)S(1)}, u32[]{:S(2)}) copy-start(bf16[16,2,40,256]{3,2,1,0:T(8,128)(2,1)S(1)} %all-to-all-done.1) | copy-start | bytes 1966084
  78.9 24.6 %all-to-all-start.3 = ((bf16[16,2,40,512]{3,2,1,0:T(8,128)(2,1)}), bf16[16,2,40,512]{3,2,1,0:T(8,128)(2,1)S(1)}, u32[]{:S(2)}, u32[]{:S(2)}) async-start(bf16[16,2,40,512]{3,2,1,0:T(8,128)(2,1)} %project_1.1), calls=%async_computation.3 | async-start | bytes 2621440 | tf_op jit(solution)/shard_map/route_1/all_to_all | solution.py:258
  84.4 24.0 %copy-start = (s32[40]{0:T(128)S(1)}, s32[40]{0:T(128)}, u32[]{:S(2)}) copy-start(s32[40]{0:T(128)} %fill_ref.3) | copy-start | bytes 484
  84.4 2.0 %collective-permute-start.11 = (bf16[512,512]{1,0:T(8,128)(2,1)S(1)}, bf16[512,512]{1,0:T(8,128)(2,1)S(1)}, u32[]{:S(2)}, u32[]{:S(2)}) collective-permute-start(bf16[512,512]{1,0:T(8,128)(2,1)S(1)} %collective-permute-done.2.refs_0_), channel_id=1, source_target_pairs={{0,16},{16,0},{32,48},{48,32},{64,80},{80,64},{96,112},{112,96},{1... | collective-permute-start | bytes 1572872 | tf_op jit(solution)/shard_map/from_twin_2/ppermute | solution.py:299
  84.5 2.9 %collective-permute-start.12 = (bf16[512,512]{1,0:T(8,128)(2,1)}, bf16[512,512]{1,0:T(8,128)(2,1)S(1)}, u32[]{:S(2)}, u32[]{:S(2)}) collective-permute-start(bf16[512,512]{1,0:T(8,128)(2,1)} %collective-permute-done.8.refs_1_), channel_id=1, source_target_pairs={{0,16},{16,0},{32,48},{48,32},{64,80},{80,64},{96,112},{112,96},{1... | collective-permute-start | bytes 1572872 | tf_op jit(solution)/shard_map/from_twin_2/ppermute | solution.py:299
  85.0 3.1 %collective-permute-start.13 = (bf16[512,512]{1,0:T(8,128)(2,1)}, bf16[512,512]{1,0:T(8,128)(2,1)S(1)}, u32[]{:S(2)}, u32[]{:S(2)}) collective-permute-start(bf16[512,512]{1,0:T(8,128)(2,1)} %collective-permute-done.9.refs_2_), channel_id=1, source_target_pairs={{0,16},{16,0},{32,48},{48,32},{64,80},{80,64},{96,112},{112,96},{1... | collective-permute-start | bytes 1572872 | tf_op jit(solution)/shard_map/from_twin_2/ppermute | solution.py:299
  85.1 3.8 %collective-permute-start.14 = (bf16[512,512]{1,0:T(8,128)(2,1)}, bf16[512,512]{1,0:T(8,128)(2,1)S(1)}, u32[]{:S(2)}, u32[]{:S(2)}) collective-permute-start(bf16[512,512]{1,0:T(8,128)(2,1)} %collective-permute-done.10.refs_3_), channel_id=1, source_target_pairs={{0,16},{16,0},{32,48},{48,32},{64,80},{80,64},{96,112},{112,96},{1... | collective-permute-start | bytes 1572872 | tf_op jit(solution)/shard_map/from_twin_2/ppermute | solution.py:299
  86.4 2.5 %copy-start.10 = (bf16[512,512]{1,0:T(8,128)(2,1)}, bf16[512,512]{1,0:T(8,128)(2,1)S(1)}, u32[]{:S(2)}) copy-start(bf16[512,512]{1,0:T(8,128)(2,1)S(1)} %collective-permute-done.11.refs_4_) | copy-start | bytes 1572868
  87.4 1.5 copy-start.11
  88.1 0.8 copy-start.12
  88.9 0.8 copy-start.13
  103.6 5.2 %copy-start.3 = (bf16[16,2,40,512]{3,2,1,0:T(8,128)(2,1)}, bf16[16,2,40,512]{3,2,1,0:T(8,128)(2,1)S(1)}, u32[]{:S(2)}) copy-start(bf16[16,2,40,512]{3,2,1,0:T(8,128)(2,1)S(1)} %all-to-all-done.3) | copy-start | bytes 3932164
  103.6 23.3 %all-to-all-start = ((bf16[16,2,40,512]{3,2,1,0:T(8,128)(2,1)}), bf16[16,2,40,512]{3,2,1,0:T(8,128)(2,1)S(1)}, u32[]{:S(2)}, u32[]{:S(2)}) async-start(bf16[16,2,40,512]{3,2,1,0:T(8,128)(2,1)} %project_2.1), calls=%async_computation | async-start | bytes 2621440 | tf_op jit(solution)/shard_map/route_2/all_to_all | solution.py:258
  126.9 4.8 %copy-start.4 = (bf16[16,2,40,512]{3,2,1,0:T(8,128)(2,1)}, bf16[16,2,40,512]{3,2,1,0:T(8,128)(2,1)S(1)}, u32[]{:S(2)}) copy-start(bf16[16,2,40,512]{3,2,1,0:T(8,128)(2,1)S(1)} %all-to-all-done) | copy-start | bytes 3932164
  126.9 23.5 %all-to-all-start.4 = ((bf16[16,2,40,512]{3,2,1,0:T(8,128)(2,1)}), bf16[16,2,40,512]{3,2,1,0:T(8,128)(2,1)S(1)}, u32[]{:S(2)}, u32[]{:S(2)}) async-start(bf16[16,2,40,512]{3,2,1,0:T(8,128)(2,1)} %bitcast.27), calls=%async_computation.4 | async-start | bytes 2621440 | tf_op jit(solution)/shard_map/all_to_all | solution.py:258
  150.4 23.4 %all-to-all-start.2 = ((bf16[16,2,40,512]{3,2,1,0:T(8,128)(2,1)}), bf16[16,2,40,512]{3,2,1,0:T(8,128)(2,1)S(1)}, u32[]{:S(2)}, u32[]{:S(2)}) async-start(bf16[16,2,40,512]{3,2,1,0:T(8,128)(2,1)} %bitcast.26), calls=%async_computation.2 | async-start | bytes 2621440 | tf_op jit(solution)/shard_map/all_to_all | solution.py:258
